TPU v7x, 128 devices: a whole 4x4x4 slice. The times are simulated.
128 devices in a mesh: ctx: 8 (over x, core), head: 16 (over y, z).
Axes of the slice: x: 4, y: 4, z: 4, core: 2. Of those that a mesh axis runs over, the one named last changes fastest.
Arguments:
- q_latent: bfloat16 [1024, 128, 576], P(('ctx', 'head')), may hold values from -84 to 84
- index_query: bfloat16 [1024, 64, 128], P('head'), may hold values from -6 to 6
- index_weight: float32 [1024, 64], P('head'), may hold values from -0.75 to 0.75
- index_keys: bfloat16 [16384, 128], P('ctx'), may hold values from -6 to 6
- latent_cache: bfloat16 [16384, 576], P('ctx'), may hold values from -6 to 6
- block_ids: int32 [8, 32], replicated, may hold values from 0 to 255, as said below
- block_counts: int32 [8], replicated, may hold values from 24 to 32, as said below
Outputs:
- attention: bfloat16 [1024, 128, 512], P('ctx', 'head')
- index_scores: float32 [1024, 16384], P('head', 'ctx')
Inputs may be any that keep to these rules, and one draw needn't show every extreme that they name: `block_ids`: row t is query tile t's list of blocks of 64 positions. Its first block_counts[t] entries are distinct, lie at or before the tile's own last block and include the 2 blocks that hold the tile's own queries; of these counted entries at most 8 lie in one context shard of 32 blocks, and exactly 8 lie in the shard of the newest positions. Entries after the count are arbitrary block ids. `block_counts`: some tile has all 32 entries counted.
All inputs are finite; a program needn't handle non-finite values.
Results may differ from a plain program's by a relative error of at most 0.0034.
Values may be sent and summed in bfloat16 or wider, within the bound.
No kernel may reach another device: no remote copies, remote signals or barrier semaphores. Data moves between devices by JAX's collectives and lax.ppermute only.
A program may use at most 128 MiB of HBM per device.

v0:
```python
import jax
import jax.numpy as jnp
from jax import lax
from jax.sharding import PartitionSpec as P

ROPE = 64
BLOCK = 64
TILE = 128
CAP = 8


softmax_scale = 192.0 ** (-0.5)


def index_block(index_query, index_weight, key_block):
    flat_query = index_query.reshape(-1, index_query.shape[2])
    raw_dots = lax.dot_general(
        flat_query, key_block, (((1,), (1,)), ((), ())), preferred_element_type=jnp.float32
    )
    gated_dots = jax.nn.relu(raw_dots * index_query.shape[2] ** (-0.5)).reshape(
        index_query.shape[0], index_query.shape[1], -1
    )
    return jnp.sum(gated_dots * index_weight[:, :, None], axis=1)


def attend_rows(query_block, key_rows, allowed, latent_width):
    rows_here = query_block.shape[0]
    heads_here = query_block.shape[1]
    flat_query = query_block.reshape(rows_here * heads_here, -1)
    raw_scores = lax.dot_general(
        flat_query, key_rows, (((1,), (1,)), ((), ())), preferred_element_type=jnp.float32
    )
    raw_scores = raw_scores.reshape(rows_here, heads_here, -1) * softmax_scale
    masked = jnp.where(allowed[:, None, :], raw_scores, -jnp.inf)
    row_max = jnp.max(masked, axis=2, keepdims=True)
    exp_scores = jnp.exp(masked - row_max)
    totals = jnp.sum(exp_scores, axis=2, keepdims=True)
    weights = exp_scores.astype(jnp.bfloat16).reshape(rows_here * heads_here, -1)
    full_sum = jnp.dot(weights, key_rows, preferred_element_type=jnp.float32)
    weighted_sum = full_sum.reshape(rows_here, heads_here, -1)[:, :, :latent_width]
    return (weighted_sum / totals).astype(jnp.bfloat16)


def slot_tables(block_ids, block_counts, blocks_dev, shards, capacity):
    entry_index = jnp.arange(block_ids.shape[1], dtype=jnp.int32)
    is_valid = entry_index[None, :] < block_counts[:, None]
    shard_of = block_ids // blocks_dev
    local_of = block_ids - shard_of * blocks_dev
    earlier = (
        (shard_of[:, :, None] == shard_of[:, None, :])
        & is_valid[:, None, :]
        & (entry_index[None, None, :] < entry_index[None, :, None])
    )
    rank_of = jnp.sum(earlier.astype(jnp.int32), axis=2)
    shard_hit = (
        shard_of[:, :, None] == jnp.arange(shards, dtype=jnp.int32)[None, None, :]
    ) & is_valid[:, :, None]
    rank_hit = rank_of[:, :, None] == jnp.arange(capacity, dtype=jnp.int32)[None, None, :]
    slot_hits = (shard_hit[:, :, :, None] & rank_hit[:, :, None, :]).astype(jnp.int32)
    slot_local = jnp.sum(slot_hits * local_of[:, :, None, None], axis=1)
    slot_live = jnp.sum(slot_hits, axis=1) > 0
    return (slot_local, slot_live)


def piece_rows(owned_slots, first_row, count_rows):
    row_index = first_row + jnp.arange(count_rows, dtype=jnp.int32)
    slot_index = row_index // BLOCK
    return jnp.take(owned_slots, slot_index, axis=1) * BLOCK + (row_index % BLOCK)[None, :]


def body(q_latent, index_query, index_weight, index_keys, latent_cache, block_ids, block_counts):
    shards = lax.axis_size("ctx")
    groups = lax.axis_size("head")
    shard_here = lax.axis_index("ctx")
    group_here = lax.axis_index("head")
    keys_dev = latent_cache.shape[0]
    feature_width = latent_cache.shape[1]
    latent_width = feature_width - ROPE
    blocks_dev = keys_dev // BLOCK
    slot_local, slot_live = slot_tables(block_ids, block_counts, blocks_dev, shards, CAP)
    head_query = lax.all_to_all(q_latent, "head", split_axis=1, concat_axis=0, tiled=True)
    owned_slots = lax.dynamic_index_in_dim(slot_local, shard_here, axis=1, keepdims=False)
    span_rows = CAP * BLOCK
    piece_len = span_rows // groups
    row_ids = piece_rows(owned_slots, group_here * piece_len, piece_len)
    target_ids = jnp.repeat(row_ids, groups, axis=0).reshape(-1)
    outgoing = jnp.take(latent_cache, target_ids, axis=0).reshape(
        shards * groups, piece_len, feature_width
    )
    incoming = lax.all_to_all(outgoing, ("ctx", "head"), split_axis=0, concat_axis=0, tiled=True)
    gathered = incoming.reshape(shards, span_rows, feature_width)
    key_span = 8 * BLOCK
    query_rows = index_query.shape[0]

    def score_span(block_index, scores_sofar):
        key_block = lax.dynamic_slice_in_dim(index_keys, block_index * key_span, key_span, 0)
        block_scores = index_block(index_query, index_weight, key_block)
        return lax.dynamic_update_slice_in_dim(
            scores_sofar, block_scores, block_index * key_span, 1
        )

    index_scores = lax.fori_loop(
        0, keys_dev // key_span, score_span, jnp.zeros((query_rows, keys_dev), jnp.float32)
    )
    recv_local = lax.dynamic_index_in_dim(slot_local, shard_here, axis=0, keepdims=False)
    recv_live = lax.dynamic_index_in_dim(slot_live, shard_here, axis=0, keepdims=False)
    shard_base = jnp.arange(shards, dtype=jnp.int32)[:, None] * blocks_dev + recv_local
    key_pos = (
        shard_base[:, :, None] * BLOCK + jnp.arange(BLOCK, dtype=jnp.int32)[None, None, :]
    ).reshape(-1)
    key_live = jnp.broadcast_to(recv_live[:, :, None], recv_live.shape + (BLOCK,)).reshape(-1)
    query_pos = shards * (keys_dev - TILE) + shard_here * TILE + jnp.arange(TILE, dtype=jnp.int32)
    allowed = key_live[None, :] & (key_pos[None, :] <= query_pos[:, None])
    key_rows = gathered.reshape(-1, feature_width)
    attention = attend_rows(head_query, key_rows, allowed, latent_width)
    return (attention, index_scores)


def solution(mesh):
    return jax.shard_map(
        body,
        mesh=mesh,
        in_specs=(
            P(("ctx", "head"), None, None),
            P("head", None, None),
            P("head", None),
            P("ctx", None),
            P("ctx", None),
            P(),
            P(),
        ),
        out_specs=(P("ctx", "head", None), P("head", "ctx")),
        check_vma=False,
    )
```

profile of v0, /device:TPU:1, one launch (start us, length us, event | category | flops | bytes accessed | tf_op | source)
XLA Modules:
  0.0 162.4 jit_solution(8896964466984360652)
XLA Ops:
  0.6 2.9 %copy.37 = bf16[8,128,576]{2,0,1:T(8,128)(2,1)} copy(bf16[8,128,576]{1,2,0:T(8,128)(2,1)} %param.9) | data formatting | bytes 2359296 | tf_op args[0]
  3.5 8.6 %all-to-all-start.1 = ((bf16[8,128,576]{2,0,1:T(8,128)(2,1)}), bf16[8,128,576]{2,0,1:T(8,128)(2,1)}, u32[]{:S(2)}, u32[]{:S(2)}) async-start(bf16[8,128,576]{2,0,1:T(8,128)(2,1)} %copy.37), calls=%async_computation.1 | async-start | bytes 2621440 | tf_op jit(solution)/shard_map/all_to_all | solution.py:81
  12.3 0.7 multiply_subtract_fusion
  13.0 0.7 iota_compare_fusion.3
  13.7 0.3 convert_reduce_fusion
  14.0 2.2 %fusion.17 = (s32[8,8,8]{2,1,0:T(8,128)S(1)}, s32[8,8,8]{2,1,0:T(8,128)S(1)}) fusion(pred[8,32,8]{1,2,0:T(8,128)(4,1)S(1)} %get-tuple-element.117, pred[8,32,8]{1,2,0:T(8,128)(4,1)S(1)} %get-tuple-element.118, s32[8,32]{1,0:T(8,128)S(1)} %get-tuple-element.113), kind=kLoop, calls=%fused_computation.24 | loop fusion | flops 80896 | bytes 9216 | tf_op jit(solution)/shard_map/reduce_sum | solution.py:61
  16.3 0.1 copy.34
  16.4 0.6 gather_fusion
  16.9 0.1 add_bitcast_fusion
  17.0 0.1 copy.35
  17.1 0.1 reshape_reshape.9
  17.3 3.1 %copy.36 = bf16[2048,576]{1,0:T(8,128)(2,1)S(1)} copy(bf16[2048,576]{0,1:T(8,128)(2,1)} %param.13) | data formatting | bytes 4718592 | tf_op args[4]
  20.4 0.1 fusion.24
  20.4 0.1 iota_add_fusion
  20.5 0.1 add.175
  20.6 0.1 broadcast_in_dim.42
  20.7 0.1 and.124
  20.8 17.6 %gather_fusion.1 = bf16[4096,576]{1,0:T(8,128)(2,1)} fusion(bf16[2048,576]{1,0:T(8,128)(2,1)S(1)} %copy.36, s32[4096]{0:T(1024)S(1)} %broadcast_clamp_fusion), kind=kCustom, calls=%fused_computation.1 | custom fusion | bytes 9453568 | tf_op jit(solution)/shard_map/jit(_take)/gather | solution.py:87
  38.4 6.2 %broadcast_select_fusion = bf16[128,32,576]{2,1,0:T(8,128)(2,1)} fusion(bf16[128,32,576]{2,1,0:T(8,128)(2,1)} %bitcast.81, pred[128,32]{1,0:T(8,128)(4,1)S(1)} %fusion.21), kind=kLoop, calls=%fused_computation.18 | loop fusion | flops 2359296 | bytes 9441280 | tf_op jit(solution)/shard_map/jit(_take)/select_n | solution.py:87
  44.6 0.0 copy-start
  44.6 0.0 copy-start.2
  44.6 0.0 all-to-all-done.1
  44.6 10.5 %all-to-all-start = ((bf16[128,32,576]{2,1,0:T(8,128)(2,1)}), bf16[128,32,576]{2,1,0:T(8,128)(2,1)}, u32[]{:S(2)}, u32[]{:S(2)}) async-start(bf16[128,32,576]{2,1,0:T(8,128)(2,1)} %broadcast_select_fusion), calls=%async_computation | async-start | bytes 10485760 | tf_op jit(solution)/shard_map/all_to_all | solution.py:90
  55.1 0.4 compare_and_fusion
  55.5 0.0 copy-done
  55.6 0.0 copy-done.2
  55.6 73.6 %while.13 = (s32[]{:T(128)}, f32[64,2048]{1,0:T(8,128)S(1)}, bf16[2048,128]{1,0:T(8,128)(2,1)}, bf16[64,64,128]{2,1,0:T(8,128)(2,1)S(1)}, f32[64,64]{1,0:T(8,128...) while((s32[]{:T(128)}, f32[64,2048]{1,0:T(8,128)S(1)}, bf16[2048,128]{1,0:T(8,128)(2,1)}, ...), condition=%wide.region_7.8_spmd, body=%wide.region_5.7_spmd.sunk | while | flops 545226752 | bytes 35143828 | solution.py:102
  55.6 5.4 %maximum_bitcast_fusion.2 = f32[4096,512]{0,1:T(8,128)} fusion(bf16[4096,128]{1,0:T(8,128)(2,1)S(1)} %bitcast.80, bf16[2048,128]{1,0:T(8,128)(2,1)} %get-tuple-element.170, s32[]{:T(128)S(6)} %select_n.150), kind=kOutput, calls=%fused_computation.3.clone.1 | convolution fusion | flops 541065216 | bytes 9568260 | tf_op jit(solution)/shard_map/while/body/eval_jaxpr/dot_general | solution.py:17
  61.0 9.0 %copy.45 = f32[4096,512]{1,0:T(8,128)} copy(f32[4096,512]{0,1:T(8,128)} %maximum_bitcast_fusion.2) | data formatting | bytes 16777216 | tf_op jit(solution)/shard_map/while/body/eval_jaxpr/jit(relu)/max | solution.py:20
  70.0 4.0 %multiply_reduce_fusion.2 = f32[64,512]{1,0:T(8,128)S(1)} fusion(f32[64,64]{1,0:T(8,128)S(1)} %get-tuple-element.172, f32[4096,512]{1,0:T(8,128)} %copy.45), kind=kLoop, calls=%fused_computation.2.clone.1 | loop fusion | flops 4161536 | bytes 8536064 | tf_op jit(solution)/shard_map/while/body/eval_jaxpr/reduce_sum | solution.py:23
  74.0 5.4 %maximum_bitcast_fusion.2 = f32[4096,512]{0,1:T(8,128)} fusion(bf16[4096,128]{1,0:T(8,128)(2,1)S(1)} %bitcast.80, bf16[2048,128]{1,0:T(8,128)(2,1)} %get-tuple-element.170, s32[]{:T(128)S(6)} %select_n.150), kind=kOutput, calls=%fused_computation.3.clone.1 | convolution fusion | flops 541065216 | bytes 9568260 | tf_op jit(solution)/shard_map/while/body/eval_jaxpr/dot_general | solution.py:17
  79.4 9.0 %copy.45 = f32[4096,512]{1,0:T(8,128)} copy(f32[4096,512]{0,1:T(8,128)} %maximum_bitcast_fusion.2) | data formatting | bytes 16777216 | tf_op jit(solution)/shard_map/while/body/eval_jaxpr/jit(relu)/max | solution.py:20
  88.4 4.0 %multiply_reduce_fusion.2 = f32[64,512]{1,0:T(8,128)S(1)} fusion(f32[64,64]{1,0:T(8,128)S(1)} %get-tuple-element.172, f32[4096,512]{1,0:T(8,128)} %copy.45), kind=kLoop, calls=%fused_computation.2.clone.1 | loop fusion | flops 4161536 | bytes 8536064 | tf_op jit(solution)/shard_map/while/body/eval_jaxpr/reduce_sum | solution.py:23
  92.4 5.4 %maximum_bitcast_fusion.2 = f32[4096,512]{0,1:T(8,128)} fusion(bf16[4096,128]{1,0:T(8,128)(2,1)S(1)} %bitcast.80, bf16[2048,128]{1,0:T(8,128)(2,1)} %get-tuple-element.170, s32[]{:T(128)S(6)} %select_n.150), kind=kOutput, calls=%fused_computation.3.clone.1 | convolution fusion | flops 541065216 | bytes 9568260 | tf_op jit(solution)/shard_map/while/body/eval_jaxpr/dot_general | solution.py:17
  97.8 9.0 %copy.45 = f32[4096,512]{1,0:T(8,128)} copy(f32[4096,512]{0,1:T(8,128)} %maximum_bitcast_fusion.2) | data formatting | bytes 16777216 | tf_op jit(solution)/shard_map/while/body/eval_jaxpr/jit(relu)/max | solution.py:20
  106.8 4.0 %multiply_reduce_fusion.2 = f32[64,512]{1,0:T(8,128)S(1)} fusion(f32[64,64]{1,0:T(8,128)S(1)} %get-tuple-element.172, f32[4096,512]{1,0:T(8,128)} %copy.45), kind=kLoop, calls=%fused_computation.2.clone.1 | loop fusion | flops 4161536 | bytes 8536064 | tf_op jit(solution)/shard_map/while/body/eval_jaxpr/reduce_sum | solution.py:23
  110.8 5.4 %maximum_bitcast_fusion.2 = f32[4096,512]{0,1:T(8,128)} fusion(bf16[4096,128]{1,0:T(8,128)(2,1)S(1)} %bitcast.80, bf16[2048,128]{1,0:T(8,128)(2,1)} %get-tuple-element.170, s32[]{:T(128)S(6)} %select_n.150), kind=kOutput, calls=%fused_computation.3.clone.1 | convolution fusion | flops 541065216 | bytes 9568260 | tf_op jit(solution)/shard_map/while/body/eval_jaxpr/dot_general | solution.py:17
  116.2 9.0 %copy.45 = f32[4096,512]{1,0:T(8,128)} copy(f32[4096,512]{0,1:T(8,128)} %maximum_bitcast_fusion.2) | data formatting | bytes 16777216 | tf_op jit(solution)/shard_map/while/body/eval_jaxpr/jit(relu)/max | solution.py:20
  125.2 4.0 %multiply_reduce_fusion.2 = f32[64,512]{1,0:T(8,128)S(1)} fusion(f32[64,64]{1,0:T(8,128)S(1)} %get-tuple-element.172, f32[4096,512]{1,0:T(8,128)} %copy.45), kind=kLoop, calls=%fused_computation.2.clone.1 | loop fusion | flops 4161536 | bytes 8536064 | tf_op jit(solution)/shard_map/while/body/eval_jaxpr/reduce_sum | solution.py:23
  129.2 0.0 copy-start.3
  129.2 1.7 %copy.39 = bf16[16,8,8,576]{3,2,1,0:T(8,128)(2,1)S(1)} copy(bf16[16,8,8,576]{3,1,2,0:T(8,128)(2,1)} %bitcast.15) | data formatting | bytes 2359296 | tf_op jit(solution)/shard_map/all_to_all | solution.py:81
  130.9 0.0 all-to-all-done
  131.0 9.8 %fusion.4 = (f32[1024]{0:T(1024)S(1)}, f32[4096,1024]{0,1:T(8,128)S(1)}) fusion(pred[128,4096]{1,0:T(8,128)(4,1)S(1)} %compare_and_fusion, bf16[4096,576]{1,0:T(8,128)(2,1)} %bitcast.12, bf16[1024,576]{1,0:T(8,128)(2,1)S(1)} %bitcast.82), kind=kOutput, calls=%fused_computation.11 | convolution fusion | flops 4844420096 | bytes 23203840 | tf_op jit(solution)/shard_map/dot_general | solution.py:30
  140.7 0.0 copy-done.3
  140.8 0.0 copy-start.1
  140.8 5.7 %copy-done.1 = f32[4096,1024]{0,1:T(8,128)} copy-done((f32[4096,1024]{0,1:T(8,128)}, f32[4096,1024]{0,1:T(8,128)S(1)}, u32[]{:S(2)}) %copy-start.1) | copy-done | bytes 16777240
  146.5 5.5 %fusion.2 = f32[1024]{0:T(1024)S(1)} fusion(f32[4096,1024]{0,1:T(8,128)S(1)} %get-tuple-element.116, f32[1024]{0:T(1024)S(1)} %get-tuple-element.115, pred[128,4096]{1,0:T(8,128)(4,1)S(1)} %compare_and_fusion), kind=kLoop, calls=%fused_computation.9 | loop fusion | flops 16776192 | bytes 17309696 | tf_op jit(solution)/shard_map/reduce_sum | solution.py:37
  152.0 0.1 div.54
  152.1 10.3 %divide_convert_fusion = bf16[128,8,512]{2,1,0:T(8,128)(2,1)} fusion(f32[128,8]{1,0:T(8,128)S(1)} %div.54, bf16[4096,576,1]{1,0,2:T(8,128)(2,1)} %bitcast.19, f32[4096,1024]{0,1:T(8,128)} %copy-done.1, f32[1024]{0:T(1024)S(1)} %get-tuple-element.115, pred[128,4096]{1,0:T(8,128)(4,1)S(1)} %compare_and_fusion), kind=kOutput, calls=%fused_computation.20 | convolution fusion | flops 4312793088 | bytes 22552576 | tf_op jit(solution)/shard_map/dot_general | solution.py:39
  (19 shorter events, 0.3 us)
Async XLA Ops:
  3.5 41.0 %all-to-all-start.1 = ((bf16[8,128,576]{2,0,1:T(8,128)(2,1)}), bf16[8,128,576]{2,0,1:T(8,128)(2,1)}, u32[]{:S(2)}, u32[]{:S(2)}) async-start(bf16[8,128,576]{2,0,1:T(8,128)(2,1)} %copy.37), calls=%async_computation.1 | async-start | bytes 2621440 | tf_op jit(solution)/shard_map/all_to_all | solution.py:81
  44.6 11.0 %copy-start = (bf16[64,64,128]{2,1,0:T(8,128)(2,1)S(1)}, bf16[64,64,128]{2,1,0:T(8,128)(2,1)}, u32[]{:S(2)}) copy-start(bf16[64,64,128]{2,1,0:T(8,128)(2,1)} %param.10) | copy-start | bytes 3145732
  44.6 11.0 %copy-start.2 = (f32[64,64]{1,0:T(8,128)S(1)}, f32[64,64]{1,0:T(8,128)}, u32[]{:S(2)}) copy-start(f32[64,64]{1,0:T(8,128)} %param.11) | copy-start | bytes 49156
  44.6 86.4 %all-to-all-start = ((bf16[128,32,576]{2,1,0:T(8,128)(2,1)}), bf16[128,32,576]{2,1,0:T(8,128)(2,1)}, u32[]{:S(2)}, u32[]{:S(2)}) async-start(bf16[128,32,576]{2,1,0:T(8,128)(2,1)} %broadcast_select_fusion), calls=%async_computation | async-start | bytes 10485760 | tf_op jit(solution)/shard_map/all_to_all | solution.py:90
  129.2 11.5 %copy-start.3 = (f32[64,2048]{1,0:T(8,128)}, f32[64,2048]{1,0:T(8,128)S(1)}, u32[]{:S(2)}) copy-start(f32[64,2048]{1,0:T(8,128)S(1)} %get-tuple-element.100) | copy-start | bytes 1572868
  140.8 5.7 %copy-start.1 = (f32[4096,1024]{0,1:T(8,128)}, f32[4096,1024]{0,1:T(8,128)S(1)}, u32[]{:S(2)}) copy-start(f32[4096,1024]{0,1:T(8,128)S(1)} %get-tuple-element.116) | copy-start | bytes 50331652
where the time goes:
time: 164 us; the launch traced here: 162 us
  local copies, waits for them, and re-layouts  68.2 us (42%)
  matrix products  41.7 us (25%)
  other arithmetic  32.4 us (20%)
  starting transfers between devices  19.1 us (12%)
    max x4, local copies, waits for them, and re-layouts, index_block(): jax.nn.relu(raw_dots * index_query.shape[2] ** (-0.5))  35.9 us
    dot_general x4, matrix products, index_block(): lax.dot_general(flat_query, key_block, (((1,), (1,)), ((), ())), preferre...  21.5 us
    gather x1, local copies, waits for them, and re-layouts, body(): jnp.take(latent_cache, target_ids, axis=0)  17.6 us
    reduce_sum x4, other arithmetic, index_block(): return jnp.sum(gated_dots * index_weight[:, :, None], axis=1)  15.9 us
    unnamed x10, local copies, waits for them, and re-layouts  11.7 us
    all_to_all x1, starting transfers between devices, body(): lax.all_to_all(outgoing, ('ctx', 'head'), split_axis=0, concat_axis=0, ti...  10.5 us
    dot_general x1, matrix products, attend_rows(): full_sum = jnp.dot(weights, key_rows, preferred_element_type=jnp.float32)  10.3 us
    dot_general x1, matrix products, attend_rows(): lax.dot_general(flat_query, key_rows, (((1,), (1,)), ((), ())), preferred...  9.78 us
  transfers between devices with their start and end apart: 2, of which 0 were waited for; matrix products, arithmetic and copies ran while one was open for 66% of the time, Pallas kernels for 0%

commit v1 on v0

v1 whole, which is shorter than its diff:
```python
import functools

import jax
import jax.numpy as jnp
from jax import lax
from jax.experimental import pallas as pl
from jax.experimental.pallas import tpu as pltpu
from jax.sharding import PartitionSpec as P

BLOCK = 64
TILE = 128
CAP = 8
NSEL = 32
SHARDS = 8
PART = 16
SCALE = 192.0 ** (-0.5)
INDEX_SCALE = 128.0 ** (-0.5)
F32 = jnp.float32
BF16 = jnp.bfloat16
VMEM = pl.BlockSpec(memory_space=pltpu.VMEM)
SMEM = pl.BlockSpec(memory_space=pltpu.SMEM)


def iota(shape, dim):
    return lax.broadcasted_iota(jnp.int32, shape, dim)


def gather_kernel(pos_ref, ids_ref, counts_ref, cache_ref, out_ref):
    shard, row_y, row_z = pos_ref[0], pos_ref[1], pos_ref[2]
    tiles, entries = ids_ref.shape
    ids = jnp.where(iota((tiles, entries), 1) < counts_ref[...], ids_ref[...], -1)
    lane = iota((tiles, 128), 1)
    block_of_lane = lane + shard * 32
    member = jnp.zeros((tiles, 128), F32)
    for j in range(entries):
        member = jnp.where(ids[:, j : j + 1] == block_of_lane, 1.0, member)
    member = jnp.where(lane < 32, member, 0.0)
    before = (iota((128, 128), 0) < iota((128, 128), 1)).astype(BF16)
    rank = jnp.dot(member.astype(BF16), before, preferred_element_type=F32)
    rank = jnp.where(member > 0.0, rank, -1.0)
    slot = (lane >> 4).astype(F32)
    part = lane & 15
    row = jnp.where(part < 8, row_z * 8 + part, 24 + row_y * 8 + part)
    target = jnp.full((tiles, 128), -1, jnp.int32)
    for b in range(32):
        target = jnp.where(rank[:, b : b + 1] == slot, b * BLOCK + row, target)
    keys = cache_ref.shape[1]
    key_index = iota((keys, 128), 0)
    for t in range(0, tiles, 2):
        hot = jnp.concatenate(
            [(key_index == target[u : u + 1, :]).astype(F32).astype(BF16) for u in (t, t + 1)], axis=1
        )
        got = jnp.dot(cache_ref[...], hot, preferred_element_type=F32).astype(BF16)
        out_ref[t] = got[:, :128]
        out_ref[t + 1] = got[:, 128:]


def gather_parts(pos, block_ids, block_counts, cache_t):
    width, keys = cache_t.shape
    return pl.pallas_call(
        gather_kernel,
        out_shape=jax.ShapeDtypeStruct((block_ids.shape[0], width, 128), BF16),
        in_specs=[SMEM, VMEM, VMEM, VMEM],
        out_specs=VMEM,
        cost_estimate=pl.CostEstimate(
            flops=2 * width * keys * 1024, bytes_accessed=2 * width * keys * 2, transcendentals=0
        ),
        name="gather_parts",
    )(pos, block_ids, block_counts.reshape(-1, 1), cache_t)


def compact_kernel(pos_ref, ids_ref, counts_ref, parts_ref, first_ref, second_ref):
    tile = pos_ref[0]
    tiles, entries = ids_ref.shape
    ids = jnp.where(iota((tiles, entries), 1) < counts_ref[...], ids_ref[...], -1)
    mine = jnp.where(iota((tiles, entries), 0) == tile, ids, -1)
    column = iota((8, 512), 1)
    entry = (column & 255) >> 3
    part = (column & 7) + ((column >> 8) << 3)
    source = entry * PART + part
    end = jnp.zeros((1, 1), jnp.int32)
    for s in range(SHARDS):
        here = jnp.sum((mine >> 5 == s).astype(F32), axis=(0, 1), keepdims=True).astype(jnp.int32)
        end = end + here
        source = source + jnp.where(entry >= end, 128 - 16 * here, 0)
    source = source[0:1]
    row = iota((128, 512), 0)
    total = jnp.zeros((first_ref.shape[0], 512), F32)
    for s in range(0, SHARDS, 2):
        pick = jnp.concatenate(
            [(row + u * 128 == source).astype(F32).astype(BF16) for u in (s, s + 1)], axis=0
        )
        pair = jnp.concatenate([parts_ref[s], parts_ref[s + 1]], axis=1)
        total = total + jnp.dot(pair, pick, preferred_element_type=F32)
    total = total.astype(BF16)
    first_ref[...] = total[:, :256]
    second_ref[...] = total[:, 256:]


def compact_parts(pos, block_ids, block_counts, parts):
    width = parts.shape[1]
    half = jax.ShapeDtypeStruct((width, 256), BF16)
    return pl.pallas_call(
        compact_kernel,
        out_shape=(half, half),
        in_specs=[SMEM, VMEM, VMEM, VMEM],
        out_specs=(VMEM, VMEM),
        cost_estimate=pl.CostEstimate(
            flops=2 * width * 1024 * 512, bytes_accessed=width * 1536 * 2, transcendentals=0
        ),
        name="compact_parts",
    )(pos, block_ids, block_counts.reshape(-1, 1), parts)


def index_kernel(query_ref, weight_ref, keys_ref, out_ref):
    rows, heads, dim = query_ref.shape
    flat = query_ref[...].reshape(rows * heads, dim)
    weight = weight_ref[...] * INDEX_SCALE
    span = 256
    for c in range(keys_ref.shape[0] // span):
        dots = lax.dot_general(
            flat, keys_ref[c * span : (c + 1) * span, :], (((1,), (1,)), ((), ())), preferred_element_type=F32
        ).reshape(rows, heads, span)
        out_ref[:, c * span : (c + 1) * span] = jnp.sum(
            jnp.maximum(dots, 0.0) * weight[:, :, None], axis=1
        )


def index_scores_of(index_query, index_weight, index_keys):
    rows, heads, dim = index_query.shape
    keys = index_keys.shape[0]
    step = 8
    return pl.pallas_call(
        index_kernel,
        grid=(rows // step,),
        out_shape=jax.ShapeDtypeStruct((rows, keys), F32),
        in_specs=[
            pl.BlockSpec((step, heads, dim), lambda i: (i, 0, 0)),
            pl.BlockSpec((step, heads), lambda i: (i, 0)),
            pl.BlockSpec((keys, dim), lambda i: (0, 0)),
        ],
        out_specs=pl.BlockSpec((step, keys), lambda i: (i, 0)),
        cost_estimate=pl.CostEstimate(
            flops=8 * rows * heads * dim * keys, bytes_accessed=rows * heads * dim * 2 + rows * keys * 4, transcendentals=0
        ),
        name="index_scores",
    )(index_query, index_weight, index_keys)


def attend_kernel(pos_ref, q_ref, *refs):
    parts, out_ref = refs[:-1], refs[-1]
    rows = q_ref.shape[0]
    count, row_y, row_z = pos_ref[3], pos_ref[1], pos_ref[2]
    first_query = pl.program_id(0) * (rows // 8)
    query = first_query + (iota((rows, 128), 0) >> 3) + (count - 2) * BLOCK
    lane = iota((rows, 128), 1) + 128
    key = ((lane >> 3) * BLOCK) + (lane & 7)
    q = q_ref[...]
    scores = []
    top = None
    for p, part in enumerate(parts):
        offset = lax.rem(row_z - p + 4, 4) * 8 if p < 4 else 32 + lax.rem(row_y - (p - 4) + 4, 4) * 8
        s = jnp.dot(q, part[...], preferred_element_type=F32)
        s = jnp.concatenate([s[:, :128], jnp.where(key + offset <= query, s[:, 128:], -jnp.inf)], axis=1)
        scores.append(s)
        m = jnp.maximum(s[:, :128], s[:, 128:])
        top = m if top is None else jnp.maximum(top, m)
    top = jnp.max(top, axis=1, keepdims=True) * SCALE
    total = None
    mixed = None
    for s, part in zip(scores, parts):
        e = jnp.exp(s * SCALE - top)
        t = e[:, :128] + e[:, 128:]
        total = t if total is None else total + t
        o = lax.dot_general(
            e.astype(BF16), part[0:512, :], (((1,), (1,)), ((), ())), preferred_element_type=F32
        )
        mixed = o if mixed is None else mixed + o
    total = jnp.sum(total, axis=1, keepdims=True)
    out_ref[...] = (mixed / total).astype(BF16)


def attend(pos, q, parts):
    rows, width = q.shape
    step = 128
    part_spec = pl.BlockSpec((width, 256), lambda i: (0, 0))
    keys = 256 * len(parts)
    return pl.pallas_call(
        attend_kernel,
        grid=(rows // step,),
        out_shape=jax.ShapeDtypeStruct((rows, 512), BF16),
        in_specs=[SMEM, pl.BlockSpec((step, width), lambda i: (i, 0))] + [part_spec] * len(parts),
        out_specs=pl.BlockSpec((step, 512), lambda i: (i, 0)),
        cost_estimate=pl.CostEstimate(
            flops=2 * rows * keys * (width + 512),
            bytes_accessed=rows * (width + 512) * 2 + keys * width * 2,
            transcendentals=rows * keys,
        ),
        name="attend",
    )(pos, q, *parts)


def line(dy, dz):
    return [(y * 4 + z, ((y + dy) % 4) * 4 + (z + dz) % 4) for y in range(4) for z in range(4)]


def body(q_latent, index_query, index_weight, index_keys, latent_cache, block_ids, block_counts):
    shard_here = lax.axis_index("ctx")
    group_here = lax.axis_index("head")
    count_here = lax.dynamic_index_in_dim(block_counts, shard_here, keepdims=False)
    pos = jnp.stack([shard_here, group_here // 4, group_here % 4, count_here]).astype(jnp.int32)
    outgoing = gather_parts(pos, block_ids, block_counts, latent_cache.T)
    incoming = lax.all_to_all(outgoing, "ctx", split_axis=0, concat_axis=0, tiled=True)
    head_query = lax.all_to_all(q_latent, "head", split_axis=1, concat_axis=0, tiled=True)
    index_scores = index_scores_of(index_query, index_weight, index_keys)
    first, second = compact_parts(pos, block_ids, block_counts, incoming)
    firsts = [first] + [lax.ppermute(first, "head", line(0, d)) for d in (1, 2, 3)]
    seconds = [second] + [lax.ppermute(second, "head", line(d, 0)) for d in (1, 2, 3)]
    rows, heads, width = head_query.shape
    attention = attend(pos, head_query.reshape(rows * heads, width), firsts + seconds)
    return attention.reshape(rows, heads, 512), index_scores


def solution(mesh):
    return jax.shard_map(
        body,
        mesh=mesh,
        in_specs=(
            P(("ctx", "head"), None, None),
            P("head", None, None),
            P("head", None),
            P("ctx", None),
            P("ctx", None),
            P(),
            P(),
        ),
        out_specs=(P("ctx", "head", None), P("head", "ctx")),
        check_vma=False,
    )
```

time: 164 us -> 93.8 us (0.57)
  local copies, waits for them, and re-layouts: 68.2 us -> 7 us
  matrix products: 41.7 us -> 0 us
  Pallas kernels: 0 us -> 31.8 us
  other arithmetic: 32.4 us -> 1.31 us
  waiting for transfers between devices: 0.01 us -> 26.6 us
  starting transfers between devices: 19.1 us -> 24.7 us
    dot_general x6 -> x0, matrix products: 41.7 us -> none  [the longest x4 21.5 us: index_block(): lax.dot_general(flat_query, key_block, (((1,), (1,)), ((), ())), preferre...]
    max x4 -> x0, local copies, waits for them, and re-layouts: 35.9 us -> none  [index_block(): jax.nn.relu(raw_dots * index_query.shape[2] ** (-0.5))]
    pallas_call x0 -> x4, Pallas kernels: none -> 31.8 us  [the longest x1 14.6 us: attend(): pl.pallas_call(attend_kernel, grid=(rows // step,), out_shape=jax.ShapeDt...]
    reduce_sum x7 -> x0, other arithmetic: 24 us -> none  [the longest x4 15.9 us: index_block(): return jnp.sum(gated_dots * index_weight[:, :, None], axis=1)]
    gather x2 -> x0, local copies, waits for them, and re-layouts: 18.2 us -> none  [the longest x1 17.6 us: body(): jnp.take(latent_cache, target_ids, axis=0)]
    all_to_all x1, waiting for transfers between devices: 0.01 us -> 14.3 us  [body(): lax.all_to_all(outgoing, 'ctx', split_axis=0, concat_axis=0, tiled=True)]
    ppermute x0 -> x6, waiting for transfers between devices: none -> 12.2 us  [the longest x3 12.2 us: body(): lax.ppermute(first, 'head', line(0, d))]
    ppermute x0 -> x6, starting transfers between devices: none -> 11.1 us  [the longest x3 6.12 us: body(): lax.ppermute(second, 'head', line(d, 0))]
  transfers between devices with their start and end apart: 2 -> 8, of which waited for: 0 -> 2; matrix products, arithmetic and copies ran while one was open for 66% -> 4% of each run, Pallas kernels for 0% -> 12%
where the time goes in v1:
time: 93.8 us; the launch traced here: 92.1 us
  Pallas kernels  31.8 us (34%)
  waiting for transfers between devices  26.6 us (28%)
  starting transfers between devices  24.7 us (26%)
  local copies, waits for them, and re-layouts  7 us (7%)
  other arithmetic  1.31 us (1%)
    pallas_call x1, Pallas kernels, attend(): pl.pallas_call(attend_kernel, grid=(rows // step,), out_shape=jax.ShapeDt...  14.6 us
    all_to_all x1, waiting for transfers between devices, body(): lax.all_to_all(outgoing, 'ctx', split_axis=0, concat_axis=0, tiled=True)  14.3 us
    ppermute x3, waiting for transfers between devices, body(): lax.ppermute(first, 'head', line(0, d))  12.2 us
    pallas_call x1, Pallas kernels, index_scores_of(): pl.pallas_call(index_kernel, grid=(rows // step,), out_shape=jax.ShapeDty...  8.32 us
    all_to_all x1, starting transfers between devices, body(): lax.all_to_all(q_latent, 'head', split_axis=1, concat_axis=0, tiled=True)  7.77 us
    ppermute x3, starting transfers between devices, body(): lax.ppermute(second, 'head', line(d, 0))  6.12 us
    all_to_all x1, starting transfers between devices, body(): lax.all_to_all(outgoing, 'ctx', split_axis=0, concat_axis=0, tiled=True)  5.92 us
    pallas_call x1, Pallas kernels, gather_parts(): pl.pallas_call(gather_kernel, out_shape=jax.ShapeDtypeStruct((block_ids.s...  5.77 us
  transfers between devices with their start and end apart: 8, of which 2 were waited for; matrix products, arithmetic and copies ran while one was open for 4% of the time, Pallas kernels for 12%

profile of v1, /device:TPU:1, one launch (start us, length us, event | category | flops | bytes accessed | tf_op | source)
XLA Modules:
  0.0 92.1 jit_solution(3073381493220948872)
XLA Ops:
  0.6 1.3 %dynamic_slice.4 = s32[1]{0:T(128)} dynamic-slice(s32[8]{0:T(128)} %param.13, s32[]{:T(128)S(6)} %select_n.17), dynamic_slice_sizes={1} | dynamic-slice | bytes 12 | tf_op jit(solution)/shard_map/jit(dynamic_index_in_dim)/dynamic_slice | solution.py:210
  2.0 1.3 %copy.20.counts_ref = s32[8,1]{1,0:T(8,128)} copy(s32[8,1]{0,1:T(1,128)} %bitcast.12) | data formatting | bytes 64 | tf_op jit(solution)/shard_map/reshape | solution.py:112
  3.3 1.3 %pad_add_fusion.pos_ref = s32[4]{0:T(128)} fusion(s32[1]{0:T(128)} %dynamic_slice.4, s32[1]{0:T(128)} %bitcast.2, s32[1]{0:T(128)} %bitcast.1, s32[1]{0:T(128)} %bitcast), kind=kLoop, calls=%fused_computation | loop fusion | flops 12 | bytes 32 | tf_op jit(solution)/shard_map/stack | solution.py:211
  4.6 5.8 %gather_parts.1 = bf16[8,576,128]{2,1,0:T(8,128)(2,1)} custom-call(s32[4]{0:T(128)} %pad_add_fusion.pos_ref, s32[8,32]{1,0:T(8,128)} %ids_ref.3, s32[8,1]{1,0:T(8,128)} %copy.20.counts_ref, bf16[576,2048]{1,0:T(8,128)(2,1)} %bitcast.13), custom_call_target="tpu_custom_call" | custom-call | flops 2415919104 | bytes 4718592 | tf_op jit(solution)/shard_map/gather_parts/pallas_call | solution.py:60
  10.4 0.0 copy-start
  10.4 5.9 %all-to-all-start.1 = ((bf16[8,576,128]{2,1,0:T(8,128)(2,1)}), bf16[8,576,128]{2,1,0:T(8,128)(2,1)S(1)}, u32[]{:S(2)}, u32[]{:S(2)}) async-start(bf16[8,576,128]{2,1,0:T(8,128)(2,1)} %gather_parts.1), calls=%async_computation.1 | async-start | bytes 2359296 | tf_op jit(solution)/shard_map/all_to_all | solution.py:213
  16.3 0.0 copy-done
  16.3 2.0 %copy.16 = bf16[8,128,576]{2,0,1:T(8,128)(2,1)} copy(bf16[8,128,576]{1,2,0:T(8,128)(2,1)S(1)} %copy-done) | data formatting | bytes 2359296 | tf_op args[0]
  18.3 14.3 %all-to-all-done.1.parts_ref = bf16[8,576,128]{2,1,0:T(8,128)(2,1)S(1)} async-done(((bf16[8,576,128]{2,1,0:T(8,128)(2,1)}), bf16[8,576,128]{2,1,0:T(8,128)(2,1)S(1)}, u32[]{:S(2)}, u32[]{:S(2)}) %all-to-all-start.1) | async-done | bytes 1179680 | tf_op jit(solution)/shard_map/all_to_all | solution.py:213
  32.7 0.0 copy-start.1
  32.7 7.8 %all-to-all-start = ((bf16[8,128,576]{2,0,1:T(8,128)(2,1)}), bf16[8,128,576]{2,0,1:T(8,128)(2,1)S(1)}, u32[]{:S(2)}, u32[]{:S(2)}) async-start(bf16[8,128,576]{2,0,1:T(8,128)(2,1)} %copy.16), calls=%async_computation | async-start | bytes 2621440 | tf_op jit(solution)/shard_map/all_to_all | solution.py:214
  40.4 0.0 copy-done.1
  40.4 3.1 %compact_parts.1 = (bf16[576,256]{1,0:T(8,128)(2,1)}, bf16[576,256]{1,0:T(8,128)(2,1)}) custom-call(s32[4]{0:T(128)} %pad_add_fusion.pos_ref, s32[8,32]{1,0:T(8,128)} %ids_ref.3, s32[8,1]{1,0:T(8,128)} %copy.20.counts_ref, bf16[8,576,128]{2,1,0:T(8,128)(2,1)} %copy-done.1), custom_call_target="tpu_custom_call" | custom-call | flops 603979776 | bytes 1769472 | tf_op jit(solution)/shard_map/compact_parts/pallas_call | solution.py:103
  43.6 1.4 %collective-permute-start = (bf16[576,256]{1,0:T(8,128)(2,1)}, bf16[576,256]{1,0:T(8,128)(2,1)S(1)}, u32[]{:S(2)}, u32[]{:S(2)}) collective-permute-start(bf16[576,256]{1,0:T(8,128)(2,1)} %get-tuple-element.4.refs_0_), channel_id=1, source_target_pairs={{0,1},{1,2},{2,3},{3,0},{4,5},{5,6},{6,7},{7,4},{8,9},{9,10},{10,1... | collective-permute-start | bytes 884744 | tf_op jit(solution)/shard_map/ppermute | solution.py:217
  44.9 2.4 %collective-permute-start.1 = (bf16[576,256]{1,0:T(8,128)(2,1)}, bf16[576,256]{1,0:T(8,128)(2,1)S(1)}, u32[]{:S(2)}, u32[]{:S(2)}) collective-permute-start(bf16[576,256]{1,0:T(8,128)(2,1)} %get-tuple-element.4.refs_0_), channel_id=1, source_target_pairs={{0,2},{1,3},{2,0},{3,1},{4,6},{5,7},{6,4},{7,5},{8,10},{9,11},{10,... | collective-permute-start | bytes 884744 | tf_op jit(solution)/shard_map/ppermute | solution.py:217
  47.3 1.2 %collective-permute-start.2 = (bf16[576,256]{1,0:T(8,128)(2,1)}, bf16[576,256]{1,0:T(8,128)(2,1)S(1)}, u32[]{:S(2)}, u32[]{:S(2)}) collective-permute-start(bf16[576,256]{1,0:T(8,128)(2,1)} %get-tuple-element.4.refs_0_), channel_id=1, source_target_pairs={{0,3},{1,0},{2,1},{3,2},{4,7},{5,4},{6,5},{7,6},{8,11},{9,8},{10,9... | collective-permute-start | bytes 884744 | tf_op jit(solution)/shard_map/ppermute | solution.py:217
  48.5 1.2 %collective-permute-start.3 = (bf16[576,256]{1,0:T(8,128)(2,1)}, bf16[576,256]{1,0:T(8,128)(2,1)S(1)}, u32[]{:S(2)}, u32[]{:S(2)}) collective-permute-start(bf16[576,256]{1,0:T(8,128)(2,1)} %get-tuple-element.5.refs_4_), channel_id=1, source_target_pairs={{0,4},{1,5},{2,6},{3,7},{4,8},{5,9},{6,10},{7,11},{8,12},{9,13},{1... | collective-permute-start | bytes 884744 | tf_op jit(solution)/shard_map/ppermute | solution.py:218
  49.7 2.4 %collective-permute-start.4 = (bf16[576,256]{1,0:T(8,128)(2,1)}, bf16[576,256]{1,0:T(8,128)(2,1)S(1)}, u32[]{:S(2)}, u32[]{:S(2)}) collective-permute-start(bf16[576,256]{1,0:T(8,128)(2,1)} %get-tuple-element.5.refs_4_), channel_id=1, source_target_pairs={{0,8},{1,9},{2,10},{3,11},{4,12},{5,13},{6,14},{7,15},{8,0},{9,1},... | collective-permute-start | bytes 884744 | tf_op jit(solution)/shard_map/ppermute | solution.py:218
  52.1 12.2 %collective-permute-done.refs_1_ = bf16[576,256]{1,0:T(8,128)(2,1)S(1)} collective-permute-done((bf16[576,256]{1,0:T(8,128)(2,1)}, bf16[576,256]{1,0:T(8,128)(2,1)S(1)}, u32[]{:S(2)}, u32[]{:S(2)}) %collective-permute-start) | collective-permute-done | bytes 294944 | tf_op jit(solution)/shard_map/ppermute | solution.py:217
  64.3 0.0 copy-start.2
  64.3 2.5 %collective-permute-start.5 = (bf16[576,256]{1,0:T(8,128)(2,1)}, bf16[576,256]{1,0:T(8,128)(2,1)S(1)}, u32[]{:S(2)}, u32[]{:S(2)}) collective-permute-start(bf16[576,256]{1,0:T(8,128)(2,1)} %get-tuple-element.5.refs_4_), channel_id=1, source_target_pairs={{0,12},{1,13},{2,14},{3,15},{4,0},{5,1},{6,2},{7,3},{8,4},{9,5},{1... | collective-permute-start | bytes 884744 | tf_op jit(solution)/shard_map/ppermute | solution.py:218
  66.8 8.3 %index_scores.1 = f32[64,2048]{1,0:T(8,128)} custom-call(bf16[64,64,128]{2,1,0:T(8,128)(2,1)} %query_ref.1, f32[64,64]{1,0:T(8,128)} %weight_ref.1, bf16[2048,128]{1,0:T(8,128)(2,1)} %keys_ref.1), custom_call_target="tpu_custom_call" | custom-call | flops 8589934592 | bytes 1572864 | tf_op jit(solution)/shard_map/index_scores/pallas_call | solution.py:133
  75.2 0.0 copy-done.2
  75.2 0.0 all-to-all-done
  75.2 1.3 %copy.18 = bf16[16,8,8,576]{3,2,1,0:T(8,128)(2,1)} copy(bf16[16,8,8,576]{3,1,2,0:T(8,128)(2,1)S(1)} %bitcast.10) | data formatting | bytes 2359296 | tf_op jit(solution)/shard_map/all_to_all | solution.py:214
  76.5 0.0 collective-permute-done.1.refs_2_
  76.5 0.0 copy-start.3
  76.5 0.0 collective-permute-done.2.refs_3_
  76.5 0.0 copy-start.4
  76.5 0.0 collective-permute-done.3.refs_5_
  76.5 0.0 copy-start.5
  76.5 0.0 collective-permute-done.4.refs_6_
  76.5 0.0 copy-start.6
  76.5 0.0 collective-permute-done.5.refs_7_
  76.6 0.0 copy-start.7
  76.6 0.6 copy-done.3
  77.2 0.1 copy-done.4
  77.3 0.1 copy-done.5
  77.4 0.1 copy-done.6
  77.5 0.1 copy-done.7
  77.6 14.6 %attend.1 = bf16[1024,512]{1,0:T(8,128)(2,1)} custom-call(s32[4]{0:T(128)} %pad_add_fusion.pos_ref, bf16[1024,576]{1,0:T(8,128)(2,1)} %bitcast.11, bf16[576,256]{1,0:T(8,128)(2,1)} %get-tuple-element.4.refs_0_, bf16[576,256]{1,0:T(8,128)(2,1)} %copy-done.2, bf16[576,256]{1,0:T(8,128)(2,1)} %copy-done.3, bf16[576,256]{1,0:T(8,128)(2,1)} %copy-done.4, ...), custom_call_target="tpu_custom_call" | custom-call | flops 4563402752 | bytes 4587520 | tf_op jit(solution)/shard_map/attend/pallas_call | solution.py:188
Async XLA Ops:
  10.4 5.9 %copy-start = (bf16[8,128,576]{1,2,0:T(8,128)(2,1)S(1)}, bf16[8,128,576]{1,2,0:T(8,128)(2,1)}, u32[]{:S(2)}) copy-start(bf16[8,128,576]{1,2,0:T(8,128)(2,1)} %param.7) | copy-start | bytes 3538948
  10.4 22.3 %all-to-all-start.1 = ((bf16[8,576,128]{2,1,0:T(8,128)(2,1)}), bf16[8,576,128]{2,1,0:T(8,128)(2,1)S(1)}, u32[]{:S(2)}, u32[]{:S(2)}) async-start(bf16[8,576,128]{2,1,0:T(8,128)(2,1)} %gather_parts.1), calls=%async_computation.1 | async-start | bytes 2359296 | tf_op jit(solution)/shard_map/all_to_all | solution.py:213
  32.7 7.8 %copy-start.1 = (bf16[8,576,128]{2,1,0:T(8,128)(2,1)}, bf16[8,576,128]{2,1,0:T(8,128)(2,1)S(1)}, u32[]{:S(2)}) copy-start(bf16[8,576,128]{2,1,0:T(8,128)(2,1)S(1)} %all-to-all-done.1.parts_ref) | copy-start | bytes 3538948
  32.7 42.5 %all-to-all-start = ((bf16[8,128,576]{2,0,1:T(8,128)(2,1)}), bf16[8,128,576]{2,0,1:T(8,128)(2,1)S(1)}, u32[]{:S(2)}, u32[]{:S(2)}) async-start(bf16[8,128,576]{2,0,1:T(8,128)(2,1)} %copy.16), calls=%async_computation | async-start | bytes 2621440 | tf_op jit(solution)/shard_map/all_to_all | solution.py:214
  43.6 20.7 %collective-permute-start = (bf16[576,256]{1,0:T(8,128)(2,1)}, bf16[576,256]{1,0:T(8,128)(2,1)S(1)}, u32[]{:S(2)}, u32[]{:S(2)}) collective-permute-start(bf16[576,256]{1,0:T(8,128)(2,1)} %get-tuple-element.4.refs_0_), channel_id=1, source_target_pairs={{0,1},{1,2},{2,3},{3,0},{4,5},{5,6},{6,7},{7,4},{8,9},{9,10},{10,1... | collective-permute-start | bytes 884744 | tf_op jit(solution)/shard_map/ppermute | solution.py:217
  44.9 31.6 %collective-permute-start.1 = (bf16[576,256]{1,0:T(8,128)(2,1)}, bf16[576,256]{1,0:T(8,128)(2,1)S(1)}, u32[]{:S(2)}, u32[]{:S(2)}) collective-permute-start(bf16[576,256]{1,0:T(8,128)(2,1)} %get-tuple-element.4.refs_0_), channel_id=1, source_target_pairs={{0,2},{1,3},{2,0},{3,1},{4,6},{5,7},{6,4},{7,5},{8,10},{9,11},{10,... | collective-permute-start | bytes 884744 | tf_op jit(solution)/shard_map/ppermute | solution.py:217
  47.3 29.2 %collective-permute-start.2 = (bf16[576,256]{1,0:T(8,128)(2,1)}, bf16[576,256]{1,0:T(8,128)(2,1)S(1)}, u32[]{:S(2)}, u32[]{:S(2)}) collective-permute-start(bf16[576,256]{1,0:T(8,128)(2,1)} %get-tuple-element.4.refs_0_), channel_id=1, source_target_pairs={{0,3},{1,0},{2,1},{3,2},{4,7},{5,4},{6,5},{7,6},{8,11},{9,8},{10,9... | collective-permute-start | bytes 884744 | tf_op jit(solution)/shard_map/ppermute | solution.py:217
  48.5 28.0 %collective-permute-start.3 = (bf16[576,256]{1,0:T(8,128)(2,1)}, bf16[576,256]{1,0:T(8,128)(2,1)S(1)}, u32[]{:S(2)}, u32[]{:S(2)}) collective-permute-start(bf16[576,256]{1,0:T(8,128)(2,1)} %get-tuple-element.5.refs_4_), channel_id=1, source_target_pairs={{0,4},{1,5},{2,6},{3,7},{4,8},{5,9},{6,10},{7,11},{8,12},{9,13},{1... | collective-permute-start | bytes 884744 | tf_op jit(solution)/shard_map/ppermute | solution.py:218
  49.7 26.8 %collective-permute-start.4 = (bf16[576,256]{1,0:T(8,128)(2,1)}, bf16[576,256]{1,0:T(8,128)(2,1)S(1)}, u32[]{:S(2)}, u32[]{:S(2)}) collective-permute-start(bf16[576,256]{1,0:T(8,128)(2,1)} %get-tuple-element.5.refs_4_), channel_id=1, source_target_pairs={{0,8},{1,9},{2,10},{3,11},{4,12},{5,13},{6,14},{7,15},{8,0},{9,1},... | collective-permute-start | bytes 884744 | tf_op jit(solution)/shard_map/ppermute | solution.py:218
  64.3 10.9 %copy-start.2 = (bf16[576,256]{1,0:T(8,128)(2,1)}, bf16[576,256]{1,0:T(8,128)(2,1)S(1)}, u32[]{:S(2)}) copy-start(bf16[576,256]{1,0:T(8,128)(2,1)S(1)} %collective-permute-done.refs_1_) | copy-start | bytes 884740
  64.3 12.2 %collective-permute-start.5 = (bf16[576,256]{1,0:T(8,128)(2,1)}, bf16[576,256]{1,0:T(8,128)(2,1)S(1)}, u32[]{:S(2)}, u32[]{:S(2)}) collective-permute-start(bf16[576,256]{1,0:T(8,128)(2,1)} %get-tuple-element.5.refs_4_), channel_id=1, source_target_pairs={{0,12},{1,13},{2,14},{3,15},{4,0},{5,1},{6,2},{7,3},{8,4},{9,5},{1... | collective-permute-start | bytes 884744 | tf_op jit(solution)/shard_map/ppermute | solution.py:218
  76.5 0.7 copy-start.3
  76.5 0.8 copy-start.4
  76.5 0.9 copy-start.5
  76.5 1.0 %copy-start.6 = (bf16[576,256]{1,0:T(8,128)(2,1)}, bf16[576,256]{1,0:T(8,128)(2,1)S(1)}, u32[]{:S(2)}) copy-start(bf16[576,256]{1,0:T(8,128)(2,1)S(1)} %collective-permute-done.4.refs_6_) | copy-start | bytes 884740
  76.6 1.0 %copy-start.7 = (bf16[576,256]{1,0:T(8,128)(2,1)}, bf16[576,256]{1,0:T(8,128)(2,1)S(1)}, u32[]{:S(2)}) copy-start(bf16[576,256]{1,0:T(8,128)(2,1)S(1)} %collective-permute-done.5.refs_7_) | copy-start | bytes 884740

commit v2 on v1

v2 whole, which is shorter than its diff:
```python
import jax
import jax.numpy as jnp
from jax import lax
from jax.experimental import pallas as pl
from jax.experimental.pallas import tpu as pltpu
from jax.sharding import PartitionSpec as P


BLOCK = 64
SHARDS = 8
PART = 16
SCALE = 192.0 ** (-0.5)
INDEX_SCALE = 128.0 ** (-0.5)
F32 = jnp.float32
BF16 = jnp.bfloat16
VMEM = pl.BlockSpec(memory_space=pltpu.VMEM)
SMEM = pl.BlockSpec(memory_space=pltpu.SMEM)


def iota(shape, dim):
    return lax.broadcasted_iota(jnp.int32, shape, dim)


def valid_ids(ids_ref, counts_ref):
    tiles, entries = ids_ref.shape
    tile = iota((tiles, entries), 0)
    count = jnp.zeros((tiles, entries), jnp.int32)
    for t in range(tiles):
        count = jnp.where(tile == t, counts_ref[t], count)
    return jnp.where(iota((tiles, entries), 1) < count, ids_ref[...], -1)


def place():
    group = lax.axis_index("head")
    return lax.axis_index("ctx"), group >> 2, group & 3


def row_of(part, row_y, row_z):
    return jnp.where(part < 8, row_z * 8 + part, 24 + row_y * 8 + part)


def hot(index, target):
    return (index == target).astype(F32).astype(BF16)


def gather_kernel(ids_ref, counts_ref, cache_ref, *out_refs):
    shard, row_y, row_z = place()
    ids = valid_ids(ids_ref, counts_ref)
    tiles, entries = ids.shape
    keys = cache_ref.shape[1]
    blocks = keys // BLOCK
    lane = iota((tiles, 128), 1)
    block_of_lane = jnp.where(lane < blocks, lane + shard * blocks, -2)
    member = jnp.zeros((tiles, 128), F32)
    for j in range(entries):
        member = jnp.where(ids[:, j : j + 1] == block_of_lane, 1.0, member)
    before = (iota((128, 128), 0) < iota((128, 128), 1)).astype(BF16)
    rank = jnp.dot(member.astype(BF16), before, preferred_element_type=F32)
    rank = jnp.where(member > 0.0, rank, -1.0)
    slot = (lane >> 4).astype(F32)
    target = jnp.full((tiles, 128), -1, jnp.int32)
    for b in range(blocks):
        target = jnp.where(rank[:, b : b + 1] == slot, b * PART + (lane & 15), target)
    column = iota((512, 128), 1)
    keep = hot(iota((512, 128), 0), (column >> 4) * BLOCK + row_of(column & 15, row_y, row_z))
    own = jnp.concatenate(
        [
            jnp.dot(cache_ref[:, c : c + 512], keep, preferred_element_type=F32).astype(BF16)
            for c in range(0, keys, 512)
        ],
        axis=1,
    )
    index = iota((own.shape[1], 128), 0)
    for d in range(0, tiles, 2):
        pair = []
        for u in (d, d + 1):
            chosen = iota((tiles, 128), 0) == ((shard + u) & 7)
            pair.append(hot(index, jnp.sum(jnp.where(chosen, target, 0), axis=0, keepdims=True)))
        got = jnp.dot(own, jnp.concatenate(pair, axis=1), preferred_element_type=F32).astype(BF16)
        out_refs[d][...] = got[:, :128]
        out_refs[d + 1][...] = got[:, 128:]


def gather_parts(block_ids, block_counts, cache_t):
    width, keys = cache_t.shape
    tiles = block_ids.shape[0]
    return pl.pallas_call(
        gather_kernel,
        out_shape=[jax.ShapeDtypeStruct((width, 128), BF16)] * tiles,
        in_specs=[VMEM, SMEM, VMEM],
        out_specs=[VMEM] * tiles,
        cost_estimate=pl.CostEstimate(
            flops=2 * width * keys * 1024, bytes_accessed=2 * width * keys * 2, transcendentals=0
        ),
        compiler_params=pltpu.CompilerParams(vmem_limit_bytes=24 << 20),
        name="gather_parts",
    )(block_ids, block_counts, cache_t)


def compact_kernel(ids_ref, counts_ref, *refs):
    part_refs, (first_ref, second_ref) = refs[:-2], refs[-2:]
    tile = lax.axis_index("ctx")
    ids = valid_ids(ids_ref, counts_ref)
    mine = jnp.sum(jnp.where(iota(ids.shape, 0) == tile, ids, 0), axis=0, keepdims=True)
    owner = jnp.where(mine < 0, 2 * SHARDS, mine >> 5)
    shard = iota(ids.shape, 0)
    here = jnp.sum((owner == shard).astype(F32), axis=1, keepdims=True).astype(jnp.int32)
    end = jnp.sum((owner <= shard).astype(F32), axis=1, keepdims=True).astype(jnp.int32)
    column = iota((SHARDS, 512), 1)
    entry = (column & 255) >> 3
    skipped = jnp.sum(jnp.where(entry >= end, 128 - 16 * here, 0), axis=0, keepdims=True)
    part = (column & 7) + ((column >> 8) << 3)
    source = (entry * PART + part)[0:1] + skipped
    row = iota((128, 512), 0)
    total = jnp.zeros((first_ref.shape[0], 512), F32)
    for d in range(0, SHARDS, 2):
        pick = jnp.concatenate([hot(row + ((tile - u) & 7) * 128, source) for u in (d, d + 1)], axis=0)
        pair = jnp.concatenate([part_refs[d][...], part_refs[d + 1][...]], axis=1)
        total = total + jnp.dot(pair, pick, preferred_element_type=F32)
    total = total.astype(BF16)
    first_ref[...] = total[:, :256]
    second_ref[...] = total[:, 256:]


def compact_parts(block_ids, block_counts, parts):
    width = parts[0].shape[0]
    half = jax.ShapeDtypeStruct((width, 256), BF16)
    return pl.pallas_call(
        compact_kernel,
        out_shape=(half, half),
        in_specs=[VMEM, SMEM] + [VMEM] * len(parts),
        out_specs=(VMEM, VMEM),
        cost_estimate=pl.CostEstimate(
            flops=2 * width * 1024 * 512, bytes_accessed=width * 1536 * 2, transcendentals=0
        ),
        compiler_params=pltpu.CompilerParams(vmem_limit_bytes=24 << 20),
        name="compact_parts",
    )(block_ids, block_counts, *parts)


def q_prep_kernel(q_ref, out_ref):
    groups, rows, heads, width = out_ref.shape
    for i in range(rows):
        out_ref[:, i] = q_ref[i].T.reshape(groups, heads, width)


def q_by_group(q_latent, groups):
    rows, heads, width = q_latent.shape
    return pl.pallas_call(
        q_prep_kernel,
        out_shape=jax.ShapeDtypeStruct((groups, rows, heads // groups, width), BF16),
        in_specs=[VMEM],
        out_specs=VMEM,
        cost_estimate=pl.CostEstimate(flops=0, bytes_accessed=rows * heads * width * 4, transcendentals=0),
        compiler_params=pltpu.CompilerParams(vmem_limit_bytes=16 << 20),
        name="q_by_group",
    )(q_latent.transpose(0, 2, 1))


def index_kernel(query_ref, weight_ref, keys_ref, out_ref):
    rows, heads, dim = query_ref.shape
    flat = query_ref[...].reshape(rows * heads, dim)
    weight = weight_ref[...] * INDEX_SCALE
    span = 256
    for c in range(keys_ref.shape[0] // span):
        dots = lax.dot_general(
            flat, keys_ref[c * span : (c + 1) * span, :], (((1,), (1,)), ((), ())), preferred_element_type=F32
        ).reshape(rows, heads, span)
        out_ref[:, c * span : (c + 1) * span] = jnp.sum(
            jnp.maximum(dots, 0.0) * weight[:, :, None], axis=1
        )


def index_scores_of(index_query, index_weight, index_keys):
    rows, heads, dim = index_query.shape
    keys = index_keys.shape[0]
    step = 8
    return pl.pallas_call(
        index_kernel,
        grid=(rows // step,),
        out_shape=jax.ShapeDtypeStruct((rows, keys), F32),
        in_specs=[
            pl.BlockSpec((step, heads, dim), lambda i: (i, 0, 0)),
            pl.BlockSpec((step, heads), lambda i: (i, 0)),
            pl.BlockSpec((keys, dim), lambda i: (0, 0)),
        ],
        out_specs=pl.BlockSpec((step, keys), lambda i: (i, 0)),
        cost_estimate=pl.CostEstimate(
            flops=8 * rows * heads * dim * keys, bytes_accessed=rows * heads * dim * 2 + rows * keys * 4, transcendentals=0
        ),
        compiler_params=pltpu.CompilerParams(vmem_limit_bytes=32 << 20),
        name="index_scores",
    )(index_query, index_weight, index_keys)


def attend_kernel(counts_ref, q_ref, *refs):
    parts, out_ref = refs[:-1], refs[-1]
    rows = q_ref.shape[0]
    tile, row_y, row_z = place()
    count = counts_ref[tile]
    first_query = pl.program_id(0) * (rows // 8)
    query = first_query + (iota((rows, 128), 0) >> 3) + (count - 2) * BLOCK
    lane = iota((rows, 128), 1) + 128
    key = ((lane >> 3) * BLOCK) + (lane & 7)
    q = q_ref[...]
    scores = []
    top = None
    for p, part in enumerate(parts):
        offset = lax.rem(row_z - p + 4, 4) * 8 if p < 4 else 32 + lax.rem(row_y - (p - 4) + 4, 4) * 8
        s = jnp.dot(q, part[...], preferred_element_type=F32)
        s = jnp.concatenate([s[:, :128], jnp.where(key + offset <= query, s[:, 128:], -jnp.inf)], axis=1)
        scores.append(s)
        m = jnp.maximum(s[:, :128], s[:, 128:])
        top = m if top is None else jnp.maximum(top, m)
    top = jnp.max(top, axis=1, keepdims=True) * SCALE
    total = None
    mixed = None
    for s, part in zip(scores, parts):
        e = jnp.exp(s * SCALE - top)
        t = e[:, :128] + e[:, 128:]
        total = t if total is None else total + t
        o = lax.dot_general(
            e.astype(BF16), part[0:512, :], (((1,), (1,)), ((), ())), preferred_element_type=F32
        )
        mixed = o if mixed is None else mixed + o
    total = jnp.sum(total, axis=1, keepdims=True)
    out_ref[...] = (mixed / total).astype(BF16)


def attend(block_counts, q, parts):
    rows, width = q.shape
    step = 128
    part_spec = pl.BlockSpec((width, 256), lambda i: (0, 0))
    keys = 256 * len(parts)
    return pl.pallas_call(
        attend_kernel,
        grid=(rows // step,),
        out_shape=jax.ShapeDtypeStruct((rows, 512), BF16),
        in_specs=[SMEM, pl.BlockSpec((step, width), lambda i: (i, 0))] + [part_spec] * len(parts),
        out_specs=pl.BlockSpec((step, 512), lambda i: (i, 0)),
        cost_estimate=pl.CostEstimate(
            flops=2 * rows * keys * (width + 512),
            bytes_accessed=rows * (width + 512) * 2 + keys * width * 2,
            transcendentals=rows * keys,
        ),
        compiler_params=pltpu.CompilerParams(vmem_limit_bytes=32 << 20),
        name="attend",
    )(block_counts, q, *parts)


def turn(d):
    return [(i, (i + d) % SHARDS) for i in range(SHARDS)]


def line(dy, dz):
    return [(y * 4 + z, ((y + dy) % 4) * 4 + (z + dz) % 4) for y in range(4) for z in range(4)]


def body(q_latent, index_query, index_weight, index_keys, latent_cache, block_ids, block_counts):
    rows, heads, width = q_latent.shape
    groups = lax.axis_size("head")
    outgoing = gather_parts(block_ids, block_counts, latent_cache.T)
    incoming = [outgoing[0]] + [lax.ppermute(outgoing[d], "ctx", turn(d)) for d in range(1, SHARDS)]
    by_group = q_by_group(q_latent, groups)
    head_query = lax.all_to_all(by_group, "head", split_axis=0, concat_axis=0, tiled=True)
    index_scores = index_scores_of(index_query, index_weight, index_keys)
    first, second = compact_parts(block_ids, block_counts, incoming)
    firsts = [first] + [lax.ppermute(first, "head", line(0, d)) for d in (1, 2, 3)]
    seconds = [second] + [lax.ppermute(second, "head", line(d, 0)) for d in (1, 2, 3)]
    attention = attend(block_counts, head_query.reshape(-1, width), firsts + seconds)
    return attention.reshape(rows * groups, heads // groups, 512), index_scores


def solution(mesh):
    return jax.shard_map(
        body,
        mesh=mesh,
        in_specs=(
            P(("ctx", "head"), None, None),
            P("head", None, None),
            P("head", None),
            P("ctx", None),
            P("ctx", None),
            P(),
            P(),
        ),
        out_specs=(P("ctx", "head", None), P("head", "ctx")),
        check_vma=False,
    )
```

time: 93.8 us -> 75.5 us (0.80)
  the two profiles are of different devices: /device:TPU:1 before, /device:TPU:72 now
where the time goes in v2:
time: 75.5 us; the launch traced here: 75.2 us
  starting transfers between devices  30.2 us (40%)
  Pallas kernels  24.8 us (33%)
  waiting for transfers between devices  14.7 us (19%)
  local copies, waits for them, and re-layouts  4.7 us (6%)
  between operations  0.78 us (1%)
    ppermute x3, waiting for transfers between devices, body(): lax.ppermute(first, 'head', line(0, d))  14.7 us
    pallas_call x1, Pallas kernels, attend(): pl.pallas_call(attend_kernel, grid=(rows // step,), out_shape=jax.ShapeDt...  13.4 us
    ppermute x7, starting transfers between devices, body(): lax.ppermute(outgoing[d], 'ctx', turn(d))  11.1 us
    ppermute x3, starting transfers between devices, body(): lax.ppermute(second, 'head', line(d, 0))  8.18 us
    all_to_all x1, starting transfers between devices, body(): lax.all_to_all(by_group, 'head', split_axis=0, concat_axis=0, tiled=True)  7.63 us
    pallas_call x1, Pallas kernels, index_scores_of(): pl.pallas_call(index_kernel, grid=(rows // step,), out_shape=jax.ShapeDty...  6.5 us
    unnamed x22, local copies, waits for them, and re-layouts  4.7 us
    ppermute x3, starting transfers between devices, body(): lax.ppermute(first, 'head', line(0, d))  3.26 us
  transfers between devices with their start and end apart: 14, of which 1 were waited for; matrix products, arithmetic and copies ran while one was open for 0% of the time, Pallas kernels for 13%

profile of v2, /device:TPU:72, one launch (start us, length us, event | category | flops | bytes accessed | tf_op | source)
XLA Modules:
  0.0 75.2 jit_solution(6186591444736321992)
XLA Ops:
  0.6 0.0 copy-start.1
  0.6 1.7 %copy-done.1 = bf16[2048,576]{0,1:T(8,128)(2,1)S(1)} copy-done((bf16[2048,576]{0,1:T(8,128)(2,1)S(1)}, bf16[2048,576]{0,1:T(8,128)(2,1)}, u32[]{:S(2)}) %copy-start.1) | copy-done | bytes 2359320
  2.3 0.0 copy-start.7
  2.3 0.7 copy-done.7
  3.0 0.0 copy-start.9
  3.0 0.7 copy-done.9
  3.6 0.0 copy-start
  3.6 2.0 %gather_parts.1 = (bf16[576,128]{1,0:T(8,128)(2,1)S(1)}, bf16[576,128]{1,0:T(8,128)(2,1)S(1)}, bf16[576,128]{1,0:T(8,128)(2,1)S(1)}, bf16[576,128]{1,0:T(8,128)(...) custom-call(s32[8,32]{1,0:T(8,128)S(1)} %copy-done.7, ...), custom_call_target="tpu_custom_call" | custom-call | flops 2415919104 | bytes 4718592 | tf_op jit(solution)/shard_map/gather_parts/pallas_call | solution.py:87
  5.7 0.0 collective-permute-start
  5.7 1.6 %collective-permute-start.1 = (bf16[576,128]{1,0:T(8,128)(2,1)S(1)}, bf16[576,128]{1,0:T(8,128)(2,1)S(1)}, u32[]{:S(2)}, u32[]{:S(2)}) collective-permute-start(bf16[576,128]{1,0:T(8,128)(2,1)S(1)} %get-tuple-element.14), channel_id=1, source_target_pairs={{0,32},{16,48},{32,64},{48,80},{64,96},{80,112},{96,0},{112,16},{1... | collective-permute-start | bytes 442376 | tf_op jit(solution)/shard_map/ppermute | solution.py:263
  7.3 2.0 %collective-permute-start.2 = (bf16[576,128]{1,0:T(8,128)(2,1)S(1)}, bf16[576,128]{1,0:T(8,128)(2,1)S(1)}, u32[]{:S(2)}, u32[]{:S(2)}) collective-permute-start(bf16[576,128]{1,0:T(8,128)(2,1)S(1)} %get-tuple-element.15), channel_id=1, source_target_pairs={{0,48},{16,64},{32,80},{48,96},{64,112},{80,0},{96,16},{112,32},{1... | collective-permute-start | bytes 442376 | tf_op jit(solution)/shard_map/ppermute | solution.py:263
  9.3 2.0 %collective-permute-start.3 = (bf16[576,128]{1,0:T(8,128)(2,1)S(1)}, bf16[576,128]{1,0:T(8,128)(2,1)S(1)}, u32[]{:S(2)}, u32[]{:S(2)}) collective-permute-start(bf16[576,128]{1,0:T(8,128)(2,1)S(1)} %get-tuple-element.16), channel_id=1, source_target_pairs={{0,64},{16,80},{32,96},{48,112},{64,0},{80,16},{96,32},{112,48},{1... | collective-permute-start | bytes 442376 | tf_op jit(solution)/shard_map/ppermute | solution.py:263
  11.3 1.6 %collective-permute-start.4 = (bf16[576,128]{1,0:T(8,128)(2,1)S(1)}, bf16[576,128]{1,0:T(8,128)(2,1)S(1)}, u32[]{:S(2)}, u32[]{:S(2)}) collective-permute-start(bf16[576,128]{1,0:T(8,128)(2,1)S(1)} %get-tuple-element.17), channel_id=1, source_target_pairs={{0,80},{16,96},{32,112},{48,0},{64,16},{80,32},{96,48},{112,64},{1... | collective-permute-start | bytes 442376 | tf_op jit(solution)/shard_map/ppermute | solution.py:263
  13.0 0.0 collective-permute-done.refs_1_
  13.0 1.4 %collective-permute-start.5 = (bf16[576,128]{1,0:T(8,128)(2,1)S(1)}, bf16[576,128]{1,0:T(8,128)(2,1)S(1)}, u32[]{:S(2)}, u32[]{:S(2)}) collective-permute-start(bf16[576,128]{1,0:T(8,128)(2,1)S(1)} %get-tuple-element.18), channel_id=1, source_target_pairs={{0,96},{16,112},{32,0},{48,16},{64,32},{80,48},{96,64},{112,80},{1... | collective-permute-start | bytes 442376 | tf_op jit(solution)/shard_map/ppermute | solution.py:263
  14.4 0.0 collective-permute-done.1.refs_2_
  14.4 2.4 %collective-permute-start.6 = (bf16[576,128]{1,0:T(8,128)(2,1)S(1)}, bf16[576,128]{1,0:T(8,128)(2,1)S(1)}, u32[]{:S(2)}, u32[]{:S(2)}) collective-permute-start(bf16[576,128]{1,0:T(8,128)(2,1)S(1)} %get-tuple-element.19), channel_id=1, source_target_pairs={{0,112},{16,0},{32,16},{48,32},{64,48},{80,64},{96,80},{112,96},{1... | collective-permute-start | bytes 442376 | tf_op jit(solution)/shard_map/ppermute | solution.py:263
  16.8 0.0 copy-done
  16.8 1.5 %q_by_group.1 = bf16[16,8,8,576]{3,2,1,0:T(8,128)(2,1)} custom-call(bf16[8,576,128]{2,1,0:T(8,128)(2,1)S(1)} %bitcast.5), custom_call_target="tpu_custom_call" | custom-call | bytes 2359296 | tf_op jit(solution)/shard_map/q_by_group/pallas_call | solution.py:149
  18.3 0.0 copy-start.8
  18.3 0.0 copy-start.10
  18.3 7.6 %all-to-all-start = ((bf16[16,8,8,576]{3,2,1,0:T(8,128)(2,1)}), bf16[16,8,8,576]{3,2,1,0:T(8,128)(2,1)S(1)}, u32[]{:S(2)}, u32[]{:S(2)}) async-start(bf16[16,8,8,576]{3,2,1,0:T(8,128)(2,1)} %q_by_group.1), calls=%async_computation | async-start | bytes 2621440 | tf_op jit(solution)/shard_map/all_to_all | solution.py:265
  25.9 0.0 copy-start.2
  25.9 0.0 copy-start.3
  26.0 0.0 copy-start.6
  26.0 0.0 collective-permute-done.2.refs_3_
  26.0 0.0 collective-permute-done.3.refs_4_
  26.0 0.0 collective-permute-done.4.refs_5_
  26.0 0.0 collective-permute-done.5.refs_6_
  26.0 0.0 collective-permute-done.6.refs_7_
  26.0 0.0 copy-done.8
  26.0 0.0 copy-done.10
  26.0 1.4 %compact_parts.1 = (bf16[576,256]{1,0:T(8,128)(2,1)S(1)}, bf16[576,256]{1,0:T(8,128)(2,1)S(1)}) custom-call(s32[8,32]{1,0:T(8,128)S(1)} %copy-done.8, s32[8]{0:T(128)S(1)} %copy-done.10, bf16[576,128]{1,0:T(8,128)(2,1)S(1)} %get-tuple-element.12.refs_0_, bf16[576,128]{1,0:T(8,128)(2,1)S(1)} %collective-permute-done.refs_1_, ...), custom_call_target="tpu_custom_call" | custom-call | flops 603979776 | bytes 1769472 | tf_op jit(solution)/shard_map/compact_parts/pallas_call | solution.py:128
  27.5 1.2 %collective-permute-start.7 = (bf16[576,256]{1,0:T(8,128)(2,1)S(1)}, bf16[576,256]{1,0:T(8,128)(2,1)S(1)}, u32[]{:S(2)}, u32[]{:S(2)}) collective-permute-start(bf16[576,256]{1,0:T(8,128)(2,1)S(1)} %get-tuple-element.20.refs_0_), channel_id=1, source_target_pairs={{0,1},{1,2},{2,3},{3,0},{4,5},{5,6},{6,7},{7,4},{8,9},{9,10},{10,1... | collective-permute-start | bytes 884744 | tf_op jit(solution)/shard_map/ppermute | solution.py:268
  28.7 0.9 %collective-permute-start.8 = (bf16[576,256]{1,0:T(8,128)(2,1)S(1)}, bf16[576,256]{1,0:T(8,128)(2,1)S(1)}, u32[]{:S(2)}, u32[]{:S(2)}) collective-permute-start(bf16[576,256]{1,0:T(8,128)(2,1)S(1)} %get-tuple-element.20.refs_0_), channel_id=1, source_target_pairs={{0,2},{1,3},{2,0},{3,1},{4,6},{5,7},{6,4},{7,5},{8,10},{9,11},{10,... | collective-permute-start | bytes 884744 | tf_op jit(solution)/shard_map/ppermute | solution.py:268
  29.6 1.2 %collective-permute-start.9 = (bf16[576,256]{1,0:T(8,128)(2,1)S(1)}, bf16[576,256]{1,0:T(8,128)(2,1)S(1)}, u32[]{:S(2)}, u32[]{:S(2)}) collective-permute-start(bf16[576,256]{1,0:T(8,128)(2,1)S(1)} %get-tuple-element.20.refs_0_), channel_id=1, source_target_pairs={{0,3},{1,0},{2,1},{3,2},{4,7},{5,4},{6,5},{7,6},{8,11},{9,8},{10,9... | collective-permute-start | bytes 884744 | tf_op jit(solution)/shard_map/ppermute | solution.py:268
  30.7 1.5 %collective-permute-start.10 = (bf16[576,256]{1,0:T(8,128)(2,1)S(1)}, bf16[576,256]{1,0:T(8,128)(2,1)S(1)}, u32[]{:S(2)}, u32[]{:S(2)}) collective-permute-start(bf16[576,256]{1,0:T(8,128)(2,1)S(1)} %get-tuple-element.21.refs_4_), channel_id=1, source_target_pairs={{0,4},{1,5},{2,6},{3,7},{4,8},{5,9},{6,10},{7,11},{8,12},{9,13},{1... | collective-permute-start | bytes 884744 | tf_op jit(solution)/shard_map/ppermute | solution.py:269
  32.2 0.7 collective-permute-start.11
  32.9 14.7 %collective-permute-done.7.refs_1_ = bf16[576,256]{1,0:T(8,128)(2,1)S(1)} collective-permute-done((bf16[576,256]{1,0:T(8,128)(2,1)S(1)}, bf16[576,256]{1,0:T(8,128)(2,1)S(1)}, u32[]{:S(2)}, u32[]{:S(2)}) %collective-permute-start.7) | collective-permute-done | bytes 294944 | tf_op jit(solution)/shard_map/ppermute | solution.py:268
  47.6 6.0 %collective-permute-start.12 = (bf16[576,256]{1,0:T(8,128)(2,1)S(1)}, bf16[576,256]{1,0:T(8,128)(2,1)S(1)}, u32[]{:S(2)}, u32[]{:S(2)}) collective-permute-start(bf16[576,256]{1,0:T(8,128)(2,1)S(1)} %get-tuple-element.21.refs_4_), channel_id=1, source_target_pairs={{0,12},{1,13},{2,14},{3,15},{4,0},{5,1},{6,2},{7,3},{8,4},{9,5},{1... | collective-permute-start | bytes 884744 | tf_op jit(solution)/shard_map/ppermute | solution.py:269
  53.6 0.0 copy-done.2
  53.6 0.0 copy-done.3
  53.6 0.0 copy-done.6
  53.6 6.5 %index_scores.1 = f32[64,2048]{1,0:T(8,128)} custom-call(bf16[64,64,128]{2,1,0:T(8,128)(2,1)S(1)} %copy-done.2, f32[64,64]{1,0:T(8,128)S(1)} %copy-done.6, bf16[2048,128]{1,0:T(8,128)(2,1)S(1)} %copy-done.3), custom_call_target="tpu_custom_call" | custom-call | flops 8589934592 | bytes 1572864 | tf_op jit(solution)/shard_map/index_scores/pallas_call | solution.py:178
  60.1 0.0 collective-permute-done.8.refs_2_
  60.1 0.0 collective-permute-done.9.refs_3_
  60.1 0.0 collective-permute-done.10.refs_5_
  60.2 0.0 collective-permute-done.11.refs_6_
  60.2 0.0 collective-permute-done.12.refs_7_
  60.2 0.0 copy-start.4
  60.2 0.7 copy-done.4
  60.9 0.0 all-to-all-done
  60.9 0.0 copy-start.5
  60.9 1.0 %copy-done.5 = bf16[576,256]{1,0:T(8,128)(2,1)S(1)} copy-done((bf16[576,256]{1,0:T(8,128)(2,1)S(1)}, bf16[576,256]{1,0:T(8,128)(2,1)}, u32[]{:S(2)}) %copy-start.5) | copy-done | bytes 294936
  61.9 13.4 %attend.1 = bf16[1024,512]{1,0:T(8,128)(2,1)} custom-call(s32[8]{0:T(128)S(1)} %copy-done.10, bf16[1024,576]{1,0:T(8,128)(2,1)S(1)} %bitcast.4, bf16[576,256]{1,0:T(8,128)(2,1)S(1)} %get-tuple-element.20.refs_0_, bf16[576,256]{1,0:T(8,128)(2,1)S(1)} %collective-permute-done.7.refs_1_, bf16[576,256]{1,0:T(8,128)(2,1)S(1)} %collective-permute-done.8.refs_2_, ...), custom_call_target="tpu_custom_call" | custom-call | flops 4563402752 | bytes 4587520 | tf_op jit(solution)/shard_map/attend/pallas_call | solution.py:235
Async XLA Ops:
  0.6 1.7 %copy-start.1 = (bf16[2048,576]{0,1:T(8,128)(2,1)S(1)}, bf16[2048,576]{0,1:T(8,128)(2,1)}, u32[]{:S(2)}) copy-start(bf16[2048,576]{0,1:T(8,128)(2,1)} %param.11) | copy-start | bytes 7077892
  2.3 0.7 copy-start.7
  3.0 0.7 copy-start.9
  3.6 13.2 %copy-start = (bf16[8,128,576]{1,2,0:T(8,128)(2,1)S(1)}, bf16[8,128,576]{1,2,0:T(8,128)(2,1)}, u32[]{:S(2)}) copy-start(bf16[8,128,576]{1,2,0:T(8,128)(2,1)} %param.7) | copy-start | bytes 3538948
  5.7 7.3 %collective-permute-start = (bf16[576,128]{1,0:T(8,128)(2,1)S(1)}, bf16[576,128]{1,0:T(8,128)(2,1)S(1)}, u32[]{:S(2)}, u32[]{:S(2)}) collective-permute-start(bf16[576,128]{1,0:T(8,128)(2,1)S(1)} %get-tuple-element.13), channel_id=1, source_target_pairs={{0,16},{16,32},{32,48},{48,64},{64,80},{80,96},{96,112},{112,0},{1... | collective-permute-start | bytes 442376 | tf_op jit(solution)/shard_map/ppermute | solution.py:263
  5.7 8.7 %collective-permute-start.1 = (bf16[576,128]{1,0:T(8,128)(2,1)S(1)}, bf16[576,128]{1,0:T(8,128)(2,1)S(1)}, u32[]{:S(2)}, u32[]{:S(2)}) collective-permute-start(bf16[576,128]{1,0:T(8,128)(2,1)S(1)} %get-tuple-element.14), channel_id=1, source_target_pairs={{0,32},{16,48},{32,64},{48,80},{64,96},{80,112},{96,0},{112,16},{1... | collective-permute-start | bytes 442376 | tf_op jit(solution)/shard_map/ppermute | solution.py:263
  7.3 18.7 %collective-permute-start.2 = (bf16[576,128]{1,0:T(8,128)(2,1)S(1)}, bf16[576,128]{1,0:T(8,128)(2,1)S(1)}, u32[]{:S(2)}, u32[]{:S(2)}) collective-permute-start(bf16[576,128]{1,0:T(8,128)(2,1)S(1)} %get-tuple-element.15), channel_id=1, source_target_pairs={{0,48},{16,64},{32,80},{48,96},{64,112},{80,0},{96,16},{112,32},{1... | collective-permute-start | bytes 442376 | tf_op jit(solution)/shard_map/ppermute | solution.py:263
  9.3 16.7 %collective-permute-start.3 = (bf16[576,128]{1,0:T(8,128)(2,1)S(1)}, bf16[576,128]{1,0:T(8,128)(2,1)S(1)}, u32[]{:S(2)}, u32[]{:S(2)}) collective-permute-start(bf16[576,128]{1,0:T(8,128)(2,1)S(1)} %get-tuple-element.16), channel_id=1, source_target_pairs={{0,64},{16,80},{32,96},{48,112},{64,0},{80,16},{96,32},{112,48},{1... | collective-permute-start | bytes 442376 | tf_op jit(solution)/shard_map/ppermute | solution.py:263
  11.3 14.7 %collective-permute-start.4 = (bf16[576,128]{1,0:T(8,128)(2,1)S(1)}, bf16[576,128]{1,0:T(8,128)(2,1)S(1)}, u32[]{:S(2)}, u32[]{:S(2)}) collective-permute-start(bf16[576,128]{1,0:T(8,128)(2,1)S(1)} %get-tuple-element.17), channel_id=1, source_target_pairs={{0,80},{16,96},{32,112},{48,0},{64,16},{80,32},{96,48},{112,64},{1... | collective-permute-start | bytes 442376 | tf_op jit(solution)/shard_map/ppermute | solution.py:263
  13.0 13.0 %collective-permute-start.5 = (bf16[576,128]{1,0:T(8,128)(2,1)S(1)}, bf16[576,128]{1,0:T(8,128)(2,1)S(1)}, u32[]{:S(2)}, u32[]{:S(2)}) collective-permute-start(bf16[576,128]{1,0:T(8,128)(2,1)S(1)} %get-tuple-element.18), channel_id=1, source_target_pairs={{0,96},{16,112},{32,0},{48,16},{64,32},{80,48},{96,64},{112,80},{1... | collective-permute-start | bytes 442376 | tf_op jit(solution)/shard_map/ppermute | solution.py:263
  14.4 11.6 %collective-permute-start.6 = (bf16[576,128]{1,0:T(8,128)(2,1)S(1)}, bf16[576,128]{1,0:T(8,128)(2,1)S(1)}, u32[]{:S(2)}, u32[]{:S(2)}) collective-permute-start(bf16[576,128]{1,0:T(8,128)(2,1)S(1)} %get-tuple-element.19), channel_id=1, source_target_pairs={{0,112},{16,0},{32,16},{48,32},{64,48},{80,64},{96,80},{112,96},{1... | collective-permute-start | bytes 442376 | tf_op jit(solution)/shard_map/ppermute | solution.py:263
  18.3 7.7 %copy-start.8 = (s32[8,32]{1,0:T(8,128)S(1)}, s32[8,32]{1,0:T(8,128)}, u32[]{:S(2)}) copy-start(s32[8,32]{1,0:T(8,128)} %ids_ref.3) | copy-start | bytes 3076
  18.3 7.7 %copy-start.10 = (s32[8]{0:T(128)S(1)}, s32[8]{0:T(128)}, u32[]{:S(2)}) copy-start(s32[8]{0:T(128)} %counts_ref.5) | copy-start | bytes 100
  18.3 42.6 %all-to-all-start = ((bf16[16,8,8,576]{3,2,1,0:T(8,128)(2,1)}), bf16[16,8,8,576]{3,2,1,0:T(8,128)(2,1)S(1)}, u32[]{:S(2)}, u32[]{:S(2)}) async-start(bf16[16,8,8,576]{3,2,1,0:T(8,128)(2,1)} %q_by_group.1), calls=%async_computation | async-start | bytes 2621440 | tf_op jit(solution)/shard_map/all_to_all | solution.py:265
  25.9 27.7 %copy-start.2 = (bf16[64,64,128]{2,1,0:T(8,128)(2,1)S(1)}, bf16[64,64,128]{2,1,0:T(8,128)(2,1)}, u32[]{:S(2)}) copy-start(bf16[64,64,128]{2,1,0:T(8,128)(2,1)} %query_ref.1) | copy-start | bytes 3145732
  25.9 27.7 %copy-start.3 = (bf16[2048,128]{1,0:T(8,128)(2,1)S(1)}, bf16[2048,128]{1,0:T(8,128)(2,1)}, u32[]{:S(2)}) copy-start(bf16[2048,128]{1,0:T(8,128)(2,1)} %keys_ref.1) | copy-start | bytes 1572868
  26.0 27.7 %copy-start.6 = (f32[64,64]{1,0:T(8,128)S(1)}, f32[64,64]{1,0:T(8,128)}, u32[]{:S(2)}) copy-start(f32[64,64]{1,0:T(8,128)} %weight_ref.1) | copy-start | bytes 49156
  27.5 20.1 %collective-permute-start.7 = (bf16[576,256]{1,0:T(8,128)(2,1)S(1)}, bf16[576,256]{1,0:T(8,128)(2,1)S(1)}, u32[]{:S(2)}, u32[]{:S(2)}) collective-permute-start(bf16[576,256]{1,0:T(8,128)(2,1)S(1)} %get-tuple-element.20.refs_0_), channel_id=1, source_target_pairs={{0,1},{1,2},{2,3},{3,0},{4,5},{5,6},{6,7},{7,4},{8,9},{9,10},{10,1... | collective-permute-start | bytes 884744 | tf_op jit(solution)/shard_map/ppermute | solution.py:268
  28.7 31.4 %collective-permute-start.8 = (bf16[576,256]{1,0:T(8,128)(2,1)S(1)}, bf16[576,256]{1,0:T(8,128)(2,1)S(1)}, u32[]{:S(2)}, u32[]{:S(2)}) collective-permute-start(bf16[576,256]{1,0:T(8,128)(2,1)S(1)} %get-tuple-element.20.refs_0_), channel_id=1, source_target_pairs={{0,2},{1,3},{2,0},{3,1},{4,6},{5,7},{6,4},{7,5},{8,10},{9,11},{10,... | collective-permute-start | bytes 884744 | tf_op jit(solution)/shard_map/ppermute | solution.py:268
  29.6 30.6 %collective-permute-start.9 = (bf16[576,256]{1,0:T(8,128)(2,1)S(1)}, bf16[576,256]{1,0:T(8,128)(2,1)S(1)}, u32[]{:S(2)}, u32[]{:S(2)}) collective-permute-start(bf16[576,256]{1,0:T(8,128)(2,1)S(1)} %get-tuple-element.20.refs_0_), channel_id=1, source_target_pairs={{0,3},{1,0},{2,1},{3,2},{4,7},{5,4},{6,5},{7,6},{8,11},{9,8},{10,9... | collective-permute-start | bytes 884744 | tf_op jit(solution)/shard_map/ppermute | solution.py:268
  30.7 29.4 %collective-permute-start.10 = (bf16[576,256]{1,0:T(8,128)(2,1)S(1)}, bf16[576,256]{1,0:T(8,128)(2,1)S(1)}, u32[]{:S(2)}, u32[]{:S(2)}) collective-permute-start(bf16[576,256]{1,0:T(8,128)(2,1)S(1)} %get-tuple-element.21.refs_4_), channel_id=1, source_target_pairs={{0,4},{1,5},{2,6},{3,7},{4,8},{5,9},{6,10},{7,11},{8,12},{9,13},{1... | collective-permute-start | bytes 884744 | tf_op jit(solution)/shard_map/ppermute | solution.py:269
  32.2 27.9 %collective-permute-start.11 = (bf16[576,256]{1,0:T(8,128)(2,1)S(1)}, bf16[576,256]{1,0:T(8,128)(2,1)S(1)}, u32[]{:S(2)}, u32[]{:S(2)}) collective-permute-start(bf16[576,256]{1,0:T(8,128)(2,1)S(1)} %get-tuple-element.21.refs_4_), channel_id=1, source_target_pairs={{0,8},{1,9},{2,10},{3,11},{4,12},{5,13},{6,14},{7,15},{8,0},{9,1},... | collective-permute-start | bytes 884744 | tf_op jit(solution)/shard_map/ppermute | solution.py:269
  47.6 12.5 %collective-permute-start.12 = (bf16[576,256]{1,0:T(8,128)(2,1)S(1)}, bf16[576,256]{1,0:T(8,128)(2,1)S(1)}, u32[]{:S(2)}, u32[]{:S(2)}) collective-permute-start(bf16[576,256]{1,0:T(8,128)(2,1)S(1)} %get-tuple-element.21.refs_4_), channel_id=1, source_target_pairs={{0,12},{1,13},{2,14},{3,15},{4,0},{5,1},{6,2},{7,3},{8,4},{9,5},{1... | collective-permute-start | bytes 884744 | tf_op jit(solution)/shard_map/ppermute | solution.py:269
  60.2 0.7 copy-start.4
  60.9 1.0 %copy-start.5 = (bf16[576,256]{1,0:T(8,128)(2,1)S(1)}, bf16[576,256]{1,0:T(8,128)(2,1)}, u32[]{:S(2)}) copy-start(bf16[576,256]{1,0:T(8,128)(2,1)} %copy-done.4) | copy-start | bytes 884740

commit v3 on v2

v3 whole, which is shorter than its diff:
```python
import jax
import jax.numpy as jnp
from jax import lax
from jax.experimental import pallas as pl
from jax.experimental.pallas import tpu as pltpu
from jax.sharding import PartitionSpec as P


BLOCK = 64
SHARDS = 8
PART = 16
SCALE = 192.0 ** (-0.5)
INDEX_SCALE = 128.0 ** (-0.5)
F32 = jnp.float32
BF16 = jnp.bfloat16
VMEM = pl.BlockSpec(memory_space=pltpu.VMEM)
SMEM = pl.BlockSpec(memory_space=pltpu.SMEM)


def iota(shape, dim):
    return lax.broadcasted_iota(jnp.int32, shape, dim)


def valid_ids(ids_ref, counts_ref):
    tiles, entries = ids_ref.shape
    tile = iota((tiles, entries), 0)
    count = jnp.zeros((tiles, entries), jnp.int32)
    for t in range(tiles):
        count = jnp.where(tile == t, counts_ref[t], count)
    return jnp.where(iota((tiles, entries), 1) < count, ids_ref[...], -1)


def place():
    group = lax.axis_index("head")
    row_y, row_z = group >> 2, group & 3
    return lax.axis_index("ctx"), (row_y + 2 * row_z) & 3, (2 * row_y + row_z) & 3


def row_of(part, first, second):
    return jnp.where(part < 8, first * 8 + part, 24 + second * 8 + part)


def hot(index, target):
    return (index == target).astype(F32).astype(BF16)


def slot_sources(ids, tile):
    mine = jnp.sum(jnp.where(iota(ids.shape, 0) == tile, ids, 0), axis=0, keepdims=True)
    owner = jnp.where(mine < 0, 2 * SHARDS, mine >> 5)
    shard = iota(ids.shape, 0)
    here = jnp.sum((owner == shard).astype(F32), axis=1, keepdims=True).astype(jnp.int32)
    end = jnp.sum((owner <= shard).astype(F32), axis=1, keepdims=True).astype(jnp.int32)
    column = iota((SHARDS, 512), 1)
    entry = (column & 255) >> 3
    skipped = jnp.sum(jnp.where(entry >= end, 128 - 16 * here, 0), axis=0, keepdims=True)
    part = (column & 7) + ((column >> 8) << 3)
    return entry * PART + part + skipped, end[SHARDS - 1 :, :]


def gather_kernel(ids_ref, counts_ref, cache_ref, *refs):
    out_refs, (source_ref, past_ref, held, sems) = refs[:-4], refs[-4:]
    keys = cache_ref.shape[1]
    copies = []
    for i, c in enumerate(range(0, keys, 512)):
        copies.append(pltpu.make_async_copy(cache_ref.at[:, pl.ds(c, 512)], held.at[i], sems.at[i]))
        copies[i].start()
    shard, first, second = place()
    ids = valid_ids(ids_ref, counts_ref)
    tiles, entries = ids.shape
    blocks = keys // BLOCK
    lane = iota((tiles, 128), 1)
    block_of_lane = jnp.where(lane < blocks, lane + shard * blocks, -2)
    member = jnp.zeros((tiles, 128), F32)
    for j in range(entries):
        member = jnp.where(ids[:, j : j + 1] == block_of_lane, 1.0, member)
    before = (iota((128, 128), 0) < iota((128, 128), 1)).astype(BF16)
    rank = jnp.dot(member.astype(BF16), before, preferred_element_type=F32)
    rank = jnp.where(member > 0.0, rank, -1.0)
    slot = (lane >> 4).astype(F32)
    target = jnp.full((tiles, 128), -1, jnp.int32)
    for b in range(blocks):
        target = jnp.where(rank[:, b : b + 1] == slot, b * PART + (lane & 15), target)
    column = iota((512, 128), 1)
    keep = hot(iota((512, 128), 0), (column >> 4) * BLOCK + row_of(column & 15, first, second))
    own = []
    for i, copy in enumerate(copies):
        copy.wait()
        own.append(jnp.dot(held[i], keep, preferred_element_type=F32).astype(BF16))
    own = jnp.concatenate(own, axis=1)
    index = iota((own.shape[1], 128), 0)
    for d in range(0, tiles, 2):
        pair = []
        for u in (d, d + 1):
            chosen = iota((tiles, 128), 0) == ((shard + u) & 7)
            pair.append(hot(index, jnp.sum(jnp.where(chosen, target, 0), axis=0, keepdims=True)))
        got = jnp.dot(own, jnp.concatenate(pair, axis=1), preferred_element_type=F32).astype(BF16)
        out_refs[d][...] = got[:, :128]
        out_refs[d + 1][...] = got[:, 128:]
    source, count = slot_sources(ids, shard)
    source_ref[...] = source
    past_ref[...] = jnp.broadcast_to((count - 2) * BLOCK, past_ref.shape)


def gather_parts(block_ids, block_counts, cache_t):
    width, keys = cache_t.shape
    tiles = block_ids.shape[0]
    return pl.pallas_call(
        gather_kernel,
        out_shape=[jax.ShapeDtypeStruct((width, 128), BF16)] * tiles
        + [jax.ShapeDtypeStruct((SHARDS, 512), jnp.int32), jax.ShapeDtypeStruct((8, 128), jnp.int32)],
        in_specs=[VMEM, SMEM, pl.BlockSpec(memory_space=pltpu.HBM)],
        out_specs=[VMEM] * (tiles + 2),
        scratch_shapes=[pltpu.VMEM((keys // 512, width, 512), BF16), pltpu.SemaphoreType.DMA((keys // 512,))],
        cost_estimate=pl.CostEstimate(
            flops=2 * width * keys * 1024, bytes_accessed=2 * width * keys * 2, transcendentals=0
        ),
        name="gather_parts",
    )(block_ids, block_counts, cache_t)


def compact_kernel(source_ref, *refs):
    part_refs, (own_ref, up_ref, down_ref, right_ref, left_ref) = refs[:-5], refs[-5:]
    tile = lax.axis_index("ctx")
    source = source_ref[0:1, :]
    row = iota((128, 512), 0)
    total = jnp.zeros((own_ref.shape[0], 512), F32)
    for d in range(0, SHARDS, 2):
        pick = jnp.concatenate([hot(row + ((tile - u) & 7) * 128, source) for u in (d, d + 1)], axis=0)
        pair = jnp.concatenate([part_refs[d][...], part_refs[d + 1][...]], axis=1)
        total = total + jnp.dot(pair, pick, preferred_element_type=F32)
    total = total.astype(BF16)
    own_ref[...] = total
    up_ref[...] = total[:, :384]
    down_ref[:, :256] = total[:, :256]
    down_ref[:, 256:] = total[:, 384:]
    right_ref[:, :256] = total[:, 256:]
    right_ref[:, 256:] = total[:, :128]
    left_ref[:, :256] = total[:, 256:]
    left_ref[:, 256:] = total[:, 128:256]


def compact_parts(source, parts):
    width = parts[0].shape[0]
    sent = jax.ShapeDtypeStruct((width, 384), BF16)
    return pl.pallas_call(
        compact_kernel,
        out_shape=[jax.ShapeDtypeStruct((width, 512), BF16)] + [sent] * 4,
        in_specs=[VMEM] * (1 + len(parts)),
        out_specs=[VMEM] * 5,
        cost_estimate=pl.CostEstimate(
            flops=2 * width * 1024 * 512, bytes_accessed=width * 1536 * 2, transcendentals=0
        ),
        compiler_params=pltpu.CompilerParams(vmem_limit_bytes=12 << 20),
        name="compact_parts",
    )(source, *parts)


def q_prep_kernel(q_ref, out_ref):
    groups, rows, heads, width = out_ref.shape
    for i in range(rows):
        out_ref[:, i] = q_ref[i].T.reshape(groups, heads, width)


def q_by_group(q_latent, groups):
    rows, heads, width = q_latent.shape
    return pl.pallas_call(
        q_prep_kernel,
        out_shape=jax.ShapeDtypeStruct((groups, rows, heads // groups, width), BF16),
        in_specs=[VMEM],
        out_specs=VMEM,
        cost_estimate=pl.CostEstimate(flops=0, bytes_accessed=rows * heads * width * 4, transcendentals=0),
        compiler_params=pltpu.CompilerParams(vmem_limit_bytes=8 << 20),
        name="q_by_group",
    )(q_latent.transpose(0, 2, 1))


def index_kernel(query_ref, weight_ref, keys_ref, out_ref):
    rows, heads, dim = query_ref.shape
    flat = query_ref[...].reshape(rows * heads, dim)
    weight = weight_ref[...] * INDEX_SCALE
    span = 256
    for c in range(keys_ref.shape[0] // span):
        dots = lax.dot_general(
            flat, keys_ref[c * span : (c + 1) * span, :], (((1,), (1,)), ((), ())), preferred_element_type=F32
        ).reshape(rows, heads, span)
        out_ref[:, c * span : (c + 1) * span] = jnp.sum(
            jnp.maximum(dots, 0.0) * weight[:, :, None], axis=1
        )


def index_scores_of(index_query, index_weight, index_keys):
    rows, heads, dim = index_query.shape
    keys = index_keys.shape[0]
    step = 8
    return pl.pallas_call(
        index_kernel,
        grid=(rows // step,),
        out_shape=jax.ShapeDtypeStruct((rows, keys), F32),
        in_specs=[
            pl.BlockSpec((step, heads, dim), lambda i: (i, 0, 0)),
            pl.BlockSpec((step, heads), lambda i: (i, 0)),
            pl.BlockSpec((keys, dim), lambda i: (0, 0)),
        ],
        out_specs=pl.BlockSpec((step, keys), lambda i: (i, 0)),
        cost_estimate=pl.CostEstimate(
            flops=8 * rows * heads * dim * keys, bytes_accessed=rows * heads * dim * 2 + rows * keys * 4, transcendentals=0
        ),
        compiler_params=pltpu.CompilerParams(vmem_limit_bytes=16 << 20),
        name="index_scores",
    )(index_query, index_weight, index_keys)


def masked_scores(q, keys, tiles, limit):
    scores = jnp.dot(q, keys, preferred_element_type=F32)
    rows = q.shape[0]
    lane = iota((rows, 128), 1)
    offset = (lane >> 3) * BLOCK + (lane & 7)
    pieces = []
    for t, first_key in enumerate(tiles):
        piece = scores[:, t * 128 : (t + 1) * 128]
        if first_key is not None:
            piece = jnp.where(offset <= limit - first_key, piece, -jnp.inf)
        pieces.append(piece)
    return jnp.concatenate(pieces, axis=1)


def own_kernel(past_ref, q_ref, keys_ref, top_ref, total_ref, mixed_ref):
    _, first, second = place()
    past = past_ref[0:1, :]
    late = 16 * BLOCK
    tiles = (None, late + first * 8, None, late + 32 + second * 8)
    rows, step = q_ref.shape[0], 256
    for a in range(0, rows, step):
        limit = past + a // 8 + (iota((step, 128), 0) >> 3)
        scores = masked_scores(q_ref[a : a + step, :], keys_ref[...], tiles, limit)
        top = jnp.max(scores, axis=1, keepdims=True)
        weights = jnp.exp((scores - top) * SCALE)
        top_ref[a : a + step, :] = jnp.broadcast_to(top, (step, 128))
        total_ref[a : a + step, :] = jnp.broadcast_to(jnp.sum(weights, axis=1, keepdims=True), (step, 128))
        mixed_ref[a : a + step, :] = lax.dot_general(
            weights.astype(BF16), keys_ref[0:512, :], (((1,), (1,)), ((), ())), preferred_element_type=F32
        )


def attend_own(past, q, keys):
    rows, width = q.shape
    count = keys.shape[1]
    return pl.pallas_call(
        own_kernel,
        out_shape=[
            jax.ShapeDtypeStruct((rows, 128), F32),
            jax.ShapeDtypeStruct((rows, 128), F32),
            jax.ShapeDtypeStruct((rows, 512), F32),
        ],
        in_specs=[VMEM] * 3,
        out_specs=[VMEM] * 3,
        cost_estimate=pl.CostEstimate(
            flops=2 * rows * count * (width + 512), bytes_accessed=rows * 4352, transcendentals=rows * count
        ),
        compiler_params=pltpu.CompilerParams(vmem_limit_bytes=16 << 20),
        name="attend_own",
    )(past, q, keys)


def rest_kernel(past_ref, q_ref, top_ref, total_ref, mixed_ref, up_ref, down_ref, right_ref, left_ref, out_ref, keys_ref):
    _, first, second = place()
    past = past_ref[0:1, :]
    late = 16 * BLOCK

    def of_first(step):
        return late + ((first + step) & 3) * 8

    def of_second(step):
        return late + 32 + ((second + step) & 3) * 8

    tiles = (
        (None, of_first(-1), None)
        + (None, of_first(1), of_second(2))
        + (None, of_second(-1), None)
        + (None, of_second(1), of_first(2))
    )
    for i, ref in enumerate((up_ref, down_ref, right_ref, left_ref)):
        keys_ref[:, i * 384 : (i + 1) * 384] = ref[...]
    rows, step = q_ref.shape[0], 256
    for a in range(0, rows, step):
        limit = past + a // 8 + (iota((step, 128), 0) >> 3)
        scores = masked_scores(q_ref[a : a + step, :], keys_ref[...], tiles, limit)
        before = top_ref[a : a + step, 0:1]
        top = jnp.maximum(jnp.max(scores, axis=1, keepdims=True), before)
        weights = jnp.exp((scores - top) * SCALE)
        fade = jnp.exp((before - top) * SCALE)
        total = total_ref[a : a + step, 0:1] * fade + jnp.sum(weights, axis=1, keepdims=True)
        mixed = mixed_ref[a : a + step, :] * fade + lax.dot_general(
            weights.astype(BF16), keys_ref[0:512, :], (((1,), (1,)), ((), ())), preferred_element_type=F32
        )
        out_ref[a : a + step, :] = (mixed / total).astype(BF16)


def attend_rest(past, q, state, parts):
    rows, width = q.shape
    count = sum(part.shape[1] for part in parts)
    return pl.pallas_call(
        rest_kernel,
        out_shape=jax.ShapeDtypeStruct((rows, 512), BF16),
        in_specs=[VMEM] * (5 + len(parts)),
        out_specs=VMEM,
        scratch_shapes=[pltpu.VMEM((width, count), BF16)],
        cost_estimate=pl.CostEstimate(
            flops=2 * rows * count * (width + 512), bytes_accessed=rows * 5376, transcendentals=rows * count
        ),
        compiler_params=pltpu.CompilerParams(vmem_limit_bytes=24 << 20),
        name="attend_rest",
    )(past, q, *state, *parts)


def turn(d):
    return [(i, (i + d) % SHARDS) for i in range(SHARDS)]


def line(dy, dz):
    return [(y * 4 + z, ((y + dy) % 4) * 4 + (z + dz) % 4) for y in range(4) for z in range(4)]


def body(q_latent, index_query, index_weight, index_keys, latent_cache, block_ids, block_counts):
    rows, heads, width = q_latent.shape
    groups = lax.axis_size("head")
    *outgoing, source, past = gather_parts(block_ids, block_counts, latent_cache.T)
    incoming = [outgoing[0]] + [lax.ppermute(outgoing[d], "ctx", turn(d)) for d in range(1, SHARDS)]
    by_group = q_by_group(q_latent, groups)
    head_query = lax.all_to_all(by_group, "head", split_axis=0, concat_axis=0, tiled=True)
    index_scores = index_scores_of(index_query, index_weight, index_keys)
    own, up, down, right, left = compact_parts(source, incoming)
    parts = [
        lax.ppermute(part, "head", line(*step))
        for part, step in ((up, (1, 0)), (down, (-1, 0)), (right, (0, 1)), (left, (0, -1)))
    ]
    flat_query = head_query.reshape(-1, width)
    state = attend_own(past, flat_query, own)
    attention = attend_rest(past, flat_query, state, parts)
    return attention.reshape(rows * groups, heads // groups, 512), index_scores


def solution(mesh):
    return jax.shard_map(
        body,
        mesh=mesh,
        in_specs=(
            P(("ctx", "head"), None, None),
            P("head", None, None),
            P("head", None),
            P("ctx", None),
            P("ctx", None),
            P(),
            P(),
        ),
        out_specs=(P("ctx", "head", None), P("head", "ctx")),
        check_vma=False,
    )
```

time: 75.5 us -> 64.4 us (0.85)
  the two profiles are of different devices: /device:TPU:72 before, /device:TPU:1 now
where the time goes in v3:
time: 64.4 us; the launch traced here: 64.1 us
  Pallas kernels  25.2 us (39%)
  starting transfers between devices  24 us (37%)
  waiting for transfers between devices  12.2 us (19%)
  local copies, waits for them, and re-layouts  1.93 us (3%)
  between operations  0.77 us (1%)
    ppermute x7, starting transfers between devices, body(): lax.ppermute(outgoing[d], 'ctx', turn(d))  10.6 us
    ppermute x7, waiting for transfers between devices, body(): lax.ppermute(outgoing[d], 'ctx', turn(d))  9.26 us
    pallas_call x1, Pallas kernels, attend_rest(): pl.pallas_call(rest_kernel, out_shape=jax.ShapeDtypeStruct((rows, 512), B...  8.24 us
    all_to_all x1, starting transfers between devices, body(): lax.all_to_all(by_group, 'head', split_axis=0, concat_axis=0, tiled=True)  7.91 us
    pallas_call x1, Pallas kernels, index_scores_of(): pl.pallas_call(index_kernel, grid=(rows // step,), out_shape=jax.ShapeDty...  6.51 us
    ppermute x4, starting transfers between devices, body(): lax.ppermute(part, 'head', line(*step))  5.53 us
    pallas_call x1, Pallas kernels, gather_parts(): pl.pallas_call(gather_kernel, out_shape=[jax.ShapeDtypeStruct((width, 128...  5.05 us
    ppermute x4, waiting for transfers between devices, body(): lax.ppermute(part, 'head', line(*step))  2.93 us
  transfers between devices with their start and end apart: 12, of which 7 were waited for; matrix products, arithmetic and copies ran while one was open for 0% of the time, Pallas kernels for 19%

profile of v3, /device:TPU:1, one launch (start us, length us, event | category | flops | bytes accessed | tf_op | source)
XLA Modules:
  0.0 64.1 jit_solution(11335642989510669949)
XLA Ops:
  0.6 0.0 copy-start
  0.6 5.1 %gather_parts.1 = (bf16[576,128]{1,0:T(8,128)(2,1)}, bf16[576,128]{1,0:T(8,128)(2,1)}, bf16[576,128]{1,0:T(8,128)(2,1)}, bf16[576,128]{1,0:T(8,128)(2,1)}, bf16[...) custom-call(s32[8,32]{1,0:T(8,128)} %ids_ref.1, ...), custom_call_target="tpu_custom_call" | custom-call | flops 2415919104 | bytes 4718592 | tf_op jit(solution)/shard_map/gather_parts/pallas_call | solution.py:107
  5.7 2.6 %collective-permute-start = (bf16[576,128]{1,0:T(8,128)(2,1)}, bf16[576,128]{1,0:T(8,128)(2,1)S(1)}, u32[]{:S(2)}, u32[]{:S(2)}) collective-permute-start(bf16[576,128]{1,0:T(8,128)(2,1)} %get-tuple-element.23), channel_id=1, source_target_pairs={{0,16},{16,32},{32,48},{48,64},{64,80},{80,96},{96,112},{112,0},{1... | collective-permute-start | bytes 442376 | tf_op jit(solution)/shard_map/ppermute | solution.py:328
  8.3 1.2 %collective-permute-start.1 = (bf16[576,128]{1,0:T(8,128)(2,1)}, bf16[576,128]{1,0:T(8,128)(2,1)S(1)}, u32[]{:S(2)}, u32[]{:S(2)}) collective-permute-start(bf16[576,128]{1,0:T(8,128)(2,1)} %get-tuple-element.24), channel_id=1, source_target_pairs={{0,32},{16,48},{32,64},{48,80},{64,96},{80,112},{96,0},{112,16},{1... | collective-permute-start | bytes 442376 | tf_op jit(solution)/shard_map/ppermute | solution.py:328
  9.5 0.0 copy-done
  9.5 1.5 %q_by_group.1 = bf16[16,8,8,576]{3,2,1,0:T(8,128)(2,1)} custom-call(bf16[8,576,128]{2,1,0:T(8,128)(2,1)S(1)} %bitcast.6), custom_call_target="tpu_custom_call" | custom-call | bytes 2359296 | tf_op jit(solution)/shard_map/q_by_group/pallas_call | solution.py:166
  11.0 0.0 copy-start.13
  11.0 0.0 copy-start.12
  11.0 0.0 copy-start.11
  11.0 0.0 copy-start.10
  11.0 0.0 copy-start.9
  11.0 0.0 copy-start.6
  11.0 0.0 copy-start.7
  11.0 7.9 %all-to-all-start = ((bf16[16,8,8,576]{3,2,1,0:T(8,128)(2,1)}), bf16[16,8,8,576]{3,2,1,0:T(8,128)(2,1)S(1)}, u32[]{:S(2)}, u32[]{:S(2)}) async-start(bf16[16,8,8,576]{3,2,1,0:T(8,128)(2,1)} %q_by_group.1), calls=%async_computation | async-start | bytes 2621440 | tf_op jit(solution)/shard_map/all_to_all | solution.py:330
  19.0 0.0 copy-start.1
  19.0 0.0 copy-start.2
  19.0 0.0 copy-start.3
  19.0 0.0 copy-done.13
  19.0 1.9 %collective-permute-start.2 = (bf16[576,128]{1,0:T(8,128)(2,1)S(1)}, bf16[576,128]{1,0:T(8,128)(2,1)S(1)}, u32[]{:S(2)}, u32[]{:S(2)}) collective-permute-start(bf16[576,128]{1,0:T(8,128)(2,1)S(1)} %copy-done.13), channel_id=1, source_target_pairs={{0,48},{16,64},{32,80},{48,96},{64,112},{80,0},{96,16},{112,32},{1... | collective-permute-start | bytes 442376 | tf_op jit(solution)/shard_map/ppermute | solution.py:328
  21.0 0.0 copy-done.12
  21.0 0.5 collective-permute-start.3
  21.5 0.0 copy-done.11
  21.5 1.7 %collective-permute-start.4 = (bf16[576,128]{1,0:T(8,128)(2,1)S(1)}, bf16[576,128]{1,0:T(8,128)(2,1)S(1)}, u32[]{:S(2)}, u32[]{:S(2)}) collective-permute-start(bf16[576,128]{1,0:T(8,128)(2,1)S(1)} %copy-done.11), channel_id=1, source_target_pairs={{0,80},{16,96},{32,112},{48,0},{64,16},{80,32},{96,48},{112,64},{1... | collective-permute-start | bytes 442376 | tf_op jit(solution)/shard_map/ppermute | solution.py:328
  23.1 0.0 collective-permute-done.refs_1_
  23.2 0.0 copy-done.10
  23.2 0.7 %collective-permute-start.5 = (bf16[576,128]{1,0:T(8,128)(2,1)S(1)}, bf16[576,128]{1,0:T(8,128)(2,1)S(1)}, u32[]{:S(2)}, u32[]{:S(2)}) collective-permute-start(bf16[576,128]{1,0:T(8,128)(2,1)S(1)} %copy-done.10), channel_id=1, source_target_pairs={{0,96},{16,112},{32,0},{48,16},{64,32},{80,48},{96,64},{112,80},{1... | collective-permute-start | bytes 442376 | tf_op jit(solution)/shard_map/ppermute | solution.py:328
  23.8 0.0 collective-permute-done.1.refs_2_
  23.8 0.0 copy-done.9
  23.8 2.0 %collective-permute-start.6 = (bf16[576,128]{1,0:T(8,128)(2,1)S(1)}, bf16[576,128]{1,0:T(8,128)(2,1)S(1)}, u32[]{:S(2)}, u32[]{:S(2)}) collective-permute-start(bf16[576,128]{1,0:T(8,128)(2,1)S(1)} %copy-done.9), channel_id=1, source_target_pairs={{0,112},{16,0},{32,16},{48,32},{64,48},{80,64},{96,80},{112,96},{1... | collective-permute-start | bytes 442376 | tf_op jit(solution)/shard_map/ppermute | solution.py:328
  25.8 0.8 %collective-permute-done.2.refs_3_ = bf16[576,128]{1,0:T(8,128)(2,1)S(1)} collective-permute-done((bf16[576,128]{1,0:T(8,128)(2,1)S(1)}, bf16[576,128]{1,0:T(8,128)(2,1)S(1)}, u32[]{:S(2)}, u32[]{:S(2)}) %collective-permute-start.2) | collective-permute-done | bytes 147488 | tf_op jit(solution)/shard_map/ppermute | solution.py:328
  26.6 1.7 %collective-permute-done.3.refs_4_ = bf16[576,128]{1,0:T(8,128)(2,1)S(1)} collective-permute-done((bf16[576,128]{1,0:T(8,128)(2,1)S(1)}, bf16[576,128]{1,0:T(8,128)(2,1)S(1)}, u32[]{:S(2)}, u32[]{:S(2)}) %collective-permute-start.3) | collective-permute-done | bytes 147488 | tf_op jit(solution)/shard_map/ppermute | solution.py:328
  28.3 2.3 %collective-permute-done.4.refs_5_ = bf16[576,128]{1,0:T(8,128)(2,1)S(1)} collective-permute-done((bf16[576,128]{1,0:T(8,128)(2,1)S(1)}, bf16[576,128]{1,0:T(8,128)(2,1)S(1)}, u32[]{:S(2)}, u32[]{:S(2)}) %collective-permute-start.4) | collective-permute-done | bytes 147488 | tf_op jit(solution)/shard_map/ppermute | solution.py:328
  30.6 2.9 %collective-permute-done.5.refs_6_ = bf16[576,128]{1,0:T(8,128)(2,1)S(1)} collective-permute-done((bf16[576,128]{1,0:T(8,128)(2,1)S(1)}, bf16[576,128]{1,0:T(8,128)(2,1)S(1)}, u32[]{:S(2)}, u32[]{:S(2)}) %collective-permute-start.5) | collective-permute-done | bytes 147488 | tf_op jit(solution)/shard_map/ppermute | solution.py:328
  33.5 1.5 %collective-permute-done.6.refs_7_ = bf16[576,128]{1,0:T(8,128)(2,1)S(1)} collective-permute-done((bf16[576,128]{1,0:T(8,128)(2,1)S(1)}, bf16[576,128]{1,0:T(8,128)(2,1)S(1)}, u32[]{:S(2)}, u32[]{:S(2)}) %collective-permute-start.6) | collective-permute-done | bytes 147488 | tf_op jit(solution)/shard_map/ppermute | solution.py:328
  35.0 0.0 copy-done.6
  35.0 0.0 copy-done.7
  35.0 1.6 %compact_parts.1 = (bf16[576,512]{1,0:T(8,128)(2,1)S(1)}, bf16[576,384]{1,0:T(8,128)(2,1)S(1)}, bf16[576,384]{1,0:T(8,128)(2,1)S(1)}, bf16[576,384]{1,0:T(8,128)(2,1)S(1)}, bf16[576,384]{1,0:T(8,128)(2,1)}) custom-call(s32[8,512]{1,0:T(8,128)S(1)} %copy-done.7, bf16[576,128]{1,0:T(8,128)(2,1)S(1)} %copy-done.6, ...), custom_call_target="tpu_custom_call" | custom-call | flops 603979776 | bytes 1769472 | tf_op jit(solution)/shard_map/compact_parts/pallas_call | solution.py:145
  36.6 0.0 copy-start.4
  36.6 0.8 %copy-done.4 = bf16[576,512]{1,0:T(8,128)(2,1)} copy-done((bf16[576,512]{1,0:T(8,128)(2,1)}, bf16[576,512]{1,0:T(8,128)(2,1)S(1)}, u32[]{:S(2)}) %copy-start.4) | copy-done | bytes 589848
  37.4 2.9 %collective-permute-start.10 = (bf16[576,384]{1,0:T(8,128)(2,1)}, bf16[576,384]{1,0:T(8,128)(2,1)S(1)}, u32[]{:S(2)}, u32[]{:S(2)}) collective-permute-start(bf16[576,384]{1,0:T(8,128)(2,1)} %get-tuple-element.37), channel_id=1, source_target_pairs={{0,3},{1,0},{2,1},{3,2},{4,7},{5,4},{6,5},{7,6},{8,11},{9,8},{10,9... | collective-permute-start | bytes 1327112 | tf_op jit(solution)/shard_map/ppermute | solution.py:334
  40.3 1.2 %collective-permute-start.7 = (bf16[576,384]{1,0:T(8,128)(2,1)S(1)}, bf16[576,384]{1,0:T(8,128)(2,1)S(1)}, u32[]{:S(2)}, u32[]{:S(2)}) collective-permute-start(bf16[576,384]{1,0:T(8,128)(2,1)S(1)} %get-tuple-element.34), channel_id=1, source_target_pairs={{0,4},{1,5},{2,6},{3,7},{4,8},{5,9},{6,10},{7,11},{8,12},{9,13},{1... | collective-permute-start | bytes 1327112 | tf_op jit(solution)/shard_map/ppermute | solution.py:334
  41.5 1.5 %collective-permute-start.8 = (bf16[576,384]{1,0:T(8,128)(2,1)S(1)}, bf16[576,384]{1,0:T(8,128)(2,1)}, u32[]{:S(2)}, u32[]{:S(2)}) collective-permute-start(bf16[576,384]{1,0:T(8,128)(2,1)S(1)} %get-tuple-element.35), channel_id=1, source_target_pairs={{0,12},{1,13},{2,14},{3,15},{4,0},{5,1},{6,2},{7,3},{8,4},{9,5},{1... | collective-permute-start | bytes 1327112 | tf_op jit(solution)/shard_map/ppermute | solution.py:334
  43.0 0.0 copy-start.8
  43.0 0.0 collective-permute-start.9
  43.0 0.0 copy-done.1
  43.0 0.0 copy-done.2
  43.0 0.0 copy-done.3
  43.0 6.5 %index_scores.1 = f32[64,2048]{1,0:T(8,128)} custom-call(bf16[64,64,128]{2,1,0:T(8,128)(2,1)S(1)} %copy-done.1, f32[64,64]{1,0:T(8,128)S(1)} %copy-done.3, bf16[2048,128]{1,0:T(8,128)(2,1)S(1)} %copy-done.2), custom_call_target="tpu_custom_call" | custom-call | flops 8589934592 | bytes 1572864 | tf_op jit(solution)/shard_map/index_scores/pallas_call | solution.py:195
  49.5 0.0 all-to-all-done
  49.5 0.0 copy-done.8
  49.5 0.0 copy-start.5
  49.5 1.1 %copy-done.5 = bf16[576,512]{1,0:T(8,128)(2,1)S(1)} copy-done((bf16[576,512]{1,0:T(8,128)(2,1)S(1)}, bf16[576,512]{1,0:T(8,128)(2,1)}, u32[]{:S(2)}) %copy-start.5) | copy-done | bytes 589848
  50.6 2.3 %attend_own.1 = (f32[1024,128]{1,0:T(8,128)S(1)}, f32[1024,128]{1,0:T(8,128)S(1)}, f32[1024,512]{1,0:T(8,128)S(1)}) custom-call(s32[8,128]{1,0:T(8,128)S(1)} %copy-done.8, bf16[1024,576]{1,0:T(8,128)(2,1)S(1)} %bitcast.4, bf16[576,512]{1,0:T(8,128)(2,1)S(1)} %copy-done.5), custom_call_target="tpu_custom_call" | custom-call | flops 1140850688 | bytes 4456448 | tf_op jit(solution)/shard_map/attend_own/pallas_call | solution.py:248
  52.9 0.0 collective-permute-done.10.left_ref
  52.9 0.8 %collective-permute-done.7.up_ref = bf16[576,384]{1,0:T(8,128)(2,1)S(1)} collective-permute-done((bf16[576,384]{1,0:T(8,128)(2,1)S(1)}, bf16[576,384]{1,0:T(8,128)(2,1)S(1)}, u32[]{:S(2)}, u32[]{:S(2)}) %collective-permute-start.7) | collective-permute-done | bytes 442400 | tf_op jit(solution)/shard_map/ppermute | solution.py:334
  53.7 0.0 collective-permute-done.8.down_ref
  53.7 2.1 %collective-permute-done.9.right_ref = bf16[576,384]{1,0:T(8,128)(2,1)} collective-permute-done((bf16[576,384]{1,0:T(8,128)(2,1)S(1)}, bf16[576,384]{1,0:T(8,128)(2,1)}, u32[]{:S(2)}, u32[]{:S(2)}) %collective-permute-start.9) | collective-permute-done | bytes 442400 | tf_op jit(solution)/shard_map/ppermute | solution.py:334
  55.9 8.2 %attend_rest.1 = bf16[1024,512]{1,0:T(8,128)(2,1)} custom-call(s32[8,128]{1,0:T(8,128)S(1)} %copy-done.8, bf16[1024,576]{1,0:T(8,128)(2,1)S(1)} %bitcast.5, f32[1024,128]{1,0:T(8,128)S(1)} %get-tuple-element.31.top_ref, f32[1024,128]{1,0:T(8,128)S(1)} %get-tuple-element.32.total_ref, f32[1024,512]{1,0:T(8,128)S(1)} %get-tuple-element.33.mixed_ref, ...), custom_call_target="tpu_custom_call" | custom-call | flops 3422552064 | bytes 5505024 | tf_op jit(solution)/shard_map/attend_rest/pallas_call | solution.py:302
Async XLA Ops:
  0.6 8.9 %copy-start = (bf16[8,128,576]{1,2,0:T(8,128)(2,1)S(1)}, bf16[8,128,576]{1,2,0:T(8,128)(2,1)}, u32[]{:S(2)}) copy-start(bf16[8,128,576]{1,2,0:T(8,128)(2,1)} %param.7) | copy-start | bytes 3538948
  5.7 17.4 %collective-permute-start = (bf16[576,128]{1,0:T(8,128)(2,1)}, bf16[576,128]{1,0:T(8,128)(2,1)S(1)}, u32[]{:S(2)}, u32[]{:S(2)}) collective-permute-start(bf16[576,128]{1,0:T(8,128)(2,1)} %get-tuple-element.23), channel_id=1, source_target_pairs={{0,16},{16,32},{32,48},{48,64},{64,80},{80,96},{96,112},{112,0},{1... | collective-permute-start | bytes 442376 | tf_op jit(solution)/shard_map/ppermute | solution.py:328
  8.3 15.5 %collective-permute-start.1 = (bf16[576,128]{1,0:T(8,128)(2,1)}, bf16[576,128]{1,0:T(8,128)(2,1)S(1)}, u32[]{:S(2)}, u32[]{:S(2)}) collective-permute-start(bf16[576,128]{1,0:T(8,128)(2,1)} %get-tuple-element.24), channel_id=1, source_target_pairs={{0,32},{16,48},{32,64},{48,80},{64,96},{80,112},{96,0},{112,16},{1... | collective-permute-start | bytes 442376 | tf_op jit(solution)/shard_map/ppermute | solution.py:328
  11.0 8.0 %copy-start.13 = (bf16[576,128]{1,0:T(8,128)(2,1)S(1)}, bf16[576,128]{1,0:T(8,128)(2,1)}, u32[]{:S(2)}) copy-start(bf16[576,128]{1,0:T(8,128)(2,1)} %get-tuple-element.25) | copy-start | bytes 442372
  11.0 10.0 %copy-start.12 = (bf16[576,128]{1,0:T(8,128)(2,1)S(1)}, bf16[576,128]{1,0:T(8,128)(2,1)}, u32[]{:S(2)}) copy-start(bf16[576,128]{1,0:T(8,128)(2,1)} %get-tuple-element.26) | copy-start | bytes 442372
  11.0 10.5 %copy-start.11 = (bf16[576,128]{1,0:T(8,128)(2,1)S(1)}, bf16[576,128]{1,0:T(8,128)(2,1)}, u32[]{:S(2)}) copy-start(bf16[576,128]{1,0:T(8,128)(2,1)} %get-tuple-element.27) | copy-start | bytes 442372
  11.0 12.2 %copy-start.10 = (bf16[576,128]{1,0:T(8,128)(2,1)S(1)}, bf16[576,128]{1,0:T(8,128)(2,1)}, u32[]{:S(2)}) copy-start(bf16[576,128]{1,0:T(8,128)(2,1)} %get-tuple-element.28) | copy-start | bytes 442372
  11.0 12.8 %copy-start.9 = (bf16[576,128]{1,0:T(8,128)(2,1)S(1)}, bf16[576,128]{1,0:T(8,128)(2,1)}, u32[]{:S(2)}) copy-start(bf16[576,128]{1,0:T(8,128)(2,1)} %get-tuple-element.29) | copy-start | bytes 442372
  11.0 24.0 %copy-start.6 = (bf16[576,128]{1,0:T(8,128)(2,1)S(1)}, bf16[576,128]{1,0:T(8,128)(2,1)}, u32[]{:S(2)}) copy-start(bf16[576,128]{1,0:T(8,128)(2,1)} %get-tuple-element.22.refs_0_) | copy-start | bytes 442372
  11.0 24.0 %copy-start.7 = (s32[8,512]{1,0:T(8,128)S(1)}, s32[8,512]{1,0:T(8,128)}, u32[]{:S(2)}) copy-start(s32[8,512]{1,0:T(8,128)} %get-tuple-element.21.source_ref) | copy-start | bytes 49156
  11.0 38.5 %all-to-all-start = ((bf16[16,8,8,576]{3,2,1,0:T(8,128)(2,1)}), bf16[16,8,8,576]{3,2,1,0:T(8,128)(2,1)S(1)}, u32[]{:S(2)}, u32[]{:S(2)}) async-start(bf16[16,8,8,576]{3,2,1,0:T(8,128)(2,1)} %q_by_group.1), calls=%async_computation | async-start | bytes 2621440 | tf_op jit(solution)/shard_map/all_to_all | solution.py:330
  19.0 24.0 %copy-start.1 = (bf16[64,64,128]{2,1,0:T(8,128)(2,1)S(1)}, bf16[64,64,128]{2,1,0:T(8,128)(2,1)}, u32[]{:S(2)}) copy-start(bf16[64,64,128]{2,1,0:T(8,128)(2,1)} %query_ref.1) | copy-start | bytes 3145732
  19.0 24.0 %copy-start.2 = (bf16[2048,128]{1,0:T(8,128)(2,1)S(1)}, bf16[2048,128]{1,0:T(8,128)(2,1)}, u32[]{:S(2)}) copy-start(bf16[2048,128]{1,0:T(8,128)(2,1)} %keys_ref.1) | copy-start | bytes 1572868
  19.0 24.0 %copy-start.3 = (f32[64,64]{1,0:T(8,128)S(1)}, f32[64,64]{1,0:T(8,128)}, u32[]{:S(2)}) copy-start(f32[64,64]{1,0:T(8,128)} %weight_ref.1) | copy-start | bytes 49156
  19.0 7.6 %collective-permute-start.2 = (bf16[576,128]{1,0:T(8,128)(2,1)S(1)}, bf16[576,128]{1,0:T(8,128)(2,1)S(1)}, u32[]{:S(2)}, u32[]{:S(2)}) collective-permute-start(bf16[576,128]{1,0:T(8,128)(2,1)S(1)} %copy-done.13), channel_id=1, source_target_pairs={{0,48},{16,64},{32,80},{48,96},{64,112},{80,0},{96,16},{112,32},{1... | collective-permute-start | bytes 442376 | tf_op jit(solution)/shard_map/ppermute | solution.py:328
  21.0 7.4 %collective-permute-start.3 = (bf16[576,128]{1,0:T(8,128)(2,1)S(1)}, bf16[576,128]{1,0:T(8,128)(2,1)S(1)}, u32[]{:S(2)}, u32[]{:S(2)}) collective-permute-start(bf16[576,128]{1,0:T(8,128)(2,1)S(1)} %copy-done.12), channel_id=1, source_target_pairs={{0,64},{16,80},{32,96},{48,112},{64,0},{80,16},{96,32},{112,48},{1... | collective-permute-start | bytes 442376 | tf_op jit(solution)/shard_map/ppermute | solution.py:328
  21.5 9.1 %collective-permute-start.4 = (bf16[576,128]{1,0:T(8,128)(2,1)S(1)}, bf16[576,128]{1,0:T(8,128)(2,1)S(1)}, u32[]{:S(2)}, u32[]{:S(2)}) collective-permute-start(bf16[576,128]{1,0:T(8,128)(2,1)S(1)} %copy-done.11), channel_id=1, source_target_pairs={{0,80},{16,96},{32,112},{48,0},{64,16},{80,32},{96,48},{112,64},{1... | collective-permute-start | bytes 442376 | tf_op jit(solution)/shard_map/ppermute | solution.py:328
  23.2 10.4 %collective-permute-start.5 = (bf16[576,128]{1,0:T(8,128)(2,1)S(1)}, bf16[576,128]{1,0:T(8,128)(2,1)S(1)}, u32[]{:S(2)}, u32[]{:S(2)}) collective-permute-start(bf16[576,128]{1,0:T(8,128)(2,1)S(1)} %copy-done.10), channel_id=1, source_target_pairs={{0,96},{16,112},{32,0},{48,16},{64,32},{80,48},{96,64},{112,80},{1... | collective-permute-start | bytes 442376 | tf_op jit(solution)/shard_map/ppermute | solution.py:328
  23.8 11.2 %collective-permute-start.6 = (bf16[576,128]{1,0:T(8,128)(2,1)S(1)}, bf16[576,128]{1,0:T(8,128)(2,1)S(1)}, u32[]{:S(2)}, u32[]{:S(2)}) collective-permute-start(bf16[576,128]{1,0:T(8,128)(2,1)S(1)} %copy-done.9), channel_id=1, source_target_pairs={{0,112},{16,0},{32,16},{48,32},{64,48},{80,64},{96,80},{112,96},{1... | collective-permute-start | bytes 442376 | tf_op jit(solution)/shard_map/ppermute | solution.py:328
  36.6 0.8 %copy-start.4 = (bf16[576,512]{1,0:T(8,128)(2,1)}, bf16[576,512]{1,0:T(8,128)(2,1)S(1)}, u32[]{:S(2)}) copy-start(bf16[576,512]{1,0:T(8,128)(2,1)S(1)} %get-tuple-element.30.keys_ref) | copy-start | bytes 1769476
  37.4 15.5 %collective-permute-start.10 = (bf16[576,384]{1,0:T(8,128)(2,1)}, bf16[576,384]{1,0:T(8,128)(2,1)S(1)}, u32[]{:S(2)}, u32[]{:S(2)}) collective-permute-start(bf16[576,384]{1,0:T(8,128)(2,1)} %get-tuple-element.37), channel_id=1, source_target_pairs={{0,3},{1,0},{2,1},{3,2},{4,7},{5,4},{6,5},{7,6},{8,11},{9,8},{10,9... | collective-permute-start | bytes 1327112 | tf_op jit(solution)/shard_map/ppermute | solution.py:334
  40.3 13.4 %collective-permute-start.7 = (bf16[576,384]{1,0:T(8,128)(2,1)S(1)}, bf16[576,384]{1,0:T(8,128)(2,1)S(1)}, u32[]{:S(2)}, u32[]{:S(2)}) collective-permute-start(bf16[576,384]{1,0:T(8,128)(2,1)S(1)} %get-tuple-element.34), channel_id=1, source_target_pairs={{0,4},{1,5},{2,6},{3,7},{4,8},{5,9},{6,10},{7,11},{8,12},{9,13},{1... | collective-permute-start | bytes 1327112 | tf_op jit(solution)/shard_map/ppermute | solution.py:334
  41.5 12.2 %collective-permute-start.8 = (bf16[576,384]{1,0:T(8,128)(2,1)S(1)}, bf16[576,384]{1,0:T(8,128)(2,1)}, u32[]{:S(2)}, u32[]{:S(2)}) collective-permute-start(bf16[576,384]{1,0:T(8,128)(2,1)S(1)} %get-tuple-element.35), channel_id=1, source_target_pairs={{0,12},{1,13},{2,14},{3,15},{4,0},{5,1},{6,2},{7,3},{8,4},{9,5},{1... | collective-permute-start | bytes 1327112 | tf_op jit(solution)/shard_map/ppermute | solution.py:334
  43.0 6.5 %copy-start.8 = (s32[8,128]{1,0:T(8,128)S(1)}, s32[8,128]{1,0:T(8,128)}, u32[]{:S(2)}) copy-start(s32[8,128]{1,0:T(8,128)} %get-tuple-element.20.past_ref) | copy-start | bytes 12292
  43.0 12.9 %collective-permute-start.9 = (bf16[576,384]{1,0:T(8,128)(2,1)S(1)}, bf16[576,384]{1,0:T(8,128)(2,1)}, u32[]{:S(2)}, u32[]{:S(2)}) collective-permute-start(bf16[576,384]{1,0:T(8,128)(2,1)S(1)} %get-tuple-element.36), channel_id=1, source_target_pairs={{0,1},{1,2},{2,3},{3,0},{4,5},{5,6},{6,7},{7,4},{8,9},{9,10},{10,1... | collective-permute-start | bytes 1327112 | tf_op jit(solution)/shard_map/ppermute | solution.py:334
  49.5 1.1 %copy-start.5 = (bf16[576,512]{1,0:T(8,128)(2,1)S(1)}, bf16[576,512]{1,0:T(8,128)(2,1)}, u32[]{:S(2)}) copy-start(bf16[576,512]{1,0:T(8,128)(2,1)} %copy-done.4) | copy-start | bytes 1769476

commit v4 on v3

--- a/solution.py
+++ b/solution.py
@@ -19,6 +19,10 @@
 
 def iota(shape, dim):
     return lax.broadcasted_iota(jnp.int32, shape, dim)
+
+
+def in_hbm(x):
+    return pltpu.with_memory_space_constraint(x, pltpu.HBM)
 
 
 def valid_ids(ids_ref, counts_ref):
@@ -58,7 +62,7 @@
 
 
 def gather_kernel(ids_ref, counts_ref, cache_ref, *refs):
-    out_refs, (source_ref, past_ref, held, sems) = refs[:-4], refs[-4:]
+    out_refs, (source_ref, other_ref, past_ref, held, sems) = refs[:-5], refs[-5:]
     keys = cache_ref.shape[1]
     copies = []
     for i, c in enumerate(range(0, keys, 512)):
@@ -88,71 +92,91 @@
         own.append(jnp.dot(held[i], keep, preferred_element_type=F32).astype(BF16))
     own = jnp.concatenate(own, axis=1)
     index = iota((own.shape[1], 128), 0)
-    for d in range(0, tiles, 2):
+    for d, out_ref in enumerate(out_refs):
+        near = (shard + 2 * d) & 7
         pair = []
-        for u in (d, d + 1):
-            chosen = iota((tiles, 128), 0) == ((shard + u) & 7)
+        for tile in (near, near ^ 1):
+            chosen = iota((tiles, 128), 0) == tile
             pair.append(hot(index, jnp.sum(jnp.where(chosen, target, 0), axis=0, keepdims=True)))
-        got = jnp.dot(own, jnp.concatenate(pair, axis=1), preferred_element_type=F32).astype(BF16)
-        out_refs[d][...] = got[:, :128]
-        out_refs[d + 1][...] = got[:, 128:]
+        got = jnp.dot(own, jnp.concatenate(pair, axis=1), preferred_element_type=F32)
+        out_ref[...] = got.astype(BF16)
     source, count = slot_sources(ids, shard)
     source_ref[...] = source
     past_ref[...] = jnp.broadcast_to((count - 2) * BLOCK, past_ref.shape)
+    other_ref[...] = slot_sources(ids, shard ^ 1)[0]
 
 
 def gather_parts(block_ids, block_counts, cache_t):
     width, keys = cache_t.shape
-    tiles = block_ids.shape[0]
+    tables = [pltpu.HBM((SHARDS, n), jnp.int32) for n in (512, 512, 128)]
+    chips = SHARDS // 2
     return pl.pallas_call(
         gather_kernel,
-        out_shape=[jax.ShapeDtypeStruct((width, 128), BF16)] * tiles
-        + [jax.ShapeDtypeStruct((SHARDS, 512), jnp.int32), jax.ShapeDtypeStruct((8, 128), jnp.int32)],
+        out_shape=[pltpu.HBM((width, 256), BF16)] + [jax.ShapeDtypeStruct((width, 256), BF16)] * (chips - 1) + tables,
         in_specs=[VMEM, SMEM, pl.BlockSpec(memory_space=pltpu.HBM)],
-        out_specs=[VMEM] * (tiles + 2),
+        out_specs=[VMEM] * (chips + 3),
         scratch_shapes=[pltpu.VMEM((keys // 512, width, 512), BF16), pltpu.SemaphoreType.DMA((keys // 512,))],
         cost_estimate=pl.CostEstimate(
             flops=2 * width * keys * 1024, bytes_accessed=2 * width * keys * 2, transcendentals=0
         ),
+        compiler_params=pltpu.CompilerParams(vmem_limit_bytes=16 << 20),
         name="gather_parts",
-    )(block_ids, block_counts, cache_t)
-
-
-def compact_kernel(source_ref, *refs):
-    part_refs, (own_ref, up_ref, down_ref, right_ref, left_ref) = refs[:-5], refs[-5:]
-    tile = lax.axis_index("ctx")
-    source = source_ref[0:1, :]
+    )(in_hbm(block_ids), in_hbm(block_counts), in_hbm(cache_t))
+
+
+def compact_kernel(source_ref, other_ref, *refs):
+    part_refs, (own_out, other_out) = refs[:-2], refs[-2:]
+    shard = lax.axis_index("ctx")
     row = iota((128, 512), 0)
-    total = jnp.zeros((own_ref.shape[0], 512), F32)
-    for d in range(0, SHARDS, 2):
-        pick = jnp.concatenate([hot(row + ((tile - u) & 7) * 128, source) for u in (d, d + 1)], axis=0)
-        pair = jnp.concatenate([part_refs[d][...], part_refs[d + 1][...]], axis=1)
-        total = total + jnp.dot(pair, pick, preferred_element_type=F32)
-    total = total.astype(BF16)
-    own_ref[...] = total
-    up_ref[...] = total[:, :384]
-    down_ref[:, :256] = total[:, :256]
-    down_ref[:, 256:] = total[:, 384:]
-    right_ref[:, :256] = total[:, 256:]
-    right_ref[:, 256:] = total[:, :128]
-    left_ref[:, :256] = total[:, 256:]
-    left_ref[:, 256:] = total[:, 128:256]
-
-
-def compact_parts(source, parts):
+    for table_ref, out_ref, left in ((source_ref, own_out, 0), (other_ref, other_out, 128)):
+        source = table_ref[0:1, :]
+        total = jnp.zeros(out_ref.shape, F32)
+        for d in range(0, len(part_refs), 2):
+            pick = jnp.concatenate([hot(row + ((shard - 2 * u) & 7) * 128, source) for u in (d, d + 1)], axis=0)
+            pair = jnp.concatenate([part_refs[u][:, left : left + 128] for u in (d, d + 1)], axis=1)
+            total = total + jnp.dot(pair, pick, preferred_element_type=F32)
+        out_ref[...] = total.astype(BF16)
+
+
+def compact_parts(source, other, parts):
     width = parts[0].shape[0]
-    sent = jax.ShapeDtypeStruct((width, 384), BF16)
     return pl.pallas_call(
         compact_kernel,
-        out_shape=[jax.ShapeDtypeStruct((width, 512), BF16)] + [sent] * 4,
-        in_specs=[VMEM] * (1 + len(parts)),
-        out_specs=[VMEM] * 5,
+        out_shape=[jax.ShapeDtypeStruct((width, 512), BF16)] * 2,
+        in_specs=[VMEM] * (2 + len(parts)),
+        out_specs=[VMEM] * 2,
         cost_estimate=pl.CostEstimate(
             flops=2 * width * 1024 * 512, bytes_accessed=width * 1536 * 2, transcendentals=0
         ),
         compiler_params=pltpu.CompilerParams(vmem_limit_bytes=12 << 20),
         name="compact_parts",
-    )(source, *parts)
+    )(in_hbm(source), in_hbm(other), in_hbm(parts[0]), *parts[1:])
+
+
+def spread_kernel(own_ref, other_ref, up_ref, down_ref, right_ref, left_ref):
+    first = own_ref[:, :256] + other_ref[:, :256]
+    second = own_ref[:, 256:] + other_ref[:, 256:]
+    up_ref[:, :256] = first
+    up_ref[:, 256:] = second[:, :128]
+    down_ref[:, :256] = first
+    down_ref[:, 256:] = second[:, 128:]
+    right_ref[:, :256] = second
+    right_ref[:, 256:] = first[:, :128]
+    left_ref[:, :256] = second
+    left_ref[:, 256:] = first[:, 128:]
+
+
+def spread_parts(own, other):
+    width = own.shape[0]
+    return pl.pallas_call(
+        spread_kernel,
+        out_shape=[jax.ShapeDtypeStruct((width, 384), BF16)] * 4,
+        in_specs=[VMEM] * 2,
+        out_specs=[VMEM] * 4,
+        cost_estimate=pl.CostEstimate(flops=width * 512, bytes_accessed=width * 2560 * 2, transcendentals=0),
+        compiler_params=pltpu.CompilerParams(vmem_limit_bytes=8 << 20),
+        name="spread_parts",
+    )(own, other)
 
 
 def q_prep_kernel(q_ref, out_ref):
@@ -224,11 +248,13 @@
     return jnp.concatenate(pieces, axis=1)
 
 
-def own_kernel(past_ref, q_ref, keys_ref, top_ref, total_ref, mixed_ref):
+def own_kernel(past_ref, q_ref, up_ref, down_ref, top_ref, total_ref, mixed_ref, keys_ref):
     _, first, second = place()
     past = past_ref[0:1, :]
     late = 16 * BLOCK
     tiles = (None, late + first * 8, None, late + 32 + second * 8)
+    keys_ref[:, :384] = up_ref[...]
+    keys_ref[:, 384:] = down_ref[:, 256:]
     rows, step = q_ref.shape[0], 256
     for a in range(0, rows, step):
         limit = past + a // 8 + (iota((step, 128), 0) >> 3)
@@ -242,9 +268,9 @@
         )
 
 
-def attend_own(past, q, keys):
+def attend_own(past, q, up, down):
     rows, width = q.shape
-    count = keys.shape[1]
+    count = 512
     return pl.pallas_call(
         own_kernel,
         out_shape=[
@@ -252,14 +278,15 @@
             jax.ShapeDtypeStruct((rows, 128), F32),
             jax.ShapeDtypeStruct((rows, 512), F32),
         ],
-        in_specs=[VMEM] * 3,
+        in_specs=[VMEM] * 4,
         out_specs=[VMEM] * 3,
+        scratch_shapes=[pltpu.VMEM((width, count), BF16)],
         cost_estimate=pl.CostEstimate(
             flops=2 * rows * count * (width + 512), bytes_accessed=rows * 4352, transcendentals=rows * count
         ),
         compiler_params=pltpu.CompilerParams(vmem_limit_bytes=16 << 20),
         name="attend_own",
-    )(past, q, keys)
+    )(in_hbm(past), q, up, down)
 
 
 def rest_kernel(past_ref, q_ref, top_ref, total_ref, mixed_ref, up_ref, down_ref, right_ref, left_ref, out_ref, keys_ref):
@@ -310,7 +337,7 @@
         ),
         compiler_params=pltpu.CompilerParams(vmem_limit_bytes=24 << 20),
         name="attend_rest",
-    )(past, q, *state, *parts)
+    )(in_hbm(past), q, *state, *parts)
 
 
 def turn(d):
@@ -324,18 +351,20 @@
 def body(q_latent, index_query, index_weight, index_keys, latent_cache, block_ids, block_counts):
     rows, heads, width = q_latent.shape
     groups = lax.axis_size("head")
-    *outgoing, source, past = gather_parts(block_ids, block_counts, latent_cache.T)
-    incoming = [outgoing[0]] + [lax.ppermute(outgoing[d], "ctx", turn(d)) for d in range(1, SHARDS)]
+    *outgoing, source, other, past = gather_parts(block_ids, block_counts, latent_cache.T)
+    incoming = [outgoing[0]] + [lax.ppermute(outgoing[d], "ctx", turn(2 * d)) for d in range(1, SHARDS // 2)]
     by_group = q_by_group(q_latent, groups)
     head_query = lax.all_to_all(by_group, "head", split_axis=0, concat_axis=0, tiled=True)
     index_scores = index_scores_of(index_query, index_weight, index_keys)
-    own, up, down, right, left = compact_parts(source, incoming)
+    mine, theirs = compact_parts(source, other, incoming)
+    theirs = lax.ppermute(theirs, "ctx", [(i, i ^ 1) for i in range(SHARDS)])
+    up, down, right, left = spread_parts(mine, theirs)
     parts = [
         lax.ppermute(part, "head", line(*step))
         for part, step in ((up, (1, 0)), (down, (-1, 0)), (right, (0, 1)), (left, (0, -1)))
     ]
     flat_query = head_query.reshape(-1, width)
-    state = attend_own(past, flat_query, own)
+    state = attend_own(past, flat_query, up, down)
     attention = attend_rest(past, flat_query, state, parts)
     return attention.reshape(rows * groups, heads // groups, 512), index_scores
 

time: 64.4 us -> 72.6 us (1.13)
  waiting for transfers between devices: 12.2 us -> 20.9 us
  starting transfers between devices: 24 us -> 20.5 us
  Pallas kernels: 25.2 us -> 28.3 us
    all_to_all x1, waiting for transfers between devices: 0.01 us -> 5.16 us  [body(): lax.all_to_all(by_group, 'head', split_axis=0, concat_axis=0, tiled=True)]
    ppermute x7 -> x4, starting transfers between devices: 10.6 us -> 7.24 us  [the longest x3 5.7 us: body(): lax.ppermute(outgoing[d], 'ctx', turn(2 * d))]
    ppermute x7 -> x4, waiting for transfers between devices: 9.26 us -> 11.6 us  [the longest x3 11.6 us: body(): lax.ppermute(outgoing[d], 'ctx', turn(2 * d))]
    pallas_call x1 -> x2, Pallas kernels: 5.05 us -> 6.25 us  [the longest x1 4.88 us: gather_parts(): pl.pallas_call(gather_kernel, out_shape=[pltpu.HBM((width, 256), BF16)] +...]
    ppermute x4, waiting for transfers between devices: 2.93 us -> 4.11 us  [body(): lax.ppermute(part, 'head', line(*step))]
    pallas_call x1, Pallas kernels: 2.31 us -> 3.4 us  [attend_own(): pl.pallas_call(own_kernel, out_shape=[jax.ShapeDtypeStruct((rows, 128), F...]
    pallas_call x1, Pallas kernels: 1.59 us -> 2.6 us  [compact_parts(): pl.pallas_call(compact_kernel, out_shape=[jax.ShapeDtypeStruct((width, 51...]
    unnamed x28 -> x8, local copies, waits for them, and re-layouts: 1.93 us -> 1.81 us
  transfers between devices with their start and end apart: 12 -> 9, of which waited for: 7 -> 5; matrix products, arithmetic and copies ran while one was open for 0% -> 0% of each run, Pallas kernels for 19% -> 18%
where the time goes in v4:
time: 72.6 us; the launch traced here: 72.2 us
  Pallas kernels  28.3 us (39%)
  waiting for transfers between devices  20.9 us (29%)
  starting transfers between devices  20.5 us (28%)
  local copies, waits for them, and re-layouts  1.81 us (2%)
    ppermute x3, waiting for transfers between devices, body(): lax.ppermute(outgoing[d], 'ctx', turn(2 * d))  11.6 us
    pallas_call x1, Pallas kernels, attend_rest(): pl.pallas_call(rest_kernel, out_shape=jax.ShapeDtypeStruct((rows, 512), B...  8.12 us
    all_to_all x1, starting transfers between devices, body(): lax.all_to_all(by_group, 'head', split_axis=0, concat_axis=0, tiled=True)  7.9 us
    pallas_call x1, Pallas kernels, index_scores_of(): pl.pallas_call(index_kernel, grid=(rows // step,), out_shape=jax.ShapeDty...  6.48 us
    ppermute x3, starting transfers between devices, body(): lax.ppermute(outgoing[d], 'ctx', turn(2 * d))  5.7 us
    ppermute x4, starting transfers between devices, body(): lax.ppermute(part, 'head', line(*step))  5.35 us
    all_to_all x1, waiting for transfers between devices, body(): lax.all_to_all(by_group, 'head', split_axis=0, concat_axis=0, tiled=True)  5.16 us
    pallas_call x1, Pallas kernels, gather_parts(): pl.pallas_call(gather_kernel, out_shape=[pltpu.HBM((width, 256), BF16)] +...  4.88 us
  transfers between devices with their start and end apart: 9, of which 5 were waited for; matrix products, arithmetic and copies ran while one was open for 0% of the time, Pallas kernels for 18%

profile of v4, /device:TPU:1, one launch (start us, length us, event | category | flops | bytes accessed | tf_op | source)
XLA Modules:
  0.0 72.2 jit_solution(10967688450380378624)
XLA Ops:
  0.6 4.9 %gather_parts.1 = (bf16[576,256]{1,0:T(8,128)(2,1)}, bf16[576,256]{1,0:T(8,128)(2,1)S(1)}, bf16[576,256]{1,0:T(8,128)(2,1)S(1)}, bf16[576,256]{1,0:T(8,128)(2,1)...) custom-call(s32[8,32]{1,0:T(8,128)} %ids_ref.1, s32[8]{0:T(128)} %counts_ref.1, bf16[576,2048]{1,0:T(8,128)(2,1)} %bitcast.7), custom_call_target="tpu_custom_call" | custom-call | flops 2415919104 | bytes 4718592 | tf_op jit(solution)/shard_map/gather_parts/pallas_call | solution.py:113
  5.5 0.0 copy-start
  5.5 2.1 %collective-permute-start = (bf16[576,256]{1,0:T(8,128)(2,1)S(1)}, bf16[576,256]{1,0:T(8,128)(2,1)S(1)}, u32[]{:S(2)}, u32[]{:S(2)}) collective-permute-start(bf16[576,256]{1,0:T(8,128)(2,1)S(1)} %get-tuple-element.22), channel_id=1, source_target_pairs={{0,32},{16,48},{32,64},{48,80},{64,96},{80,112},{96,0},{112,16},{1... | collective-permute-start | bytes 884744 | tf_op jit(solution)/shard_map/ppermute | solution.py:355
  7.6 2.4 %collective-permute-start.1 = (bf16[576,256]{1,0:T(8,128)(2,1)S(1)}, bf16[576,256]{1,0:T(8,128)(2,1)S(1)}, u32[]{:S(2)}, u32[]{:S(2)}) collective-permute-start(bf16[576,256]{1,0:T(8,128)(2,1)S(1)} %get-tuple-element.23), channel_id=1, source_target_pairs={{0,64},{16,80},{32,96},{48,112},{64,0},{80,16},{96,32},{112,48},{1... | collective-permute-start | bytes 884744 | tf_op jit(solution)/shard_map/ppermute | solution.py:355
  10.1 1.2 %collective-permute-start.2 = (bf16[576,256]{1,0:T(8,128)(2,1)S(1)}, bf16[576,256]{1,0:T(8,128)(2,1)S(1)}, u32[]{:S(2)}, u32[]{:S(2)}) collective-permute-start(bf16[576,256]{1,0:T(8,128)(2,1)S(1)} %get-tuple-element.24), channel_id=1, source_target_pairs={{0,96},{16,112},{32,0},{48,16},{64,32},{80,48},{96,64},{112,80},{1... | collective-permute-start | bytes 884744 | tf_op jit(solution)/shard_map/ppermute | solution.py:355
  11.2 4.0 %collective-permute-done.refs_1_ = bf16[576,256]{1,0:T(8,128)(2,1)S(1)} collective-permute-done((bf16[576,256]{1,0:T(8,128)(2,1)S(1)}, bf16[576,256]{1,0:T(8,128)(2,1)S(1)}, u32[]{:S(2)}, u32[]{:S(2)}) %collective-permute-start) | collective-permute-done | bytes 294944 | tf_op jit(solution)/shard_map/ppermute | solution.py:355
  15.2 7.6 %collective-permute-done.1.refs_2_ = bf16[576,256]{1,0:T(8,128)(2,1)S(1)} collective-permute-done((bf16[576,256]{1,0:T(8,128)(2,1)S(1)}, bf16[576,256]{1,0:T(8,128)(2,1)S(1)}, u32[]{:S(2)}, u32[]{:S(2)}) %collective-permute-start.1) | collective-permute-done | bytes 294944 | tf_op jit(solution)/shard_map/ppermute | solution.py:355
  22.8 0.0 collective-permute-done.2.refs_3_
  22.8 2.6 %compact_parts.1 = (bf16[576,512]{1,0:T(8,128)(2,1)S(1)}, bf16[576,512]{1,0:T(8,128)(2,1)}) custom-call(s32[8,512]{1,0:T(8,128)} %get-tuple-element.19.source_ref, s32[8,512]{1,0:T(8,128)} %get-tuple-element.20.other_ref, bf16[576,256]{1,0:T(8,128)(2,1)} %get-tuple-element.21.refs_0_, bf16[576,256]{1,0:T(8,128)(2,1)S(1)} %collective-permute-done.refs_1_, ...), custom_call_target="tpu_custom_call" | custom-call | flops 603979776 | bytes 1769472 | tf_op jit(solution)/shard_map/compact_parts/pallas_call | solution.py:143
  25.4 1.5 %collective-permute-start.3 = (bf16[576,512]{1,0:T(8,128)(2,1)}, bf16[576,512]{1,0:T(8,128)(2,1)S(1)}, u32[]{:S(2)}, u32[]{:S(2)}) collective-permute-start(bf16[576,512]{1,0:T(8,128)(2,1)} %get-tuple-element.26), channel_id=1, source_target_pairs={{0,16},{16,0},{32,48},{48,32},{64,80},{80,64},{96,112},{112,96},{1... | collective-permute-start | bytes 1769480 | tf_op jit(solution)/shard_map/ppermute | solution.py:360
  27.0 0.0 copy-done
  27.0 1.5 %q_by_group.1 = bf16[16,8,8,576]{3,2,1,0:T(8,128)(2,1)} custom-call(bf16[8,576,128]{2,1,0:T(8,128)(2,1)S(1)} %bitcast.6), custom_call_target="tpu_custom_call" | custom-call | bytes 2359296 | tf_op jit(solution)/shard_map/q_by_group/pallas_call | solution.py:190
  28.4 0.0 copy-start.1
  28.4 7.9 %all-to-all-start = ((bf16[16,8,8,576]{3,2,1,0:T(8,128)(2,1)}), bf16[16,8,8,576]{3,2,1,0:T(8,128)(2,1)S(1)}, u32[]{:S(2)}, u32[]{:S(2)}) async-start(bf16[16,8,8,576]{3,2,1,0:T(8,128)(2,1)} %q_by_group.1), calls=%async_computation | async-start | bytes 2621440 | tf_op jit(solution)/shard_map/all_to_all | solution.py:357
  36.4 0.0 collective-permute-done.3.other_ref
  36.4 1.4 %spread_parts.1 = (bf16[576,384]{1,0:T(8,128)(2,1)}, bf16[576,384]{1,0:T(8,128)(2,1)}, bf16[576,384]{1,0:T(8,128)(2,1)}, bf16[576,384]{1,0:T(8,128)(2,1)}) custom-call(bf16[576,512]{1,0:T(8,128)(2,1)S(1)} %get-tuple-element.25.own_ref, bf16[576,512]{1,0:T(8,128)(2,1)S(1)} %collective-permute-done.3.other_ref), custom_call_target="tpu_custom_call" | custom-call | flops 294912 | bytes 2949120 | tf_op jit(solution)/shard_map/spread_parts/pallas_call | solution.py:171
  37.7 1.4 %collective-permute-start.4 = (bf16[576,384]{1,0:T(8,128)(2,1)}, bf16[576,384]{1,0:T(8,128)(2,1)S(1)}, u32[]{:S(2)}, u32[]{:S(2)}) collective-permute-start(bf16[576,384]{1,0:T(8,128)(2,1)} %get-tuple-element.27.up_ref), channel_id=1, source_target_pairs={{0,4},{1,5},{2,6},{3,7},{4,8},{5,9},{6,10},{7,11},{8,12},{9,13},{1... | collective-permute-start | bytes 1327112 | tf_op jit(solution)/shard_map/ppermute | solution.py:363
  39.1 1.3 %collective-permute-start.5 = (bf16[576,384]{1,0:T(8,128)(2,1)}, bf16[576,384]{1,0:T(8,128)(2,1)S(1)}, u32[]{:S(2)}, u32[]{:S(2)}) collective-permute-start(bf16[576,384]{1,0:T(8,128)(2,1)} %get-tuple-element.28.down_ref), channel_id=1, source_target_pairs={{0,12},{1,13},{2,14},{3,15},{4,0},{5,1},{6,2},{7,3},{8,4},{9,5},{1... | collective-permute-start | bytes 1327112 | tf_op jit(solution)/shard_map/ppermute | solution.py:363
  40.4 1.4 %collective-permute-start.6 = (bf16[576,384]{1,0:T(8,128)(2,1)}, bf16[576,384]{1,0:T(8,128)(2,1)}, u32[]{:S(2)}, u32[]{:S(2)}) collective-permute-start(bf16[576,384]{1,0:T(8,128)(2,1)} %get-tuple-element.32), channel_id=1, source_target_pairs={{0,1},{1,2},{2,3},{3,0},{4,5},{5,6},{6,7},{7,4},{8,9},{9,10},{10,1... | collective-permute-start | bytes 1327112 | tf_op jit(solution)/shard_map/ppermute | solution.py:363
  41.8 1.3 %collective-permute-start.7 = (bf16[576,384]{1,0:T(8,128)(2,1)}, bf16[576,384]{1,0:T(8,128)(2,1)}, u32[]{:S(2)}, u32[]{:S(2)}) collective-permute-start(bf16[576,384]{1,0:T(8,128)(2,1)} %get-tuple-element.33), channel_id=1, source_target_pairs={{0,3},{1,0},{2,1},{3,2},{4,7},{5,4},{6,5},{7,6},{8,11},{9,8},{10,9... | collective-permute-start | bytes 1327112 | tf_op jit(solution)/shard_map/ppermute | solution.py:363
  43.1 0.0 copy-done.1
  43.1 0.0 copy-start.2
  43.1 1.0 %copy-done.2 = bf16[2048,128]{1,0:T(8,128)(2,1)S(1)} copy-done((bf16[2048,128]{1,0:T(8,128)(2,1)S(1)}, bf16[2048,128]{1,0:T(8,128)(2,1)}, u32[]{:S(2)}) %copy-start.2) | copy-done | bytes 524312
  44.1 0.0 copy-start.3
  44.1 0.8 %copy-done.3 = f32[64,64]{1,0:T(8,128)S(1)} copy-done((f32[64,64]{1,0:T(8,128)S(1)}, f32[64,64]{1,0:T(8,128)}, u32[]{:S(2)}) %copy-start.3) | copy-done | bytes 16408
  44.9 6.5 %index_scores.1 = f32[64,2048]{1,0:T(8,128)} custom-call(bf16[64,64,128]{2,1,0:T(8,128)(2,1)S(1)} %copy-done.1, f32[64,64]{1,0:T(8,128)S(1)} %copy-done.3, bf16[2048,128]{1,0:T(8,128)(2,1)S(1)} %copy-done.2), custom_call_target="tpu_custom_call" | custom-call | flops 8589934592 | bytes 1572864 | tf_op jit(solution)/shard_map/index_scores/pallas_call | solution.py:219
  51.4 5.2 %all-to-all-done = bf16[16,8,8,576]{3,2,1,0:T(8,128)(2,1)S(1)} async-done(((bf16[16,8,8,576]{3,2,1,0:T(8,128)(2,1)}), bf16[16,8,8,576]{3,2,1,0:T(8,128)(2,1)S(1)}, u32[]{:S(2)}, u32[]{:S(2)}) %all-to-all-start) | async-done | bytes 1179680 | tf_op jit(solution)/shard_map/all_to_all | solution.py:357
  56.5 3.4 %attend_own.1 = (f32[1024,128]{1,0:T(8,128)S(1)}, f32[1024,128]{1,0:T(8,128)S(1)}, f32[1024,512]{1,0:T(8,128)S(1)}) custom-call(s32[8,128]{1,0:T(8,128)} %get-tuple-element.18.past_ref, bf16[1024,576]{1,0:T(8,128)(2,1)S(1)} %bitcast.4, bf16[576,384]{1,0:T(8,128)(2,1)} %get-tuple-element.27.up_ref, bf16[576,384]{1,0:T(8,128)(2,1)} %get-tuple-element.28.down_ref), custom_call_target="tpu_custom_call" | custom-call | flops 1140850688 | bytes 4456448 | tf_op jit(solution)/shard_map/attend_own/pallas_call | solution.py:274
  59.9 3.3 %collective-permute-done.4.up_ref = bf16[576,384]{1,0:T(8,128)(2,1)S(1)} collective-permute-done((bf16[576,384]{1,0:T(8,128)(2,1)}, bf16[576,384]{1,0:T(8,128)(2,1)S(1)}, u32[]{:S(2)}, u32[]{:S(2)}) %collective-permute-start.4) | collective-permute-done | bytes 442400 | tf_op jit(solution)/shard_map/ppermute | solution.py:363
  63.3 0.0 collective-permute-done.5.down_ref
  63.3 0.8 %collective-permute-done.6.right_ref = bf16[576,384]{1,0:T(8,128)(2,1)} collective-permute-done((bf16[576,384]{1,0:T(8,128)(2,1)}, bf16[576,384]{1,0:T(8,128)(2,1)}, u32[]{:S(2)}, u32[]{:S(2)}) %collective-permute-start.6) | collective-permute-done | bytes 442400 | tf_op jit(solution)/shard_map/ppermute | solution.py:363
  64.1 0.0 collective-permute-done.7.left_ref
  64.1 8.1 %attend_rest.1 = bf16[1024,512]{1,0:T(8,128)(2,1)} custom-call(s32[8,128]{1,0:T(8,128)} %get-tuple-element.18.past_ref, bf16[1024,576]{1,0:T(8,128)(2,1)S(1)} %bitcast.5, f32[1024,128]{1,0:T(8,128)S(1)} %get-tuple-element.29.top_ref, f32[1024,128]{1,0:T(8,128)S(1)} %get-tuple-element.30.total_ref, f32[1024,512]{1,0:T(8,128)S(1)} %get-tuple-element.31.mixed_ref, ...), custom_call_target="tpu_custom_call" | custom-call | flops 3422552064 | bytes 5505024 | tf_op jit(solution)/shard_map/attend_rest/pallas_call | solution.py:329
Async XLA Ops:
  5.5 21.4 %copy-start = (bf16[8,128,576]{1,2,0:T(8,128)(2,1)S(1)}, bf16[8,128,576]{1,2,0:T(8,128)(2,1)}, u32[]{:S(2)}) copy-start(bf16[8,128,576]{1,2,0:T(8,128)(2,1)} %param.7) | copy-start | bytes 3538948
  5.5 9.7 %collective-permute-start = (bf16[576,256]{1,0:T(8,128)(2,1)S(1)}, bf16[576,256]{1,0:T(8,128)(2,1)S(1)}, u32[]{:S(2)}, u32[]{:S(2)}) collective-permute-start(bf16[576,256]{1,0:T(8,128)(2,1)S(1)} %get-tuple-element.22), channel_id=1, source_target_pairs={{0,32},{16,48},{32,64},{48,80},{64,96},{80,112},{96,0},{112,16},{1... | collective-permute-start | bytes 884744 | tf_op jit(solution)/shard_map/ppermute | solution.py:355
  7.6 15.2 %collective-permute-start.1 = (bf16[576,256]{1,0:T(8,128)(2,1)S(1)}, bf16[576,256]{1,0:T(8,128)(2,1)S(1)}, u32[]{:S(2)}, u32[]{:S(2)}) collective-permute-start(bf16[576,256]{1,0:T(8,128)(2,1)S(1)} %get-tuple-element.23), channel_id=1, source_target_pairs={{0,64},{16,80},{32,96},{48,112},{64,0},{80,16},{96,32},{112,48},{1... | collective-permute-start | bytes 884744 | tf_op jit(solution)/shard_map/ppermute | solution.py:355
  10.1 12.7 %collective-permute-start.2 = (bf16[576,256]{1,0:T(8,128)(2,1)S(1)}, bf16[576,256]{1,0:T(8,128)(2,1)S(1)}, u32[]{:S(2)}, u32[]{:S(2)}) collective-permute-start(bf16[576,256]{1,0:T(8,128)(2,1)S(1)} %get-tuple-element.24), channel_id=1, source_target_pairs={{0,96},{16,112},{32,0},{48,16},{64,32},{80,48},{96,64},{112,80},{1... | collective-permute-start | bytes 884744 | tf_op jit(solution)/shard_map/ppermute | solution.py:355
  25.4 10.9 %collective-permute-start.3 = (bf16[576,512]{1,0:T(8,128)(2,1)}, bf16[576,512]{1,0:T(8,128)(2,1)S(1)}, u32[]{:S(2)}, u32[]{:S(2)}) collective-permute-start(bf16[576,512]{1,0:T(8,128)(2,1)} %get-tuple-element.26), channel_id=1, source_target_pairs={{0,16},{16,0},{32,48},{48,32},{64,80},{80,64},{96,112},{112,96},{1... | collective-permute-start | bytes 1769480 | tf_op jit(solution)/shard_map/ppermute | solution.py:360
  28.4 14.7 %copy-start.1 = (bf16[64,64,128]{2,1,0:T(8,128)(2,1)S(1)}, bf16[64,64,128]{2,1,0:T(8,128)(2,1)}, u32[]{:S(2)}) copy-start(bf16[64,64,128]{2,1,0:T(8,128)(2,1)} %query_ref.1) | copy-start | bytes 3145732
  28.4 28.1 %all-to-all-start = ((bf16[16,8,8,576]{3,2,1,0:T(8,128)(2,1)}), bf16[16,8,8,576]{3,2,1,0:T(8,128)(2,1)S(1)}, u32[]{:S(2)}, u32[]{:S(2)}) async-start(bf16[16,8,8,576]{3,2,1,0:T(8,128)(2,1)} %q_by_group.1), calls=%async_computation | async-start | bytes 2621440 | tf_op jit(solution)/shard_map/all_to_all | solution.py:357
  37.7 25.5 %collective-permute-start.4 = (bf16[576,384]{1,0:T(8,128)(2,1)}, bf16[576,384]{1,0:T(8,128)(2,1)S(1)}, u32[]{:S(2)}, u32[]{:S(2)}) collective-permute-start(bf16[576,384]{1,0:T(8,128)(2,1)} %get-tuple-element.27.up_ref), channel_id=1, source_target_pairs={{0,4},{1,5},{2,6},{3,7},{4,8},{5,9},{6,10},{7,11},{8,12},{9,13},{1... | collective-permute-start | bytes 1327112 | tf_op jit(solution)/shard_map/ppermute | solution.py:363
  39.1 24.2 %collective-permute-start.5 = (bf16[576,384]{1,0:T(8,128)(2,1)}, bf16[576,384]{1,0:T(8,128)(2,1)S(1)}, u32[]{:S(2)}, u32[]{:S(2)}) collective-permute-start(bf16[576,384]{1,0:T(8,128)(2,1)} %get-tuple-element.28.down_ref), channel_id=1, source_target_pairs={{0,12},{1,13},{2,14},{3,15},{4,0},{5,1},{6,2},{7,3},{8,4},{9,5},{1... | collective-permute-start | bytes 1327112 | tf_op jit(solution)/shard_map/ppermute | solution.py:363
  40.4 23.6 %collective-permute-start.6 = (bf16[576,384]{1,0:T(8,128)(2,1)}, bf16[576,384]{1,0:T(8,128)(2,1)}, u32[]{:S(2)}, u32[]{:S(2)}) collective-permute-start(bf16[576,384]{1,0:T(8,128)(2,1)} %get-tuple-element.32), channel_id=1, source_target_pairs={{0,1},{1,2},{2,3},{3,0},{4,5},{5,6},{6,7},{7,4},{8,9},{9,10},{10,1... | collective-permute-start | bytes 1327112 | tf_op jit(solution)/shard_map/ppermute | solution.py:363
  41.8 22.3 %collective-permute-start.7 = (bf16[576,384]{1,0:T(8,128)(2,1)}, bf16[576,384]{1,0:T(8,128)(2,1)}, u32[]{:S(2)}, u32[]{:S(2)}) collective-permute-start(bf16[576,384]{1,0:T(8,128)(2,1)} %get-tuple-element.33), channel_id=1, source_target_pairs={{0,3},{1,0},{2,1},{3,2},{4,7},{5,4},{6,5},{7,6},{8,11},{9,8},{10,9... | collective-permute-start | bytes 1327112 | tf_op jit(solution)/shard_map/ppermute | solution.py:363
  43.1 1.0 %copy-start.2 = (bf16[2048,128]{1,0:T(8,128)(2,1)S(1)}, bf16[2048,128]{1,0:T(8,128)(2,1)}, u32[]{:S(2)}) copy-start(bf16[2048,128]{1,0:T(8,128)(2,1)} %keys_ref.1) | copy-start | bytes 1572868
  44.1 0.8 %copy-start.3 = (f32[64,64]{1,0:T(8,128)S(1)}, f32[64,64]{1,0:T(8,128)}, u32[]{:S(2)}) copy-start(f32[64,64]{1,0:T(8,128)} %weight_ref.1) | copy-start | bytes 49156

commit v5 on v3

--- a/solution.py
+++ b/solution.py
@@ -19,6 +19,10 @@
 
 def iota(shape, dim):
     return lax.broadcasted_iota(jnp.int32, shape, dim)
+
+
+def in_hbm(x):
+    return pltpu.with_memory_space_constraint(x, pltpu.HBM)
 
 
 def valid_ids(ids_ref, counts_ref):
@@ -57,14 +61,22 @@
     return entry * PART + part + skipped, end[SHARDS - 1 :, :]
 
 
-def gather_kernel(ids_ref, counts_ref, cache_ref, *refs):
-    out_refs, (source_ref, past_ref, held, sems) = refs[:-4], refs[-4:]
+def gather_kernel(ids_hbm, counts_hbm, cache_ref, *refs):
+    out_refs, (source_ref, past_ref, ids_ref, counts_ref, held, sems) = refs[:-6], refs[-6:]
     keys = cache_ref.shape[1]
+    lists = [
+        pltpu.make_async_copy(ids_hbm, ids_ref, sems.at[keys // 512]),
+        pltpu.make_async_copy(counts_hbm, counts_ref, sems.at[keys // 512 + 1]),
+    ]
+    for copy in lists:
+        copy.start()
     copies = []
     for i, c in enumerate(range(0, keys, 512)):
         copies.append(pltpu.make_async_copy(cache_ref.at[:, pl.ds(c, 512)], held.at[i], sems.at[i]))
         copies[i].start()
     shard, first, second = place()
+    for copy in lists:
+        copy.wait()
     ids = valid_ids(ids_ref, counts_ref)
     tiles, entries = ids.shape
     blocks = keys // BLOCK
@@ -103,56 +115,63 @@
 
 def gather_parts(block_ids, block_counts, cache_t):
     width, keys = cache_t.shape
-    tiles = block_ids.shape[0]
+    hbm = pl.BlockSpec(memory_space=pltpu.HBM)
     return pl.pallas_call(
         gather_kernel,
-        out_shape=[jax.ShapeDtypeStruct((width, 128), BF16)] * tiles
-        + [jax.ShapeDtypeStruct((SHARDS, 512), jnp.int32), jax.ShapeDtypeStruct((8, 128), jnp.int32)],
-        in_specs=[VMEM, SMEM, pl.BlockSpec(memory_space=pltpu.HBM)],
-        out_specs=[VMEM] * (tiles + 2),
-        scratch_shapes=[pltpu.VMEM((keys // 512, width, 512), BF16), pltpu.SemaphoreType.DMA((keys // 512,))],
+        out_shape=[pltpu.HBM((width, 128), BF16)]
+        + [pltpu.VMEM((width, 128), BF16)] * (SHARDS - 1)
+        + [pltpu.HBM((SHARDS, n), jnp.int32) for n in (512, 128)],
+        in_specs=[hbm] * 3,
+        out_specs=[VMEM] * (SHARDS + 2),
+        scratch_shapes=[
+            pltpu.VMEM(block_ids.shape, jnp.int32),
+            pltpu.SMEM(block_counts.shape, jnp.int32),
+            pltpu.VMEM((keys // 512, width, 512), BF16),
+            pltpu.SemaphoreType.DMA((keys // 512 + 2,)),
+        ],
         cost_estimate=pl.CostEstimate(
             flops=2 * width * keys * 1024, bytes_accessed=2 * width * keys * 2, transcendentals=0
         ),
+        compiler_params=pltpu.CompilerParams(vmem_limit_bytes=16 << 20),
         name="gather_parts",
-    )(block_ids, block_counts, cache_t)
+    )(in_hbm(block_ids), in_hbm(block_counts), in_hbm(cache_t))
 
 
 def compact_kernel(source_ref, *refs):
-    part_refs, (own_ref, up_ref, down_ref, right_ref, left_ref) = refs[:-5], refs[-5:]
+    part_refs, (up_ref, down_ref, right_ref, left_ref) = refs[:-4], refs[-4:]
     tile = lax.axis_index("ctx")
     source = source_ref[0:1, :]
     row = iota((128, 512), 0)
-    total = jnp.zeros((own_ref.shape[0], 512), F32)
+    total = jnp.zeros((up_ref.shape[0], 512), F32)
     for d in range(0, SHARDS, 2):
         pick = jnp.concatenate([hot(row + ((tile - u) & 7) * 128, source) for u in (d, d + 1)], axis=0)
         pair = jnp.concatenate([part_refs[d][...], part_refs[d + 1][...]], axis=1)
         total = total + jnp.dot(pair, pick, preferred_element_type=F32)
     total = total.astype(BF16)
-    own_ref[...] = total
-    up_ref[...] = total[:, :384]
-    down_ref[:, :256] = total[:, :256]
-    down_ref[:, 256:] = total[:, 384:]
-    right_ref[:, :256] = total[:, 256:]
-    right_ref[:, 256:] = total[:, :128]
-    left_ref[:, :256] = total[:, 256:]
-    left_ref[:, 256:] = total[:, 128:256]
+    first, second = total[:, :256], total[:, 256:]
+    up_ref[:, :256] = first
+    up_ref[:, 256:] = second[:, :128]
+    down_ref[:, :256] = first
+    down_ref[:, 256:] = second[:, 128:]
+    right_ref[:, :256] = second
+    right_ref[:, 256:] = first[:, :128]
+    left_ref[:, :256] = second
+    left_ref[:, 256:] = first[:, 128:]
 
 
 def compact_parts(source, parts):
     width = parts[0].shape[0]
-    sent = jax.ShapeDtypeStruct((width, 384), BF16)
     return pl.pallas_call(
         compact_kernel,
-        out_shape=[jax.ShapeDtypeStruct((width, 512), BF16)] + [sent] * 4,
+        out_shape=[pltpu.VMEM((width, 384), BF16)] * 4,
         in_specs=[VMEM] * (1 + len(parts)),
-        out_specs=[VMEM] * 5,
+        out_specs=[VMEM] * 4,
         cost_estimate=pl.CostEstimate(
             flops=2 * width * 1024 * 512, bytes_accessed=width * 1536 * 2, transcendentals=0
         ),
         compiler_params=pltpu.CompilerParams(vmem_limit_bytes=12 << 20),
         name="compact_parts",
-    )(source, *parts)
+    )(in_hbm(source), in_hbm(parts[0]), *parts[1:-1], in_hbm(parts[-1]))
 
 
 def q_prep_kernel(q_ref, out_ref):
@@ -224,11 +243,13 @@
     return jnp.concatenate(pieces, axis=1)
 
 
-def own_kernel(past_ref, q_ref, keys_ref, top_ref, total_ref, mixed_ref):
+def own_kernel(past_ref, q_ref, up_ref, down_ref, top_ref, total_ref, mixed_ref, keys_ref):
     _, first, second = place()
     past = past_ref[0:1, :]
     late = 16 * BLOCK
     tiles = (None, late + first * 8, None, late + 32 + second * 8)
+    keys_ref[:, :384] = up_ref[...]
+    keys_ref[:, 384:] = down_ref[:, 256:]
     rows, step = q_ref.shape[0], 256
     for a in range(0, rows, step):
         limit = past + a // 8 + (iota((step, 128), 0) >> 3)
@@ -242,9 +263,9 @@
         )
 
 
-def attend_own(past, q, keys):
+def attend_own(past, q, up, down):
     rows, width = q.shape
-    count = keys.shape[1]
+    count = 512
     return pl.pallas_call(
         own_kernel,
         out_shape=[
@@ -252,17 +273,18 @@
             jax.ShapeDtypeStruct((rows, 128), F32),
             jax.ShapeDtypeStruct((rows, 512), F32),
         ],
-        in_specs=[VMEM] * 3,
+        in_specs=[VMEM] * 4,
         out_specs=[VMEM] * 3,
+        scratch_shapes=[pltpu.VMEM((width, count), BF16)],
         cost_estimate=pl.CostEstimate(
             flops=2 * rows * count * (width + 512), bytes_accessed=rows * 4352, transcendentals=rows * count
         ),
         compiler_params=pltpu.CompilerParams(vmem_limit_bytes=16 << 20),
         name="attend_own",
-    )(past, q, keys)
-
-
-def rest_kernel(past_ref, q_ref, top_ref, total_ref, mixed_ref, up_ref, down_ref, right_ref, left_ref, out_ref, keys_ref):
+    )(in_hbm(past), q, up, down)
+
+
+def rest_kernel(past_ref, q_ref, top_ref, total_ref, mixed_ref, up_ref, down_ref, right_ref, left_ref, out_ref, keys_ref, done_ref, sems):
     _, first, second = place()
     past = past_ref[0:1, :]
     late = 16 * BLOCK
@@ -282,6 +304,7 @@
     for i, ref in enumerate((up_ref, down_ref, right_ref, left_ref)):
         keys_ref[:, i * 384 : (i + 1) * 384] = ref[...]
     rows, step = q_ref.shape[0], 256
+    copies = []
     for a in range(0, rows, step):
         limit = past + a // 8 + (iota((step, 128), 0) >> 3)
         scores = masked_scores(q_ref[a : a + step, :], keys_ref[...], tiles, limit)
@@ -293,7 +316,15 @@
         mixed = mixed_ref[a : a + step, :] * fade + lax.dot_general(
             weights.astype(BF16), keys_ref[0:512, :], (((1,), (1,)), ((), ())), preferred_element_type=F32
         )
-        out_ref[a : a + step, :] = (mixed / total).astype(BF16)
+        done_ref[a : a + step, :] = (mixed / total).astype(BF16)
+        copies.append(
+            pltpu.make_async_copy(
+                done_ref.at[pl.ds(a, step), :], out_ref.at[pl.ds(a, step), :], sems.at[a // step]
+            )
+        )
+        copies[-1].start()
+    for copy in copies:
+        copy.wait()
 
 
 def attend_rest(past, q, state, parts):
@@ -303,14 +334,18 @@
         rest_kernel,
         out_shape=jax.ShapeDtypeStruct((rows, 512), BF16),
         in_specs=[VMEM] * (5 + len(parts)),
-        out_specs=VMEM,
-        scratch_shapes=[pltpu.VMEM((width, count), BF16)],
+        out_specs=pl.BlockSpec(memory_space=pltpu.HBM),
+        scratch_shapes=[
+            pltpu.VMEM((width, count), BF16),
+            pltpu.VMEM((rows, 512), BF16),
+            pltpu.SemaphoreType.DMA((rows // 256,)),
+        ],
         cost_estimate=pl.CostEstimate(
             flops=2 * rows * count * (width + 512), bytes_accessed=rows * 5376, transcendentals=rows * count
         ),
         compiler_params=pltpu.CompilerParams(vmem_limit_bytes=24 << 20),
         name="attend_rest",
-    )(past, q, *state, *parts)
+    )(in_hbm(past), q, *state, *parts)
 
 
 def turn(d):
@@ -329,13 +364,13 @@
     by_group = q_by_group(q_latent, groups)
     head_query = lax.all_to_all(by_group, "head", split_axis=0, concat_axis=0, tiled=True)
     index_scores = index_scores_of(index_query, index_weight, index_keys)
-    own, up, down, right, left = compact_parts(source, incoming)
+    up, down, right, left = compact_parts(source, incoming)
     parts = [
         lax.ppermute(part, "head", line(*step))
         for part, step in ((up, (1, 0)), (down, (-1, 0)), (right, (0, 1)), (left, (0, -1)))
     ]
     flat_query = head_query.reshape(-1, width)
-    state = attend_own(past, flat_query, own)
+    state = attend_own(past, flat_query, up, down)
     attention = attend_rest(past, flat_query, state, parts)
     return attention.reshape(rows * groups, heads // groups, 512), index_scores
 

time: 64.4 us -> 63.9 us (level)
  local copies, waits for them, and re-layouts: 1.93 us -> 0.68 us
    unnamed x28 -> x10, local copies, waits for them, and re-layouts: 1.93 us -> 0.68 us
  transfers between devices with their start and end apart: 12 -> 12, of which waited for: 7 -> 7; matrix products, arithmetic and copies ran while one was open for 0% -> 0% of each run, Pallas kernels for 19% -> 21%
where the time goes in v5:
time: 63.9 us; the launch traced here: 63.6 us
  Pallas kernels  25.6 us (40%)
  starting transfers between devices  23.9 us (37%)
  waiting for transfers between devices  12.6 us (20%)
  between operations  0.88 us (1%)
  local copies, waits for them, and re-layouts  0.68 us (1%)
    ppermute x7, starting transfers between devices, body(): lax.ppermute(outgoing[d], 'ctx', turn(d))  10.6 us
    ppermute x7, waiting for transfers between devices, body(): lax.ppermute(outgoing[d], 'ctx', turn(d))  9.27 us
    pallas_call x1, Pallas kernels, attend_rest(): pl.pallas_call(rest_kernel, out_shape=jax.ShapeDtypeStruct((rows, 512), B...  7.89 us
    all_to_all x1, starting transfers between devices, body(): lax.all_to_all(by_group, 'head', split_axis=0, concat_axis=0, tiled=True)  7.77 us
    pallas_call x1, Pallas kernels, index_scores_of(): pl.pallas_call(index_kernel, grid=(rows // step,), out_shape=jax.ShapeDty...  6.57 us
    ppermute x4, starting transfers between devices, body(): lax.ppermute(part, 'head', line(*step))  5.53 us
    pallas_call x1, Pallas kernels, gather_parts(): pl.pallas_call(gather_kernel, out_shape=[pltpu.HBM((width, 128), BF16)] +...  4.19 us
    ppermute x4, waiting for transfers between devices, body(): lax.ppermute(part, 'head', line(*step))  3.34 us
  transfers between devices with their start and end apart: 12, of which 7 were waited for; matrix products, arithmetic and copies ran while one was open for 0% of the time, Pallas kernels for 21%

profile of v5, /device:TPU:1, one launch (start us, length us, event | category | flops | bytes accessed | tf_op | source)
XLA Modules:
  0.0 63.6 jit_solution(11503877675676340656)
XLA Ops:
  0.6 0.0 copy-start
  0.6 4.2 %gather_parts.1 = (bf16[576,128]{1,0:T(8,128)(2,1)}, bf16[576,128]{1,0:T(8,128)(2,1)S(1)}, bf16[576,128]{1,0:T(8,128)(2,1)S(1)}, bf16[576,128]{1,0:T(8,128)(2,1)...) custom-call(s32[8,32]{1,0:T(8,128)} %ids_hbm.1, ...), custom_call_target="tpu_custom_call" | custom-call | flops 2415919104 | bytes 4718592 | tf_op jit(solution)/shard_map/gather_parts/pallas_call | solution.py:119
  4.8 2.6 %collective-permute-start = (bf16[576,128]{1,0:T(8,128)(2,1)S(1)}, bf16[576,128]{1,0:T(8,128)(2,1)S(1)}, u32[]{:S(2)}, u32[]{:S(2)}) collective-permute-start(bf16[576,128]{1,0:T(8,128)(2,1)S(1)} %get-tuple-element.22), channel_id=1, source_target_pairs={{0,16},{16,32},{32,48},{48,64},{64,80},{80,96},{96,112},{112,0},{1... | collective-permute-start | bytes 442376 | tf_op jit(solution)/shard_map/ppermute | solution.py:363
  7.4 1.2 %collective-permute-start.1 = (bf16[576,128]{1,0:T(8,128)(2,1)S(1)}, bf16[576,128]{1,0:T(8,128)(2,1)S(1)}, u32[]{:S(2)}, u32[]{:S(2)}) collective-permute-start(bf16[576,128]{1,0:T(8,128)(2,1)S(1)} %get-tuple-element.23), channel_id=1, source_target_pairs={{0,32},{16,48},{32,64},{48,80},{64,96},{80,112},{96,0},{112,16},{1... | collective-permute-start | bytes 442376 | tf_op jit(solution)/shard_map/ppermute | solution.py:363
  8.6 0.0 copy-done
  8.7 1.5 %q_by_group.1 = bf16[16,8,8,576]{3,2,1,0:T(8,128)(2,1)} custom-call(bf16[8,576,128]{2,1,0:T(8,128)(2,1)S(1)} %bitcast.6), custom_call_target="tpu_custom_call" | custom-call | bytes 2359296 | tf_op jit(solution)/shard_map/q_by_group/pallas_call | solution.py:185
  10.1 7.8 %all-to-all-start = ((bf16[16,8,8,576]{3,2,1,0:T(8,128)(2,1)}), bf16[16,8,8,576]{3,2,1,0:T(8,128)(2,1)S(1)}, u32[]{:S(2)}, u32[]{:S(2)}) async-start(bf16[16,8,8,576]{3,2,1,0:T(8,128)(2,1)} %q_by_group.1), calls=%async_computation | async-start | bytes 2621440 | tf_op jit(solution)/shard_map/all_to_all | solution.py:365
  17.9 0.0 copy-start.1
  17.9 0.0 copy-start.2
  17.9 0.0 copy-start.3
  17.9 1.9 %collective-permute-start.2 = (bf16[576,128]{1,0:T(8,128)(2,1)S(1)}, bf16[576,128]{1,0:T(8,128)(2,1)S(1)}, u32[]{:S(2)}, u32[]{:S(2)}) collective-permute-start(bf16[576,128]{1,0:T(8,128)(2,1)S(1)} %get-tuple-element.24), channel_id=1, source_target_pairs={{0,48},{16,64},{32,80},{48,96},{64,112},{80,0},{96,16},{112,32},{1... | collective-permute-start | bytes 442376 | tf_op jit(solution)/shard_map/ppermute | solution.py:363
  19.9 0.5 collective-permute-start.3
  20.4 1.7 %collective-permute-start.4 = (bf16[576,128]{1,0:T(8,128)(2,1)S(1)}, bf16[576,128]{1,0:T(8,128)(2,1)S(1)}, u32[]{:S(2)}, u32[]{:S(2)}) collective-permute-start(bf16[576,128]{1,0:T(8,128)(2,1)S(1)} %get-tuple-element.26), channel_id=1, source_target_pairs={{0,80},{16,96},{32,112},{48,0},{64,16},{80,32},{96,48},{112,64},{1... | collective-permute-start | bytes 442376 | tf_op jit(solution)/shard_map/ppermute | solution.py:363
  22.1 0.0 collective-permute-done.refs_1_
  22.1 0.7 %collective-permute-start.5 = (bf16[576,128]{1,0:T(8,128)(2,1)S(1)}, bf16[576,128]{1,0:T(8,128)(2,1)S(1)}, u32[]{:S(2)}, u32[]{:S(2)}) collective-permute-start(bf16[576,128]{1,0:T(8,128)(2,1)S(1)} %get-tuple-element.27), channel_id=1, source_target_pairs={{0,96},{16,112},{32,0},{48,16},{64,32},{80,48},{96,64},{112,80},{1... | collective-permute-start | bytes 442376 | tf_op jit(solution)/shard_map/ppermute | solution.py:363
  22.8 0.0 collective-permute-done.1.refs_2_
  22.8 1.9 %collective-permute-start.6 = (bf16[576,128]{1,0:T(8,128)(2,1)S(1)}, bf16[576,128]{1,0:T(8,128)(2,1)S(1)}, u32[]{:S(2)}, u32[]{:S(2)}) collective-permute-start(bf16[576,128]{1,0:T(8,128)(2,1)S(1)} %get-tuple-element.28), channel_id=1, source_target_pairs={{0,112},{16,0},{32,16},{48,32},{64,48},{80,64},{96,80},{112,96},{1... | collective-permute-start | bytes 442376 | tf_op jit(solution)/shard_map/ppermute | solution.py:363
  24.7 0.8 %collective-permute-done.2.refs_3_ = bf16[576,128]{1,0:T(8,128)(2,1)S(1)} collective-permute-done((bf16[576,128]{1,0:T(8,128)(2,1)S(1)}, bf16[576,128]{1,0:T(8,128)(2,1)S(1)}, u32[]{:S(2)}, u32[]{:S(2)}) %collective-permute-start.2) | collective-permute-done | bytes 147488 | tf_op jit(solution)/shard_map/ppermute | solution.py:363
  25.6 1.7 %collective-permute-done.3.refs_4_ = bf16[576,128]{1,0:T(8,128)(2,1)S(1)} collective-permute-done((bf16[576,128]{1,0:T(8,128)(2,1)S(1)}, bf16[576,128]{1,0:T(8,128)(2,1)S(1)}, u32[]{:S(2)}, u32[]{:S(2)}) %collective-permute-start.3) | collective-permute-done | bytes 147488 | tf_op jit(solution)/shard_map/ppermute | solution.py:363
  27.3 2.3 %collective-permute-done.4.refs_5_ = bf16[576,128]{1,0:T(8,128)(2,1)S(1)} collective-permute-done((bf16[576,128]{1,0:T(8,128)(2,1)S(1)}, bf16[576,128]{1,0:T(8,128)(2,1)S(1)}, u32[]{:S(2)}, u32[]{:S(2)}) %collective-permute-start.4) | collective-permute-done | bytes 147488 | tf_op jit(solution)/shard_map/ppermute | solution.py:363
  29.6 2.9 %collective-permute-done.5.refs_6_ = bf16[576,128]{1,0:T(8,128)(2,1)S(1)} collective-permute-done((bf16[576,128]{1,0:T(8,128)(2,1)S(1)}, bf16[576,128]{1,0:T(8,128)(2,1)S(1)}, u32[]{:S(2)}, u32[]{:S(2)}) %collective-permute-start.5) | collective-permute-done | bytes 147488 | tf_op jit(solution)/shard_map/ppermute | solution.py:363
  32.5 1.5 %collective-permute-done.6.refs_7_ = bf16[576,128]{1,0:T(8,128)(2,1)S(1)} collective-permute-done((bf16[576,128]{1,0:T(8,128)(2,1)S(1)}, bf16[576,128]{1,0:T(8,128)(2,1)S(1)}, u32[]{:S(2)}, u32[]{:S(2)}) %collective-permute-start.6) | collective-permute-done | bytes 147488 | tf_op jit(solution)/shard_map/ppermute | solution.py:363
  34.0 0.0 copy-start.4
  34.0 0.7 %copy-done.4 = bf16[576,128]{1,0:T(8,128)(2,1)} copy-done((bf16[576,128]{1,0:T(8,128)(2,1)}, bf16[576,128]{1,0:T(8,128)(2,1)S(1)}, u32[]{:S(2)}) %copy-start.4) | copy-done | bytes 147480
  34.6 2.5 %compact_parts.1 = (bf16[576,384]{1,0:T(8,128)(2,1)S(1)}, bf16[576,384]{1,0:T(8,128)(2,1)S(1)}, bf16[576,384]{1,0:T(8,128)(2,1)S(1)}, bf16[576,384]{1,0:T(8,128)(2,1)}) custom-call(s32[8,512]{1,0:T(8,128)} %get-tuple-element.20.source_ref, bf16[576,128]{1,0:T(8,128)(2,1)} %get-tuple-element.21.refs_0_, bf16[576,128]{1,0:T(8,128)(2,1)S(1)} %collective-permute-done.refs_1_, ...), custom_call_target="tpu_custom_call" | custom-call | flops 603979776 | bytes 1769472 | tf_op jit(solution)/shard_map/compact_parts/pallas_call | solution.py:164
  37.2 2.9 %collective-permute-start.10 = (bf16[576,384]{1,0:T(8,128)(2,1)}, bf16[576,384]{1,0:T(8,128)(2,1)S(1)}, u32[]{:S(2)}, u32[]{:S(2)}) collective-permute-start(bf16[576,384]{1,0:T(8,128)(2,1)} %get-tuple-element.35), channel_id=1, source_target_pairs={{0,3},{1,0},{2,1},{3,2},{4,7},{5,4},{6,5},{7,6},{8,11},{9,8},{10,9... | collective-permute-start | bytes 1327112 | tf_op jit(solution)/shard_map/ppermute | solution.py:369
  40.0 1.2 %collective-permute-start.7 = (bf16[576,384]{1,0:T(8,128)(2,1)S(1)}, bf16[576,384]{1,0:T(8,128)(2,1)S(1)}, u32[]{:S(2)}, u32[]{:S(2)}) collective-permute-start(bf16[576,384]{1,0:T(8,128)(2,1)S(1)} %get-tuple-element.29.up_ref), channel_id=1, source_target_pairs={{0,4},{1,5},{2,6},{3,7},{4,8},{5,9},{6,10},{7,11},{8,12},{9,13},{1... | collective-permute-start | bytes 1327112 | tf_op jit(solution)/shard_map/ppermute | solution.py:369
  41.2 1.5 %collective-permute-start.8 = (bf16[576,384]{1,0:T(8,128)(2,1)S(1)}, bf16[576,384]{1,0:T(8,128)(2,1)}, u32[]{:S(2)}, u32[]{:S(2)}) collective-permute-start(bf16[576,384]{1,0:T(8,128)(2,1)S(1)} %get-tuple-element.30.down_ref), channel_id=1, source_target_pairs={{0,12},{1,13},{2,14},{3,15},{4,0},{5,1},{6,2},{7,3},{8,4},{9,5},{1... | collective-permute-start | bytes 1327112 | tf_op jit(solution)/shard_map/ppermute | solution.py:369
  42.7 0.0 collective-permute-start.9
  42.7 0.0 copy-done.1
  42.7 0.0 copy-done.2
  42.7 0.0 copy-done.3
  42.7 6.6 %index_scores.1 = f32[64,2048]{1,0:T(8,128)} custom-call(bf16[64,64,128]{2,1,0:T(8,128)(2,1)S(1)} %copy-done.1, f32[64,64]{1,0:T(8,128)S(1)} %copy-done.3, bf16[2048,128]{1,0:T(8,128)(2,1)S(1)} %copy-done.2), custom_call_target="tpu_custom_call" | custom-call | flops 8589934592 | bytes 1572864 | tf_op jit(solution)/shard_map/index_scores/pallas_call | solution.py:214
  49.3 0.0 all-to-all-done
  49.3 2.9 %attend_own.1 = (f32[1024,128]{1,0:T(8,128)S(1)}, f32[1024,128]{1,0:T(8,128)S(1)}, f32[1024,512]{1,0:T(8,128)S(1)}) custom-call(s32[8,128]{1,0:T(8,128)} %get-tuple-element.19.past_ref, bf16[1024,576]{1,0:T(8,128)(2,1)S(1)} %bitcast.4, bf16[576,384]{1,0:T(8,128)(2,1)S(1)} %get-tuple-element.29.up_ref, bf16[576,384]{1,0:T(8,128)(2,1)S(1)} %get-tuple-element.30.down_ref), custom_call_target="tpu_custom_call" | custom-call | flops 1140850688 | bytes 4456448 | tf_op jit(solution)/shard_map/attend_own/pallas_call | solution.py:269
  52.2 0.0 collective-permute-done.10.left_ref
  52.2 1.2 %collective-permute-done.7.up_ref = bf16[576,384]{1,0:T(8,128)(2,1)S(1)} collective-permute-done((bf16[576,384]{1,0:T(8,128)(2,1)S(1)}, bf16[576,384]{1,0:T(8,128)(2,1)S(1)}, u32[]{:S(2)}, u32[]{:S(2)}) %collective-permute-start.7) | collective-permute-done | bytes 442400 | tf_op jit(solution)/shard_map/ppermute | solution.py:369
  53.5 0.0 collective-permute-done.8.down_ref
  53.5 2.1 %collective-permute-done.9.right_ref = bf16[576,384]{1,0:T(8,128)(2,1)} collective-permute-done((bf16[576,384]{1,0:T(8,128)(2,1)S(1)}, bf16[576,384]{1,0:T(8,128)(2,1)}, u32[]{:S(2)}, u32[]{:S(2)}) %collective-permute-start.9) | collective-permute-done | bytes 442400 | tf_op jit(solution)/shard_map/ppermute | solution.py:369
  55.6 7.9 %attend_rest.1 = bf16[1024,512]{1,0:T(8,128)(2,1)} custom-call(s32[8,128]{1,0:T(8,128)} %get-tuple-element.19.past_ref, bf16[1024,576]{1,0:T(8,128)(2,1)S(1)} %bitcast.5, f32[1024,128]{1,0:T(8,128)S(1)} %get-tuple-element.31.top_ref, f32[1024,128]{1,0:T(8,128)S(1)} %get-tuple-element.32.total_ref, f32[1024,512]{1,0:T(8,128)S(1)} %get-tuple-element.33.mixed_ref, ...), custom_call_target="tpu_custom_call" | custom-call | flops 3422552064 | bytes 5505024 | tf_op jit(solution)/shard_map/attend_rest/pallas_call | solution.py:333
Async XLA Ops:
  0.6 8.0 %copy-start = (bf16[8,128,576]{1,2,0:T(8,128)(2,1)S(1)}, bf16[8,128,576]{1,2,0:T(8,128)(2,1)}, u32[]{:S(2)}) copy-start(bf16[8,128,576]{1,2,0:T(8,128)(2,1)} %param.7) | copy-start | bytes 3538948
  4.8 17.3 %collective-permute-start = (bf16[576,128]{1,0:T(8,128)(2,1)S(1)}, bf16[576,128]{1,0:T(8,128)(2,1)S(1)}, u32[]{:S(2)}, u32[]{:S(2)}) collective-permute-start(bf16[576,128]{1,0:T(8,128)(2,1)S(1)} %get-tuple-element.22), channel_id=1, source_target_pairs={{0,16},{16,32},{32,48},{48,64},{64,80},{80,96},{96,112},{112,0},{1... | collective-permute-start | bytes 442376 | tf_op jit(solution)/shard_map/ppermute | solution.py:363
  7.4 15.3 %collective-permute-start.1 = (bf16[576,128]{1,0:T(8,128)(2,1)S(1)}, bf16[576,128]{1,0:T(8,128)(2,1)S(1)}, u32[]{:S(2)}, u32[]{:S(2)}) collective-permute-start(bf16[576,128]{1,0:T(8,128)(2,1)S(1)} %get-tuple-element.23), channel_id=1, source_target_pairs={{0,32},{16,48},{32,64},{48,80},{64,96},{80,112},{96,0},{112,16},{1... | collective-permute-start | bytes 442376 | tf_op jit(solution)/shard_map/ppermute | solution.py:363
  10.1 39.2 %all-to-all-start = ((bf16[16,8,8,576]{3,2,1,0:T(8,128)(2,1)}), bf16[16,8,8,576]{3,2,1,0:T(8,128)(2,1)S(1)}, u32[]{:S(2)}, u32[]{:S(2)}) async-start(bf16[16,8,8,576]{3,2,1,0:T(8,128)(2,1)} %q_by_group.1), calls=%async_computation | async-start | bytes 2621440 | tf_op jit(solution)/shard_map/all_to_all | solution.py:365
  17.9 24.8 %copy-start.1 = (bf16[64,64,128]{2,1,0:T(8,128)(2,1)S(1)}, bf16[64,64,128]{2,1,0:T(8,128)(2,1)}, u32[]{:S(2)}) copy-start(bf16[64,64,128]{2,1,0:T(8,128)(2,1)} %query_ref.1) | copy-start | bytes 3145732
  17.9 24.8 %copy-start.2 = (bf16[2048,128]{1,0:T(8,128)(2,1)S(1)}, bf16[2048,128]{1,0:T(8,128)(2,1)}, u32[]{:S(2)}) copy-start(bf16[2048,128]{1,0:T(8,128)(2,1)} %keys_ref.1) | copy-start | bytes 1572868
  17.9 24.8 %copy-start.3 = (f32[64,64]{1,0:T(8,128)S(1)}, f32[64,64]{1,0:T(8,128)}, u32[]{:S(2)}) copy-start(f32[64,64]{1,0:T(8,128)} %weight_ref.1) | copy-start | bytes 49156
  17.9 7.6 %collective-permute-start.2 = (bf16[576,128]{1,0:T(8,128)(2,1)S(1)}, bf16[576,128]{1,0:T(8,128)(2,1)S(1)}, u32[]{:S(2)}, u32[]{:S(2)}) collective-permute-start(bf16[576,128]{1,0:T(8,128)(2,1)S(1)} %get-tuple-element.24), channel_id=1, source_target_pairs={{0,48},{16,64},{32,80},{48,96},{64,112},{80,0},{96,16},{112,32},{1... | collective-permute-start | bytes 442376 | tf_op jit(solution)/shard_map/ppermute | solution.py:363
  19.9 7.4 %collective-permute-start.3 = (bf16[576,128]{1,0:T(8,128)(2,1)S(1)}, bf16[576,128]{1,0:T(8,128)(2,1)S(1)}, u32[]{:S(2)}, u32[]{:S(2)}) collective-permute-start(bf16[576,128]{1,0:T(8,128)(2,1)S(1)} %get-tuple-element.25), channel_id=1, source_target_pairs={{0,64},{16,80},{32,96},{48,112},{64,0},{80,16},{96,32},{112,48},{1... | collective-permute-start | bytes 442376 | tf_op jit(solution)/shard_map/ppermute | solution.py:363
  20.4 9.1 %collective-permute-start.4 = (bf16[576,128]{1,0:T(8,128)(2,1)S(1)}, bf16[576,128]{1,0:T(8,128)(2,1)S(1)}, u32[]{:S(2)}, u32[]{:S(2)}) collective-permute-start(bf16[576,128]{1,0:T(8,128)(2,1)S(1)} %get-tuple-element.26), channel_id=1, source_target_pairs={{0,80},{16,96},{32,112},{48,0},{64,16},{80,32},{96,48},{112,64},{1... | collective-permute-start | bytes 442376 | tf_op jit(solution)/shard_map/ppermute | solution.py:363
  22.1 10.4 %collective-permute-start.5 = (bf16[576,128]{1,0:T(8,128)(2,1)S(1)}, bf16[576,128]{1,0:T(8,128)(2,1)S(1)}, u32[]{:S(2)}, u32[]{:S(2)}) collective-permute-start(bf16[576,128]{1,0:T(8,128)(2,1)S(1)} %get-tuple-element.27), channel_id=1, source_target_pairs={{0,96},{16,112},{32,0},{48,16},{64,32},{80,48},{96,64},{112,80},{1... | collective-permute-start | bytes 442376 | tf_op jit(solution)/shard_map/ppermute | solution.py:363
  22.8 11.2 %collective-permute-start.6 = (bf16[576,128]{1,0:T(8,128)(2,1)S(1)}, bf16[576,128]{1,0:T(8,128)(2,1)S(1)}, u32[]{:S(2)}, u32[]{:S(2)}) collective-permute-start(bf16[576,128]{1,0:T(8,128)(2,1)S(1)} %get-tuple-element.28), channel_id=1, source_target_pairs={{0,112},{16,0},{32,16},{48,32},{64,48},{80,64},{96,80},{112,96},{1... | collective-permute-start | bytes 442376 | tf_op jit(solution)/shard_map/ppermute | solution.py:363
  34.0 0.7 %copy-start.4 = (bf16[576,128]{1,0:T(8,128)(2,1)}, bf16[576,128]{1,0:T(8,128)(2,1)S(1)}, u32[]{:S(2)}) copy-start(bf16[576,128]{1,0:T(8,128)(2,1)S(1)} %collective-permute-done.6.refs_7_) | copy-start | bytes 442372
  37.2 15.1 %collective-permute-start.10 = (bf16[576,384]{1,0:T(8,128)(2,1)}, bf16[576,384]{1,0:T(8,128)(2,1)S(1)}, u32[]{:S(2)}, u32[]{:S(2)}) collective-permute-start(bf16[576,384]{1,0:T(8,128)(2,1)} %get-tuple-element.35), channel_id=1, source_target_pairs={{0,3},{1,0},{2,1},{3,2},{4,7},{5,4},{6,5},{7,6},{8,11},{9,8},{10,9... | collective-permute-start | bytes 1327112 | tf_op jit(solution)/shard_map/ppermute | solution.py:369
  40.0 13.4 %collective-permute-start.7 = (bf16[576,384]{1,0:T(8,128)(2,1)S(1)}, bf16[576,384]{1,0:T(8,128)(2,1)S(1)}, u32[]{:S(2)}, u32[]{:S(2)}) collective-permute-start(bf16[576,384]{1,0:T(8,128)(2,1)S(1)} %get-tuple-element.29.up_ref), channel_id=1, source_target_pairs={{0,4},{1,5},{2,6},{3,7},{4,8},{5,9},{6,10},{7,11},{8,12},{9,13},{1... | collective-permute-start | bytes 1327112 | tf_op jit(solution)/shard_map/ppermute | solution.py:369
  41.2 12.2 %collective-permute-start.8 = (bf16[576,384]{1,0:T(8,128)(2,1)S(1)}, bf16[576,384]{1,0:T(8,128)(2,1)}, u32[]{:S(2)}, u32[]{:S(2)}) collective-permute-start(bf16[576,384]{1,0:T(8,128)(2,1)S(1)} %get-tuple-element.30.down_ref), channel_id=1, source_target_pairs={{0,12},{1,13},{2,14},{3,15},{4,0},{5,1},{6,2},{7,3},{8,4},{9,5},{1... | collective-permute-start | bytes 1327112 | tf_op jit(solution)/shard_map/ppermute | solution.py:369
  42.7 12.9 %collective-permute-start.9 = (bf16[576,384]{1,0:T(8,128)(2,1)S(1)}, bf16[576,384]{1,0:T(8,128)(2,1)}, u32[]{:S(2)}, u32[]{:S(2)}) collective-permute-start(bf16[576,384]{1,0:T(8,128)(2,1)S(1)} %get-tuple-element.34), channel_id=1, source_target_pairs={{0,1},{1,2},{2,3},{3,0},{4,5},{5,6},{6,7},{7,4},{8,9},{9,10},{10,1... | collective-permute-start | bytes 1327112 | tf_op jit(solution)/shard_map/ppermute | solution.py:369

commit v6 on v5

--- a/solution.py
+++ b/solution.py
@@ -1,3 +1,5 @@
+import functools
+
 import jax
 import jax.numpy as jnp
 from jax import lax
@@ -62,7 +64,7 @@
 
 
 def gather_kernel(ids_hbm, counts_hbm, cache_ref, *refs):
-    out_refs, (source_ref, past_ref, ids_ref, counts_ref, held, sems) = refs[:-6], refs[-6:]
+    out_refs, (source_ref, other_ref, past_ref, ids_ref, counts_ref, held, sems) = refs[:-7], refs[-7:]
     keys = cache_ref.shape[1]
     lists = [
         pltpu.make_async_copy(ids_hbm, ids_ref, sems.at[keys // 512]),
@@ -100,29 +102,31 @@
         own.append(jnp.dot(held[i], keep, preferred_element_type=F32).astype(BF16))
     own = jnp.concatenate(own, axis=1)
     index = iota((own.shape[1], 128), 0)
-    for d in range(0, tiles, 2):
+    for d, out_ref in enumerate(out_refs):
+        near = (shard + 2 * d) & 7
         pair = []
-        for u in (d, d + 1):
-            chosen = iota((tiles, 128), 0) == ((shard + u) & 7)
+        for tile in (near, near ^ 1):
+            chosen = iota((tiles, 128), 0) == tile
             pair.append(hot(index, jnp.sum(jnp.where(chosen, target, 0), axis=0, keepdims=True)))
-        got = jnp.dot(own, jnp.concatenate(pair, axis=1), preferred_element_type=F32).astype(BF16)
-        out_refs[d][...] = got[:, :128]
-        out_refs[d + 1][...] = got[:, 128:]
+        got = jnp.dot(own, jnp.concatenate(pair, axis=1), preferred_element_type=F32)
+        out_ref[...] = got.astype(BF16)
     source, count = slot_sources(ids, shard)
     source_ref[...] = source
     past_ref[...] = jnp.broadcast_to((count - 2) * BLOCK, past_ref.shape)
+    other_ref[...] = slot_sources(ids, shard ^ 1)[0]
 
 
 def gather_parts(block_ids, block_counts, cache_t):
     width, keys = cache_t.shape
     hbm = pl.BlockSpec(memory_space=pltpu.HBM)
+    chips = SHARDS // 2
     return pl.pallas_call(
         gather_kernel,
-        out_shape=[pltpu.HBM((width, 128), BF16)]
-        + [pltpu.VMEM((width, 128), BF16)] * (SHARDS - 1)
-        + [pltpu.HBM((SHARDS, n), jnp.int32) for n in (512, 128)],
+        out_shape=[pltpu.HBM((width, 256), BF16)]
+        + [pltpu.VMEM((width, 256), BF16)] * (chips - 1)
+        + [pltpu.HBM((SHARDS, n), jnp.int32) for n in (512, 512, 128)],
         in_specs=[hbm] * 3,
-        out_specs=[VMEM] * (SHARDS + 2),
+        out_specs=[VMEM] * (chips + 3),
         scratch_shapes=[
             pltpu.VMEM(block_ids.shape, jnp.int32),
             pltpu.SMEM(block_counts.shape, jnp.int32),
@@ -137,18 +141,35 @@
     )(in_hbm(block_ids), in_hbm(block_counts), in_hbm(cache_t))
 
 
-def compact_kernel(source_ref, *refs):
-    part_refs, (up_ref, down_ref, right_ref, left_ref) = refs[:-4], refs[-4:]
-    tile = lax.axis_index("ctx")
+def compact_kernel(left, source_ref, *refs):
+    part_refs, out_ref = refs[:-1], refs[-1]
+    shard = lax.axis_index("ctx")
+    row = iota((128, 512), 0)
     source = source_ref[0:1, :]
-    row = iota((128, 512), 0)
-    total = jnp.zeros((up_ref.shape[0], 512), F32)
-    for d in range(0, SHARDS, 2):
-        pick = jnp.concatenate([hot(row + ((tile - u) & 7) * 128, source) for u in (d, d + 1)], axis=0)
-        pair = jnp.concatenate([part_refs[d][...], part_refs[d + 1][...]], axis=1)
+    total = jnp.zeros(out_ref.shape, F32)
+    for d in range(0, len(part_refs), 2):
+        pick = jnp.concatenate([hot(row + ((shard - 2 * u) & 7) * 128, source) for u in (d, d + 1)], axis=0)
+        pair = jnp.concatenate([part_refs[u][:, left : left + 128] for u in (d, d + 1)], axis=1)
         total = total + jnp.dot(pair, pick, preferred_element_type=F32)
-    total = total.astype(BF16)
-    first, second = total[:, :256], total[:, 256:]
+    out_ref[...] = total.astype(BF16)
+
+
+def compact_parts(left, source, parts):
+    width = parts[0].shape[0]
+    return pl.pallas_call(
+        functools.partial(compact_kernel, left),
+        out_shape=pltpu.VMEM((width, 512), BF16),
+        in_specs=[VMEM] * (1 + len(parts)),
+        out_specs=VMEM,
+        cost_estimate=pl.CostEstimate(flops=width * 1024 * 512, bytes_accessed=width * 1536 * 2, transcendentals=0),
+        compiler_params=pltpu.CompilerParams(vmem_limit_bytes=8 << 20),
+        name="compact_parts",
+    )(in_hbm(source), in_hbm(parts[0]), *parts[1:])
+
+
+def spread_kernel(own_ref, other_ref, up_ref, down_ref, right_ref, left_ref):
+    first = own_ref[:, :256] + other_ref[:, :256]
+    second = own_ref[:, 256:] + other_ref[:, 256:]
     up_ref[:, :256] = first
     up_ref[:, 256:] = second[:, :128]
     down_ref[:, :256] = first
@@ -159,19 +180,17 @@
     left_ref[:, 256:] = first[:, 128:]
 
 
-def compact_parts(source, parts):
-    width = parts[0].shape[0]
-    return pl.pallas_call(
-        compact_kernel,
-        out_shape=[pltpu.VMEM((width, 384), BF16)] * 4,
-        in_specs=[VMEM] * (1 + len(parts)),
+def spread_parts(own, other):
+    width = own.shape[0]
+    return pl.pallas_call(
+        spread_kernel,
+        out_shape=[jax.ShapeDtypeStruct((width, 384), BF16)] * 4,
+        in_specs=[VMEM] * 2,
         out_specs=[VMEM] * 4,
-        cost_estimate=pl.CostEstimate(
-            flops=2 * width * 1024 * 512, bytes_accessed=width * 1536 * 2, transcendentals=0
-        ),
-        compiler_params=pltpu.CompilerParams(vmem_limit_bytes=12 << 20),
-        name="compact_parts",
-    )(in_hbm(source), in_hbm(parts[0]), *parts[1:-1], in_hbm(parts[-1]))
+        cost_estimate=pl.CostEstimate(flops=width * 512, bytes_accessed=width * 2560 * 2, transcendentals=0),
+        compiler_params=pltpu.CompilerParams(vmem_limit_bytes=8 << 20),
+        name="spread_parts",
+    )(own, other)
 
 
 def q_prep_kernel(q_ref, out_ref):
@@ -207,26 +226,33 @@
         )
 
 
-def index_scores_of(index_query, index_weight, index_keys):
+def more_index_kernel(query_ref, weight_ref, keys_ref, before_ref, out_ref):
+    index_kernel(query_ref, weight_ref, keys_ref, out_ref)
+
+
+def index_scores_of(index_query, index_weight, index_keys, first, steps, before=None):
     rows, heads, dim = index_query.shape
     keys = index_keys.shape[0]
     step = 8
-    return pl.pallas_call(
-        index_kernel,
-        grid=(rows // step,),
+    more = [] if before is None else [before]
+    return pl.pallas_call(
+        index_kernel if before is None else more_index_kernel,
+        grid=(steps,),
         out_shape=jax.ShapeDtypeStruct((rows, keys), F32),
         in_specs=[
-            pl.BlockSpec((step, heads, dim), lambda i: (i, 0, 0)),
-            pl.BlockSpec((step, heads), lambda i: (i, 0)),
+            pl.BlockSpec((step, heads, dim), lambda i: (i + first, 0, 0)),
+            pl.BlockSpec((step, heads), lambda i: (i + first, 0)),
             pl.BlockSpec((keys, dim), lambda i: (0, 0)),
-        ],
-        out_specs=pl.BlockSpec((step, keys), lambda i: (i, 0)),
+        ]
+        + [pl.BlockSpec(memory_space=pl.ANY)] * len(more),
+        out_specs=pl.BlockSpec((step, keys), lambda i: (i + first, 0)),
+        input_output_aliases={3: 0} if more else {},
         cost_estimate=pl.CostEstimate(
-            flops=8 * rows * heads * dim * keys, bytes_accessed=rows * heads * dim * 2 + rows * keys * 4, transcendentals=0
+            flops=8 * steps * step * heads * dim * keys, bytes_accessed=steps * step * (heads * dim * 2 + keys * 4), transcendentals=0
         ),
         compiler_params=pltpu.CompilerParams(vmem_limit_bytes=16 << 20),
         name="index_scores",
-    )(index_query, index_weight, index_keys)
+    )(in_hbm(index_query), in_hbm(index_weight), in_hbm(index_keys), *more)
 
 
 def masked_scores(q, keys, tiles, limit):
@@ -359,12 +385,16 @@
 def body(q_latent, index_query, index_weight, index_keys, latent_cache, block_ids, block_counts):
     rows, heads, width = q_latent.shape
     groups = lax.axis_size("head")
-    *outgoing, source, past = gather_parts(block_ids, block_counts, latent_cache.T)
-    incoming = [outgoing[0]] + [lax.ppermute(outgoing[d], "ctx", turn(d)) for d in range(1, SHARDS)]
+    *outgoing, source, other, past = gather_parts(block_ids, block_counts, latent_cache.T)
+    incoming = [outgoing[0]] + [lax.ppermute(outgoing[d], "ctx", turn(2 * d)) for d in range(1, SHARDS // 2)]
     by_group = q_by_group(q_latent, groups)
     head_query = lax.all_to_all(by_group, "head", split_axis=0, concat_axis=0, tiled=True)
-    index_scores = index_scores_of(index_query, index_weight, index_keys)
-    up, down, right, left = compact_parts(source, incoming)
+    some_scores = index_scores_of(index_query, index_weight, index_keys, 0, 4)
+    index_scores = index_scores_of(index_query, index_weight, index_keys, 4, 4, some_scores)
+    theirs = compact_parts(128, other, incoming)
+    theirs = lax.ppermute(theirs, "ctx", [(i, i ^ 1) for i in range(SHARDS)])
+    mine = compact_parts(0, source, incoming)
+    up, down, right, left = spread_parts(mine, theirs)
     parts = [
         lax.ppermute(part, "head", line(*step))
         for part, step in ((up, (1, 0)), (down, (-1, 0)), (right, (0, 1)), (left, (0, -1)))

time: 63.9 us -> 58.6 us (0.917)
  waiting for transfers between devices: 12.6 us -> 5.03 us
  Pallas kernels: 25.6 us -> 30.7 us
  starting transfers between devices: 23.9 us -> 21.6 us
  local copies, waits for them, and re-layouts: 0.68 us -> 0.01 us
    ppermute x7 -> x4, waiting for transfers between devices: 9.27 us -> 2.33 us  [the longest x3 2.32 us: body(): lax.ppermute(outgoing[d], 'ctx', turn(2 * d))]
    pallas_call x3 -> x6, Pallas kernels: 13.3 us -> 18.1 us  [the longest x2 9.85 us: index_scores_of(): pl.pallas_call(index_kernel if before is None else more_index_kernel, gri...]
    ppermute x7 -> x4, starting transfers between devices: 10.6 us -> 7.31 us  [the longest x3 5.7 us: body(): lax.ppermute(outgoing[d], 'ctx', turn(2 * d))]
    ppermute x4, starting transfers between devices: 5.53 us -> 6.5 us  [body(): lax.ppermute(part, 'head', line(*step))]
    unnamed x10 -> x2, local copies, waits for them, and re-layouts: 0.68 us -> 0.01 us
    ppermute x4, waiting for transfers between devices: 3.34 us -> 2.7 us  [body(): lax.ppermute(part, 'head', line(*step))]
  transfers between devices with their start and end apart: 12 -> 9, of which waited for: 7 -> 3; matrix products, arithmetic and copies ran while one was open for 0% -> 0% of each run, Pallas kernels for 21% -> 32%
where the time goes in v6:
time: 58.6 us; the launch traced here: 58.2 us
  Pallas kernels  30.7 us (52%)
  starting transfers between devices  21.6 us (37%)
  waiting for transfers between devices  5.03 us (9%)
  between operations  0.86 us (1%)
    pallas_call x2, Pallas kernels, index_scores_of(): pl.pallas_call(index_kernel if before is None else more_index_kernel, gri...  9.85 us
    pallas_call x1, Pallas kernels, attend_rest(): pl.pallas_call(rest_kernel, out_shape=jax.ShapeDtypeStruct((rows, 512), B...  7.78 us
    all_to_all x1, starting transfers between devices, body(): lax.all_to_all(by_group, 'head', split_axis=0, concat_axis=0, tiled=True)  7.77 us
    ppermute x4, starting transfers between devices, body(): lax.ppermute(part, 'head', line(*step))  6.5 us
    ppermute x3, starting transfers between devices, body(): lax.ppermute(outgoing[d], 'ctx', turn(2 * d))  5.7 us
    pallas_call x1, Pallas kernels, gather_parts(): pl.pallas_call(gather_kernel, out_shape=[pltpu.HBM((width, 256), BF16)] +...  4.2 us
    pallas_call x1, Pallas kernels, attend_own(): pl.pallas_call(own_kernel, out_shape=[jax.ShapeDtypeStruct((rows, 128), F...  3.4 us
    pallas_call x2, Pallas kernels, compact_parts(): pl.pallas_call(functools.partial(compact_kernel, left), out_shape=pltpu.V...  2.91 us
  transfers between devices with their start and end apart: 9, of which 3 were waited for; matrix products, arithmetic and copies ran while one was open for 0% of the time, Pallas kernels for 32%

profile of v6, /device:TPU:1, one launch (start us, length us, event | category | flops | bytes accessed | tf_op | source)
XLA Modules:
  0.0 58.2 jit_solution(16161300067197610048)
XLA Ops:
  0.6 0.0 copy-start
  0.6 4.2 %gather_parts.1 = (bf16[576,256]{1,0:T(8,128)(2,1)}, bf16[576,256]{1,0:T(8,128)(2,1)S(1)}, bf16[576,256]{1,0:T(8,128)(2,1)S(1)}, bf16[576,256]{1,0:T(8,128)(2,1)...) custom-call(s32[8,32]{1,0:T(8,128)} %ids_hbm.1, s32[8]{0:T(128)} %counts_hbm.1, bf16[576,2048]{1,0:T(8,128)(2,1)} %bitcast.7), custom_call_target="tpu_custom_call" | custom-call | flops 2415919104 | bytes 4718592 | tf_op jit(solution)/shard_map/gather_parts/pallas_call | solution.py:123
  4.8 2.1 %collective-permute-start = (bf16[576,256]{1,0:T(8,128)(2,1)S(1)}, bf16[576,256]{1,0:T(8,128)(2,1)S(1)}, u32[]{:S(2)}, u32[]{:S(2)}) collective-permute-start(bf16[576,256]{1,0:T(8,128)(2,1)S(1)} %get-tuple-element.19), channel_id=1, source_target_pairs={{0,32},{16,48},{32,64},{48,80},{64,96},{80,112},{96,0},{112,16},{1... | collective-permute-start | bytes 884744 | tf_op jit(solution)/shard_map/ppermute | solution.py:389
  6.9 2.5 %collective-permute-start.1 = (bf16[576,256]{1,0:T(8,128)(2,1)S(1)}, bf16[576,256]{1,0:T(8,128)(2,1)S(1)}, u32[]{:S(2)}, u32[]{:S(2)}) collective-permute-start(bf16[576,256]{1,0:T(8,128)(2,1)S(1)} %get-tuple-element.20), channel_id=1, source_target_pairs={{0,64},{16,80},{32,96},{48,112},{64,0},{80,16},{96,32},{112,48},{1... | collective-permute-start | bytes 884744 | tf_op jit(solution)/shard_map/ppermute | solution.py:389
  9.4 1.2 %collective-permute-start.2 = (bf16[576,256]{1,0:T(8,128)(2,1)S(1)}, bf16[576,256]{1,0:T(8,128)(2,1)S(1)}, u32[]{:S(2)}, u32[]{:S(2)}) collective-permute-start(bf16[576,256]{1,0:T(8,128)(2,1)S(1)} %get-tuple-element.21), channel_id=1, source_target_pairs={{0,96},{16,112},{32,0},{48,16},{64,32},{80,48},{96,64},{112,80},{1... | collective-permute-start | bytes 884744 | tf_op jit(solution)/shard_map/ppermute | solution.py:389
  10.6 0.0 copy-done
  10.6 1.5 %q_by_group.1 = bf16[16,8,8,576]{3,2,1,0:T(8,128)(2,1)} custom-call(bf16[8,576,128]{2,1,0:T(8,128)(2,1)S(1)} %bitcast.6), custom_call_target="tpu_custom_call" | custom-call | bytes 2359296 | tf_op jit(solution)/shard_map/q_by_group/pallas_call | solution.py:204
  12.0 7.8 %all-to-all-start = ((bf16[16,8,8,576]{3,2,1,0:T(8,128)(2,1)}), bf16[16,8,8,576]{3,2,1,0:T(8,128)(2,1)S(1)}, u32[]{:S(2)}, u32[]{:S(2)}) async-start(bf16[16,8,8,576]{3,2,1,0:T(8,128)(2,1)} %q_by_group.1), calls=%async_computation | async-start | bytes 2621440 | tf_op jit(solution)/shard_map/all_to_all | solution.py:391
  19.8 0.0 collective-permute-done.refs_1_
  19.8 2.3 %collective-permute-done.1.refs_2_ = bf16[576,256]{1,0:T(8,128)(2,1)S(1)} collective-permute-done((bf16[576,256]{1,0:T(8,128)(2,1)S(1)}, bf16[576,256]{1,0:T(8,128)(2,1)S(1)}, u32[]{:S(2)}, u32[]{:S(2)}) %collective-permute-start.1) | collective-permute-done | bytes 294944 | tf_op jit(solution)/shard_map/ppermute | solution.py:389
  22.1 0.0 collective-permute-done.2.refs_3_
  22.1 1.5 %compact_parts.3 = bf16[576,512]{1,0:T(8,128)(2,1)S(1)} custom-call(s32[8,512]{1,0:T(8,128)} %get-tuple-element.22.source_ref, bf16[576,256]{1,0:T(8,128)(2,1)} %get-tuple-element.18.refs_0_, bf16[576,256]{1,0:T(8,128)(2,1)S(1)} %collective-permute-done.refs_1_, bf16[576,256]{1,0:T(8,128)(2,1)S(1)} %collective-permute-done.1.refs_2_, ...), custom_call_target="tpu_custom_call" | custom-call | flops 301989888 | bytes 1769472 | tf_op jit(solution)/shard_map/compact_parts/pallas_call | solution.py:159
  23.6 1.6 %collective-permute-start.3 = (bf16[576,512]{1,0:T(8,128)(2,1)S(1)}, bf16[576,512]{1,0:T(8,128)(2,1)S(1)}, u32[]{:S(2)}, u32[]{:S(2)}) collective-permute-start(bf16[576,512]{1,0:T(8,128)(2,1)S(1)} %compact_parts.3), channel_id=1, source_target_pairs={{0,16},{16,0},{32,48},{48,32},{64,80},{80,64},{96,112},{112,96},{1... | collective-permute-start | bytes 1769480 | tf_op jit(solution)/shard_map/ppermute | solution.py:395
  25.2 4.9 %index_scores.2.before_ref = f32[64,2048]{1,0:T(8,128)} custom-call(bf16[64,64,128]{2,1,0:T(8,128)(2,1)} %query_ref.3, f32[64,64]{1,0:T(8,128)} %weight_ref.3, bf16[2048,128]{1,0:T(8,128)(2,1)} %keys_ref.3), custom_call_target="tpu_custom_call" | custom-call | flops 4294967296 | bytes 786432 | tf_op jit(solution)/shard_map/index_scores/pallas_call | solution.py:238
  30.1 1.5 %compact_parts.2.own_ref = bf16[576,512]{1,0:T(8,128)(2,1)S(1)} custom-call(s32[8,512]{1,0:T(8,128)} %get-tuple-element.17.source_ref, bf16[576,256]{1,0:T(8,128)(2,1)} %get-tuple-element.18.refs_0_, bf16[576,256]{1,0:T(8,128)(2,1)S(1)} %collective-permute-done.refs_1_, bf16[576,256]{1,0:T(8,128)(2,1)S(1)} %collective-permute-done.1.refs_2_, ...), custom_call_target="tpu_custom_call" | custom-call | flops 301989888 | bytes 1769472 | tf_op jit(solution)/shard_map/compact_parts/pallas_call | solution.py:159
  31.6 0.0 collective-permute-done.3.other_ref
  31.6 1.1 %spread_parts.1 = (bf16[576,384]{1,0:T(8,128)(2,1)}, bf16[576,384]{1,0:T(8,128)(2,1)}, bf16[576,384]{1,0:T(8,128)(2,1)S(1)}, bf16[576,384]{1,0:T(8,128)(2,1)S(1)}) custom-call(bf16[576,512]{1,0:T(8,128)(2,1)S(1)} %compact_parts.2.own_ref, bf16[576,512]{1,0:T(8,128)(2,1)S(1)} %collective-permute-done.3.other_ref), custom_call_target="tpu_custom_call" | custom-call | flops 294912 | bytes 2949120 | tf_op jit(solution)/shard_map/spread_parts/pallas_call | solution.py:185
  32.7 1.3 %collective-permute-start.4 = (bf16[576,384]{1,0:T(8,128)(2,1)}, bf16[576,384]{1,0:T(8,128)(2,1)S(1)}, u32[]{:S(2)}, u32[]{:S(2)}) collective-permute-start(bf16[576,384]{1,0:T(8,128)(2,1)} %get-tuple-element.23.up_ref), channel_id=1, source_target_pairs={{0,4},{1,5},{2,6},{3,7},{4,8},{5,9},{6,10},{7,11},{8,12},{9,13},{1... | collective-permute-start | bytes 1327112 | tf_op jit(solution)/shard_map/ppermute | solution.py:399
  34.0 1.4 %collective-permute-start.5 = (bf16[576,384]{1,0:T(8,128)(2,1)}, bf16[576,384]{1,0:T(8,128)(2,1)S(1)}, u32[]{:S(2)}, u32[]{:S(2)}) collective-permute-start(bf16[576,384]{1,0:T(8,128)(2,1)} %get-tuple-element.24.down_ref), channel_id=1, source_target_pairs={{0,12},{1,13},{2,14},{3,15},{4,0},{5,1},{6,2},{7,3},{8,4},{9,5},{1... | collective-permute-start | bytes 1327112 | tf_op jit(solution)/shard_map/ppermute | solution.py:399
  35.5 1.6 %collective-permute-start.6 = (bf16[576,384]{1,0:T(8,128)(2,1)S(1)}, bf16[576,384]{1,0:T(8,128)(2,1)S(1)}, u32[]{:S(2)}, u32[]{:S(2)}) collective-permute-start(bf16[576,384]{1,0:T(8,128)(2,1)S(1)} %get-tuple-element.28), channel_id=1, source_target_pairs={{0,1},{1,2},{2,3},{3,0},{4,5},{5,6},{6,7},{7,4},{8,9},{9,10},{10,1... | collective-permute-start | bytes 1327112 | tf_op jit(solution)/shard_map/ppermute | solution.py:399
  37.1 2.1 %collective-permute-start.7 = (bf16[576,384]{1,0:T(8,128)(2,1)S(1)}, bf16[576,384]{1,0:T(8,128)(2,1)}, u32[]{:S(2)}, u32[]{:S(2)}) collective-permute-start(bf16[576,384]{1,0:T(8,128)(2,1)S(1)} %get-tuple-element.29), channel_id=1, source_target_pairs={{0,3},{1,0},{2,1},{3,2},{4,7},{5,4},{6,5},{7,6},{8,11},{9,8},{10,9... | collective-permute-start | bytes 1327112 | tf_op jit(solution)/shard_map/ppermute | solution.py:399
  39.2 4.9 %index_scores.3 = f32[64,2048]{1,0:T(8,128)} custom-call(bf16[64,64,128]{2,1,0:T(8,128)(2,1)} %query_ref.3, f32[64,64]{1,0:T(8,128)} %weight_ref.3, bf16[2048,128]{1,0:T(8,128)(2,1)} %keys_ref.3, f32[64,2048]{1,0:T(8,128)} %index_scores.2.before_ref), custom_call_target="tpu_custom_call", output_to_operand_aliasing={{}: (3, {})} | custom-call | flops 4294967296 | bytes 786432 | tf_op jit(solution)/shard_map/index_scores/pallas_call | solution.py:238
  44.2 0.0 all-to-all-done
  44.2 3.4 %attend_own.1 = (f32[1024,128]{1,0:T(8,128)S(1)}, f32[1024,128]{1,0:T(8,128)S(1)}, f32[1024,512]{1,0:T(8,128)S(1)}) custom-call(s32[8,128]{1,0:T(8,128)} %get-tuple-element.16.past_ref, bf16[1024,576]{1,0:T(8,128)(2,1)S(1)} %bitcast.4, bf16[576,384]{1,0:T(8,128)(2,1)} %get-tuple-element.23.up_ref, bf16[576,384]{1,0:T(8,128)(2,1)} %get-tuple-element.24.down_ref), custom_call_target="tpu_custom_call" | custom-call | flops 1140850688 | bytes 4456448 | tf_op jit(solution)/shard_map/attend_own/pallas_call | solution.py:295
  47.6 0.1 collective-permute-done.4.up_ref
  47.7 0.0 collective-permute-done.5.down_ref
  47.7 2.6 %collective-permute-done.6.right_ref = bf16[576,384]{1,0:T(8,128)(2,1)S(1)} collective-permute-done((bf16[576,384]{1,0:T(8,128)(2,1)S(1)}, bf16[576,384]{1,0:T(8,128)(2,1)S(1)}, u32[]{:S(2)}, u32[]{:S(2)}) %collective-permute-start.6) | collective-permute-done | bytes 442400 | tf_op jit(solution)/shard_map/ppermute | solution.py:399
  50.3 0.0 collective-permute-done.7.left_ref
  50.3 7.8 %attend_rest.1 = bf16[1024,512]{1,0:T(8,128)(2,1)} custom-call(s32[8,128]{1,0:T(8,128)} %get-tuple-element.16.past_ref, bf16[1024,576]{1,0:T(8,128)(2,1)S(1)} %bitcast.5, f32[1024,128]{1,0:T(8,128)S(1)} %get-tuple-element.25.top_ref, f32[1024,128]{1,0:T(8,128)S(1)} %get-tuple-element.26.total_ref, f32[1024,512]{1,0:T(8,128)S(1)} %get-tuple-element.27.mixed_ref, ...), custom_call_target="tpu_custom_call" | custom-call | flops 3422552064 | bytes 5505024 | tf_op jit(solution)/shard_map/attend_rest/pallas_call | solution.py:359
Async XLA Ops:
  0.6 9.9 %copy-start = (bf16[8,128,576]{1,2,0:T(8,128)(2,1)S(1)}, bf16[8,128,576]{1,2,0:T(8,128)(2,1)}, u32[]{:S(2)}) copy-start(bf16[8,128,576]{1,2,0:T(8,128)(2,1)} %param.7) | copy-start | bytes 3538948
  4.8 15.0 %collective-permute-start = (bf16[576,256]{1,0:T(8,128)(2,1)S(1)}, bf16[576,256]{1,0:T(8,128)(2,1)S(1)}, u32[]{:S(2)}, u32[]{:S(2)}) collective-permute-start(bf16[576,256]{1,0:T(8,128)(2,1)S(1)} %get-tuple-element.19), channel_id=1, source_target_pairs={{0,32},{16,48},{32,64},{48,80},{64,96},{80,112},{96,0},{112,16},{1... | collective-permute-start | bytes 884744 | tf_op jit(solution)/shard_map/ppermute | solution.py:389
  6.9 15.2 %collective-permute-start.1 = (bf16[576,256]{1,0:T(8,128)(2,1)S(1)}, bf16[576,256]{1,0:T(8,128)(2,1)S(1)}, u32[]{:S(2)}, u32[]{:S(2)}) collective-permute-start(bf16[576,256]{1,0:T(8,128)(2,1)S(1)} %get-tuple-element.20), channel_id=1, source_target_pairs={{0,64},{16,80},{32,96},{48,112},{64,0},{80,16},{96,32},{112,48},{1... | collective-permute-start | bytes 884744 | tf_op jit(solution)/shard_map/ppermute | solution.py:389
  9.4 12.7 %collective-permute-start.2 = (bf16[576,256]{1,0:T(8,128)(2,1)S(1)}, bf16[576,256]{1,0:T(8,128)(2,1)S(1)}, u32[]{:S(2)}, u32[]{:S(2)}) collective-permute-start(bf16[576,256]{1,0:T(8,128)(2,1)S(1)} %get-tuple-element.21), channel_id=1, source_target_pairs={{0,96},{16,112},{32,0},{48,16},{64,32},{80,48},{96,64},{112,80},{1... | collective-permute-start | bytes 884744 | tf_op jit(solution)/shard_map/ppermute | solution.py:389
  12.0 32.1 %all-to-all-start = ((bf16[16,8,8,576]{3,2,1,0:T(8,128)(2,1)}), bf16[16,8,8,576]{3,2,1,0:T(8,128)(2,1)S(1)}, u32[]{:S(2)}, u32[]{:S(2)}) async-start(bf16[16,8,8,576]{3,2,1,0:T(8,128)(2,1)} %q_by_group.1), calls=%async_computation | async-start | bytes 2621440 | tf_op jit(solution)/shard_map/all_to_all | solution.py:391
  23.6 8.0 %collective-permute-start.3 = (bf16[576,512]{1,0:T(8,128)(2,1)S(1)}, bf16[576,512]{1,0:T(8,128)(2,1)S(1)}, u32[]{:S(2)}, u32[]{:S(2)}) collective-permute-start(bf16[576,512]{1,0:T(8,128)(2,1)S(1)} %compact_parts.3), channel_id=1, source_target_pairs={{0,16},{16,0},{32,48},{48,32},{64,80},{80,64},{96,112},{112,96},{1... | collective-permute-start | bytes 1769480 | tf_op jit(solution)/shard_map/ppermute | solution.py:395
  32.7 15.0 %collective-permute-start.4 = (bf16[576,384]{1,0:T(8,128)(2,1)}, bf16[576,384]{1,0:T(8,128)(2,1)S(1)}, u32[]{:S(2)}, u32[]{:S(2)}) collective-permute-start(bf16[576,384]{1,0:T(8,128)(2,1)} %get-tuple-element.23.up_ref), channel_id=1, source_target_pairs={{0,4},{1,5},{2,6},{3,7},{4,8},{5,9},{6,10},{7,11},{8,12},{9,13},{1... | collective-permute-start | bytes 1327112 | tf_op jit(solution)/shard_map/ppermute | solution.py:399
  34.0 13.7 %collective-permute-start.5 = (bf16[576,384]{1,0:T(8,128)(2,1)}, bf16[576,384]{1,0:T(8,128)(2,1)S(1)}, u32[]{:S(2)}, u32[]{:S(2)}) collective-permute-start(bf16[576,384]{1,0:T(8,128)(2,1)} %get-tuple-element.24.down_ref), channel_id=1, source_target_pairs={{0,12},{1,13},{2,14},{3,15},{4,0},{5,1},{6,2},{7,3},{8,4},{9,5},{1... | collective-permute-start | bytes 1327112 | tf_op jit(solution)/shard_map/ppermute | solution.py:399
  35.5 14.8 %collective-permute-start.6 = (bf16[576,384]{1,0:T(8,128)(2,1)S(1)}, bf16[576,384]{1,0:T(8,128)(2,1)S(1)}, u32[]{:S(2)}, u32[]{:S(2)}) collective-permute-start(bf16[576,384]{1,0:T(8,128)(2,1)S(1)} %get-tuple-element.28), channel_id=1, source_target_pairs={{0,1},{1,2},{2,3},{3,0},{4,5},{5,6},{6,7},{7,4},{8,9},{9,10},{10,1... | collective-permute-start | bytes 1327112 | tf_op jit(solution)/shard_map/ppermute | solution.py:399
  37.1 13.2 %collective-permute-start.7 = (bf16[576,384]{1,0:T(8,128)(2,1)S(1)}, bf16[576,384]{1,0:T(8,128)(2,1)}, u32[]{:S(2)}, u32[]{:S(2)}) collective-permute-start(bf16[576,384]{1,0:T(8,128)(2,1)S(1)} %get-tuple-element.29), channel_id=1, source_target_pairs={{0,3},{1,0},{2,1},{3,2},{4,7},{5,4},{6,5},{7,6},{8,11},{9,8},{10,9... | collective-permute-start | bytes 1327112 | tf_op jit(solution)/shard_map/ppermute | solution.py:399

commit v7 on v6

--- a/solution.py
+++ b/solution.py
@@ -25,6 +25,10 @@
 
 def in_hbm(x):
     return pltpu.with_memory_space_constraint(x, pltpu.HBM)
+
+
+def in_vmem(x):
+    return pltpu.with_memory_space_constraint(x, pltpu.VMEM)
 
 
 def valid_ids(ids_ref, counts_ref):
@@ -226,33 +230,26 @@
         )
 
 
-def more_index_kernel(query_ref, weight_ref, keys_ref, before_ref, out_ref):
-    index_kernel(query_ref, weight_ref, keys_ref, out_ref)
-
-
-def index_scores_of(index_query, index_weight, index_keys, first, steps, before=None):
+def index_scores_of(index_query, index_weight, index_keys):
     rows, heads, dim = index_query.shape
     keys = index_keys.shape[0]
     step = 8
-    more = [] if before is None else [before]
-    return pl.pallas_call(
-        index_kernel if before is None else more_index_kernel,
-        grid=(steps,),
+    return pl.pallas_call(
+        index_kernel,
+        grid=(rows // step,),
         out_shape=jax.ShapeDtypeStruct((rows, keys), F32),
         in_specs=[
-            pl.BlockSpec((step, heads, dim), lambda i: (i + first, 0, 0)),
-            pl.BlockSpec((step, heads), lambda i: (i + first, 0)),
+            pl.BlockSpec((step, heads, dim), lambda i: (i, 0, 0)),
+            pl.BlockSpec((step, heads), lambda i: (i, 0)),
             pl.BlockSpec((keys, dim), lambda i: (0, 0)),
-        ]
-        + [pl.BlockSpec(memory_space=pl.ANY)] * len(more),
-        out_specs=pl.BlockSpec((step, keys), lambda i: (i + first, 0)),
-        input_output_aliases={3: 0} if more else {},
+        ],
+        out_specs=pl.BlockSpec((step, keys), lambda i: (i, 0)),
         cost_estimate=pl.CostEstimate(
-            flops=8 * steps * step * heads * dim * keys, bytes_accessed=steps * step * (heads * dim * 2 + keys * 4), transcendentals=0
+            flops=8 * rows * heads * dim * keys, bytes_accessed=rows * heads * dim * 2 + rows * keys * 4, transcendentals=0
         ),
         compiler_params=pltpu.CompilerParams(vmem_limit_bytes=16 << 20),
         name="index_scores",
-    )(in_hbm(index_query), in_hbm(index_weight), in_hbm(index_keys), *more)
+    )(index_query, index_weight, index_keys)
 
 
 def masked_scores(q, keys, tiles, limit):
@@ -307,7 +304,7 @@
         ),
         compiler_params=pltpu.CompilerParams(vmem_limit_bytes=16 << 20),
         name="attend_own",
-    )(in_hbm(past), q, up, down)
+    )(in_hbm(past), q, in_vmem(up), in_vmem(down))
 
 
 def rest_kernel(past_ref, q_ref, top_ref, total_ref, mixed_ref, up_ref, down_ref, right_ref, left_ref, out_ref, keys_ref, done_ref, sems):
@@ -371,7 +368,7 @@
         ),
         compiler_params=pltpu.CompilerParams(vmem_limit_bytes=24 << 20),
         name="attend_rest",
-    )(in_hbm(past), q, *state, *parts)
+    )(in_hbm(past), q, *state, *[in_vmem(part) for part in parts])
 
 
 def turn(d):
@@ -389,8 +386,7 @@
     incoming = [outgoing[0]] + [lax.ppermute(outgoing[d], "ctx", turn(2 * d)) for d in range(1, SHARDS // 2)]
     by_group = q_by_group(q_latent, groups)
     head_query = lax.all_to_all(by_group, "head", split_axis=0, concat_axis=0, tiled=True)
-    some_scores = index_scores_of(index_query, index_weight, index_keys, 0, 4)
-    index_scores = index_scores_of(index_query, index_weight, index_keys, 4, 4, some_scores)
+    index_scores = index_scores_of(index_query, index_weight, index_keys)
     theirs = compact_parts(128, other, incoming)
     theirs = lax.ppermute(theirs, "ctx", [(i, i ^ 1) for i in range(SHARDS)])
     mine = compact_parts(0, source, incoming)

time: 58.6 us -> 69.9 us (1.19)
  waiting for transfers between devices: 5.03 us -> 21 us
  Pallas kernels: 30.7 us -> 27.3 us
  starting transfers between devices: 21.6 us -> 20.4 us
    ppermute x3, waiting for transfers between devices: 2.32 us -> 11.6 us  [body(): lax.ppermute(outgoing[d], 'ctx', turn(2 * d))]
    all_to_all x1, waiting for transfers between devices: 0.01 us -> 5.29 us  [body(): lax.all_to_all(by_group, 'head', split_axis=0, concat_axis=0, tiled=True)]
    pallas_call x2 -> x1, Pallas kernels: 9.85 us -> 6.57 us  [index_scores_of(): pl.pallas_call(index_kernel, grid=(rows // step,), out_shape=jax.ShapeDty...]
    ppermute x4, waiting for transfers between devices: 2.7 us -> 4.1 us  [body(): lax.ppermute(part, 'head', line(*step))]
    ppermute x4, starting transfers between devices: 6.5 us -> 5.35 us  [body(): lax.ppermute(part, 'head', line(*step))]
  transfers between devices with their start and end apart: 9 -> 9, of which waited for: 3 -> 5; matrix products, arithmetic and copies ran while one was open for 0% -> 0% of each run, Pallas kernels for 32% -> 20%
where the time goes in v7:
time: 69.9 us; the launch traced here: 69.6 us
  Pallas kernels  27.3 us (39%)
  waiting for transfers between devices  21 us (30%)
  starting transfers between devices  20.4 us (29%)
  between operations  0.88 us (1%)
    ppermute x3, waiting for transfers between devices, body(): lax.ppermute(outgoing[d], 'ctx', turn(2 * d))  11.6 us
    all_to_all x1, starting transfers between devices, body(): lax.all_to_all(by_group, 'head', split_axis=0, concat_axis=0, tiled=True)  7.77 us
    pallas_call x1, Pallas kernels, attend_rest(): pl.pallas_call(rest_kernel, out_shape=jax.ShapeDtypeStruct((rows, 512), B...  7.42 us
    pallas_call x1, Pallas kernels, index_scores_of(): pl.pallas_call(index_kernel, grid=(rows // step,), out_shape=jax.ShapeDty...  6.57 us
    ppermute x3, starting transfers between devices, body(): lax.ppermute(outgoing[d], 'ctx', turn(2 * d))  5.7 us
    ppermute x4, starting transfers between devices, body(): lax.ppermute(part, 'head', line(*step))  5.35 us
    all_to_all x1, waiting for transfers between devices, body(): lax.all_to_all(by_group, 'head', split_axis=0, concat_axis=0, tiled=True)  5.29 us
    pallas_call x1, Pallas kernels, gather_parts(): pl.pallas_call(gather_kernel, out_shape=[pltpu.HBM((width, 256), BF16)] +...  4.19 us
  transfers between devices with their start and end apart: 9, of which 5 were waited for; matrix products, arithmetic and copies ran while one was open for 0% of the time, Pallas kernels for 20%

profile of v7, /device:TPU:1, one launch (start us, length us, event | category | flops | bytes accessed | tf_op | source)
XLA Modules:
  0.0 69.6 jit_solution(2359899181934540260)
XLA Ops:
  0.6 4.2 %gather_parts.1 = (bf16[576,256]{1,0:T(8,128)(2,1)}, bf16[576,256]{1,0:T(8,128)(2,1)S(1)}, bf16[576,256]{1,0:T(8,128)(2,1)S(1)}, bf16[576,256]{1,0:T(8,128)(2,1)...) custom-call(s32[8,32]{1,0:T(8,128)} %ids_hbm.1, s32[8]{0:T(128)} %counts_hbm.1, bf16[576,2048]{1,0:T(8,128)(2,1)} %bitcast.7), custom_call_target="tpu_custom_call" | custom-call | flops 2415919104 | bytes 4718592 | tf_op jit(solution)/shard_map/gather_parts/pallas_call | solution.py:127
  4.8 0.0 copy-start
  4.8 2.1 %collective-permute-start = (bf16[576,256]{1,0:T(8,128)(2,1)S(1)}, bf16[576,256]{1,0:T(8,128)(2,1)S(1)}, u32[]{:S(2)}, u32[]{:S(2)}) collective-permute-start(bf16[576,256]{1,0:T(8,128)(2,1)S(1)} %get-tuple-element.19), channel_id=1, source_target_pairs={{0,32},{16,48},{32,64},{48,80},{64,96},{80,112},{96,0},{112,16},{1... | collective-permute-start | bytes 884744 | tf_op jit(solution)/shard_map/ppermute | solution.py:386
  6.9 2.4 %collective-permute-start.1 = (bf16[576,256]{1,0:T(8,128)(2,1)S(1)}, bf16[576,256]{1,0:T(8,128)(2,1)S(1)}, u32[]{:S(2)}, u32[]{:S(2)}) collective-permute-start(bf16[576,256]{1,0:T(8,128)(2,1)S(1)} %get-tuple-element.20), channel_id=1, source_target_pairs={{0,64},{16,80},{32,96},{48,112},{64,0},{80,16},{96,32},{112,48},{1... | collective-permute-start | bytes 884744 | tf_op jit(solution)/shard_map/ppermute | solution.py:386
  9.4 1.2 %collective-permute-start.2 = (bf16[576,256]{1,0:T(8,128)(2,1)S(1)}, bf16[576,256]{1,0:T(8,128)(2,1)S(1)}, u32[]{:S(2)}, u32[]{:S(2)}) collective-permute-start(bf16[576,256]{1,0:T(8,128)(2,1)S(1)} %get-tuple-element.21), channel_id=1, source_target_pairs={{0,96},{16,112},{32,0},{48,16},{64,32},{80,48},{96,64},{112,80},{1... | collective-permute-start | bytes 884744 | tf_op jit(solution)/shard_map/ppermute | solution.py:386
  10.5 4.0 %collective-permute-done.refs_1_ = bf16[576,256]{1,0:T(8,128)(2,1)S(1)} collective-permute-done((bf16[576,256]{1,0:T(8,128)(2,1)S(1)}, bf16[576,256]{1,0:T(8,128)(2,1)S(1)}, u32[]{:S(2)}, u32[]{:S(2)}) %collective-permute-start) | collective-permute-done | bytes 294944 | tf_op jit(solution)/shard_map/ppermute | solution.py:386
  14.6 7.6 %collective-permute-done.1.refs_2_ = bf16[576,256]{1,0:T(8,128)(2,1)S(1)} collective-permute-done((bf16[576,256]{1,0:T(8,128)(2,1)S(1)}, bf16[576,256]{1,0:T(8,128)(2,1)S(1)}, u32[]{:S(2)}, u32[]{:S(2)}) %collective-permute-start.1) | collective-permute-done | bytes 294944 | tf_op jit(solution)/shard_map/ppermute | solution.py:386
  22.1 0.0 collective-permute-done.2.refs_3_
  22.1 1.5 %compact_parts.3 = bf16[576,512]{1,0:T(8,128)(2,1)S(1)} custom-call(s32[8,512]{1,0:T(8,128)} %get-tuple-element.22.source_ref, bf16[576,256]{1,0:T(8,128)(2,1)} %get-tuple-element.18.refs_0_, bf16[576,256]{1,0:T(8,128)(2,1)S(1)} %collective-permute-done.refs_1_, bf16[576,256]{1,0:T(8,128)(2,1)S(1)} %collective-permute-done.1.refs_2_, ...), custom_call_target="tpu_custom_call" | custom-call | flops 301989888 | bytes 1769472 | tf_op jit(solution)/shard_map/compact_parts/pallas_call | solution.py:163
  23.6 1.6 %collective-permute-start.3 = (bf16[576,512]{1,0:T(8,128)(2,1)S(1)}, bf16[576,512]{1,0:T(8,128)(2,1)S(1)}, u32[]{:S(2)}, u32[]{:S(2)}) collective-permute-start(bf16[576,512]{1,0:T(8,128)(2,1)S(1)} %compact_parts.3), channel_id=1, source_target_pairs={{0,16},{16,0},{32,48},{48,32},{64,80},{80,64},{96,112},{112,96},{1... | collective-permute-start | bytes 1769480 | tf_op jit(solution)/shard_map/ppermute | solution.py:391
  25.2 0.0 copy-done
  25.2 1.5 %q_by_group.1 = bf16[16,8,8,576]{3,2,1,0:T(8,128)(2,1)} custom-call(bf16[8,576,128]{2,1,0:T(8,128)(2,1)S(1)} %bitcast.6), custom_call_target="tpu_custom_call" | custom-call | bytes 2359296 | tf_op jit(solution)/shard_map/q_by_group/pallas_call | solution.py:208
  26.7 7.8 %all-to-all-start = ((bf16[16,8,8,576]{3,2,1,0:T(8,128)(2,1)}), bf16[16,8,8,576]{3,2,1,0:T(8,128)(2,1)S(1)}, u32[]{:S(2)}, u32[]{:S(2)}) async-start(bf16[16,8,8,576]{3,2,1,0:T(8,128)(2,1)} %q_by_group.1), calls=%async_computation | async-start | bytes 2621440 | tf_op jit(solution)/shard_map/all_to_all | solution.py:388
  34.5 0.0 copy-start.1
  34.5 0.0 copy-start.2
  34.5 0.0 copy-start.3
  34.5 1.6 %compact_parts.2.own_ref = bf16[576,512]{1,0:T(8,128)(2,1)S(1)} custom-call(s32[8,512]{1,0:T(8,128)} %get-tuple-element.17.source_ref, bf16[576,256]{1,0:T(8,128)(2,1)} %get-tuple-element.18.refs_0_, bf16[576,256]{1,0:T(8,128)(2,1)S(1)} %collective-permute-done.refs_1_, bf16[576,256]{1,0:T(8,128)(2,1)S(1)} %collective-permute-done.1.refs_2_, ...), custom_call_target="tpu_custom_call" | custom-call | flops 301989888 | bytes 1769472 | tf_op jit(solution)/shard_map/compact_parts/pallas_call | solution.py:163
  36.1 0.0 collective-permute-done.3.other_ref
  36.1 1.2 %spread_parts.1 = (bf16[576,384]{1,0:T(8,128)(2,1)}, bf16[576,384]{1,0:T(8,128)(2,1)}, bf16[576,384]{1,0:T(8,128)(2,1)}, bf16[576,384]{1,0:T(8,128)(2,1)S(1)}) custom-call(bf16[576,512]{1,0:T(8,128)(2,1)S(1)} %compact_parts.2.own_ref, bf16[576,512]{1,0:T(8,128)(2,1)S(1)} %collective-permute-done.3.other_ref), custom_call_target="tpu_custom_call" | custom-call | flops 294912 | bytes 2949120 | tf_op jit(solution)/shard_map/spread_parts/pallas_call | solution.py:189
  37.3 1.4 %collective-permute-start.4 = (bf16[576,384]{1,0:T(8,128)(2,1)}, bf16[576,384]{1,0:T(8,128)(2,1)S(1)}, u32[]{:S(2)}, u32[]{:S(2)}) collective-permute-start(bf16[576,384]{1,0:T(8,128)(2,1)} %get-tuple-element.23.up_ref), channel_id=1, source_target_pairs={{0,4},{1,5},{2,6},{3,7},{4,8},{5,9},{6,10},{7,11},{8,12},{9,13},{1... | collective-permute-start | bytes 1327112 | tf_op jit(solution)/shard_map/ppermute | solution.py:395
  38.7 1.3 %collective-permute-start.5 = (bf16[576,384]{1,0:T(8,128)(2,1)}, bf16[576,384]{1,0:T(8,128)(2,1)S(1)}, u32[]{:S(2)}, u32[]{:S(2)}) collective-permute-start(bf16[576,384]{1,0:T(8,128)(2,1)} %get-tuple-element.24.down_ref), channel_id=1, source_target_pairs={{0,12},{1,13},{2,14},{3,15},{4,0},{5,1},{6,2},{7,3},{8,4},{9,5},{1... | collective-permute-start | bytes 1327112 | tf_op jit(solution)/shard_map/ppermute | solution.py:395
  40.0 1.4 %collective-permute-start.6 = (bf16[576,384]{1,0:T(8,128)(2,1)}, bf16[576,384]{1,0:T(8,128)(2,1)S(1)}, u32[]{:S(2)}, u32[]{:S(2)}) collective-permute-start(bf16[576,384]{1,0:T(8,128)(2,1)} %get-tuple-element.28), channel_id=1, source_target_pairs={{0,1},{1,2},{2,3},{3,0},{4,5},{5,6},{6,7},{7,4},{8,9},{9,10},{10,1... | collective-permute-start | bytes 1327112 | tf_op jit(solution)/shard_map/ppermute | solution.py:395
  41.4 1.3 %collective-permute-start.7 = (bf16[576,384]{1,0:T(8,128)(2,1)S(1)}, bf16[576,384]{1,0:T(8,128)(2,1)S(1)}, u32[]{:S(2)}, u32[]{:S(2)}) collective-permute-start(bf16[576,384]{1,0:T(8,128)(2,1)S(1)} %get-tuple-element.29), channel_id=1, source_target_pairs={{0,3},{1,0},{2,1},{3,2},{4,7},{5,4},{6,5},{7,6},{8,11},{9,8},{10,9... | collective-permute-start | bytes 1327112 | tf_op jit(solution)/shard_map/ppermute | solution.py:395
  42.7 0.0 copy-done.1
  42.7 0.0 copy-done.2
  42.7 0.0 copy-done.3
  42.7 6.6 %index_scores.1 = f32[64,2048]{1,0:T(8,128)} custom-call(bf16[64,64,128]{2,1,0:T(8,128)(2,1)S(1)} %copy-done.1, f32[64,64]{1,0:T(8,128)S(1)} %copy-done.3, bf16[2048,128]{1,0:T(8,128)(2,1)S(1)} %copy-done.2), custom_call_target="tpu_custom_call" | custom-call | flops 8589934592 | bytes 1572864 | tf_op jit(solution)/shard_map/index_scores/pallas_call | solution.py:237
  49.3 5.3 %all-to-all-done = bf16[16,8,8,576]{3,2,1,0:T(8,128)(2,1)S(1)} async-done(((bf16[16,8,8,576]{3,2,1,0:T(8,128)(2,1)}), bf16[16,8,8,576]{3,2,1,0:T(8,128)(2,1)S(1)}, u32[]{:S(2)}, u32[]{:S(2)}) %all-to-all-start) | async-done | bytes 1179680 | tf_op jit(solution)/shard_map/all_to_all | solution.py:388
  54.5 3.4 %attend_own.1 = (f32[1024,128]{1,0:T(8,128)S(1)}, f32[1024,128]{1,0:T(8,128)S(1)}, f32[1024,512]{1,0:T(8,128)S(1)}) custom-call(s32[8,128]{1,0:T(8,128)} %get-tuple-element.16.past_ref, bf16[1024,576]{1,0:T(8,128)(2,1)S(1)} %bitcast.4, bf16[576,384]{1,0:T(8,128)(2,1)} %get-tuple-element.23.up_ref, bf16[576,384]{1,0:T(8,128)(2,1)} %get-tuple-element.24.down_ref), custom_call_target="tpu_custom_call" | custom-call | flops 1140850688 | bytes 4456448 | tf_op jit(solution)/shard_map/attend_own/pallas_call | solution.py:292
  57.9 3.3 %collective-permute-done.4.up_ref = bf16[576,384]{1,0:T(8,128)(2,1)S(1)} collective-permute-done((bf16[576,384]{1,0:T(8,128)(2,1)}, bf16[576,384]{1,0:T(8,128)(2,1)S(1)}, u32[]{:S(2)}, u32[]{:S(2)}) %collective-permute-start.4) | collective-permute-done | bytes 442400 | tf_op jit(solution)/shard_map/ppermute | solution.py:395
  61.3 0.0 collective-permute-done.5.down_ref
  61.3 0.8 %collective-permute-done.6.right_ref = bf16[576,384]{1,0:T(8,128)(2,1)S(1)} collective-permute-done((bf16[576,384]{1,0:T(8,128)(2,1)}, bf16[576,384]{1,0:T(8,128)(2,1)S(1)}, u32[]{:S(2)}, u32[]{:S(2)}) %collective-permute-start.6) | collective-permute-done | bytes 442400 | tf_op jit(solution)/shard_map/ppermute | solution.py:395
  62.1 0.0 collective-permute-done.7.left_ref
  62.1 7.4 %attend_rest.1 = bf16[1024,512]{1,0:T(8,128)(2,1)} custom-call(s32[8,128]{1,0:T(8,128)} %get-tuple-element.16.past_ref, bf16[1024,576]{1,0:T(8,128)(2,1)S(1)} %bitcast.5, f32[1024,128]{1,0:T(8,128)S(1)} %get-tuple-element.25.top_ref, f32[1024,128]{1,0:T(8,128)S(1)} %get-tuple-element.26.total_ref, f32[1024,512]{1,0:T(8,128)S(1)} %get-tuple-element.27.mixed_ref, ...), custom_call_target="tpu_custom_call" | custom-call | flops 3422552064 | bytes 5505024 | tf_op jit(solution)/shard_map/attend_rest/pallas_call | solution.py:356
Async XLA Ops:
  4.8 20.4 %copy-start = (bf16[8,128,576]{1,2,0:T(8,128)(2,1)S(1)}, bf16[8,128,576]{1,2,0:T(8,128)(2,1)}, u32[]{:S(2)}) copy-start(bf16[8,128,576]{1,2,0:T(8,128)(2,1)} %param.7) | copy-start | bytes 3538948
  4.8 9.7 %collective-permute-start = (bf16[576,256]{1,0:T(8,128)(2,1)S(1)}, bf16[576,256]{1,0:T(8,128)(2,1)S(1)}, u32[]{:S(2)}, u32[]{:S(2)}) collective-permute-start(bf16[576,256]{1,0:T(8,128)(2,1)S(1)} %get-tuple-element.19), channel_id=1, source_target_pairs={{0,32},{16,48},{32,64},{48,80},{64,96},{80,112},{96,0},{112,16},{1... | collective-permute-start | bytes 884744 | tf_op jit(solution)/shard_map/ppermute | solution.py:386
  6.9 15.2 %collective-permute-start.1 = (bf16[576,256]{1,0:T(8,128)(2,1)S(1)}, bf16[576,256]{1,0:T(8,128)(2,1)S(1)}, u32[]{:S(2)}, u32[]{:S(2)}) collective-permute-start(bf16[576,256]{1,0:T(8,128)(2,1)S(1)} %get-tuple-element.20), channel_id=1, source_target_pairs={{0,64},{16,80},{32,96},{48,112},{64,0},{80,16},{96,32},{112,48},{1... | collective-permute-start | bytes 884744 | tf_op jit(solution)/shard_map/ppermute | solution.py:386
  9.4 12.7 %collective-permute-start.2 = (bf16[576,256]{1,0:T(8,128)(2,1)S(1)}, bf16[576,256]{1,0:T(8,128)(2,1)S(1)}, u32[]{:S(2)}, u32[]{:S(2)}) collective-permute-start(bf16[576,256]{1,0:T(8,128)(2,1)S(1)} %get-tuple-element.21), channel_id=1, source_target_pairs={{0,96},{16,112},{32,0},{48,16},{64,32},{80,48},{96,64},{112,80},{1... | collective-permute-start | bytes 884744 | tf_op jit(solution)/shard_map/ppermute | solution.py:386
  23.6 12.5 %collective-permute-start.3 = (bf16[576,512]{1,0:T(8,128)(2,1)S(1)}, bf16[576,512]{1,0:T(8,128)(2,1)S(1)}, u32[]{:S(2)}, u32[]{:S(2)}) collective-permute-start(bf16[576,512]{1,0:T(8,128)(2,1)S(1)} %compact_parts.3), channel_id=1, source_target_pairs={{0,16},{16,0},{32,48},{48,32},{64,80},{80,64},{96,112},{112,96},{1... | collective-permute-start | bytes 1769480 | tf_op jit(solution)/shard_map/ppermute | solution.py:391
  26.7 27.9 %all-to-all-start = ((bf16[16,8,8,576]{3,2,1,0:T(8,128)(2,1)}), bf16[16,8,8,576]{3,2,1,0:T(8,128)(2,1)S(1)}, u32[]{:S(2)}, u32[]{:S(2)}) async-start(bf16[16,8,8,576]{3,2,1,0:T(8,128)(2,1)} %q_by_group.1), calls=%async_computation | async-start | bytes 2621440 | tf_op jit(solution)/shard_map/all_to_all | solution.py:388
  34.5 8.2 %copy-start.1 = (bf16[64,64,128]{2,1,0:T(8,128)(2,1)S(1)}, bf16[64,64,128]{2,1,0:T(8,128)(2,1)}, u32[]{:S(2)}) copy-start(bf16[64,64,128]{2,1,0:T(8,128)(2,1)} %query_ref.1) | copy-start | bytes 3145732
  34.5 8.2 %copy-start.2 = (bf16[2048,128]{1,0:T(8,128)(2,1)S(1)}, bf16[2048,128]{1,0:T(8,128)(2,1)}, u32[]{:S(2)}) copy-start(bf16[2048,128]{1,0:T(8,128)(2,1)} %keys_ref.1) | copy-start | bytes 1572868
  34.5 8.2 %copy-start.3 = (f32[64,64]{1,0:T(8,128)S(1)}, f32[64,64]{1,0:T(8,128)}, u32[]{:S(2)}) copy-start(f32[64,64]{1,0:T(8,128)} %weight_ref.1) | copy-start | bytes 49156
  37.3 23.9 %collective-permute-start.4 = (bf16[576,384]{1,0:T(8,128)(2,1)}, bf16[576,384]{1,0:T(8,128)(2,1)S(1)}, u32[]{:S(2)}, u32[]{:S(2)}) collective-permute-start(bf16[576,384]{1,0:T(8,128)(2,1)} %get-tuple-element.23.up_ref), channel_id=1, source_target_pairs={{0,4},{1,5},{2,6},{3,7},{4,8},{5,9},{6,10},{7,11},{8,12},{9,13},{1... | collective-permute-start | bytes 1327112 | tf_op jit(solution)/shard_map/ppermute | solution.py:395
  38.7 22.6 %collective-permute-start.5 = (bf16[576,384]{1,0:T(8,128)(2,1)}, bf16[576,384]{1,0:T(8,128)(2,1)S(1)}, u32[]{:S(2)}, u32[]{:S(2)}) collective-permute-start(bf16[576,384]{1,0:T(8,128)(2,1)} %get-tuple-element.24.down_ref), channel_id=1, source_target_pairs={{0,12},{1,13},{2,14},{3,15},{4,0},{5,1},{6,2},{7,3},{8,4},{9,5},{1... | collective-permute-start | bytes 1327112 | tf_op jit(solution)/shard_map/ppermute | solution.py:395
  40.0 22.0 %collective-permute-start.6 = (bf16[576,384]{1,0:T(8,128)(2,1)}, bf16[576,384]{1,0:T(8,128)(2,1)S(1)}, u32[]{:S(2)}, u32[]{:S(2)}) collective-permute-start(bf16[576,384]{1,0:T(8,128)(2,1)} %get-tuple-element.28), channel_id=1, source_target_pairs={{0,1},{1,2},{2,3},{3,0},{4,5},{5,6},{6,7},{7,4},{8,9},{9,10},{10,1... | collective-permute-start | bytes 1327112 | tf_op jit(solution)/shard_map/ppermute | solution.py:395
  41.4 20.7 %collective-permute-start.7 = (bf16[576,384]{1,0:T(8,128)(2,1)S(1)}, bf16[576,384]{1,0:T(8,128)(2,1)S(1)}, u32[]{:S(2)}, u32[]{:S(2)}) collective-permute-start(bf16[576,384]{1,0:T(8,128)(2,1)S(1)} %get-tuple-element.29), channel_id=1, source_target_pairs={{0,3},{1,0},{2,1},{3,2},{4,7},{5,4},{6,5},{7,6},{8,11},{9,8},{10,9... | collective-permute-start | bytes 1327112 | tf_op jit(solution)/shard_map/ppermute | solution.py:395

commit v8 on v7

--- a/solution.py
+++ b/solution.py
@@ -25,10 +25,6 @@
 
 def in_hbm(x):
     return pltpu.with_memory_space_constraint(x, pltpu.HBM)
-
-
-def in_vmem(x):
-    return pltpu.with_memory_space_constraint(x, pltpu.VMEM)
 
 
 def valid_ids(ids_ref, counts_ref):
@@ -81,11 +77,19 @@
         copies.append(pltpu.make_async_copy(cache_ref.at[:, pl.ds(c, 512)], held.at[i], sems.at[i]))
         copies[i].start()
     shard, first, second = place()
-    for copy in lists:
+    tiles, entries = ids_ref.shape
+    blocks = keys // BLOCK
+    column = iota((512, 128), 1)
+    keep = hot(iota((512, 128), 0), (column >> 4) * BLOCK + row_of(column & 15, first, second))
+
+    def kept(i):
+        return jnp.dot(held[i], keep, preferred_element_type=F32).astype(BF16)
+
+    early = len(copies) // 2
+    for copy in lists + copies[:early]:
         copy.wait()
+    own = [kept(i) for i in range(early)]
     ids = valid_ids(ids_ref, counts_ref)
-    tiles, entries = ids.shape
-    blocks = keys // BLOCK
     lane = iota((tiles, 128), 1)
     block_of_lane = jnp.where(lane < blocks, lane + shard * blocks, -2)
     member = jnp.zeros((tiles, 128), F32)
@@ -98,13 +102,9 @@
     target = jnp.full((tiles, 128), -1, jnp.int32)
     for b in range(blocks):
         target = jnp.where(rank[:, b : b + 1] == slot, b * PART + (lane & 15), target)
-    column = iota((512, 128), 1)
-    keep = hot(iota((512, 128), 0), (column >> 4) * BLOCK + row_of(column & 15, first, second))
-    own = []
-    for i, copy in enumerate(copies):
+    for copy in copies[early:]:
         copy.wait()
-        own.append(jnp.dot(held[i], keep, preferred_element_type=F32).astype(BF16))
-    own = jnp.concatenate(own, axis=1)
+    own = jnp.concatenate(own + [kept(i) for i in range(early, len(copies))], axis=1)
     index = iota((own.shape[1], 128), 0)
     for d, out_ref in enumerate(out_refs):
         near = (shard + 2 * d) & 7
@@ -198,16 +198,23 @@
 
 
 def q_prep_kernel(q_ref, out_ref):
-    groups, rows, heads, width = out_ref.shape
+    rows = q_ref.shape[0]
     for i in range(rows):
-        out_ref[:, i] = q_ref[i].T.reshape(groups, heads, width)
+        query = q_ref[i].T
+        for g in range(out_ref.shape[0]):
+            part = query[g * 8 : (g + 1) * 8, :]
+            for t in range(4):
+                out_ref[g, t * 64 + i * 8 : t * 64 + (i + 1) * 8, :] = part[:, t * 128 : (t + 1) * 128]
+            low = 256 + (i % 4) * 8
+            left = (i // 4) * 64
+            out_ref[g, low : low + 8, left : left + 64] = part[:, 512:]
 
 
 def q_by_group(q_latent, groups):
     rows, heads, width = q_latent.shape
     return pl.pallas_call(
         q_prep_kernel,
-        out_shape=jax.ShapeDtypeStruct((groups, rows, heads // groups, width), BF16),
+        out_shape=jax.ShapeDtypeStruct((groups, rows * heads * width // (groups * 128), 128), BF16),
         in_specs=[VMEM],
         out_specs=VMEM,
         cost_estimate=pl.CostEstimate(flops=0, bytes_accessed=rows * heads * width * 4, transcendentals=0),
@@ -266,11 +273,17 @@
     return jnp.concatenate(pieces, axis=1)
 
 
-def own_kernel(past_ref, q_ref, up_ref, down_ref, top_ref, total_ref, mixed_ref, keys_ref):
+def own_kernel(past_ref, packed_ref, up_ref, down_ref, top_ref, total_ref, mixed_ref, q_ref, keys_ref):
     _, first, second = place()
     past = past_ref[0:1, :]
     late = 16 * BLOCK
     tiles = (None, late + first * 8, None, late + 32 + second * 8)
+    for g in range(packed_ref.shape[0]):
+        low = g * 64
+        for t in range(4):
+            q_ref[low : low + 64, t * 128 : (t + 1) * 128] = packed_ref[g, t * 64 : (t + 1) * 64, :]
+        q_ref[low : low + 32, 512:] = packed_ref[g, 256:, :64]
+        q_ref[low + 32 : low + 64, 512:] = packed_ref[g, 256:, 64:]
     keys_ref[:, :384] = up_ref[...]
     keys_ref[:, 384:] = down_ref[:, 256:]
     rows, step = q_ref.shape[0], 256
@@ -279,15 +292,17 @@
         scores = masked_scores(q_ref[a : a + step, :], keys_ref[...], tiles, limit)
         top = jnp.max(scores, axis=1, keepdims=True)
         weights = jnp.exp((scores - top) * SCALE)
-        top_ref[a : a + step, :] = jnp.broadcast_to(top, (step, 128))
+        lane = iota((step, 128), 1)
+        top_ref[a : a + step, :] = jnp.where(lane < 64, top, past.astype(F32))
         total_ref[a : a + step, :] = jnp.broadcast_to(jnp.sum(weights, axis=1, keepdims=True), (step, 128))
         mixed_ref[a : a + step, :] = lax.dot_general(
             weights.astype(BF16), keys_ref[0:512, :], (((1,), (1,)), ((), ())), preferred_element_type=F32
         )
 
 
-def attend_own(past, q, up, down):
-    rows, width = q.shape
+def attend_own(past, packed, up, down):
+    width = up.shape[0]
+    rows = packed.size // width
     count = 512
     return pl.pallas_call(
         own_kernel,
@@ -295,21 +310,22 @@
             jax.ShapeDtypeStruct((rows, 128), F32),
             jax.ShapeDtypeStruct((rows, 128), F32),
             jax.ShapeDtypeStruct((rows, 512), F32),
+            jax.ShapeDtypeStruct((rows, width), BF16),
         ],
         in_specs=[VMEM] * 4,
-        out_specs=[VMEM] * 3,
+        out_specs=[VMEM] * 4,
         scratch_shapes=[pltpu.VMEM((width, count), BF16)],
         cost_estimate=pl.CostEstimate(
             flops=2 * rows * count * (width + 512), bytes_accessed=rows * 4352, transcendentals=rows * count
         ),
         compiler_params=pltpu.CompilerParams(vmem_limit_bytes=16 << 20),
         name="attend_own",
-    )(in_hbm(past), q, in_vmem(up), in_vmem(down))
-
-
-def rest_kernel(past_ref, q_ref, top_ref, total_ref, mixed_ref, up_ref, down_ref, right_ref, left_ref, out_ref, keys_ref, done_ref, sems):
+    )(in_hbm(past), packed, up, down)
+
+
+def rest_kernel(top_ref, total_ref, mixed_ref, q_ref, up_ref, down_ref, right_ref, left_ref, out_ref, keys_ref, done_ref, sems):
     _, first, second = place()
-    past = past_ref[0:1, :]
+    past = top_ref[0:1, 64:65].astype(jnp.int32)
     late = 16 * BLOCK
 
     def of_first(step):
@@ -350,13 +366,13 @@
         copy.wait()
 
 
-def attend_rest(past, q, state, parts):
-    rows, width = q.shape
+def attend_rest(state, parts):
+    rows, width = state[-1].shape
     count = sum(part.shape[1] for part in parts)
     return pl.pallas_call(
         rest_kernel,
         out_shape=jax.ShapeDtypeStruct((rows, 512), BF16),
-        in_specs=[VMEM] * (5 + len(parts)),
+        in_specs=[VMEM] * (4 + len(parts)),
         out_specs=pl.BlockSpec(memory_space=pltpu.HBM),
         scratch_shapes=[
             pltpu.VMEM((width, count), BF16),
@@ -368,7 +384,7 @@
         ),
         compiler_params=pltpu.CompilerParams(vmem_limit_bytes=24 << 20),
         name="attend_rest",
-    )(in_hbm(past), q, *state, *[in_vmem(part) for part in parts])
+    )(*state, *parts)
 
 
 def turn(d):
@@ -380,7 +396,7 @@
 
 
 def body(q_latent, index_query, index_weight, index_keys, latent_cache, block_ids, block_counts):
-    rows, heads, width = q_latent.shape
+    rows, heads, _ = q_latent.shape
     groups = lax.axis_size("head")
     *outgoing, source, other, past = gather_parts(block_ids, block_counts, latent_cache.T)
     incoming = [outgoing[0]] + [lax.ppermute(outgoing[d], "ctx", turn(2 * d)) for d in range(1, SHARDS // 2)]
@@ -395,9 +411,8 @@
         lax.ppermute(part, "head", line(*step))
         for part, step in ((up, (1, 0)), (down, (-1, 0)), (right, (0, 1)), (left, (0, -1)))
     ]
-    flat_query = head_query.reshape(-1, width)
-    state = attend_own(past, flat_query, up, down)
-    attention = attend_rest(past, flat_query, state, parts)
+    state = attend_own(past, head_query, up, down)
+    attention = attend_rest(state, parts)
     return attention.reshape(rows * groups, heads // groups, 512), index_scores
 
 

time: 69.9 us -> 68.5 us (0.980)
  waiting for transfers between devices: 21 us -> 19.9 us
    all_to_all x1, waiting for transfers between devices: 5.29 us -> 3.58 us  [body(): lax.all_to_all(by_group, 'head', split_axis=0, concat_axis=0, tiled=True)]
  transfers between devices with their start and end apart: 9 -> 9, of which waited for: 5 -> 5; matrix products, arithmetic and copies ran while one was open for 0% -> 0% of each run, Pallas kernels for 20% -> 21%
where the time goes in v8:
time: 68.5 us; the launch traced here: 68.1 us
  Pallas kernels  26.9 us (39%)
  starting transfers between devices  20.4 us (30%)
  waiting for transfers between devices  19.9 us (29%)
  between operations  0.88 us (1%)
    ppermute x3, waiting for transfers between devices, body(): lax.ppermute(outgoing[d], 'ctx', turn(2 * d))  11.6 us
    all_to_all x1, starting transfers between devices, body(): lax.all_to_all(by_group, 'head', split_axis=0, concat_axis=0, tiled=True)  7.77 us
    pallas_call x1, Pallas kernels, attend_rest(): pl.pallas_call(rest_kernel, out_shape=jax.ShapeDtypeStruct((rows, 512), B...  7.75 us
    pallas_call x1, Pallas kernels, index_scores_of(): pl.pallas_call(index_kernel, grid=(rows // step,), out_shape=jax.ShapeDty...  6.5 us
    ppermute x3, starting transfers between devices, body(): lax.ppermute(outgoing[d], 'ctx', turn(2 * d))  5.7 us
    ppermute x4, starting transfers between devices, body(): lax.ppermute(part, 'head', line(*step))  5.35 us
    ppermute x4, waiting for transfers between devices, body(): lax.ppermute(part, 'head', line(*step))  4.74 us
    all_to_all x1, waiting for transfers between devices, body(): lax.all_to_all(by_group, 'head', split_axis=0, concat_axis=0, tiled=True)  3.58 us
  transfers between devices with their start and end apart: 9, of which 5 were waited for; matrix products, arithmetic and copies ran while one was open for 0% of the time, Pallas kernels for 21%

profile of v8, /device:TPU:1, one launch (start us, length us, event | category | flops | bytes accessed | tf_op | source)
XLA Modules:
  0.0 68.1 jit_solution(4083152237252363896)
XLA Ops:
  0.6 3.6 %gather_parts.1 = (bf16[576,256]{1,0:T(8,128)(2,1)}, bf16[576,256]{1,0:T(8,128)(2,1)S(1)}, bf16[576,256]{1,0:T(8,128)(2,1)S(1)}, bf16[576,256]{1,0:T(8,128)(2,1)...) custom-call(s32[8,32]{1,0:T(8,128)} %ids_hbm.1, s32[8]{0:T(128)} %counts_hbm.1, bf16[576,2048]{1,0:T(8,128)(2,1)} %bitcast.4), custom_call_target="tpu_custom_call" | custom-call | flops 2415919104 | bytes 4718592 | tf_op jit(solution)/shard_map/gather_parts/pallas_call | solution.py:127
  4.2 0.0 copy-start
  4.2 2.1 %collective-permute-start = (bf16[576,256]{1,0:T(8,128)(2,1)S(1)}, bf16[576,256]{1,0:T(8,128)(2,1)S(1)}, u32[]{:S(2)}, u32[]{:S(2)}) collective-permute-start(bf16[576,256]{1,0:T(8,128)(2,1)S(1)} %get-tuple-element.20), channel_id=1, source_target_pairs={{0,32},{16,48},{32,64},{48,80},{64,96},{80,112},{96,0},{112,16},{1... | collective-permute-start | bytes 884744 | tf_op jit(solution)/shard_map/ppermute | solution.py:402
  6.3 2.5 %collective-permute-start.1 = (bf16[576,256]{1,0:T(8,128)(2,1)S(1)}, bf16[576,256]{1,0:T(8,128)(2,1)S(1)}, u32[]{:S(2)}, u32[]{:S(2)}) collective-permute-start(bf16[576,256]{1,0:T(8,128)(2,1)S(1)} %get-tuple-element.21), channel_id=1, source_target_pairs={{0,64},{16,80},{32,96},{48,112},{64,0},{80,16},{96,32},{112,48},{1... | collective-permute-start | bytes 884744 | tf_op jit(solution)/shard_map/ppermute | solution.py:402
  8.8 1.2 %collective-permute-start.2 = (bf16[576,256]{1,0:T(8,128)(2,1)S(1)}, bf16[576,256]{1,0:T(8,128)(2,1)S(1)}, u32[]{:S(2)}, u32[]{:S(2)}) collective-permute-start(bf16[576,256]{1,0:T(8,128)(2,1)S(1)} %get-tuple-element.22), channel_id=1, source_target_pairs={{0,96},{16,112},{32,0},{48,16},{64,32},{80,48},{96,64},{112,80},{1... | collective-permute-start | bytes 884744 | tf_op jit(solution)/shard_map/ppermute | solution.py:402
  9.9 4.0 %collective-permute-done.refs_1_ = bf16[576,256]{1,0:T(8,128)(2,1)S(1)} collective-permute-done((bf16[576,256]{1,0:T(8,128)(2,1)S(1)}, bf16[576,256]{1,0:T(8,128)(2,1)S(1)}, u32[]{:S(2)}, u32[]{:S(2)}) %collective-permute-start) | collective-permute-done | bytes 294944 | tf_op jit(solution)/shard_map/ppermute | solution.py:402
  13.9 7.6 %collective-permute-done.1.refs_2_ = bf16[576,256]{1,0:T(8,128)(2,1)S(1)} collective-permute-done((bf16[576,256]{1,0:T(8,128)(2,1)S(1)}, bf16[576,256]{1,0:T(8,128)(2,1)S(1)}, u32[]{:S(2)}, u32[]{:S(2)}) %collective-permute-start.1) | collective-permute-done | bytes 294944 | tf_op jit(solution)/shard_map/ppermute | solution.py:402
  21.5 0.0 collective-permute-done.2.refs_3_
  21.5 1.5 %compact_parts.3 = bf16[576,512]{1,0:T(8,128)(2,1)S(1)} custom-call(s32[8,512]{1,0:T(8,128)} %get-tuple-element.23.source_ref, bf16[576,256]{1,0:T(8,128)(2,1)} %get-tuple-element.19.refs_0_, bf16[576,256]{1,0:T(8,128)(2,1)S(1)} %collective-permute-done.refs_1_, bf16[576,256]{1,0:T(8,128)(2,1)S(1)} %collective-permute-done.1.refs_2_, ...), custom_call_target="tpu_custom_call" | custom-call | flops 301989888 | bytes 1769472 | tf_op jit(solution)/shard_map/compact_parts/pallas_call | solution.py:163
  23.0 1.6 %collective-permute-start.3 = (bf16[576,512]{1,0:T(8,128)(2,1)S(1)}, bf16[576,512]{1,0:T(8,128)(2,1)S(1)}, u32[]{:S(2)}, u32[]{:S(2)}) collective-permute-start(bf16[576,512]{1,0:T(8,128)(2,1)S(1)} %compact_parts.3), channel_id=1, source_target_pairs={{0,16},{16,0},{32,48},{48,32},{64,80},{80,64},{96,112},{112,96},{1... | collective-permute-start | bytes 1769480 | tf_op jit(solution)/shard_map/ppermute | solution.py:407
  24.6 0.0 copy-done
  24.6 1.6 %q_by_group.1 = bf16[16,288,128]{2,1,0:T(8,128)(2,1)} custom-call(bf16[8,576,128]{2,1,0:T(8,128)(2,1)S(1)} %bitcast.3), custom_call_target="tpu_custom_call" | custom-call | bytes 2359296 | tf_op jit(solution)/shard_map/q_by_group/pallas_call | solution.py:215
  26.1 7.8 %all-to-all-start = ((bf16[16,288,128]{2,1,0:T(8,128)(2,1)}), bf16[16,288,128]{2,1,0:T(8,128)(2,1)S(1)}, u32[]{:S(2)}, u32[]{:S(2)}) async-start(bf16[16,288,128]{2,1,0:T(8,128)(2,1)} %q_by_group.1), calls=%async_computation | async-start | bytes 2359296 | tf_op jit(solution)/shard_map/all_to_all | solution.py:404
  33.9 0.0 copy-start.1
  33.9 0.0 copy-start.2
  33.9 0.0 copy-start.3
  33.9 1.6 %compact_parts.2.own_ref = bf16[576,512]{1,0:T(8,128)(2,1)S(1)} custom-call(s32[8,512]{1,0:T(8,128)} %get-tuple-element.18.source_ref, bf16[576,256]{1,0:T(8,128)(2,1)} %get-tuple-element.19.refs_0_, bf16[576,256]{1,0:T(8,128)(2,1)S(1)} %collective-permute-done.refs_1_, bf16[576,256]{1,0:T(8,128)(2,1)S(1)} %collective-permute-done.1.refs_2_, ...), custom_call_target="tpu_custom_call" | custom-call | flops 301989888 | bytes 1769472 | tf_op jit(solution)/shard_map/compact_parts/pallas_call | solution.py:163
  35.5 0.0 collective-permute-done.3.other_ref
  35.5 1.1 %spread_parts.1 = (bf16[576,384]{1,0:T(8,128)(2,1)}, bf16[576,384]{1,0:T(8,128)(2,1)}, bf16[576,384]{1,0:T(8,128)(2,1)S(1)}, bf16[576,384]{1,0:T(8,128)(2,1)S(1)}) custom-call(bf16[576,512]{1,0:T(8,128)(2,1)S(1)} %compact_parts.2.own_ref, bf16[576,512]{1,0:T(8,128)(2,1)S(1)} %collective-permute-done.3.other_ref), custom_call_target="tpu_custom_call" | custom-call | flops 294912 | bytes 2949120 | tf_op jit(solution)/shard_map/spread_parts/pallas_call | solution.py:189
  36.6 1.4 %collective-permute-start.4 = (bf16[576,384]{1,0:T(8,128)(2,1)}, bf16[576,384]{1,0:T(8,128)(2,1)S(1)}, u32[]{:S(2)}, u32[]{:S(2)}) collective-permute-start(bf16[576,384]{1,0:T(8,128)(2,1)} %get-tuple-element.24.up_ref), channel_id=1, source_target_pairs={{0,4},{1,5},{2,6},{3,7},{4,8},{5,9},{6,10},{7,11},{8,12},{9,13},{1... | collective-permute-start | bytes 1327112 | tf_op jit(solution)/shard_map/ppermute | solution.py:411
  38.0 1.3 %collective-permute-start.5 = (bf16[576,384]{1,0:T(8,128)(2,1)}, bf16[576,384]{1,0:T(8,128)(2,1)S(1)}, u32[]{:S(2)}, u32[]{:S(2)}) collective-permute-start(bf16[576,384]{1,0:T(8,128)(2,1)} %get-tuple-element.25.down_ref), channel_id=1, source_target_pairs={{0,12},{1,13},{2,14},{3,15},{4,0},{5,1},{6,2},{7,3},{8,4},{9,5},{1... | collective-permute-start | bytes 1327112 | tf_op jit(solution)/shard_map/ppermute | solution.py:411
  39.3 1.4 %collective-permute-start.6 = (bf16[576,384]{1,0:T(8,128)(2,1)S(1)}, bf16[576,384]{1,0:T(8,128)(2,1)S(1)}, u32[]{:S(2)}, u32[]{:S(2)}) collective-permute-start(bf16[576,384]{1,0:T(8,128)(2,1)S(1)} %get-tuple-element.30), channel_id=1, source_target_pairs={{0,1},{1,2},{2,3},{3,0},{4,5},{5,6},{6,7},{7,4},{8,9},{9,10},{10,1... | collective-permute-start | bytes 1327112 | tf_op jit(solution)/shard_map/ppermute | solution.py:411
  40.7 1.3 %collective-permute-start.7 = (bf16[576,384]{1,0:T(8,128)(2,1)S(1)}, bf16[576,384]{1,0:T(8,128)(2,1)}, u32[]{:S(2)}, u32[]{:S(2)}) collective-permute-start(bf16[576,384]{1,0:T(8,128)(2,1)S(1)} %get-tuple-element.31), channel_id=1, source_target_pairs={{0,3},{1,0},{2,1},{3,2},{4,7},{5,4},{6,5},{7,6},{8,11},{9,8},{10,9... | collective-permute-start | bytes 1327112 | tf_op jit(solution)/shard_map/ppermute | solution.py:411
  42.0 0.0 copy-done.1
  42.0 0.0 copy-done.2
  42.0 0.0 copy-done.3
  42.0 6.5 %index_scores.1 = f32[64,2048]{1,0:T(8,128)} custom-call(bf16[64,64,128]{2,1,0:T(8,128)(2,1)S(1)} %copy-done.1, f32[64,64]{1,0:T(8,128)S(1)} %copy-done.3, bf16[2048,128]{1,0:T(8,128)(2,1)S(1)} %copy-done.2), custom_call_target="tpu_custom_call" | custom-call | flops 8589934592 | bytes 1572864 | tf_op jit(solution)/shard_map/index_scores/pallas_call | solution.py:244
  48.5 3.6 %all-to-all-done.packed_ref = bf16[16,288,128]{2,1,0:T(8,128)(2,1)S(1)} async-done(((bf16[16,288,128]{2,1,0:T(8,128)(2,1)}), bf16[16,288,128]{2,1,0:T(8,128)(2,1)S(1)}, u32[]{:S(2)}, u32[]{:S(2)}) %all-to-all-start) | async-done | bytes 1179680 | tf_op jit(solution)/shard_map/all_to_all | solution.py:404
  52.1 3.4 %attend_own.1 = (f32[1024,128]{1,0:T(8,128)S(1)}, f32[1024,128]{1,0:T(8,128)S(1)}, f32[1024,512]{1,0:T(8,128)S(1)}, bf16[1024,576]{1,0:T(8,128)(2,1)S(1)}) custom-call(s32[8,128]{1,0:T(8,128)} %get-tuple-element.17.past_ref, bf16[16,288,128]{2,1,0:T(8,128)(2,1)S(1)} %all-to-all-done.packed_ref, bf16[576,384]{1,0:T(8,128)(2,1)} %get-tuple-element.24.up_ref, ...), custom_call_target="tpu_custom_call" | custom-call | flops 1140850688 | bytes 4456448 | tf_op jit(solution)/shard_map/attend_own/pallas_call | solution.py:307
  55.5 3.8 %collective-permute-done.4.up_ref = bf16[576,384]{1,0:T(8,128)(2,1)S(1)} collective-permute-done((bf16[576,384]{1,0:T(8,128)(2,1)}, bf16[576,384]{1,0:T(8,128)(2,1)S(1)}, u32[]{:S(2)}, u32[]{:S(2)}) %collective-permute-start.4) | collective-permute-done | bytes 442400 | tf_op jit(solution)/shard_map/ppermute | solution.py:411
  59.3 0.0 collective-permute-done.5.down_ref
  59.3 0.9 %collective-permute-done.6.right_ref = bf16[576,384]{1,0:T(8,128)(2,1)S(1)} collective-permute-done((bf16[576,384]{1,0:T(8,128)(2,1)S(1)}, bf16[576,384]{1,0:T(8,128)(2,1)S(1)}, u32[]{:S(2)}, u32[]{:S(2)}) %collective-permute-start.6) | collective-permute-done | bytes 442400 | tf_op jit(solution)/shard_map/ppermute | solution.py:411
  60.2 0.0 collective-permute-done.7.left_ref
  60.2 7.8 %attend_rest.1 = bf16[1024,512]{1,0:T(8,128)(2,1)} custom-call(f32[1024,128]{1,0:T(8,128)S(1)} %get-tuple-element.26.top_ref, f32[1024,128]{1,0:T(8,128)S(1)} %get-tuple-element.27.total_ref, f32[1024,512]{1,0:T(8,128)S(1)} %get-tuple-element.28.mixed_ref, bf16[1024,576]{1,0:T(8,128)(2,1)S(1)} %get-tuple-element.29.q_ref, ...), custom_call_target="tpu_custom_call" | custom-call | flops 3422552064 | bytes 5505024 | tf_op jit(solution)/shard_map/attend_rest/pallas_call | solution.py:372
Async XLA Ops:
  4.2 20.4 %copy-start = (bf16[8,128,576]{1,2,0:T(8,128)(2,1)S(1)}, bf16[8,128,576]{1,2,0:T(8,128)(2,1)}, u32[]{:S(2)}) copy-start(bf16[8,128,576]{1,2,0:T(8,128)(2,1)} %param.7) | copy-start | bytes 3538948
  4.2 9.7 %collective-permute-start = (bf16[576,256]{1,0:T(8,128)(2,1)S(1)}, bf16[576,256]{1,0:T(8,128)(2,1)S(1)}, u32[]{:S(2)}, u32[]{:S(2)}) collective-permute-start(bf16[576,256]{1,0:T(8,128)(2,1)S(1)} %get-tuple-element.20), channel_id=1, source_target_pairs={{0,32},{16,48},{32,64},{48,80},{64,96},{80,112},{96,0},{112,16},{1... | collective-permute-start | bytes 884744 | tf_op jit(solution)/shard_map/ppermute | solution.py:402
  6.3 15.2 %collective-permute-start.1 = (bf16[576,256]{1,0:T(8,128)(2,1)S(1)}, bf16[576,256]{1,0:T(8,128)(2,1)S(1)}, u32[]{:S(2)}, u32[]{:S(2)}) collective-permute-start(bf16[576,256]{1,0:T(8,128)(2,1)S(1)} %get-tuple-element.21), channel_id=1, source_target_pairs={{0,64},{16,80},{32,96},{48,112},{64,0},{80,16},{96,32},{112,48},{1... | collective-permute-start | bytes 884744 | tf_op jit(solution)/shard_map/ppermute | solution.py:402
  8.8 12.7 %collective-permute-start.2 = (bf16[576,256]{1,0:T(8,128)(2,1)S(1)}, bf16[576,256]{1,0:T(8,128)(2,1)S(1)}, u32[]{:S(2)}, u32[]{:S(2)}) collective-permute-start(bf16[576,256]{1,0:T(8,128)(2,1)S(1)} %get-tuple-element.22), channel_id=1, source_target_pairs={{0,96},{16,112},{32,0},{48,16},{64,32},{80,48},{96,64},{112,80},{1... | collective-permute-start | bytes 884744 | tf_op jit(solution)/shard_map/ppermute | solution.py:402
  23.0 12.6 %collective-permute-start.3 = (bf16[576,512]{1,0:T(8,128)(2,1)S(1)}, bf16[576,512]{1,0:T(8,128)(2,1)S(1)}, u32[]{:S(2)}, u32[]{:S(2)}) collective-permute-start(bf16[576,512]{1,0:T(8,128)(2,1)S(1)} %compact_parts.3), channel_id=1, source_target_pairs={{0,16},{16,0},{32,48},{48,32},{64,80},{80,64},{96,112},{112,96},{1... | collective-permute-start | bytes 1769480 | tf_op jit(solution)/shard_map/ppermute | solution.py:407
  26.1 25.9 %all-to-all-start = ((bf16[16,288,128]{2,1,0:T(8,128)(2,1)}), bf16[16,288,128]{2,1,0:T(8,128)(2,1)S(1)}, u32[]{:S(2)}, u32[]{:S(2)}) async-start(bf16[16,288,128]{2,1,0:T(8,128)(2,1)} %q_by_group.1), calls=%async_computation | async-start | bytes 2359296 | tf_op jit(solution)/shard_map/all_to_all | solution.py:404
  33.9 8.1 %copy-start.1 = (bf16[64,64,128]{2,1,0:T(8,128)(2,1)S(1)}, bf16[64,64,128]{2,1,0:T(8,128)(2,1)}, u32[]{:S(2)}) copy-start(bf16[64,64,128]{2,1,0:T(8,128)(2,1)} %query_ref.1) | copy-start | bytes 3145732
  33.9 8.1 %copy-start.2 = (bf16[2048,128]{1,0:T(8,128)(2,1)S(1)}, bf16[2048,128]{1,0:T(8,128)(2,1)}, u32[]{:S(2)}) copy-start(bf16[2048,128]{1,0:T(8,128)(2,1)} %keys_ref.1) | copy-start | bytes 1572868
  33.9 8.0 %copy-start.3 = (f32[64,64]{1,0:T(8,128)S(1)}, f32[64,64]{1,0:T(8,128)}, u32[]{:S(2)}) copy-start(f32[64,64]{1,0:T(8,128)} %weight_ref.1) | copy-start | bytes 49156
  36.6 22.7 %collective-permute-start.4 = (bf16[576,384]{1,0:T(8,128)(2,1)}, bf16[576,384]{1,0:T(8,128)(2,1)S(1)}, u32[]{:S(2)}, u32[]{:S(2)}) collective-permute-start(bf16[576,384]{1,0:T(8,128)(2,1)} %get-tuple-element.24.up_ref), channel_id=1, source_target_pairs={{0,4},{1,5},{2,6},{3,7},{4,8},{5,9},{6,10},{7,11},{8,12},{9,13},{1... | collective-permute-start | bytes 1327112 | tf_op jit(solution)/shard_map/ppermute | solution.py:411
  38.0 21.3 %collective-permute-start.5 = (bf16[576,384]{1,0:T(8,128)(2,1)}, bf16[576,384]{1,0:T(8,128)(2,1)S(1)}, u32[]{:S(2)}, u32[]{:S(2)}) collective-permute-start(bf16[576,384]{1,0:T(8,128)(2,1)} %get-tuple-element.25.down_ref), channel_id=1, source_target_pairs={{0,12},{1,13},{2,14},{3,15},{4,0},{5,1},{6,2},{7,3},{8,4},{9,5},{1... | collective-permute-start | bytes 1327112 | tf_op jit(solution)/shard_map/ppermute | solution.py:411
  39.3 20.9 %collective-permute-start.6 = (bf16[576,384]{1,0:T(8,128)(2,1)S(1)}, bf16[576,384]{1,0:T(8,128)(2,1)S(1)}, u32[]{:S(2)}, u32[]{:S(2)}) collective-permute-start(bf16[576,384]{1,0:T(8,128)(2,1)S(1)} %get-tuple-element.30), channel_id=1, source_target_pairs={{0,1},{1,2},{2,3},{3,0},{4,5},{5,6},{6,7},{7,4},{8,9},{9,10},{10,1... | collective-permute-start | bytes 1327112 | tf_op jit(solution)/shard_map/ppermute | solution.py:411
  40.7 19.6 %collective-permute-start.7 = (bf16[576,384]{1,0:T(8,128)(2,1)S(1)}, bf16[576,384]{1,0:T(8,128)(2,1)}, u32[]{:S(2)}, u32[]{:S(2)}) collective-permute-start(bf16[576,384]{1,0:T(8,128)(2,1)S(1)} %get-tuple-element.31), channel_id=1, source_target_pairs={{0,3},{1,0},{2,1},{3,2},{4,7},{5,4},{6,5},{7,6},{8,11},{9,8},{10,9... | collective-permute-start | bytes 1327112 | tf_op jit(solution)/shard_map/ppermute | solution.py:411

commit v9 on v8

--- a/solution.py
+++ b/solution.py
@@ -107,7 +107,7 @@
     own = jnp.concatenate(own + [kept(i) for i in range(early, len(copies))], axis=1)
     index = iota((own.shape[1], 128), 0)
     for d, out_ref in enumerate(out_refs):
-        near = (shard + 2 * d) & 7
+        near = shard ^ (2 * d)
         pair = []
         for tile in (near, near ^ 1):
             chosen = iota((tiles, 128), 0) == tile
@@ -152,7 +152,7 @@
     source = source_ref[0:1, :]
     total = jnp.zeros(out_ref.shape, F32)
     for d in range(0, len(part_refs), 2):
-        pick = jnp.concatenate([hot(row + ((shard - 2 * u) & 7) * 128, source) for u in (d, d + 1)], axis=0)
+        pick = jnp.concatenate([hot(row + (shard ^ (2 * u)) * 128, source) for u in (d, d + 1)], axis=0)
         pair = jnp.concatenate([part_refs[u][:, left : left + 128] for u in (d, d + 1)], axis=1)
         total = total + jnp.dot(pair, pick, preferred_element_type=F32)
     out_ref[...] = total.astype(BF16)
@@ -171,17 +171,23 @@
     )(in_hbm(source), in_hbm(parts[0]), *parts[1:])
 
 
-def spread_kernel(own_ref, other_ref, up_ref, down_ref, right_ref, left_ref):
+def spread_kernel(own_ref, other_ref, y1_ref, y3_ref, z1_ref, z3_ref):
+    group = lax.axis_index("head")
+    odd_y, odd_z = (group >> 2) & 1, group & 1
     first = own_ref[:, :256] + other_ref[:, :256]
     second = own_ref[:, 256:] + other_ref[:, 256:]
-    up_ref[:, :256] = first
-    up_ref[:, 256:] = second[:, :128]
-    down_ref[:, :256] = first
-    down_ref[:, 256:] = second[:, 128:]
-    right_ref[:, :256] = second
-    right_ref[:, 256:] = first[:, :128]
-    left_ref[:, :256] = second
-    left_ref[:, 256:] = first[:, 128:]
+
+    def pick(whole, late):
+        return jnp.where(late == 1, whole[:, 128:], whole[:, :128])
+
+    y1_ref[:, :256] = first
+    y1_ref[:, 256:] = pick(second, odd_y)
+    y3_ref[:, :256] = first
+    y3_ref[:, 256:] = pick(second, 1 - odd_y)
+    z1_ref[:, :256] = second
+    z1_ref[:, 256:] = pick(first, odd_z)
+    z3_ref[:, :256] = second
+    z3_ref[:, 256:] = pick(first, 1 - odd_z)
 
 
 def spread_parts(own, other):
@@ -273,19 +279,21 @@
     return jnp.concatenate(pieces, axis=1)
 
 
-def own_kernel(past_ref, packed_ref, up_ref, down_ref, top_ref, total_ref, mixed_ref, q_ref, keys_ref):
+def own_kernel(past_ref, packed_ref, y1_ref, y3_ref, top_ref, total_ref, mixed_ref, q_ref, keys_ref):
     _, first, second = place()
     past = past_ref[0:1, :]
     late = 16 * BLOCK
-    tiles = (None, late + first * 8, None, late + 32 + second * 8)
+    odd_y = (lax.axis_index("head") >> 2) & 1
+    low = 32 + second * 8
+    tiles = (None, late + first * 8, odd_y * late + low, (1 - odd_y) * late + low)
     for g in range(packed_ref.shape[0]):
         low = g * 64
         for t in range(4):
             q_ref[low : low + 64, t * 128 : (t + 1) * 128] = packed_ref[g, t * 64 : (t + 1) * 64, :]
         q_ref[low : low + 32, 512:] = packed_ref[g, 256:, :64]
         q_ref[low + 32 : low + 64, 512:] = packed_ref[g, 256:, 64:]
-    keys_ref[:, :384] = up_ref[...]
-    keys_ref[:, 384:] = down_ref[:, 256:]
+    keys_ref[:, :384] = y1_ref[...]
+    keys_ref[:, 384:] = y3_ref[:, 256:]
     rows, step = q_ref.shape[0], 256
     for a in range(0, rows, step):
         limit = past + a // 8 + (iota((step, 128), 0) >> 3)
@@ -300,8 +308,8 @@
         )
 
 
-def attend_own(past, packed, up, down):
-    width = up.shape[0]
+def attend_own(past, packed, y1, y3):
+    width = y1.shape[0]
     rows = packed.size // width
     count = 512
     return pl.pallas_call(
@@ -320,27 +328,25 @@
         ),
         compiler_params=pltpu.CompilerParams(vmem_limit_bytes=16 << 20),
         name="attend_own",
-    )(in_hbm(past), packed, up, down)
-
-
-def rest_kernel(top_ref, total_ref, mixed_ref, q_ref, up_ref, down_ref, right_ref, left_ref, out_ref, keys_ref, done_ref, sems):
+    )(in_hbm(past), packed, y1, y3)
+
+
+def rest_kernel(top_ref, total_ref, mixed_ref, q_ref, y1_ref, y3_ref, z1_ref, z3_ref, out_ref, keys_ref, done_ref, sems):
     _, first, second = place()
+    group = lax.axis_index("head")
+    row_y, row_z = group >> 2, group & 3
+    odd_y, odd_z = row_y & 1, row_z & 1
     past = top_ref[0:1, 64:65].astype(jnp.int32)
     late = 16 * BLOCK
-
-    def of_first(step):
-        return late + ((first + step) & 3) * 8
-
-    def of_second(step):
-        return late + 32 + ((second + step) & 3) * 8
-
-    tiles = (
-        (None, of_first(-1), None)
-        + (None, of_first(1), of_second(2))
-        + (None, of_second(-1), None)
-        + (None, of_second(1), of_first(2))
-    )
-    for i, ref in enumerate((up_ref, down_ref, right_ref, left_ref)):
+    across_first, across_second = ((first + 2) & 3) * 8, 32 + ((second + 2) & 3) * 8
+    tiles = ()
+    for flip in (1, 3):
+        sent_late = 1 - odd_y if flip == 1 else odd_y
+        tiles += (None, late + (((row_y ^ flip) + 2 * row_z) & 3) * 8, sent_late * late + across_second)
+    for flip in (1, 3):
+        sent_late = 1 - odd_z if flip == 1 else odd_z
+        tiles += (None, late + 32 + ((2 * row_y + (row_z ^ flip)) & 3) * 8, sent_late * late + across_first)
+    for i, ref in enumerate((y1_ref, y3_ref, z1_ref, z3_ref)):
         keys_ref[:, i * 384 : (i + 1) * 384] = ref[...]
     rows, step = q_ref.shape[0], 256
     copies = []
@@ -387,31 +393,24 @@
     )(*state, *parts)
 
 
-def turn(d):
-    return [(i, (i + d) % SHARDS) for i in range(SHARDS)]
-
-
-def line(dy, dz):
-    return [(y * 4 + z, ((y + dy) % 4) * 4 + (z + dz) % 4) for y in range(4) for z in range(4)]
+def partners(count, flip):
+    return [(i, i ^ flip) for i in range(count)]
 
 
 def body(q_latent, index_query, index_weight, index_keys, latent_cache, block_ids, block_counts):
     rows, heads, _ = q_latent.shape
     groups = lax.axis_size("head")
     *outgoing, source, other, past = gather_parts(block_ids, block_counts, latent_cache.T)
-    incoming = [outgoing[0]] + [lax.ppermute(outgoing[d], "ctx", turn(2 * d)) for d in range(1, SHARDS // 2)]
+    incoming = [outgoing[0]] + [lax.ppermute(outgoing[d], "ctx", partners(SHARDS, 2 * d)) for d in range(1, SHARDS // 2)]
     by_group = q_by_group(q_latent, groups)
     head_query = lax.all_to_all(by_group, "head", split_axis=0, concat_axis=0, tiled=True)
     index_scores = index_scores_of(index_query, index_weight, index_keys)
     theirs = compact_parts(128, other, incoming)
-    theirs = lax.ppermute(theirs, "ctx", [(i, i ^ 1) for i in range(SHARDS)])
+    theirs = lax.ppermute(theirs, "ctx", partners(SHARDS, 1))
     mine = compact_parts(0, source, incoming)
-    up, down, right, left = spread_parts(mine, theirs)
-    parts = [
-        lax.ppermute(part, "head", line(*step))
-        for part, step in ((up, (1, 0)), (down, (-1, 0)), (right, (0, 1)), (left, (0, -1)))
-    ]
-    state = attend_own(past, head_query, up, down)
+    y1, y3, z1, z3 = spread_parts(mine, theirs)
+    parts = [lax.ppermute(part, "head", partners(groups, flip)) for part, flip in ((y1, 4), (y3, 12), (z1, 1), (z3, 3))]
+    state = attend_own(past, head_query, y1, y3)
     attention = attend_rest(state, parts)
     return attention.reshape(rows * groups, heads // groups, 512), index_scores
 

time: 68.5 us -> 70.4 us (1.028)
  waiting for transfers between devices: 19.9 us -> 21.7 us
    ppermute x8, waiting for transfers between devices: 16.3 us -> 18.8 us  [the longest x3 14.8 us: body(): lax.ppermute(outgoing[d], 'ctx', partners(SHARDS, 2 * d))]
    all_to_all x1, waiting for transfers between devices: 3.58 us -> 2.83 us  [body(): lax.all_to_all(by_group, 'head', split_axis=0, concat_axis=0, tiled=True)]
  transfers between devices with their start and end apart: 9 -> 9, of which waited for: 5 -> 6; matrix products, arithmetic and copies ran while one was open for 0% -> 0% of each run, Pallas kernels for 21% -> 20%
where the time goes in v9:
time: 70.4 us; the launch traced here: 70.1 us
  Pallas kernels  26.9 us (38%)
  waiting for transfers between devices  21.7 us (31%)
  starting transfers between devices  20.7 us (29%)
  between operations  0.88 us (1%)
    ppermute x3, waiting for transfers between devices, body(): lax.ppermute(outgoing[d], 'ctx', partners(SHARDS, 2 * d))  14.8 us
    pallas_call x1, Pallas kernels, attend_rest(): pl.pallas_call(rest_kernel, out_shape=jax.ShapeDtypeStruct((rows, 512), B...  7.82 us
    all_to_all x1, starting transfers between devices, body(): lax.all_to_all(by_group, 'head', split_axis=0, concat_axis=0, tiled=True)  7.77 us
    pallas_call x1, Pallas kernels, index_scores_of(): pl.pallas_call(index_kernel, grid=(rows // step,), out_shape=jax.ShapeDty...  6.5 us
    ppermute x4, starting transfers between devices, body(): lax.ppermute(part, 'head', partners(groups, flip))  6.12 us
    ppermute x3, starting transfers between devices, body(): lax.ppermute(outgoing[d], 'ctx', partners(SHARDS, 2 * d))  4.59 us
    ppermute x4, waiting for transfers between devices, body(): lax.ppermute(part, 'head', partners(groups, flip))  3.99 us
    pallas_call x1, Pallas kernels, gather_parts(): pl.pallas_call(gather_kernel, out_shape=[pltpu.HBM((width, 256), BF16)] +...  3.56 us
  transfers between devices with their start and end apart: 9, of which 6 were waited for; matrix products, arithmetic and copies ran while one was open for 0% of the time, Pallas kernels for 20%

profile of v9, /device:TPU:1, one launch (start us, length us, event | category | flops | bytes accessed | tf_op | source)
XLA Modules:
  0.0 70.1 jit_solution(17900719196168868902)
XLA Ops:
  0.6 3.6 %gather_parts.1 = (bf16[576,256]{1,0:T(8,128)(2,1)}, bf16[576,256]{1,0:T(8,128)(2,1)S(1)}, bf16[576,256]{1,0:T(8,128)(2,1)S(1)}, bf16[576,256]{1,0:T(8,128)(2,1)...) custom-call(s32[8,32]{1,0:T(8,128)} %ids_hbm.1, s32[8]{0:T(128)} %counts_hbm.1, bf16[576,2048]{1,0:T(8,128)(2,1)} %bitcast.4), custom_call_target="tpu_custom_call" | custom-call | flops 2415919104 | bytes 4718592 | tf_op jit(solution)/shard_map/gather_parts/pallas_call | solution.py:127
  4.2 0.0 copy-start
  4.2 2.1 %collective-permute-start = (bf16[576,256]{1,0:T(8,128)(2,1)S(1)}, bf16[576,256]{1,0:T(8,128)(2,1)S(1)}, u32[]{:S(2)}, u32[]{:S(2)}) collective-permute-start(bf16[576,256]{1,0:T(8,128)(2,1)S(1)} %get-tuple-element.20), channel_id=1, source_target_pairs={{0,32},{16,48},{32,0},{48,16},{64,96},{80,112},{96,64},{112,80},{1... | collective-permute-start | bytes 884744 | tf_op jit(solution)/shard_map/ppermute | solution.py:404
  6.3 2.5 %collective-permute-start.1 = (bf16[576,256]{1,0:T(8,128)(2,1)S(1)}, bf16[576,256]{1,0:T(8,128)(2,1)S(1)}, u32[]{:S(2)}, u32[]{:S(2)}) collective-permute-start(bf16[576,256]{1,0:T(8,128)(2,1)S(1)} %get-tuple-element.21), channel_id=1, source_target_pairs={{0,64},{16,80},{32,96},{48,112},{64,0},{80,16},{96,32},{112,48},{1... | collective-permute-start | bytes 884744 | tf_op jit(solution)/shard_map/ppermute | solution.py:404
  8.8 0.0 collective-permute-start.2
  8.8 3.8 %collective-permute-done.refs_1_ = bf16[576,256]{1,0:T(8,128)(2,1)S(1)} collective-permute-done((bf16[576,256]{1,0:T(8,128)(2,1)S(1)}, bf16[576,256]{1,0:T(8,128)(2,1)S(1)}, u32[]{:S(2)}, u32[]{:S(2)}) %collective-permute-start) | collective-permute-done | bytes 294944 | tf_op jit(solution)/shard_map/ppermute | solution.py:404
  12.6 8.9 %collective-permute-done.1.refs_2_ = bf16[576,256]{1,0:T(8,128)(2,1)S(1)} collective-permute-done((bf16[576,256]{1,0:T(8,128)(2,1)S(1)}, bf16[576,256]{1,0:T(8,128)(2,1)S(1)}, u32[]{:S(2)}, u32[]{:S(2)}) %collective-permute-start.1) | collective-permute-done | bytes 294944 | tf_op jit(solution)/shard_map/ppermute | solution.py:404
  21.6 2.1 %collective-permute-done.2.refs_3_ = bf16[576,256]{1,0:T(8,128)(2,1)S(1)} collective-permute-done((bf16[576,256]{1,0:T(8,128)(2,1)S(1)}, bf16[576,256]{1,0:T(8,128)(2,1)S(1)}, u32[]{:S(2)}, u32[]{:S(2)}) %collective-permute-start.2) | collective-permute-done | bytes 294944 | tf_op jit(solution)/shard_map/ppermute | solution.py:404
  23.6 1.5 %compact_parts.3 = bf16[576,512]{1,0:T(8,128)(2,1)S(1)} custom-call(s32[8,512]{1,0:T(8,128)} %get-tuple-element.23.source_ref, bf16[576,256]{1,0:T(8,128)(2,1)} %get-tuple-element.19.refs_0_, bf16[576,256]{1,0:T(8,128)(2,1)S(1)} %collective-permute-done.refs_1_, bf16[576,256]{1,0:T(8,128)(2,1)S(1)} %collective-permute-done.1.refs_2_, ...), custom_call_target="tpu_custom_call" | custom-call | flops 301989888 | bytes 1769472 | tf_op jit(solution)/shard_map/compact_parts/pallas_call | solution.py:163
  25.1 2.2 %collective-permute-start.3 = (bf16[576,512]{1,0:T(8,128)(2,1)S(1)}, bf16[576,512]{1,0:T(8,128)(2,1)S(1)}, u32[]{:S(2)}, u32[]{:S(2)}) collective-permute-start(bf16[576,512]{1,0:T(8,128)(2,1)S(1)} %compact_parts.3), channel_id=1, source_target_pairs={{0,16},{16,0},{32,48},{48,32},{64,80},{80,64},{96,112},{112,96},{1... | collective-permute-start | bytes 1769480 | tf_op jit(solution)/shard_map/ppermute | solution.py:409
  27.3 0.0 copy-done
  27.3 1.6 %q_by_group.1 = bf16[16,288,128]{2,1,0:T(8,128)(2,1)} custom-call(bf16[8,576,128]{2,1,0:T(8,128)(2,1)S(1)} %bitcast.3), custom_call_target="tpu_custom_call" | custom-call | bytes 2359296 | tf_op jit(solution)/shard_map/q_by_group/pallas_call | solution.py:221
  28.8 7.8 %all-to-all-start = ((bf16[16,288,128]{2,1,0:T(8,128)(2,1)}), bf16[16,288,128]{2,1,0:T(8,128)(2,1)S(1)}, u32[]{:S(2)}, u32[]{:S(2)}) async-start(bf16[16,288,128]{2,1,0:T(8,128)(2,1)} %q_by_group.1), calls=%async_computation | async-start | bytes 2359296 | tf_op jit(solution)/shard_map/all_to_all | solution.py:406
  36.6 0.0 copy-start.1
  36.6 0.0 copy-start.2
  36.6 0.0 copy-start.3
  36.6 1.6 %compact_parts.2.own_ref = bf16[576,512]{1,0:T(8,128)(2,1)S(1)} custom-call(s32[8,512]{1,0:T(8,128)} %get-tuple-element.18.source_ref, bf16[576,256]{1,0:T(8,128)(2,1)} %get-tuple-element.19.refs_0_, bf16[576,256]{1,0:T(8,128)(2,1)S(1)} %collective-permute-done.refs_1_, bf16[576,256]{1,0:T(8,128)(2,1)S(1)} %collective-permute-done.1.refs_2_, ...), custom_call_target="tpu_custom_call" | custom-call | flops 301989888 | bytes 1769472 | tf_op jit(solution)/shard_map/compact_parts/pallas_call | solution.py:163
  38.2 0.0 collective-permute-done.3.other_ref
  38.2 1.1 %spread_parts.1 = (bf16[576,384]{1,0:T(8,128)(2,1)}, bf16[576,384]{1,0:T(8,128)(2,1)}, bf16[576,384]{1,0:T(8,128)(2,1)S(1)}, bf16[576,384]{1,0:T(8,128)(2,1)S(1)}) custom-call(bf16[576,512]{1,0:T(8,128)(2,1)S(1)} %compact_parts.2.own_ref, bf16[576,512]{1,0:T(8,128)(2,1)S(1)} %collective-permute-done.3.other_ref), custom_call_target="tpu_custom_call" | custom-call | flops 294912 | bytes 2949120 | tf_op jit(solution)/shard_map/spread_parts/pallas_call | solution.py:195
  39.3 1.4 %collective-permute-start.4 = (bf16[576,384]{1,0:T(8,128)(2,1)}, bf16[576,384]{1,0:T(8,128)(2,1)S(1)}, u32[]{:S(2)}, u32[]{:S(2)}) collective-permute-start(bf16[576,384]{1,0:T(8,128)(2,1)} %get-tuple-element.24.y1_ref), channel_id=1, source_target_pairs={{0,4},{1,5},{2,6},{3,7},{4,0},{5,1},{6,2},{7,3},{8,12},{9,13},{10,... | collective-permute-start | bytes 1327112 | tf_op jit(solution)/shard_map/ppermute | solution.py:412
  40.6 1.8 %collective-permute-start.5 = (bf16[576,384]{1,0:T(8,128)(2,1)}, bf16[576,384]{1,0:T(8,128)(2,1)S(1)}, u32[]{:S(2)}, u32[]{:S(2)}) collective-permute-start(bf16[576,384]{1,0:T(8,128)(2,1)} %get-tuple-element.25.y3_ref), channel_id=1, source_target_pairs={{0,12},{1,13},{2,14},{3,15},{4,8},{5,9},{6,10},{7,11},{8,4},{9,5},... | collective-permute-start | bytes 1327112 | tf_op jit(solution)/shard_map/ppermute | solution.py:412
  42.4 1.2 %collective-permute-start.6 = (bf16[576,384]{1,0:T(8,128)(2,1)S(1)}, bf16[576,384]{1,0:T(8,128)(2,1)S(1)}, u32[]{:S(2)}, u32[]{:S(2)}) collective-permute-start(bf16[576,384]{1,0:T(8,128)(2,1)S(1)} %get-tuple-element.30), channel_id=1, source_target_pairs={{0,1},{1,0},{2,3},{3,2},{4,5},{5,4},{6,7},{7,6},{8,9},{9,8},{10,11... | collective-permute-start | bytes 1327112 | tf_op jit(solution)/shard_map/ppermute | solution.py:412
  43.6 1.8 %collective-permute-start.7 = (bf16[576,384]{1,0:T(8,128)(2,1)S(1)}, bf16[576,384]{1,0:T(8,128)(2,1)}, u32[]{:S(2)}, u32[]{:S(2)}) collective-permute-start(bf16[576,384]{1,0:T(8,128)(2,1)S(1)} %get-tuple-element.31), channel_id=1, source_target_pairs={{0,3},{1,2},{2,1},{3,0},{4,7},{5,6},{6,5},{7,4},{8,11},{9,10},{10,... | collective-permute-start | bytes 1327112 | tf_op jit(solution)/shard_map/ppermute | solution.py:412
  45.4 0.0 copy-done.1
  45.4 0.0 copy-done.2
  45.4 0.0 copy-done.3
  45.4 6.5 %index_scores.1 = f32[64,2048]{1,0:T(8,128)} custom-call(bf16[64,64,128]{2,1,0:T(8,128)(2,1)S(1)} %copy-done.1, f32[64,64]{1,0:T(8,128)S(1)} %copy-done.3, bf16[2048,128]{1,0:T(8,128)(2,1)S(1)} %copy-done.2), custom_call_target="tpu_custom_call" | custom-call | flops 8589934592 | bytes 1572864 | tf_op jit(solution)/shard_map/index_scores/pallas_call | solution.py:250
  51.9 2.8 %all-to-all-done.packed_ref = bf16[16,288,128]{2,1,0:T(8,128)(2,1)S(1)} async-done(((bf16[16,288,128]{2,1,0:T(8,128)(2,1)}), bf16[16,288,128]{2,1,0:T(8,128)(2,1)S(1)}, u32[]{:S(2)}, u32[]{:S(2)}) %all-to-all-start) | async-done | bytes 1179680 | tf_op jit(solution)/shard_map/all_to_all | solution.py:406
  54.8 3.4 %attend_own.1 = (f32[1024,128]{1,0:T(8,128)S(1)}, f32[1024,128]{1,0:T(8,128)S(1)}, f32[1024,512]{1,0:T(8,128)S(1)}, bf16[1024,576]{1,0:T(8,128)(2,1)S(1)}) custom-call(s32[8,128]{1,0:T(8,128)} %get-tuple-element.17.past_ref, bf16[16,288,128]{2,1,0:T(8,128)(2,1)S(1)} %all-to-all-done.packed_ref, bf16[576,384]{1,0:T(8,128)(2,1)} %get-tuple-element.24.y1_ref, ...), custom_call_target="tpu_custom_call" | custom-call | flops 1140850688 | bytes 4456448 | tf_op jit(solution)/shard_map/attend_own/pallas_call | solution.py:315
  58.1 2.8 %collective-permute-done.4.y1_ref = bf16[576,384]{1,0:T(8,128)(2,1)S(1)} collective-permute-done((bf16[576,384]{1,0:T(8,128)(2,1)}, bf16[576,384]{1,0:T(8,128)(2,1)S(1)}, u32[]{:S(2)}, u32[]{:S(2)}) %collective-permute-start.4) | collective-permute-done | bytes 442400 | tf_op jit(solution)/shard_map/ppermute | solution.py:412
  60.9 1.2 %collective-permute-done.5.y3_ref = bf16[576,384]{1,0:T(8,128)(2,1)S(1)} collective-permute-done((bf16[576,384]{1,0:T(8,128)(2,1)}, bf16[576,384]{1,0:T(8,128)(2,1)S(1)}, u32[]{:S(2)}, u32[]{:S(2)}) %collective-permute-start.5) | collective-permute-done | bytes 442400 | tf_op jit(solution)/shard_map/ppermute | solution.py:412
  62.1 0.0 collective-permute-done.6.z1_ref
  62.1 0.0 collective-permute-done.7.z3_ref
  62.1 7.8 %attend_rest.1 = bf16[1024,512]{1,0:T(8,128)(2,1)} custom-call(f32[1024,128]{1,0:T(8,128)S(1)} %get-tuple-element.26.top_ref, f32[1024,128]{1,0:T(8,128)S(1)} %get-tuple-element.27.total_ref, f32[1024,512]{1,0:T(8,128)S(1)} %get-tuple-element.28.mixed_ref, bf16[1024,576]{1,0:T(8,128)(2,1)S(1)} %get-tuple-element.29.q_ref, ...), custom_call_target="tpu_custom_call" | custom-call | flops 3422552064 | bytes 5505024 | tf_op jit(solution)/shard_map/attend_rest/pallas_call | solution.py:378
Async XLA Ops:
  4.2 23.1 %copy-start = (bf16[8,128,576]{1,2,0:T(8,128)(2,1)S(1)}, bf16[8,128,576]{1,2,0:T(8,128)(2,1)}, u32[]{:S(2)}) copy-start(bf16[8,128,576]{1,2,0:T(8,128)(2,1)} %param.7) | copy-start | bytes 3538948
  4.2 8.4 %collective-permute-start = (bf16[576,256]{1,0:T(8,128)(2,1)S(1)}, bf16[576,256]{1,0:T(8,128)(2,1)S(1)}, u32[]{:S(2)}, u32[]{:S(2)}) collective-permute-start(bf16[576,256]{1,0:T(8,128)(2,1)S(1)} %get-tuple-element.20), channel_id=1, source_target_pairs={{0,32},{16,48},{32,0},{48,16},{64,96},{80,112},{96,64},{112,80},{1... | collective-permute-start | bytes 884744 | tf_op jit(solution)/shard_map/ppermute | solution.py:404
  6.3 15.2 %collective-permute-start.1 = (bf16[576,256]{1,0:T(8,128)(2,1)S(1)}, bf16[576,256]{1,0:T(8,128)(2,1)S(1)}, u32[]{:S(2)}, u32[]{:S(2)}) collective-permute-start(bf16[576,256]{1,0:T(8,128)(2,1)S(1)} %get-tuple-element.21), channel_id=1, source_target_pairs={{0,64},{16,80},{32,96},{48,112},{64,0},{80,16},{96,32},{112,48},{1... | collective-permute-start | bytes 884744 | tf_op jit(solution)/shard_map/ppermute | solution.py:404
  8.8 14.9 %collective-permute-start.2 = (bf16[576,256]{1,0:T(8,128)(2,1)S(1)}, bf16[576,256]{1,0:T(8,128)(2,1)S(1)}, u32[]{:S(2)}, u32[]{:S(2)}) collective-permute-start(bf16[576,256]{1,0:T(8,128)(2,1)S(1)} %get-tuple-element.22), channel_id=1, source_target_pairs={{0,96},{16,112},{32,64},{48,80},{64,32},{80,48},{96,0},{112,16},{1... | collective-permute-start | bytes 884744 | tf_op jit(solution)/shard_map/ppermute | solution.py:404
  25.1 13.1 %collective-permute-start.3 = (bf16[576,512]{1,0:T(8,128)(2,1)S(1)}, bf16[576,512]{1,0:T(8,128)(2,1)S(1)}, u32[]{:S(2)}, u32[]{:S(2)}) collective-permute-start(bf16[576,512]{1,0:T(8,128)(2,1)S(1)} %compact_parts.3), channel_id=1, source_target_pairs={{0,16},{16,0},{32,48},{48,32},{64,80},{80,64},{96,112},{112,96},{1... | collective-permute-start | bytes 1769480 | tf_op jit(solution)/shard_map/ppermute | solution.py:409
  28.8 25.9 %all-to-all-start = ((bf16[16,288,128]{2,1,0:T(8,128)(2,1)}), bf16[16,288,128]{2,1,0:T(8,128)(2,1)S(1)}, u32[]{:S(2)}, u32[]{:S(2)}) async-start(bf16[16,288,128]{2,1,0:T(8,128)(2,1)} %q_by_group.1), calls=%async_computation | async-start | bytes 2359296 | tf_op jit(solution)/shard_map/all_to_all | solution.py:406
  36.6 8.8 %copy-start.1 = (bf16[64,64,128]{2,1,0:T(8,128)(2,1)S(1)}, bf16[64,64,128]{2,1,0:T(8,128)(2,1)}, u32[]{:S(2)}) copy-start(bf16[64,64,128]{2,1,0:T(8,128)(2,1)} %query_ref.1) | copy-start | bytes 3145732
  36.6 8.8 %copy-start.2 = (bf16[2048,128]{1,0:T(8,128)(2,1)S(1)}, bf16[2048,128]{1,0:T(8,128)(2,1)}, u32[]{:S(2)}) copy-start(bf16[2048,128]{1,0:T(8,128)(2,1)} %keys_ref.1) | copy-start | bytes 1572868
  36.6 8.8 %copy-start.3 = (f32[64,64]{1,0:T(8,128)S(1)}, f32[64,64]{1,0:T(8,128)}, u32[]{:S(2)}) copy-start(f32[64,64]{1,0:T(8,128)} %weight_ref.1) | copy-start | bytes 49156
  39.3 21.6 %collective-permute-start.4 = (bf16[576,384]{1,0:T(8,128)(2,1)}, bf16[576,384]{1,0:T(8,128)(2,1)S(1)}, u32[]{:S(2)}, u32[]{:S(2)}) collective-permute-start(bf16[576,384]{1,0:T(8,128)(2,1)} %get-tuple-element.24.y1_ref), channel_id=1, source_target_pairs={{0,4},{1,5},{2,6},{3,7},{4,0},{5,1},{6,2},{7,3},{8,12},{9,13},{10,... | collective-permute-start | bytes 1327112 | tf_op jit(solution)/shard_map/ppermute | solution.py:412
  40.6 21.4 %collective-permute-start.5 = (bf16[576,384]{1,0:T(8,128)(2,1)}, bf16[576,384]{1,0:T(8,128)(2,1)S(1)}, u32[]{:S(2)}, u32[]{:S(2)}) collective-permute-start(bf16[576,384]{1,0:T(8,128)(2,1)} %get-tuple-element.25.y3_ref), channel_id=1, source_target_pairs={{0,12},{1,13},{2,14},{3,15},{4,8},{5,9},{6,10},{7,11},{8,4},{9,5},... | collective-permute-start | bytes 1327112 | tf_op jit(solution)/shard_map/ppermute | solution.py:412
  42.4 19.7 %collective-permute-start.6 = (bf16[576,384]{1,0:T(8,128)(2,1)S(1)}, bf16[576,384]{1,0:T(8,128)(2,1)S(1)}, u32[]{:S(2)}, u32[]{:S(2)}) collective-permute-start(bf16[576,384]{1,0:T(8,128)(2,1)S(1)} %get-tuple-element.30), channel_id=1, source_target_pairs={{0,1},{1,0},{2,3},{3,2},{4,5},{5,4},{6,7},{7,6},{8,9},{9,8},{10,11... | collective-permute-start | bytes 1327112 | tf_op jit(solution)/shard_map/ppermute | solution.py:412
  43.6 18.5 %collective-permute-start.7 = (bf16[576,384]{1,0:T(8,128)(2,1)S(1)}, bf16[576,384]{1,0:T(8,128)(2,1)}, u32[]{:S(2)}, u32[]{:S(2)}) collective-permute-start(bf16[576,384]{1,0:T(8,128)(2,1)S(1)} %get-tuple-element.31), channel_id=1, source_target_pairs={{0,3},{1,2},{2,1},{3,0},{4,7},{5,6},{6,5},{7,4},{8,11},{9,10},{10,... | collective-permute-start | bytes 1327112 | tf_op jit(solution)/shard_map/ppermute | solution.py:412

commit v10 on v8

--- a/solution.py
+++ b/solution.py
@@ -323,7 +323,8 @@
     )(in_hbm(past), packed, up, down)
 
 
-def rest_kernel(top_ref, total_ref, mixed_ref, q_ref, up_ref, down_ref, right_ref, left_ref, out_ref, keys_ref, done_ref, sems):
+def more_kernel(along_y, top_ref, total_ref, mixed_ref, q_ref, plus_ref, minus_ref, *refs):
+    out_refs, (keys_ref, done_ref, sems) = refs[:-3], refs[-3:]
     _, first, second = place()
     past = top_ref[0:1, 64:65].astype(jnp.int32)
     late = 16 * BLOCK
@@ -334,14 +335,10 @@
     def of_second(step):
         return late + 32 + ((second + step) & 3) * 8
 
-    tiles = (
-        (None, of_first(-1), None)
-        + (None, of_first(1), of_second(2))
-        + (None, of_second(-1), None)
-        + (None, of_second(1), of_first(2))
-    )
-    for i, ref in enumerate((up_ref, down_ref, right_ref, left_ref)):
-        keys_ref[:, i * 384 : (i + 1) * 384] = ref[...]
+    near, far = (of_first, of_second) if along_y else (of_second, of_first)
+    tiles = (None, near(-1), None, None, near(1), far(2))
+    keys_ref[:, :384] = plus_ref[...]
+    keys_ref[:, 384:] = minus_ref[...]
     rows, step = q_ref.shape[0], 256
     copies = []
     for a in range(0, rows, step):
@@ -355,10 +352,16 @@
         mixed = mixed_ref[a : a + step, :] * fade + lax.dot_general(
             weights.astype(BF16), keys_ref[0:512, :], (((1,), (1,)), ((), ())), preferred_element_type=F32
         )
+        if along_y:
+            top_out, total_out, mixed_out = out_refs
+            top_out[a : a + step, :] = jnp.where(iota((step, 128), 1) < 64, top, past.astype(F32))
+            total_out[a : a + step, :] = jnp.broadcast_to(total, (step, 128))
+            mixed_out[a : a + step, :] = mixed
+            continue
         done_ref[a : a + step, :] = (mixed / total).astype(BF16)
         copies.append(
             pltpu.make_async_copy(
-                done_ref.at[pl.ds(a, step), :], out_ref.at[pl.ds(a, step), :], sems.at[a // step]
+                done_ref.at[pl.ds(a, step), :], out_refs[0].at[pl.ds(a, step), :], sems.at[a // step]
             )
         )
         copies[-1].start()
@@ -366,25 +369,29 @@
         copy.wait()
 
 
-def attend_rest(state, parts):
-    rows, width = state[-1].shape
+def attend_more(along_y, state, q, parts):
+    rows, width = q.shape
     count = sum(part.shape[1] for part in parts)
-    return pl.pallas_call(
-        rest_kernel,
-        out_shape=jax.ShapeDtypeStruct((rows, 512), BF16),
+    if along_y:
+        out_shape, out_specs = [jax.ShapeDtypeStruct(x.shape, x.dtype) for x in state], [VMEM] * 3
+    else:
+        out_shape, out_specs = jax.ShapeDtypeStruct((rows, 512), BF16), pl.BlockSpec(memory_space=pltpu.HBM)
+    return pl.pallas_call(
+        functools.partial(more_kernel, along_y),
+        out_shape=out_shape,
         in_specs=[VMEM] * (4 + len(parts)),
-        out_specs=pl.BlockSpec(memory_space=pltpu.HBM),
+        out_specs=out_specs,
         scratch_shapes=[
             pltpu.VMEM((width, count), BF16),
-            pltpu.VMEM((rows, 512), BF16),
+            pltpu.VMEM((8, 512) if along_y else (rows, 512), BF16),
             pltpu.SemaphoreType.DMA((rows // 256,)),
         ],
         cost_estimate=pl.CostEstimate(
             flops=2 * rows * count * (width + 512), bytes_accessed=rows * 5376, transcendentals=rows * count
         ),
-        compiler_params=pltpu.CompilerParams(vmem_limit_bytes=24 << 20),
-        name="attend_rest",
-    )(*state, *parts)
+        compiler_params=pltpu.CompilerParams(vmem_limit_bytes=16 << 20),
+        name="attend_more",
+    )(*state, q, *parts)
 
 
 def turn(d):
@@ -399,7 +406,8 @@
     rows, heads, _ = q_latent.shape
     groups = lax.axis_size("head")
     *outgoing, source, other, past = gather_parts(block_ids, block_counts, latent_cache.T)
-    incoming = [outgoing[0]] + [lax.ppermute(outgoing[d], "ctx", turn(2 * d)) for d in range(1, SHARDS // 2)]
+    incoming = [outgoing[0]] + [lax.ppermute(outgoing[d], "ctx", turn(2 * d)) for d in (2, 1, 3)]
+    incoming = [incoming[0], incoming[2], incoming[1], incoming[3]]
     by_group = q_by_group(q_latent, groups)
     head_query = lax.all_to_all(by_group, "head", split_axis=0, concat_axis=0, tiled=True)
     index_scores = index_scores_of(index_query, index_weight, index_keys)
@@ -407,12 +415,11 @@
     theirs = lax.ppermute(theirs, "ctx", [(i, i ^ 1) for i in range(SHARDS)])
     mine = compact_parts(0, source, incoming)
     up, down, right, left = spread_parts(mine, theirs)
-    parts = [
-        lax.ppermute(part, "head", line(*step))
-        for part, step in ((up, (1, 0)), (down, (-1, 0)), (right, (0, 1)), (left, (0, -1)))
-    ]
-    state = attend_own(past, head_query, up, down)
-    attention = attend_rest(state, parts)
+    y_parts = [lax.ppermute(part, "head", line(*step)) for part, step in ((up, (1, 0)), (down, (-1, 0)))]
+    z_parts = [lax.ppermute(part, "head", line(*step)) for part, step in ((right, (0, 1)), (left, (0, -1)))]
+    *state, query = attend_own(past, head_query, up, down)
+    state = attend_more(True, state, query, y_parts)
+    attention = attend_more(False, state, query, z_parts)
     return attention.reshape(rows * groups, heads // groups, 512), index_scores
 
 

time: 68.5 us -> 68.8 us (level)
  Pallas kernels: 26.9 us -> 28.3 us
  waiting for transfers between devices: 19.9 us -> 18.9 us
    pallas_call x1 -> x2, Pallas kernels: 7.75 us -> 8.99 us  [attend_more(): pl.pallas_call(functools.partial(more_kernel, along_y), out_shape=out_sha...]
    ppermute x4, waiting for transfers between devices: 4.74 us -> 3.83 us  [body(): lax.ppermute(part, 'head', line(*step))]
  transfers between devices with their start and end apart: 9 -> 9, of which waited for: 5 -> 4; matrix products, arithmetic and copies ran while one was open for 0% -> 0% of each run, Pallas kernels for 21% -> 27%
where the time goes in v10:
time: 68.8 us; the launch traced here: 68.5 us
  Pallas kernels  28.3 us (41%)
  starting transfers between devices  20.4 us (30%)
  waiting for transfers between devices  18.9 us (27%)
  between operations  0.9 us (1%)
    ppermute x3, waiting for transfers between devices, body(): lax.ppermute(outgoing[d], 'ctx', turn(2 * d))  11.6 us
    pallas_call x2, Pallas kernels, attend_more(): pl.pallas_call(functools.partial(more_kernel, along_y), out_shape=out_sha...  8.99 us
    all_to_all x1, starting transfers between devices, body(): lax.all_to_all(by_group, 'head', split_axis=0, concat_axis=0, tiled=True)  7.77 us
    pallas_call x1, Pallas kernels, index_scores_of(): pl.pallas_call(index_kernel, grid=(rows // step,), out_shape=jax.ShapeDty...  6.5 us
    ppermute x3, starting transfers between devices, body(): lax.ppermute(outgoing[d], 'ctx', turn(2 * d))  5.7 us
    ppermute x4, starting transfers between devices, body(): lax.ppermute(part, 'head', line(*step))  5.35 us
    ppermute x4, waiting for transfers between devices, body(): lax.ppermute(part, 'head', line(*step))  3.83 us
    pallas_call x1, Pallas kernels, gather_parts(): pl.pallas_call(gather_kernel, out_shape=[pltpu.HBM((width, 256), BF16)] +...  3.56 us
  transfers between devices with their start and end apart: 9, of which 4 were waited for; matrix products, arithmetic and copies ran while one was open for 0% of the time, Pallas kernels for 27%

profile of v10, /device:TPU:1, one launch (start us, length us, event | category | flops | bytes accessed | tf_op | source)
XLA Modules:
  0.0 68.5 jit_solution(11053855540208565768)
XLA Ops:
  0.6 3.6 %gather_parts.1 = (bf16[576,256]{1,0:T(8,128)(2,1)}, bf16[576,256]{1,0:T(8,128)(2,1)S(1)}, bf16[576,256]{1,0:T(8,128)(2,1)S(1)}, bf16[576,256]{1,0:T(8,128)(2,1)...) custom-call(s32[8,32]{1,0:T(8,128)} %ids_hbm.1, s32[8]{0:T(128)} %counts_hbm.1, bf16[576,2048]{1,0:T(8,128)(2,1)} %bitcast.5), custom_call_target="tpu_custom_call" | custom-call | flops 2415919104 | bytes 4718592 | tf_op jit(solution)/shard_map/gather_parts/pallas_call | solution.py:127
  4.2 0.0 copy-start
  4.2 2.1 %collective-permute-start = (bf16[576,256]{1,0:T(8,128)(2,1)S(1)}, bf16[576,256]{1,0:T(8,128)(2,1)S(1)}, u32[]{:S(2)}, u32[]{:S(2)}) collective-permute-start(bf16[576,256]{1,0:T(8,128)(2,1)S(1)} %get-tuple-element.23), channel_id=1, source_target_pairs={{0,32},{16,48},{32,64},{48,80},{64,96},{80,112},{96,0},{112,16},{1... | collective-permute-start | bytes 884744 | tf_op jit(solution)/shard_map/ppermute | solution.py:409
  6.3 2.5 %collective-permute-start.1 = (bf16[576,256]{1,0:T(8,128)(2,1)S(1)}, bf16[576,256]{1,0:T(8,128)(2,1)S(1)}, u32[]{:S(2)}, u32[]{:S(2)}) collective-permute-start(bf16[576,256]{1,0:T(8,128)(2,1)S(1)} %get-tuple-element.24), channel_id=1, source_target_pairs={{0,64},{16,80},{32,96},{48,112},{64,0},{80,16},{96,32},{112,48},{1... | collective-permute-start | bytes 884744 | tf_op jit(solution)/shard_map/ppermute | solution.py:409
  8.8 1.2 %collective-permute-start.2 = (bf16[576,256]{1,0:T(8,128)(2,1)S(1)}, bf16[576,256]{1,0:T(8,128)(2,1)S(1)}, u32[]{:S(2)}, u32[]{:S(2)}) collective-permute-start(bf16[576,256]{1,0:T(8,128)(2,1)S(1)} %get-tuple-element.25), channel_id=1, source_target_pairs={{0,96},{16,112},{32,0},{48,16},{64,32},{80,48},{96,64},{112,80},{1... | collective-permute-start | bytes 884744 | tf_op jit(solution)/shard_map/ppermute | solution.py:409
  9.9 4.0 %collective-permute-done.refs_1_ = bf16[576,256]{1,0:T(8,128)(2,1)S(1)} collective-permute-done((bf16[576,256]{1,0:T(8,128)(2,1)S(1)}, bf16[576,256]{1,0:T(8,128)(2,1)S(1)}, u32[]{:S(2)}, u32[]{:S(2)}) %collective-permute-start) | collective-permute-done | bytes 294944 | tf_op jit(solution)/shard_map/ppermute | solution.py:409
  13.9 7.6 %collective-permute-done.1.refs_2_ = bf16[576,256]{1,0:T(8,128)(2,1)S(1)} collective-permute-done((bf16[576,256]{1,0:T(8,128)(2,1)S(1)}, bf16[576,256]{1,0:T(8,128)(2,1)S(1)}, u32[]{:S(2)}, u32[]{:S(2)}) %collective-permute-start.1) | collective-permute-done | bytes 294944 | tf_op jit(solution)/shard_map/ppermute | solution.py:409
  21.5 0.0 collective-permute-done.2.refs_3_
  21.5 1.5 %compact_parts.3 = bf16[576,512]{1,0:T(8,128)(2,1)S(1)} custom-call(s32[8,512]{1,0:T(8,128)} %get-tuple-element.26.source_ref, bf16[576,256]{1,0:T(8,128)(2,1)} %get-tuple-element.22.refs_0_, bf16[576,256]{1,0:T(8,128)(2,1)S(1)} %collective-permute-done.refs_1_, bf16[576,256]{1,0:T(8,128)(2,1)S(1)} %collective-permute-done.1.refs_2_, ...), custom_call_target="tpu_custom_call" | custom-call | flops 301989888 | bytes 1769472 | tf_op jit(solution)/shard_map/compact_parts/pallas_call | solution.py:163
  23.0 1.6 %collective-permute-start.3 = (bf16[576,512]{1,0:T(8,128)(2,1)S(1)}, bf16[576,512]{1,0:T(8,128)(2,1)S(1)}, u32[]{:S(2)}, u32[]{:S(2)}) collective-permute-start(bf16[576,512]{1,0:T(8,128)(2,1)S(1)} %compact_parts.3), channel_id=1, source_target_pairs={{0,16},{16,0},{32,48},{48,32},{64,80},{80,64},{96,112},{112,96},{1... | collective-permute-start | bytes 1769480 | tf_op jit(solution)/shard_map/ppermute | solution.py:415
  24.6 0.0 copy-done
  24.6 1.6 %q_by_group.1 = bf16[16,288,128]{2,1,0:T(8,128)(2,1)} custom-call(bf16[8,576,128]{2,1,0:T(8,128)(2,1)S(1)} %bitcast.3), custom_call_target="tpu_custom_call" | custom-call | bytes 2359296 | tf_op jit(solution)/shard_map/q_by_group/pallas_call | solution.py:215
  26.2 7.8 %all-to-all-start = ((bf16[16,288,128]{2,1,0:T(8,128)(2,1)}), bf16[16,288,128]{2,1,0:T(8,128)(2,1)S(1)}, u32[]{:S(2)}, u32[]{:S(2)}) async-start(bf16[16,288,128]{2,1,0:T(8,128)(2,1)} %q_by_group.1), calls=%async_computation | async-start | bytes 2359296 | tf_op jit(solution)/shard_map/all_to_all | solution.py:412
  33.9 0.0 copy-start.1
  33.9 0.0 copy-start.2
  34.0 0.0 copy-start.3
  34.0 1.6 %compact_parts.2.own_ref = bf16[576,512]{1,0:T(8,128)(2,1)S(1)} custom-call(s32[8,512]{1,0:T(8,128)} %get-tuple-element.21.source_ref, bf16[576,256]{1,0:T(8,128)(2,1)} %get-tuple-element.22.refs_0_, bf16[576,256]{1,0:T(8,128)(2,1)S(1)} %collective-permute-done.refs_1_, bf16[576,256]{1,0:T(8,128)(2,1)S(1)} %collective-permute-done.1.refs_2_, ...), custom_call_target="tpu_custom_call" | custom-call | flops 301989888 | bytes 1769472 | tf_op jit(solution)/shard_map/compact_parts/pallas_call | solution.py:163
  35.5 0.0 collective-permute-done.3.other_ref
  35.6 1.2 %spread_parts.1 = (bf16[576,384]{1,0:T(8,128)(2,1)}, bf16[576,384]{1,0:T(8,128)(2,1)}, bf16[576,384]{1,0:T(8,128)(2,1)}, bf16[576,384]{1,0:T(8,128)(2,1)S(1)}) custom-call(bf16[576,512]{1,0:T(8,128)(2,1)S(1)} %compact_parts.2.own_ref, bf16[576,512]{1,0:T(8,128)(2,1)S(1)} %collective-permute-done.3.other_ref), custom_call_target="tpu_custom_call" | custom-call | flops 294912 | bytes 2949120 | tf_op jit(solution)/shard_map/spread_parts/pallas_call | solution.py:189
  36.8 1.4 %collective-permute-start.4 = (bf16[576,384]{1,0:T(8,128)(2,1)}, bf16[576,384]{1,0:T(8,128)(2,1)S(1)}, u32[]{:S(2)}, u32[]{:S(2)}) collective-permute-start(bf16[576,384]{1,0:T(8,128)(2,1)} %get-tuple-element.27.up_ref), channel_id=1, source_target_pairs={{0,4},{1,5},{2,6},{3,7},{4,8},{5,9},{6,10},{7,11},{8,12},{9,13},{1... | collective-permute-start | bytes 1327112 | tf_op jit(solution)/shard_map/ppermute | solution.py:418
  38.2 1.3 %collective-permute-start.5 = (bf16[576,384]{1,0:T(8,128)(2,1)}, bf16[576,384]{1,0:T(8,128)(2,1)S(1)}, u32[]{:S(2)}, u32[]{:S(2)}) collective-permute-start(bf16[576,384]{1,0:T(8,128)(2,1)} %get-tuple-element.28.down_ref), channel_id=1, source_target_pairs={{0,12},{1,13},{2,14},{3,15},{4,0},{5,1},{6,2},{7,3},{8,4},{9,5},{1... | collective-permute-start | bytes 1327112 | tf_op jit(solution)/shard_map/ppermute | solution.py:418
  39.5 1.4 %collective-permute-start.6 = (bf16[576,384]{1,0:T(8,128)(2,1)}, bf16[576,384]{1,0:T(8,128)(2,1)S(1)}, u32[]{:S(2)}, u32[]{:S(2)}) collective-permute-start(bf16[576,384]{1,0:T(8,128)(2,1)} %get-tuple-element.36), channel_id=1, source_target_pairs={{0,1},{1,2},{2,3},{3,0},{4,5},{5,6},{6,7},{7,4},{8,9},{9,10},{10,1... | collective-permute-start | bytes 1327112 | tf_op jit(solution)/shard_map/ppermute | solution.py:419
  40.8 1.3 %collective-permute-start.7 = (bf16[576,384]{1,0:T(8,128)(2,1)S(1)}, bf16[576,384]{1,0:T(8,128)(2,1)S(1)}, u32[]{:S(2)}, u32[]{:S(2)}) collective-permute-start(bf16[576,384]{1,0:T(8,128)(2,1)S(1)} %get-tuple-element.37), channel_id=1, source_target_pairs={{0,3},{1,0},{2,1},{3,2},{4,7},{5,4},{6,5},{7,6},{8,11},{9,8},{10,9... | collective-permute-start | bytes 1327112 | tf_op jit(solution)/shard_map/ppermute | solution.py:419
  42.1 0.0 copy-done.1
  42.1 0.0 copy-done.2
  42.1 0.0 copy-done.3
  42.2 6.5 %index_scores.1 = f32[64,2048]{1,0:T(8,128)} custom-call(bf16[64,64,128]{2,1,0:T(8,128)(2,1)S(1)} %copy-done.1, f32[64,64]{1,0:T(8,128)S(1)} %copy-done.3, bf16[2048,128]{1,0:T(8,128)(2,1)S(1)} %copy-done.2), custom_call_target="tpu_custom_call" | custom-call | flops 8589934592 | bytes 1572864 | tf_op jit(solution)/shard_map/index_scores/pallas_call | solution.py:244
  48.6 3.4 %all-to-all-done.packed_ref = bf16[16,288,128]{2,1,0:T(8,128)(2,1)S(1)} async-done(((bf16[16,288,128]{2,1,0:T(8,128)(2,1)}), bf16[16,288,128]{2,1,0:T(8,128)(2,1)S(1)}, u32[]{:S(2)}, u32[]{:S(2)}) %all-to-all-start) | async-done | bytes 1179680 | tf_op jit(solution)/shard_map/all_to_all | solution.py:412
  52.1 3.4 %attend_own.1 = (f32[1024,128]{1,0:T(8,128)S(1)}, f32[1024,128]{1,0:T(8,128)S(1)}, f32[1024,512]{1,0:T(8,128)S(1)}, bf16[1024,576]{1,0:T(8,128)(2,1)S(1)}) custom-call(s32[8,128]{1,0:T(8,128)} %get-tuple-element.20.past_ref, bf16[16,288,128]{2,1,0:T(8,128)(2,1)S(1)} %all-to-all-done.packed_ref, bf16[576,384]{1,0:T(8,128)(2,1)} %get-tuple-element.27.up_ref, ...), custom_call_target="tpu_custom_call" | custom-call | flops 1140850688 | bytes 4456448 | tf_op jit(solution)/shard_map/attend_own/pallas_call | solution.py:307
  55.5 3.8 %collective-permute-done.4.plus_ref = bf16[576,384]{1,0:T(8,128)(2,1)S(1)} collective-permute-done((bf16[576,384]{1,0:T(8,128)(2,1)}, bf16[576,384]{1,0:T(8,128)(2,1)S(1)}, u32[]{:S(2)}, u32[]{:S(2)}) %collective-permute-start.4) | collective-permute-done | bytes 442400 | tf_op jit(solution)/shard_map/ppermute | solution.py:418
  59.3 0.0 collective-permute-done.5.minus_ref
  59.3 4.1 %attend_more.2 = (f32[1024,128]{1,0:T(8,128)S(1)}, f32[1024,128]{1,0:T(8,128)S(1)}, f32[1024,512]{1,0:T(8,128)S(1)}) custom-call(f32[1024,128]{1,0:T(8,128)S(1)} %get-tuple-element.29.top_ref, f32[1024,128]{1,0:T(8,128)S(1)} %get-tuple-element.30.total_ref, f32[1024,512]{1,0:T(8,128)S(1)} %get-tuple-element.31.mixed_ref, ...), custom_call_target="tpu_custom_call" | custom-call | flops 1711276032 | bytes 5505024 | tf_op jit(solution)/shard_map/attend_more/pallas_call | solution.py:379
  63.5 0.0 collective-permute-done.6.plus_ref
  63.5 0.0 collective-permute-done.7.minus_ref
  63.5 4.9 %attend_more.3 = bf16[1024,512]{1,0:T(8,128)(2,1)} custom-call(f32[1024,128]{1,0:T(8,128)S(1)} %get-tuple-element.33.top_ref, f32[1024,128]{1,0:T(8,128)S(1)} %get-tuple-element.34.total_ref, f32[1024,512]{1,0:T(8,128)S(1)} %get-tuple-element.35.mixed_ref, bf16[1024,576]{1,0:T(8,128)(2,1)S(1)} %get-tuple-element.32.q_ref, ...), custom_call_target="tpu_custom_call" | custom-call | flops 1711276032 | bytes 5505024 | tf_op jit(solution)/shard_map/attend_more/pallas_call | solution.py:379
Async XLA Ops:
  4.2 20.4 %copy-start = (bf16[8,128,576]{1,2,0:T(8,128)(2,1)S(1)}, bf16[8,128,576]{1,2,0:T(8,128)(2,1)}, u32[]{:S(2)}) copy-start(bf16[8,128,576]{1,2,0:T(8,128)(2,1)} %param.7) | copy-start | bytes 3538948
  4.2 9.7 %collective-permute-start = (bf16[576,256]{1,0:T(8,128)(2,1)S(1)}, bf16[576,256]{1,0:T(8,128)(2,1)S(1)}, u32[]{:S(2)}, u32[]{:S(2)}) collective-permute-start(bf16[576,256]{1,0:T(8,128)(2,1)S(1)} %get-tuple-element.23), channel_id=1, source_target_pairs={{0,32},{16,48},{32,64},{48,80},{64,96},{80,112},{96,0},{112,16},{1... | collective-permute-start | bytes 884744 | tf_op jit(solution)/shard_map/ppermute | solution.py:409
  6.3 15.2 %collective-permute-start.1 = (bf16[576,256]{1,0:T(8,128)(2,1)S(1)}, bf16[576,256]{1,0:T(8,128)(2,1)S(1)}, u32[]{:S(2)}, u32[]{:S(2)}) collective-permute-start(bf16[576,256]{1,0:T(8,128)(2,1)S(1)} %get-tuple-element.24), channel_id=1, source_target_pairs={{0,64},{16,80},{32,96},{48,112},{64,0},{80,16},{96,32},{112,48},{1... | collective-permute-start | bytes 884744 | tf_op jit(solution)/shard_map/ppermute | solution.py:409
  8.8 12.7 %collective-permute-start.2 = (bf16[576,256]{1,0:T(8,128)(2,1)S(1)}, bf16[576,256]{1,0:T(8,128)(2,1)S(1)}, u32[]{:S(2)}, u32[]{:S(2)}) collective-permute-start(bf16[576,256]{1,0:T(8,128)(2,1)S(1)} %get-tuple-element.25), channel_id=1, source_target_pairs={{0,96},{16,112},{32,0},{48,16},{64,32},{80,48},{96,64},{112,80},{1... | collective-permute-start | bytes 884744 | tf_op jit(solution)/shard_map/ppermute | solution.py:409
  23.0 12.6 %collective-permute-start.3 = (bf16[576,512]{1,0:T(8,128)(2,1)S(1)}, bf16[576,512]{1,0:T(8,128)(2,1)S(1)}, u32[]{:S(2)}, u32[]{:S(2)}) collective-permute-start(bf16[576,512]{1,0:T(8,128)(2,1)S(1)} %compact_parts.3), channel_id=1, source_target_pairs={{0,16},{16,0},{32,48},{48,32},{64,80},{80,64},{96,112},{112,96},{1... | collective-permute-start | bytes 1769480 | tf_op jit(solution)/shard_map/ppermute | solution.py:415
  26.2 25.9 %all-to-all-start = ((bf16[16,288,128]{2,1,0:T(8,128)(2,1)}), bf16[16,288,128]{2,1,0:T(8,128)(2,1)S(1)}, u32[]{:S(2)}, u32[]{:S(2)}) async-start(bf16[16,288,128]{2,1,0:T(8,128)(2,1)} %q_by_group.1), calls=%async_computation | async-start | bytes 2359296 | tf_op jit(solution)/shard_map/all_to_all | solution.py:412
  33.9 8.2 %copy-start.1 = (bf16[64,64,128]{2,1,0:T(8,128)(2,1)S(1)}, bf16[64,64,128]{2,1,0:T(8,128)(2,1)}, u32[]{:S(2)}) copy-start(bf16[64,64,128]{2,1,0:T(8,128)(2,1)} %query_ref.1) | copy-start | bytes 3145732
  33.9 8.2 %copy-start.2 = (bf16[2048,128]{1,0:T(8,128)(2,1)S(1)}, bf16[2048,128]{1,0:T(8,128)(2,1)}, u32[]{:S(2)}) copy-start(bf16[2048,128]{1,0:T(8,128)(2,1)} %keys_ref.1) | copy-start | bytes 1572868
  34.0 8.2 %copy-start.3 = (f32[64,64]{1,0:T(8,128)S(1)}, f32[64,64]{1,0:T(8,128)}, u32[]{:S(2)}) copy-start(f32[64,64]{1,0:T(8,128)} %weight_ref.1) | copy-start | bytes 49156
  36.8 22.5 %collective-permute-start.4 = (bf16[576,384]{1,0:T(8,128)(2,1)}, bf16[576,384]{1,0:T(8,128)(2,1)S(1)}, u32[]{:S(2)}, u32[]{:S(2)}) collective-permute-start(bf16[576,384]{1,0:T(8,128)(2,1)} %get-tuple-element.27.up_ref), channel_id=1, source_target_pairs={{0,4},{1,5},{2,6},{3,7},{4,8},{5,9},{6,10},{7,11},{8,12},{9,13},{1... | collective-permute-start | bytes 1327112 | tf_op jit(solution)/shard_map/ppermute | solution.py:418
  38.2 21.2 %collective-permute-start.5 = (bf16[576,384]{1,0:T(8,128)(2,1)}, bf16[576,384]{1,0:T(8,128)(2,1)S(1)}, u32[]{:S(2)}, u32[]{:S(2)}) collective-permute-start(bf16[576,384]{1,0:T(8,128)(2,1)} %get-tuple-element.28.down_ref), channel_id=1, source_target_pairs={{0,12},{1,13},{2,14},{3,15},{4,0},{5,1},{6,2},{7,3},{8,4},{9,5},{1... | collective-permute-start | bytes 1327112 | tf_op jit(solution)/shard_map/ppermute | solution.py:418
  39.5 24.0 %collective-permute-start.6 = (bf16[576,384]{1,0:T(8,128)(2,1)}, bf16[576,384]{1,0:T(8,128)(2,1)S(1)}, u32[]{:S(2)}, u32[]{:S(2)}) collective-permute-start(bf16[576,384]{1,0:T(8,128)(2,1)} %get-tuple-element.36), channel_id=1, source_target_pairs={{0,1},{1,2},{2,3},{3,0},{4,5},{5,6},{6,7},{7,4},{8,9},{9,10},{10,1... | collective-permute-start | bytes 1327112 | tf_op jit(solution)/shard_map/ppermute | solution.py:419
  40.8 22.6 %collective-permute-start.7 = (bf16[576,384]{1,0:T(8,128)(2,1)S(1)}, bf16[576,384]{1,0:T(8,128)(2,1)S(1)}, u32[]{:S(2)}, u32[]{:S(2)}) collective-permute-start(bf16[576,384]{1,0:T(8,128)(2,1)S(1)} %get-tuple-element.37), channel_id=1, source_target_pairs={{0,3},{1,0},{2,1},{3,2},{4,7},{5,4},{6,5},{7,6},{8,11},{9,8},{10,9... | collective-permute-start | bytes 1327112 | tf_op jit(solution)/shard_map/ppermute | solution.py:419

commit v11 on v8

--- a/solution.py
+++ b/solution.py
@@ -12,6 +12,7 @@
 SHARDS = 8
 PART = 16
 SCALE = 192.0 ** (-0.5)
+SCALE_LOG2 = SCALE * 1.4426950408889634
 INDEX_SCALE = 128.0 ** (-0.5)
 F32 = jnp.float32
 BF16 = jnp.bfloat16
@@ -286,13 +287,20 @@
         q_ref[low + 32 : low + 64, 512:] = packed_ref[g, 256:, 64:]
     keys_ref[:, :384] = up_ref[...]
     keys_ref[:, 384:] = down_ref[:, 256:]
-    rows, step = q_ref.shape[0], 256
+    rows, step = q_ref.shape[0], 512
+    lane = iota((step, 128), 1)
+
+    def scores_at(a):
+        limit = past + a // 8 + (iota((step, 128), 0) >> 3)
+        return masked_scores(q_ref[a : a + step, :], keys_ref[...], tiles, limit)
+
+    coming = scores_at(0)
     for a in range(0, rows, step):
-        limit = past + a // 8 + (iota((step, 128), 0) >> 3)
-        scores = masked_scores(q_ref[a : a + step, :], keys_ref[...], tiles, limit)
+        scores = coming
+        if a + step < rows:
+            coming = scores_at(a + step)
         top = jnp.max(scores, axis=1, keepdims=True)
-        weights = jnp.exp((scores - top) * SCALE)
-        lane = iota((step, 128), 1)
+        weights = jnp.exp2((scores - top) * SCALE_LOG2)
         top_ref[a : a + step, :] = jnp.where(lane < 64, top, past.astype(F32))
         total_ref[a : a + step, :] = jnp.broadcast_to(jnp.sum(weights, axis=1, keepdims=True), (step, 128))
         mixed_ref[a : a + step, :] = lax.dot_general(
@@ -342,20 +350,27 @@
     )
     for i, ref in enumerate((up_ref, down_ref, right_ref, left_ref)):
         keys_ref[:, i * 384 : (i + 1) * 384] = ref[...]
-    rows, step = q_ref.shape[0], 256
+    rows, step = q_ref.shape[0], 512
     copies = []
+
+    def scores_at(a):
+        limit = past + a // 8 + (iota((step, 128), 0) >> 3)
+        return masked_scores(q_ref[a : a + step, :], keys_ref[...], tiles, limit)
+
+    coming = scores_at(0)
     for a in range(0, rows, step):
-        limit = past + a // 8 + (iota((step, 128), 0) >> 3)
-        scores = masked_scores(q_ref[a : a + step, :], keys_ref[...], tiles, limit)
+        scores = coming
+        if a + step < rows:
+            coming = scores_at(a + step)
         before = top_ref[a : a + step, 0:1]
         top = jnp.maximum(jnp.max(scores, axis=1, keepdims=True), before)
-        weights = jnp.exp((scores - top) * SCALE)
-        fade = jnp.exp((before - top) * SCALE)
-        total = total_ref[a : a + step, 0:1] * fade + jnp.sum(weights, axis=1, keepdims=True)
-        mixed = mixed_ref[a : a + step, :] * fade + lax.dot_general(
+        weights = jnp.exp2((scores - top) * SCALE_LOG2)
+        fade = jnp.exp2((before - top) * SCALE_LOG2)
+        share = 1.0 / (total_ref[a : a + step, 0:1] * fade + jnp.sum(weights, axis=1, keepdims=True))
+        added = lax.dot_general(
             weights.astype(BF16), keys_ref[0:512, :], (((1,), (1,)), ((), ())), preferred_element_type=F32
         )
-        done_ref[a : a + step, :] = (mixed / total).astype(BF16)
+        done_ref[a : a + step, :] = ((mixed_ref[a : a + step, :] * fade + added) * share).astype(BF16)
         copies.append(
             pltpu.make_async_copy(
                 done_ref.at[pl.ds(a, step), :], out_ref.at[pl.ds(a, step), :], sems.at[a // step]
@@ -377,7 +392,7 @@
         scratch_shapes=[
             pltpu.VMEM((width, count), BF16),
             pltpu.VMEM((rows, 512), BF16),
-            pltpu.SemaphoreType.DMA((rows // 256,)),
+            pltpu.SemaphoreType.DMA((rows // 512,)),
         ],
         cost_estimate=pl.CostEstimate(
             flops=2 * rows * count * (width + 512), bytes_accessed=rows * 5376, transcendentals=rows * count
@@ -399,7 +414,8 @@
     rows, heads, _ = q_latent.shape
     groups = lax.axis_size("head")
     *outgoing, source, other, past = gather_parts(block_ids, block_counts, latent_cache.T)
-    incoming = [outgoing[0]] + [lax.ppermute(outgoing[d], "ctx", turn(2 * d)) for d in range(1, SHARDS // 2)]
+    incoming = [outgoing[0]] + [lax.ppermute(outgoing[d], "ctx", turn(2 * d)) for d in (2, 1, 3)]
+    incoming = [incoming[0], incoming[2], incoming[1], incoming[3]]
     by_group = q_by_group(q_latent, groups)
     head_query = lax.all_to_all(by_group, "head", split_axis=0, concat_axis=0, tiled=True)
     index_scores = index_scores_of(index_query, index_weight, index_keys)

time: 68.5 us -> 67.3 us (0.982)
  Pallas kernels: 26.9 us -> 25.1 us
  waiting for transfers between devices: 19.9 us -> 20.6 us
    pallas_call x1, Pallas kernels: 7.75 us -> 6.62 us  [attend_rest(): pl.pallas_call(rest_kernel, out_shape=jax.ShapeDtypeStruct((rows, 512), B...]
  transfers between devices with their start and end apart: 9 -> 9, of which waited for: 5 -> 5; matrix products, arithmetic and copies ran while one was open for 0% -> 0% of each run, Pallas kernels for 21% -> 20%
where the time goes in v11:
time: 67.3 us; the launch traced here: 67 us
  Pallas kernels  25.1 us (37%)
  waiting for transfers between devices  20.6 us (31%)
  starting transfers between devices  20.4 us (30%)
  between operations  0.88 us (1%)
    ppermute x3, waiting for transfers between devices, body(): lax.ppermute(outgoing[d], 'ctx', turn(2 * d))  11.6 us
    all_to_all x1, starting transfers between devices, body(): lax.all_to_all(by_group, 'head', split_axis=0, concat_axis=0, tiled=True)  7.77 us
    pallas_call x1, Pallas kernels, attend_rest(): pl.pallas_call(rest_kernel, out_shape=jax.ShapeDtypeStruct((rows, 512), B...  6.62 us
    pallas_call x1, Pallas kernels, index_scores_of(): pl.pallas_call(index_kernel, grid=(rows // step,), out_shape=jax.ShapeDty...  6.5 us
    ppermute x3, starting transfers between devices, body(): lax.ppermute(outgoing[d], 'ctx', turn(2 * d))  5.7 us
    ppermute x4, waiting for transfers between devices, body(): lax.ppermute(part, 'head', line(*step))  5.4 us
    ppermute x4, starting transfers between devices, body(): lax.ppermute(part, 'head', line(*step))  5.35 us
    all_to_all x1, waiting for transfers between devices, body(): lax.all_to_all(by_group, 'head', split_axis=0, concat_axis=0, tiled=True)  3.58 us
  transfers between devices with their start and end apart: 9, of which 5 were waited for; matrix products, arithmetic and copies ran while one was open for 0% of the time, Pallas kernels for 20%

profile of v11, /device:TPU:1, one launch (start us, length us, event | category | flops | bytes accessed | tf_op | source)
XLA Modules:
  0.0 67.0 jit_solution(7497236360528184872)
XLA Ops:
  0.6 3.6 %gather_parts.1 = (bf16[576,256]{1,0:T(8,128)(2,1)}, bf16[576,256]{1,0:T(8,128)(2,1)S(1)}, bf16[576,256]{1,0:T(8,128)(2,1)S(1)}, bf16[576,256]{1,0:T(8,128)(2,1)...) custom-call(s32[8,32]{1,0:T(8,128)} %ids_hbm.1, s32[8]{0:T(128)} %counts_hbm.1, bf16[576,2048]{1,0:T(8,128)(2,1)} %bitcast.4), custom_call_target="tpu_custom_call" | custom-call | flops 2415919104 | bytes 4718592 | tf_op jit(solution)/shard_map/gather_parts/pallas_call | solution.py:128
  4.2 0.0 copy-start
  4.2 2.1 %collective-permute-start = (bf16[576,256]{1,0:T(8,128)(2,1)S(1)}, bf16[576,256]{1,0:T(8,128)(2,1)S(1)}, u32[]{:S(2)}, u32[]{:S(2)}) collective-permute-start(bf16[576,256]{1,0:T(8,128)(2,1)S(1)} %get-tuple-element.20), channel_id=1, source_target_pairs={{0,32},{16,48},{32,64},{48,80},{64,96},{80,112},{96,0},{112,16},{1... | collective-permute-start | bytes 884744 | tf_op jit(solution)/shard_map/ppermute | solution.py:417
  6.3 2.5 %collective-permute-start.1 = (bf16[576,256]{1,0:T(8,128)(2,1)S(1)}, bf16[576,256]{1,0:T(8,128)(2,1)S(1)}, u32[]{:S(2)}, u32[]{:S(2)}) collective-permute-start(bf16[576,256]{1,0:T(8,128)(2,1)S(1)} %get-tuple-element.21), channel_id=1, source_target_pairs={{0,64},{16,80},{32,96},{48,112},{64,0},{80,16},{96,32},{112,48},{1... | collective-permute-start | bytes 884744 | tf_op jit(solution)/shard_map/ppermute | solution.py:417
  8.8 1.2 %collective-permute-start.2 = (bf16[576,256]{1,0:T(8,128)(2,1)S(1)}, bf16[576,256]{1,0:T(8,128)(2,1)S(1)}, u32[]{:S(2)}, u32[]{:S(2)}) collective-permute-start(bf16[576,256]{1,0:T(8,128)(2,1)S(1)} %get-tuple-element.22), channel_id=1, source_target_pairs={{0,96},{16,112},{32,0},{48,16},{64,32},{80,48},{96,64},{112,80},{1... | collective-permute-start | bytes 884744 | tf_op jit(solution)/shard_map/ppermute | solution.py:417
  9.9 4.0 %collective-permute-done.refs_1_ = bf16[576,256]{1,0:T(8,128)(2,1)S(1)} collective-permute-done((bf16[576,256]{1,0:T(8,128)(2,1)S(1)}, bf16[576,256]{1,0:T(8,128)(2,1)S(1)}, u32[]{:S(2)}, u32[]{:S(2)}) %collective-permute-start) | collective-permute-done | bytes 294944 | tf_op jit(solution)/shard_map/ppermute | solution.py:417
  13.9 7.6 %collective-permute-done.1.refs_2_ = bf16[576,256]{1,0:T(8,128)(2,1)S(1)} collective-permute-done((bf16[576,256]{1,0:T(8,128)(2,1)S(1)}, bf16[576,256]{1,0:T(8,128)(2,1)S(1)}, u32[]{:S(2)}, u32[]{:S(2)}) %collective-permute-start.1) | collective-permute-done | bytes 294944 | tf_op jit(solution)/shard_map/ppermute | solution.py:417
  21.5 0.0 collective-permute-done.2.refs_3_
  21.5 1.5 %compact_parts.3 = bf16[576,512]{1,0:T(8,128)(2,1)S(1)} custom-call(s32[8,512]{1,0:T(8,128)} %get-tuple-element.23.source_ref, bf16[576,256]{1,0:T(8,128)(2,1)} %get-tuple-element.19.refs_0_, bf16[576,256]{1,0:T(8,128)(2,1)S(1)} %collective-permute-done.refs_1_, bf16[576,256]{1,0:T(8,128)(2,1)S(1)} %collective-permute-done.1.refs_2_, ...), custom_call_target="tpu_custom_call" | custom-call | flops 301989888 | bytes 1769472 | tf_op jit(solution)/shard_map/compact_parts/pallas_call | solution.py:164
  23.0 1.6 %collective-permute-start.3 = (bf16[576,512]{1,0:T(8,128)(2,1)S(1)}, bf16[576,512]{1,0:T(8,128)(2,1)S(1)}, u32[]{:S(2)}, u32[]{:S(2)}) collective-permute-start(bf16[576,512]{1,0:T(8,128)(2,1)S(1)} %compact_parts.3), channel_id=1, source_target_pairs={{0,16},{16,0},{32,48},{48,32},{64,80},{80,64},{96,112},{112,96},{1... | collective-permute-start | bytes 1769480 | tf_op jit(solution)/shard_map/ppermute | solution.py:423
  24.6 0.0 copy-done
  24.6 1.6 %q_by_group.1 = bf16[16,288,128]{2,1,0:T(8,128)(2,1)} custom-call(bf16[8,576,128]{2,1,0:T(8,128)(2,1)S(1)} %bitcast.3), custom_call_target="tpu_custom_call" | custom-call | bytes 2359296 | tf_op jit(solution)/shard_map/q_by_group/pallas_call | solution.py:216
  26.1 7.8 %all-to-all-start = ((bf16[16,288,128]{2,1,0:T(8,128)(2,1)}), bf16[16,288,128]{2,1,0:T(8,128)(2,1)S(1)}, u32[]{:S(2)}, u32[]{:S(2)}) async-start(bf16[16,288,128]{2,1,0:T(8,128)(2,1)} %q_by_group.1), calls=%async_computation | async-start | bytes 2359296 | tf_op jit(solution)/shard_map/all_to_all | solution.py:420
  33.9 0.0 copy-start.1
  33.9 0.0 copy-start.2
  33.9 0.0 copy-start.3
  33.9 1.6 %compact_parts.2.own_ref = bf16[576,512]{1,0:T(8,128)(2,1)S(1)} custom-call(s32[8,512]{1,0:T(8,128)} %get-tuple-element.18.source_ref, bf16[576,256]{1,0:T(8,128)(2,1)} %get-tuple-element.19.refs_0_, bf16[576,256]{1,0:T(8,128)(2,1)S(1)} %collective-permute-done.refs_1_, bf16[576,256]{1,0:T(8,128)(2,1)S(1)} %collective-permute-done.1.refs_2_, ...), custom_call_target="tpu_custom_call" | custom-call | flops 301989888 | bytes 1769472 | tf_op jit(solution)/shard_map/compact_parts/pallas_call | solution.py:164
  35.5 0.0 collective-permute-done.3.other_ref
  35.5 1.1 %spread_parts.1 = (bf16[576,384]{1,0:T(8,128)(2,1)}, bf16[576,384]{1,0:T(8,128)(2,1)}, bf16[576,384]{1,0:T(8,128)(2,1)S(1)}, bf16[576,384]{1,0:T(8,128)(2,1)S(1)}) custom-call(bf16[576,512]{1,0:T(8,128)(2,1)S(1)} %compact_parts.2.own_ref, bf16[576,512]{1,0:T(8,128)(2,1)S(1)} %collective-permute-done.3.other_ref), custom_call_target="tpu_custom_call" | custom-call | flops 294912 | bytes 2949120 | tf_op jit(solution)/shard_map/spread_parts/pallas_call | solution.py:190
  36.6 1.4 %collective-permute-start.4 = (bf16[576,384]{1,0:T(8,128)(2,1)}, bf16[576,384]{1,0:T(8,128)(2,1)S(1)}, u32[]{:S(2)}, u32[]{:S(2)}) collective-permute-start(bf16[576,384]{1,0:T(8,128)(2,1)} %get-tuple-element.24.up_ref), channel_id=1, source_target_pairs={{0,4},{1,5},{2,6},{3,7},{4,8},{5,9},{6,10},{7,11},{8,12},{9,13},{1... | collective-permute-start | bytes 1327112 | tf_op jit(solution)/shard_map/ppermute | solution.py:427
  38.0 1.3 %collective-permute-start.5 = (bf16[576,384]{1,0:T(8,128)(2,1)}, bf16[576,384]{1,0:T(8,128)(2,1)S(1)}, u32[]{:S(2)}, u32[]{:S(2)}) collective-permute-start(bf16[576,384]{1,0:T(8,128)(2,1)} %get-tuple-element.25.down_ref), channel_id=1, source_target_pairs={{0,12},{1,13},{2,14},{3,15},{4,0},{5,1},{6,2},{7,3},{8,4},{9,5},{1... | collective-permute-start | bytes 1327112 | tf_op jit(solution)/shard_map/ppermute | solution.py:427
  39.3 1.4 %collective-permute-start.6 = (bf16[576,384]{1,0:T(8,128)(2,1)S(1)}, bf16[576,384]{1,0:T(8,128)(2,1)S(1)}, u32[]{:S(2)}, u32[]{:S(2)}) collective-permute-start(bf16[576,384]{1,0:T(8,128)(2,1)S(1)} %get-tuple-element.30), channel_id=1, source_target_pairs={{0,1},{1,2},{2,3},{3,0},{4,5},{5,6},{6,7},{7,4},{8,9},{9,10},{10,1... | collective-permute-start | bytes 1327112 | tf_op jit(solution)/shard_map/ppermute | solution.py:427
  40.7 1.3 %collective-permute-start.7 = (bf16[576,384]{1,0:T(8,128)(2,1)S(1)}, bf16[576,384]{1,0:T(8,128)(2,1)}, u32[]{:S(2)}, u32[]{:S(2)}) collective-permute-start(bf16[576,384]{1,0:T(8,128)(2,1)S(1)} %get-tuple-element.31), channel_id=1, source_target_pairs={{0,3},{1,0},{2,1},{3,2},{4,7},{5,4},{6,5},{7,6},{8,11},{9,8},{10,9... | collective-permute-start | bytes 1327112 | tf_op jit(solution)/shard_map/ppermute | solution.py:427
  42.0 0.0 copy-done.1
  42.0 0.0 copy-done.2
  42.0 0.0 copy-done.3
  42.0 6.5 %index_scores.1 = f32[64,2048]{1,0:T(8,128)} custom-call(bf16[64,64,128]{2,1,0:T(8,128)(2,1)S(1)} %copy-done.1, f32[64,64]{1,0:T(8,128)S(1)} %copy-done.3, bf16[2048,128]{1,0:T(8,128)(2,1)S(1)} %copy-done.2), custom_call_target="tpu_custom_call" | custom-call | flops 8589934592 | bytes 1572864 | tf_op jit(solution)/shard_map/index_scores/pallas_call | solution.py:245
  48.5 3.6 %all-to-all-done.packed_ref = bf16[16,288,128]{2,1,0:T(8,128)(2,1)S(1)} async-done(((bf16[16,288,128]{2,1,0:T(8,128)(2,1)}), bf16[16,288,128]{2,1,0:T(8,128)(2,1)S(1)}, u32[]{:S(2)}, u32[]{:S(2)}) %all-to-all-start) | async-done | bytes 1179680 | tf_op jit(solution)/shard_map/all_to_all | solution.py:420
  52.1 2.8 %attend_own.1 = (f32[1024,128]{1,0:T(8,128)S(1)}, f32[1024,128]{1,0:T(8,128)S(1)}, f32[1024,512]{1,0:T(8,128)S(1)}, bf16[1024,576]{1,0:T(8,128)(2,1)S(1)}) custom-call(s32[8,128]{1,0:T(8,128)} %get-tuple-element.17.past_ref, bf16[16,288,128]{2,1,0:T(8,128)(2,1)S(1)} %all-to-all-done.packed_ref, bf16[576,384]{1,0:T(8,128)(2,1)} %get-tuple-element.24.up_ref, ...), custom_call_target="tpu_custom_call" | custom-call | flops 1140850688 | bytes 4456448 | tf_op jit(solution)/shard_map/attend_own/pallas_call | solution.py:315
  54.8 4.5 %collective-permute-done.4.up_ref = bf16[576,384]{1,0:T(8,128)(2,1)S(1)} collective-permute-done((bf16[576,384]{1,0:T(8,128)(2,1)}, bf16[576,384]{1,0:T(8,128)(2,1)S(1)}, u32[]{:S(2)}, u32[]{:S(2)}) %collective-permute-start.4) | collective-permute-done | bytes 442400 | tf_op jit(solution)/shard_map/ppermute | solution.py:427
  59.3 0.0 collective-permute-done.5.down_ref
  59.3 0.9 %collective-permute-done.6.right_ref = bf16[576,384]{1,0:T(8,128)(2,1)S(1)} collective-permute-done((bf16[576,384]{1,0:T(8,128)(2,1)S(1)}, bf16[576,384]{1,0:T(8,128)(2,1)S(1)}, u32[]{:S(2)}, u32[]{:S(2)}) %collective-permute-start.6) | collective-permute-done | bytes 442400 | tf_op jit(solution)/shard_map/ppermute | solution.py:427
  60.2 0.0 collective-permute-done.7.left_ref
  60.2 6.6 %attend_rest.1 = bf16[1024,512]{1,0:T(8,128)(2,1)} custom-call(f32[1024,128]{1,0:T(8,128)S(1)} %get-tuple-element.26.top_ref, f32[1024,128]{1,0:T(8,128)S(1)} %get-tuple-element.27.total_ref, f32[1024,512]{1,0:T(8,128)S(1)} %get-tuple-element.28.mixed_ref, bf16[1024,576]{1,0:T(8,128)(2,1)S(1)} %get-tuple-element.29.q_ref, ...), custom_call_target="tpu_custom_call" | custom-call | flops 3422552064 | bytes 5505024 | tf_op jit(solution)/shard_map/attend_rest/pallas_call | solution.py:387
Async XLA Ops:
  4.2 20.4 %copy-start = (bf16[8,128,576]{1,2,0:T(8,128)(2,1)S(1)}, bf16[8,128,576]{1,2,0:T(8,128)(2,1)}, u32[]{:S(2)}) copy-start(bf16[8,128,576]{1,2,0:T(8,128)(2,1)} %param.7) | copy-start | bytes 3538948
  4.2 9.7 %collective-permute-start = (bf16[576,256]{1,0:T(8,128)(2,1)S(1)}, bf16[576,256]{1,0:T(8,128)(2,1)S(1)}, u32[]{:S(2)}, u32[]{:S(2)}) collective-permute-start(bf16[576,256]{1,0:T(8,128)(2,1)S(1)} %get-tuple-element.20), channel_id=1, source_target_pairs={{0,32},{16,48},{32,64},{48,80},{64,96},{80,112},{96,0},{112,16},{1... | collective-permute-start | bytes 884744 | tf_op jit(solution)/shard_map/ppermute | solution.py:417
  6.3 15.2 %collective-permute-start.1 = (bf16[576,256]{1,0:T(8,128)(2,1)S(1)}, bf16[576,256]{1,0:T(8,128)(2,1)S(1)}, u32[]{:S(2)}, u32[]{:S(2)}) collective-permute-start(bf16[576,256]{1,0:T(8,128)(2,1)S(1)} %get-tuple-element.21), channel_id=1, source_target_pairs={{0,64},{16,80},{32,96},{48,112},{64,0},{80,16},{96,32},{112,48},{1... | collective-permute-start | bytes 884744 | tf_op jit(solution)/shard_map/ppermute | solution.py:417
  8.8 12.7 %collective-permute-start.2 = (bf16[576,256]{1,0:T(8,128)(2,1)S(1)}, bf16[576,256]{1,0:T(8,128)(2,1)S(1)}, u32[]{:S(2)}, u32[]{:S(2)}) collective-permute-start(bf16[576,256]{1,0:T(8,128)(2,1)S(1)} %get-tuple-element.22), channel_id=1, source_target_pairs={{0,96},{16,112},{32,0},{48,16},{64,32},{80,48},{96,64},{112,80},{1... | collective-permute-start | bytes 884744 | tf_op jit(solution)/shard_map/ppermute | solution.py:417
  23.0 12.6 %collective-permute-start.3 = (bf16[576,512]{1,0:T(8,128)(2,1)S(1)}, bf16[576,512]{1,0:T(8,128)(2,1)S(1)}, u32[]{:S(2)}, u32[]{:S(2)}) collective-permute-start(bf16[576,512]{1,0:T(8,128)(2,1)S(1)} %compact_parts.3), channel_id=1, source_target_pairs={{0,16},{16,0},{32,48},{48,32},{64,80},{80,64},{96,112},{112,96},{1... | collective-permute-start | bytes 1769480 | tf_op jit(solution)/shard_map/ppermute | solution.py:423
  26.1 25.9 %all-to-all-start = ((bf16[16,288,128]{2,1,0:T(8,128)(2,1)}), bf16[16,288,128]{2,1,0:T(8,128)(2,1)S(1)}, u32[]{:S(2)}, u32[]{:S(2)}) async-start(bf16[16,288,128]{2,1,0:T(8,128)(2,1)} %q_by_group.1), calls=%async_computation | async-start | bytes 2359296 | tf_op jit(solution)/shard_map/all_to_all | solution.py:420
  33.9 8.1 %copy-start.1 = (bf16[64,64,128]{2,1,0:T(8,128)(2,1)S(1)}, bf16[64,64,128]{2,1,0:T(8,128)(2,1)}, u32[]{:S(2)}) copy-start(bf16[64,64,128]{2,1,0:T(8,128)(2,1)} %query_ref.1) | copy-start | bytes 3145732
  33.9 8.1 %copy-start.2 = (bf16[2048,128]{1,0:T(8,128)(2,1)S(1)}, bf16[2048,128]{1,0:T(8,128)(2,1)}, u32[]{:S(2)}) copy-start(bf16[2048,128]{1,0:T(8,128)(2,1)} %keys_ref.1) | copy-start | bytes 1572868
  33.9 8.0 %copy-start.3 = (f32[64,64]{1,0:T(8,128)S(1)}, f32[64,64]{1,0:T(8,128)}, u32[]{:S(2)}) copy-start(f32[64,64]{1,0:T(8,128)} %weight_ref.1) | copy-start | bytes 49156
  36.6 22.7 %collective-permute-start.4 = (bf16[576,384]{1,0:T(8,128)(2,1)}, bf16[576,384]{1,0:T(8,128)(2,1)S(1)}, u32[]{:S(2)}, u32[]{:S(2)}) collective-permute-start(bf16[576,384]{1,0:T(8,128)(2,1)} %get-tuple-element.24.up_ref), channel_id=1, source_target_pairs={{0,4},{1,5},{2,6},{3,7},{4,8},{5,9},{6,10},{7,11},{8,12},{9,13},{1... | collective-permute-start | bytes 1327112 | tf_op jit(solution)/shard_map/ppermute | solution.py:427
  38.0 21.3 %collective-permute-start.5 = (bf16[576,384]{1,0:T(8,128)(2,1)}, bf16[576,384]{1,0:T(8,128)(2,1)S(1)}, u32[]{:S(2)}, u32[]{:S(2)}) collective-permute-start(bf16[576,384]{1,0:T(8,128)(2,1)} %get-tuple-element.25.down_ref), channel_id=1, source_target_pairs={{0,12},{1,13},{2,14},{3,15},{4,0},{5,1},{6,2},{7,3},{8,4},{9,5},{1... | collective-permute-start | bytes 1327112 | tf_op jit(solution)/shard_map/ppermute | solution.py:427
  39.3 20.9 %collective-permute-start.6 = (bf16[576,384]{1,0:T(8,128)(2,1)S(1)}, bf16[576,384]{1,0:T(8,128)(2,1)S(1)}, u32[]{:S(2)}, u32[]{:S(2)}) collective-permute-start(bf16[576,384]{1,0:T(8,128)(2,1)S(1)} %get-tuple-element.30), channel_id=1, source_target_pairs={{0,1},{1,2},{2,3},{3,0},{4,5},{5,6},{6,7},{7,4},{8,9},{9,10},{10,1... | collective-permute-start | bytes 1327112 | tf_op jit(solution)/shard_map/ppermute | solution.py:427
  40.7 19.6 %collective-permute-start.7 = (bf16[576,384]{1,0:T(8,128)(2,1)S(1)}, bf16[576,384]{1,0:T(8,128)(2,1)}, u32[]{:S(2)}, u32[]{:S(2)}) collective-permute-start(bf16[576,384]{1,0:T(8,128)(2,1)S(1)} %get-tuple-element.31), channel_id=1, source_target_pairs={{0,3},{1,0},{2,1},{3,2},{4,7},{5,4},{6,5},{7,6},{8,11},{9,8},{10,9... | collective-permute-start | bytes 1327112 | tf_op jit(solution)/shard_map/ppermute | solution.py:427

commit v12 on v11

--- a/solution.py
+++ b/solution.py
@@ -176,9 +176,8 @@
     first = own_ref[:, :256] + other_ref[:, :256]
     second = own_ref[:, 256:] + other_ref[:, 256:]
     up_ref[:, :256] = first
-    up_ref[:, 256:] = second[:, :128]
-    down_ref[:, :256] = first
-    down_ref[:, 256:] = second[:, 128:]
+    up_ref[:, 256:] = second
+    down_ref[...] = first
     right_ref[:, :256] = second
     right_ref[:, 256:] = first[:, :128]
     left_ref[:, :256] = second
@@ -189,7 +188,7 @@
     width = own.shape[0]
     return pl.pallas_call(
         spread_kernel,
-        out_shape=[jax.ShapeDtypeStruct((width, 384), BF16)] * 4,
+        out_shape=[jax.ShapeDtypeStruct((width, n), BF16) for n in (512, 256, 384, 384)],
         in_specs=[VMEM] * 2,
         out_specs=[VMEM] * 4,
         cost_estimate=pl.CostEstimate(flops=width * 512, bytes_accessed=width * 2560 * 2, transcendentals=0),
@@ -274,7 +273,7 @@
     return jnp.concatenate(pieces, axis=1)
 
 
-def own_kernel(past_ref, packed_ref, up_ref, down_ref, top_ref, total_ref, mixed_ref, q_ref, keys_ref):
+def own_kernel(past_ref, packed_ref, keys_ref, top_ref, total_ref, mixed_ref, q_ref):
     _, first, second = place()
     past = past_ref[0:1, :]
     late = 16 * BLOCK
@@ -285,8 +284,6 @@
             q_ref[low : low + 64, t * 128 : (t + 1) * 128] = packed_ref[g, t * 64 : (t + 1) * 64, :]
         q_ref[low : low + 32, 512:] = packed_ref[g, 256:, :64]
         q_ref[low + 32 : low + 64, 512:] = packed_ref[g, 256:, 64:]
-    keys_ref[:, :384] = up_ref[...]
-    keys_ref[:, 384:] = down_ref[:, 256:]
     rows, step = q_ref.shape[0], 512
     lane = iota((step, 128), 1)
 
@@ -308,8 +305,8 @@
         )
 
 
-def attend_own(past, packed, up, down):
-    width = up.shape[0]
+def attend_own(past, packed, keys):
+    width = keys.shape[0]
     rows = packed.size // width
     count = 512
     return pl.pallas_call(
@@ -320,15 +317,14 @@
             jax.ShapeDtypeStruct((rows, 512), F32),
             jax.ShapeDtypeStruct((rows, width), BF16),
         ],
-        in_specs=[VMEM] * 4,
+        in_specs=[VMEM] * 3,
         out_specs=[VMEM] * 4,
-        scratch_shapes=[pltpu.VMEM((width, count), BF16)],
         cost_estimate=pl.CostEstimate(
             flops=2 * rows * count * (width + 512), bytes_accessed=rows * 4352, transcendentals=rows * count
         ),
         compiler_params=pltpu.CompilerParams(vmem_limit_bytes=16 << 20),
         name="attend_own",
-    )(in_hbm(past), packed, up, down)
+    )(in_hbm(past), packed, keys)
 
 
 def rest_kernel(top_ref, total_ref, mixed_ref, q_ref, up_ref, down_ref, right_ref, left_ref, out_ref, keys_ref, done_ref, sems):
@@ -343,13 +339,15 @@
         return late + 32 + ((second + step) & 3) * 8
 
     tiles = (
-        (None, of_first(-1), None)
-        + (None, of_first(1), of_second(2))
+        (None, of_first(-1), None, of_second(2))
+        + (None, of_first(1))
         + (None, of_second(-1), None)
         + (None, of_second(1), of_first(2))
     )
-    for i, ref in enumerate((up_ref, down_ref, right_ref, left_ref)):
-        keys_ref[:, i * 384 : (i + 1) * 384] = ref[...]
+    low = 0
+    for ref in (up_ref, down_ref, right_ref, left_ref):
+        keys_ref[:, low : low + ref.shape[1]] = ref[...]
+        low += ref.shape[1]
     rows, step = q_ref.shape[0], 512
     copies = []
 
@@ -423,11 +421,12 @@
     theirs = lax.ppermute(theirs, "ctx", [(i, i ^ 1) for i in range(SHARDS)])
     mine = compact_parts(0, source, incoming)
     up, down, right, left = spread_parts(mine, theirs)
-    parts = [
-        lax.ppermute(part, "head", line(*step))
-        for part, step in ((up, (1, 0)), (down, (-1, 0)), (right, (0, 1)), (left, (0, -1)))
-    ]
-    state = attend_own(past, head_query, up, down)
+    from_up = lax.ppermute(up, "head", line(1, 0))
+    from_right = lax.ppermute(right, "head", line(0, 1))
+    from_left = lax.ppermute(left, "head", line(0, -1))
+    from_down = lax.ppermute(down, "head", line(-1, 0))
+    parts = (from_up, from_down, from_right, from_left)
+    state = attend_own(past, head_query, up)
     attention = attend_rest(state, parts)
     return attention.reshape(rows * groups, heads // groups, 512), index_scores
 

time: 67.3 us -> 69.5 us (1.033)
  waiting for transfers between devices: 20.6 us -> 23.2 us
    ppermute x4, waiting for transfers between devices: 5.4 us -> 8.11 us  [the longest x1 5.15 us: body(): from_right = lax.ppermute(right, 'head', line(0, 1))]
  transfers between devices with their start and end apart: 9 -> 9, of which waited for: 5 -> 6; matrix products, arithmetic and copies ran while one was open for 0% -> 0% of each run, Pallas kernels for 20% -> 19%
where the time goes in v12:
time: 69.5 us; the launch traced here: 69.2 us
  Pallas kernels  24.7 us (36%)
  waiting for transfers between devices  23.2 us (33%)
  starting transfers between devices  20.4 us (29%)
  between operations  0.88 us (1%)
    ppermute x3, waiting for transfers between devices, body(): lax.ppermute(outgoing[d], 'ctx', turn(2 * d))  11.6 us
    all_to_all x1, starting transfers between devices, body(): lax.all_to_all(by_group, 'head', split_axis=0, concat_axis=0, tiled=True)  7.77 us
    pallas_call x1, Pallas kernels, attend_rest(): pl.pallas_call(rest_kernel, out_shape=jax.ShapeDtypeStruct((rows, 512), B...  6.61 us
    pallas_call x1, Pallas kernels, index_scores_of(): pl.pallas_call(index_kernel, grid=(rows // step,), out_shape=jax.ShapeDty...  6.57 us
    ppermute x3, starting transfers between devices, body(): lax.ppermute(outgoing[d], 'ctx', turn(2 * d))  5.7 us
    ppermute x1, waiting for transfers between devices, body(): from_right = lax.ppermute(right, 'head', line(0, 1))  5.15 us
    pallas_call x1, Pallas kernels, gather_parts(): pl.pallas_call(gather_kernel, out_shape=[pltpu.HBM((width, 256), BF16)] +...  3.56 us
    all_to_all x1, waiting for transfers between devices, body(): lax.all_to_all(by_group, 'head', split_axis=0, concat_axis=0, tiled=True)  3.53 us
  transfers between devices with their start and end apart: 9, of which 6 were waited for; matrix products, arithmetic and copies ran while one was open for 0% of the time, Pallas kernels for 19%

profile of v12, /device:TPU:1, one launch (start us, length us, event | category | flops | bytes accessed | tf_op | source)
XLA Modules:
  0.0 69.2 jit_solution(17036209048164020355)
XLA Ops:
  0.6 3.6 %gather_parts.1 = (bf16[576,256]{1,0:T(8,128)(2,1)}, bf16[576,256]{1,0:T(8,128)(2,1)S(1)}, bf16[576,256]{1,0:T(8,128)(2,1)S(1)}, bf16[576,256]{1,0:T(8,128)(2,1)...) custom-call(s32[8,32]{1,0:T(8,128)} %ids_hbm.1, s32[8]{0:T(128)} %counts_hbm.1, bf16[576,2048]{1,0:T(8,128)(2,1)} %bitcast.4), custom_call_target="tpu_custom_call" | custom-call | flops 2415919104 | bytes 4718592 | tf_op jit(solution)/shard_map/gather_parts/pallas_call | solution.py:128
  4.2 0.0 copy-start
  4.2 2.1 %collective-permute-start = (bf16[576,256]{1,0:T(8,128)(2,1)S(1)}, bf16[576,256]{1,0:T(8,128)(2,1)S(1)}, u32[]{:S(2)}, u32[]{:S(2)}) collective-permute-start(bf16[576,256]{1,0:T(8,128)(2,1)S(1)} %get-tuple-element.20), channel_id=1, source_target_pairs={{0,32},{16,48},{32,64},{48,80},{64,96},{80,112},{96,0},{112,16},{1... | collective-permute-start | bytes 884744 | tf_op jit(solution)/shard_map/ppermute | solution.py:415
  6.3 2.5 %collective-permute-start.1 = (bf16[576,256]{1,0:T(8,128)(2,1)S(1)}, bf16[576,256]{1,0:T(8,128)(2,1)S(1)}, u32[]{:S(2)}, u32[]{:S(2)}) collective-permute-start(bf16[576,256]{1,0:T(8,128)(2,1)S(1)} %get-tuple-element.21), channel_id=1, source_target_pairs={{0,64},{16,80},{32,96},{48,112},{64,0},{80,16},{96,32},{112,48},{1... | collective-permute-start | bytes 884744 | tf_op jit(solution)/shard_map/ppermute | solution.py:415
  8.8 1.2 %collective-permute-start.2 = (bf16[576,256]{1,0:T(8,128)(2,1)S(1)}, bf16[576,256]{1,0:T(8,128)(2,1)S(1)}, u32[]{:S(2)}, u32[]{:S(2)}) collective-permute-start(bf16[576,256]{1,0:T(8,128)(2,1)S(1)} %get-tuple-element.22), channel_id=1, source_target_pairs={{0,96},{16,112},{32,0},{48,16},{64,32},{80,48},{96,64},{112,80},{1... | collective-permute-start | bytes 884744 | tf_op jit(solution)/shard_map/ppermute | solution.py:415
  9.9 4.0 %collective-permute-done.refs_1_ = bf16[576,256]{1,0:T(8,128)(2,1)S(1)} collective-permute-done((bf16[576,256]{1,0:T(8,128)(2,1)S(1)}, bf16[576,256]{1,0:T(8,128)(2,1)S(1)}, u32[]{:S(2)}, u32[]{:S(2)}) %collective-permute-start) | collective-permute-done | bytes 294944 | tf_op jit(solution)/shard_map/ppermute | solution.py:415
  13.9 7.6 %collective-permute-done.1.refs_2_ = bf16[576,256]{1,0:T(8,128)(2,1)S(1)} collective-permute-done((bf16[576,256]{1,0:T(8,128)(2,1)S(1)}, bf16[576,256]{1,0:T(8,128)(2,1)S(1)}, u32[]{:S(2)}, u32[]{:S(2)}) %collective-permute-start.1) | collective-permute-done | bytes 294944 | tf_op jit(solution)/shard_map/ppermute | solution.py:415
  21.5 0.0 collective-permute-done.2.refs_3_
  21.5 1.5 %compact_parts.3 = bf16[576,512]{1,0:T(8,128)(2,1)S(1)} custom-call(s32[8,512]{1,0:T(8,128)} %get-tuple-element.23.source_ref, bf16[576,256]{1,0:T(8,128)(2,1)} %get-tuple-element.19.refs_0_, bf16[576,256]{1,0:T(8,128)(2,1)S(1)} %collective-permute-done.refs_1_, bf16[576,256]{1,0:T(8,128)(2,1)S(1)} %collective-permute-done.1.refs_2_, ...), custom_call_target="tpu_custom_call" | custom-call | flops 301989888 | bytes 1769472 | tf_op jit(solution)/shard_map/compact_parts/pallas_call | solution.py:164
  23.0 1.6 %collective-permute-start.3 = (bf16[576,512]{1,0:T(8,128)(2,1)S(1)}, bf16[576,512]{1,0:T(8,128)(2,1)S(1)}, u32[]{:S(2)}, u32[]{:S(2)}) collective-permute-start(bf16[576,512]{1,0:T(8,128)(2,1)S(1)} %compact_parts.3), channel_id=1, source_target_pairs={{0,16},{16,0},{32,48},{48,32},{64,80},{80,64},{96,112},{112,96},{1... | collective-permute-start | bytes 1769480 | tf_op jit(solution)/shard_map/ppermute | solution.py:421
  24.6 0.0 copy-done
  24.6 1.6 %q_by_group.1 = bf16[16,288,128]{2,1,0:T(8,128)(2,1)} custom-call(bf16[8,576,128]{2,1,0:T(8,128)(2,1)S(1)} %bitcast.3), custom_call_target="tpu_custom_call" | custom-call | bytes 2359296 | tf_op jit(solution)/shard_map/q_by_group/pallas_call | solution.py:215
  26.1 7.8 %all-to-all-start = ((bf16[16,288,128]{2,1,0:T(8,128)(2,1)}), bf16[16,288,128]{2,1,0:T(8,128)(2,1)S(1)}, u32[]{:S(2)}, u32[]{:S(2)}) async-start(bf16[16,288,128]{2,1,0:T(8,128)(2,1)} %q_by_group.1), calls=%async_computation | async-start | bytes 2359296 | tf_op jit(solution)/shard_map/all_to_all | solution.py:418
  33.9 0.0 copy-start.1
  33.9 0.0 copy-start.2
  33.9 0.0 copy-start.3
  33.9 1.6 %compact_parts.2.own_ref = bf16[576,512]{1,0:T(8,128)(2,1)S(1)} custom-call(s32[8,512]{1,0:T(8,128)} %get-tuple-element.18.source_ref, bf16[576,256]{1,0:T(8,128)(2,1)} %get-tuple-element.19.refs_0_, bf16[576,256]{1,0:T(8,128)(2,1)S(1)} %collective-permute-done.refs_1_, bf16[576,256]{1,0:T(8,128)(2,1)S(1)} %collective-permute-done.1.refs_2_, ...), custom_call_target="tpu_custom_call" | custom-call | flops 301989888 | bytes 1769472 | tf_op jit(solution)/shard_map/compact_parts/pallas_call | solution.py:164
  35.5 0.0 collective-permute-done.3.other_ref
  35.5 1.1 %spread_parts.1 = (bf16[576,512]{1,0:T(8,128)(2,1)S(1)}, bf16[576,256]{1,0:T(8,128)(2,1)S(1)}, bf16[576,384]{1,0:T(8,128)(2,1)}, bf16[576,384]{1,0:T(8,128)(2,1)}) custom-call(bf16[576,512]{1,0:T(8,128)(2,1)S(1)} %compact_parts.2.own_ref, bf16[576,512]{1,0:T(8,128)(2,1)S(1)} %collective-permute-done.3.other_ref), custom_call_target="tpu_custom_call" | custom-call | flops 294912 | bytes 2949120 | tf_op jit(solution)/shard_map/spread_parts/pallas_call | solution.py:189
  36.6 1.4 %collective-permute-start.4 = (bf16[576,512]{1,0:T(8,128)(2,1)S(1)}, bf16[576,512]{1,0:T(8,128)(2,1)S(1)}, u32[]{:S(2)}, u32[]{:S(2)}) collective-permute-start(bf16[576,512]{1,0:T(8,128)(2,1)S(1)} %get-tuple-element.24.keys_ref), channel_id=1, source_target_pairs={{0,4},{1,5},{2,6},{3,7},{4,8},{5,9},{6,10},{7,11},{8,12},{9,13},{1... | collective-permute-start | bytes 1769480 | tf_op jit(solution)/shard_map/ppermute | solution.py:424
  38.0 1.2 %collective-permute-start.6 = (bf16[576,384]{1,0:T(8,128)(2,1)}, bf16[576,384]{1,0:T(8,128)(2,1)S(1)}, u32[]{:S(2)}, u32[]{:S(2)}) collective-permute-start(bf16[576,384]{1,0:T(8,128)(2,1)} %get-tuple-element.30), channel_id=1, source_target_pairs={{0,1},{1,2},{2,3},{3,0},{4,5},{5,6},{6,7},{7,4},{8,9},{9,10},{10,1... | collective-permute-start | bytes 1327112 | tf_op jit(solution)/shard_map/ppermute | solution.py:425
  39.1 1.5 %collective-permute-start.7 = (bf16[576,384]{1,0:T(8,128)(2,1)}, bf16[576,384]{1,0:T(8,128)(2,1)S(1)}, u32[]{:S(2)}, u32[]{:S(2)}) collective-permute-start(bf16[576,384]{1,0:T(8,128)(2,1)} %get-tuple-element.31), channel_id=1, source_target_pairs={{0,3},{1,0},{2,1},{3,2},{4,7},{5,4},{6,5},{7,6},{8,11},{9,8},{10,9... | collective-permute-start | bytes 1327112 | tf_op jit(solution)/shard_map/ppermute | solution.py:426
  40.6 1.3 %collective-permute-start.5 = (bf16[576,256]{1,0:T(8,128)(2,1)S(1)}, bf16[576,256]{1,0:T(8,128)(2,1)}, u32[]{:S(2)}, u32[]{:S(2)}) collective-permute-start(bf16[576,256]{1,0:T(8,128)(2,1)S(1)} %get-tuple-element.29), channel_id=1, source_target_pairs={{0,12},{1,13},{2,14},{3,15},{4,0},{5,1},{6,2},{7,3},{8,4},{9,5},{1... | collective-permute-start | bytes 884744 | tf_op jit(solution)/shard_map/ppermute | solution.py:427
  42.0 0.0 copy-done.1
  42.0 0.0 copy-done.2
  42.0 0.0 copy-done.3
  42.0 6.6 %index_scores.1 = f32[64,2048]{1,0:T(8,128)} custom-call(bf16[64,64,128]{2,1,0:T(8,128)(2,1)S(1)} %copy-done.1, f32[64,64]{1,0:T(8,128)S(1)} %copy-done.3, bf16[2048,128]{1,0:T(8,128)(2,1)S(1)} %copy-done.2), custom_call_target="tpu_custom_call" | custom-call | flops 8589934592 | bytes 1572864 | tf_op jit(solution)/shard_map/index_scores/pallas_call | solution.py:244
  48.5 3.5 %all-to-all-done.packed_ref = bf16[16,288,128]{2,1,0:T(8,128)(2,1)S(1)} async-done(((bf16[16,288,128]{2,1,0:T(8,128)(2,1)}), bf16[16,288,128]{2,1,0:T(8,128)(2,1)S(1)}, u32[]{:S(2)}, u32[]{:S(2)}) %all-to-all-start) | async-done | bytes 1179680 | tf_op jit(solution)/shard_map/all_to_all | solution.py:418
  52.1 2.3 %attend_own.1 = (f32[1024,128]{1,0:T(8,128)S(1)}, f32[1024,128]{1,0:T(8,128)S(1)}, f32[1024,512]{1,0:T(8,128)S(1)}, bf16[1024,576]{1,0:T(8,128)(2,1)S(1)}) custom-call(s32[8,128]{1,0:T(8,128)} %get-tuple-element.17.past_ref, bf16[16,288,128]{2,1,0:T(8,128)(2,1)S(1)} %all-to-all-done.packed_ref, bf16[576,512]{1,0:T(8,128)(2,1)S(1)} %get-tuple-element.24.keys_ref), custom_call_target="tpu_custom_call" | custom-call | flops 1140850688 | bytes 4456448 | tf_op jit(solution)/shard_map/attend_own/pallas_call | solution.py:312
  54.3 0.7 %collective-permute-done.5.down_ref = bf16[576,256]{1,0:T(8,128)(2,1)} collective-permute-done((bf16[576,256]{1,0:T(8,128)(2,1)S(1)}, bf16[576,256]{1,0:T(8,128)(2,1)}, u32[]{:S(2)}, u32[]{:S(2)}) %collective-permute-start.5) | collective-permute-done | bytes 294944 | tf_op jit(solution)/shard_map/ppermute | solution.py:427
  55.1 5.2 %collective-permute-done.6.right_ref = bf16[576,384]{1,0:T(8,128)(2,1)S(1)} collective-permute-done((bf16[576,384]{1,0:T(8,128)(2,1)}, bf16[576,384]{1,0:T(8,128)(2,1)S(1)}, u32[]{:S(2)}, u32[]{:S(2)}) %collective-permute-start.6) | collective-permute-done | bytes 442400 | tf_op jit(solution)/shard_map/ppermute | solution.py:425
  60.2 0.0 collective-permute-done.7.left_ref
  60.2 2.2 %collective-permute-done.4.up_ref = bf16[576,512]{1,0:T(8,128)(2,1)S(1)} collective-permute-done((bf16[576,512]{1,0:T(8,128)(2,1)S(1)}, bf16[576,512]{1,0:T(8,128)(2,1)S(1)}, u32[]{:S(2)}, u32[]{:S(2)}) %collective-permute-start.4) | collective-permute-done | bytes 589856 | tf_op jit(solution)/shard_map/ppermute | solution.py:424
  62.5 6.6 %attend_rest.1 = bf16[1024,512]{1,0:T(8,128)(2,1)} custom-call(f32[1024,128]{1,0:T(8,128)S(1)} %get-tuple-element.25.top_ref, f32[1024,128]{1,0:T(8,128)S(1)} %get-tuple-element.26.total_ref, f32[1024,512]{1,0:T(8,128)S(1)} %get-tuple-element.27.mixed_ref, bf16[1024,576]{1,0:T(8,128)(2,1)S(1)} %get-tuple-element.28.q_ref, ...), custom_call_target="tpu_custom_call" | custom-call | flops 3422552064 | bytes 5505024 | tf_op jit(solution)/shard_map/attend_rest/pallas_call | solution.py:385
Async XLA Ops:
  4.2 20.4 %copy-start = (bf16[8,128,576]{1,2,0:T(8,128)(2,1)S(1)}, bf16[8,128,576]{1,2,0:T(8,128)(2,1)}, u32[]{:S(2)}) copy-start(bf16[8,128,576]{1,2,0:T(8,128)(2,1)} %param.7) | copy-start | bytes 3538948
  4.2 9.7 %collective-permute-start = (bf16[576,256]{1,0:T(8,128)(2,1)S(1)}, bf16[576,256]{1,0:T(8,128)(2,1)S(1)}, u32[]{:S(2)}, u32[]{:S(2)}) collective-permute-start(bf16[576,256]{1,0:T(8,128)(2,1)S(1)} %get-tuple-element.20), channel_id=1, source_target_pairs={{0,32},{16,48},{32,64},{48,80},{64,96},{80,112},{96,0},{112,16},{1... | collective-permute-start | bytes 884744 | tf_op jit(solution)/shard_map/ppermute | solution.py:415
  6.3 15.2 %collective-permute-start.1 = (bf16[576,256]{1,0:T(8,128)(2,1)S(1)}, bf16[576,256]{1,0:T(8,128)(2,1)S(1)}, u32[]{:S(2)}, u32[]{:S(2)}) collective-permute-start(bf16[576,256]{1,0:T(8,128)(2,1)S(1)} %get-tuple-element.21), channel_id=1, source_target_pairs={{0,64},{16,80},{32,96},{48,112},{64,0},{80,16},{96,32},{112,48},{1... | collective-permute-start | bytes 884744 | tf_op jit(solution)/shard_map/ppermute | solution.py:415
  8.8 12.7 %collective-permute-start.2 = (bf16[576,256]{1,0:T(8,128)(2,1)S(1)}, bf16[576,256]{1,0:T(8,128)(2,1)S(1)}, u32[]{:S(2)}, u32[]{:S(2)}) collective-permute-start(bf16[576,256]{1,0:T(8,128)(2,1)S(1)} %get-tuple-element.22), channel_id=1, source_target_pairs={{0,96},{16,112},{32,0},{48,16},{64,32},{80,48},{96,64},{112,80},{1... | collective-permute-start | bytes 884744 | tf_op jit(solution)/shard_map/ppermute | solution.py:415
  23.0 12.6 %collective-permute-start.3 = (bf16[576,512]{1,0:T(8,128)(2,1)S(1)}, bf16[576,512]{1,0:T(8,128)(2,1)S(1)}, u32[]{:S(2)}, u32[]{:S(2)}) collective-permute-start(bf16[576,512]{1,0:T(8,128)(2,1)S(1)} %compact_parts.3), channel_id=1, source_target_pairs={{0,16},{16,0},{32,48},{48,32},{64,80},{80,64},{96,112},{112,96},{1... | collective-permute-start | bytes 1769480 | tf_op jit(solution)/shard_map/ppermute | solution.py:421
  26.1 25.9 %all-to-all-start = ((bf16[16,288,128]{2,1,0:T(8,128)(2,1)}), bf16[16,288,128]{2,1,0:T(8,128)(2,1)S(1)}, u32[]{:S(2)}, u32[]{:S(2)}) async-start(bf16[16,288,128]{2,1,0:T(8,128)(2,1)} %q_by_group.1), calls=%async_computation | async-start | bytes 2359296 | tf_op jit(solution)/shard_map/all_to_all | solution.py:418
  33.9 8.0 %copy-start.1 = (bf16[64,64,128]{2,1,0:T(8,128)(2,1)S(1)}, bf16[64,64,128]{2,1,0:T(8,128)(2,1)}, u32[]{:S(2)}) copy-start(bf16[64,64,128]{2,1,0:T(8,128)(2,1)} %query_ref.1) | copy-start | bytes 3145732
  33.9 8.0 %copy-start.2 = (bf16[2048,128]{1,0:T(8,128)(2,1)S(1)}, bf16[2048,128]{1,0:T(8,128)(2,1)}, u32[]{:S(2)}) copy-start(bf16[2048,128]{1,0:T(8,128)(2,1)} %keys_ref.1) | copy-start | bytes 1572868
  33.9 8.0 %copy-start.3 = (f32[64,64]{1,0:T(8,128)S(1)}, f32[64,64]{1,0:T(8,128)}, u32[]{:S(2)}) copy-start(f32[64,64]{1,0:T(8,128)} %weight_ref.1) | copy-start | bytes 49156
  36.6 25.9 %collective-permute-start.4 = (bf16[576,512]{1,0:T(8,128)(2,1)S(1)}, bf16[576,512]{1,0:T(8,128)(2,1)S(1)}, u32[]{:S(2)}, u32[]{:S(2)}) collective-permute-start(bf16[576,512]{1,0:T(8,128)(2,1)S(1)} %get-tuple-element.24.keys_ref), channel_id=1, source_target_pairs={{0,4},{1,5},{2,6},{3,7},{4,8},{5,9},{6,10},{7,11},{8,12},{9,13},{1... | collective-permute-start | bytes 1769480 | tf_op jit(solution)/shard_map/ppermute | solution.py:424
  38.0 22.3 %collective-permute-start.6 = (bf16[576,384]{1,0:T(8,128)(2,1)}, bf16[576,384]{1,0:T(8,128)(2,1)S(1)}, u32[]{:S(2)}, u32[]{:S(2)}) collective-permute-start(bf16[576,384]{1,0:T(8,128)(2,1)} %get-tuple-element.30), channel_id=1, source_target_pairs={{0,1},{1,2},{2,3},{3,0},{4,5},{5,6},{6,7},{7,4},{8,9},{9,10},{10,1... | collective-permute-start | bytes 1327112 | tf_op jit(solution)/shard_map/ppermute | solution.py:425
  39.1 21.1 %collective-permute-start.7 = (bf16[576,384]{1,0:T(8,128)(2,1)}, bf16[576,384]{1,0:T(8,128)(2,1)S(1)}, u32[]{:S(2)}, u32[]{:S(2)}) collective-permute-start(bf16[576,384]{1,0:T(8,128)(2,1)} %get-tuple-element.31), channel_id=1, source_target_pairs={{0,3},{1,0},{2,1},{3,2},{4,7},{5,4},{6,5},{7,6},{8,11},{9,8},{10,9... | collective-permute-start | bytes 1327112 | tf_op jit(solution)/shard_map/ppermute | solution.py:426
  40.6 14.4 %collective-permute-start.5 = (bf16[576,256]{1,0:T(8,128)(2,1)S(1)}, bf16[576,256]{1,0:T(8,128)(2,1)}, u32[]{:S(2)}, u32[]{:S(2)}) collective-permute-start(bf16[576,256]{1,0:T(8,128)(2,1)S(1)} %get-tuple-element.29), channel_id=1, source_target_pairs={{0,12},{1,13},{2,14},{3,15},{4,0},{5,1},{6,2},{7,3},{8,4},{9,5},{1... | collective-permute-start | bytes 884744 | tf_op jit(solution)/shard_map/ppermute | solution.py:427

commit v13 on v11

--- a/solution.py
+++ b/solution.py
@@ -348,14 +348,25 @@
         + (None, of_second(-1), None)
         + (None, of_second(1), of_first(2))
     )
-    for i, ref in enumerate((up_ref, down_ref, right_ref, left_ref)):
-        keys_ref[:, i * 384 : (i + 1) * 384] = ref[...]
     rows, step = q_ref.shape[0], 512
+    fetches = [
+        pltpu.make_async_copy(ref, keys_ref.at[:, pl.ds(768 + i * 384, 384)], sems.at[rows // step + i])
+        for i, ref in enumerate((right_ref, left_ref))
+    ]
+    for fetch in fetches:
+        fetch.start()
+    keys_ref[:, :384] = up_ref[...]
+    keys_ref[:, 384:768] = down_ref[...]
     copies = []
 
     def scores_at(a):
         limit = past + a // 8 + (iota((step, 128), 0) >> 3)
-        return masked_scores(q_ref[a : a + step, :], keys_ref[...], tiles, limit)
+        q = q_ref[a : a + step, :]
+        near = masked_scores(q, keys_ref[:, :768], tiles[:6], limit)
+        if a == 0:
+            for fetch in fetches:
+                fetch.wait()
+        return jnp.concatenate([near, masked_scores(q, keys_ref[:, 768:], tiles[6:], limit)], axis=1)
 
     coming = scores_at(0)
     for a in range(0, rows, step):
@@ -387,12 +398,12 @@
     return pl.pallas_call(
         rest_kernel,
         out_shape=jax.ShapeDtypeStruct((rows, 512), BF16),
-        in_specs=[VMEM] * (4 + len(parts)),
+        in_specs=[VMEM] * 6 + [pl.BlockSpec(memory_space=pl.ANY)] * 2,
         out_specs=pl.BlockSpec(memory_space=pltpu.HBM),
         scratch_shapes=[
             pltpu.VMEM((width, count), BF16),
             pltpu.VMEM((rows, 512), BF16),
-            pltpu.SemaphoreType.DMA((rows // 512,)),
+            pltpu.SemaphoreType.DMA((rows // 512 + 2,)),
         ],
         cost_estimate=pl.CostEstimate(
             flops=2 * rows * count * (width + 512), bytes_accessed=rows * 5376, transcendentals=rows * count

time: 67.3 us -> 66.8 us (level)
  no operation moved by 1% of the time
where the time goes in v13:
time: 66.8 us; the launch traced here: 66.4 us
  Pallas kernels  24.5 us (37%)
  waiting for transfers between devices  20.6 us (31%)
  starting transfers between devices  20.4 us (31%)
  between operations  0.88 us (1%)
    ppermute x3, waiting for transfers between devices, body(): lax.ppermute(outgoing[d], 'ctx', turn(2 * d))  11.6 us
    all_to_all x1, starting transfers between devices, body(): lax.all_to_all(by_group, 'head', split_axis=0, concat_axis=0, tiled=True)  7.77 us
    pallas_call x1, Pallas kernels, index_scores_of(): pl.pallas_call(index_kernel, grid=(rows // step,), out_shape=jax.ShapeDty...  6.5 us
    pallas_call x1, Pallas kernels, attend_rest(): pl.pallas_call(rest_kernel, out_shape=jax.ShapeDtypeStruct((rows, 512), B...  6.05 us
    ppermute x3, starting transfers between devices, body(): lax.ppermute(outgoing[d], 'ctx', turn(2 * d))  5.7 us
    ppermute x4, waiting for transfers between devices, body(): lax.ppermute(part, 'head', line(*step))  5.4 us
    ppermute x4, starting transfers between devices, body(): lax.ppermute(part, 'head', line(*step))  5.35 us
    all_to_all x1, waiting for transfers between devices, body(): lax.all_to_all(by_group, 'head', split_axis=0, concat_axis=0, tiled=True)  3.58 us
  transfers between devices with their start and end apart: 9, of which 5 were waited for; matrix products, arithmetic and copies ran while one was open for 0% of the time, Pallas kernels for 20%

profile of v13, /device:TPU:1, one launch (start us, length us, event | category | flops | bytes accessed | tf_op | source)
XLA Modules:
  0.0 66.4 jit_solution(12445201014062211814)
XLA Ops:
  0.6 3.6 %gather_parts.1 = (bf16[576,256]{1,0:T(8,128)(2,1)}, bf16[576,256]{1,0:T(8,128)(2,1)S(1)}, bf16[576,256]{1,0:T(8,128)(2,1)S(1)}, bf16[576,256]{1,0:T(8,128)(2,1)...) custom-call(s32[8,32]{1,0:T(8,128)} %ids_hbm.1, s32[8]{0:T(128)} %counts_hbm.1, bf16[576,2048]{1,0:T(8,128)(2,1)} %bitcast.4), custom_call_target="tpu_custom_call" | custom-call | flops 2415919104 | bytes 4718592 | tf_op jit(solution)/shard_map/gather_parts/pallas_call | solution.py:128
  4.2 0.0 copy-start
  4.2 2.1 %collective-permute-start = (bf16[576,256]{1,0:T(8,128)(2,1)S(1)}, bf16[576,256]{1,0:T(8,128)(2,1)S(1)}, u32[]{:S(2)}, u32[]{:S(2)}) collective-permute-start(bf16[576,256]{1,0:T(8,128)(2,1)S(1)} %get-tuple-element.20), channel_id=1, source_target_pairs={{0,32},{16,48},{32,64},{48,80},{64,96},{80,112},{96,0},{112,16},{1... | collective-permute-start | bytes 884744 | tf_op jit(solution)/shard_map/ppermute | solution.py:428
  6.3 2.5 %collective-permute-start.1 = (bf16[576,256]{1,0:T(8,128)(2,1)S(1)}, bf16[576,256]{1,0:T(8,128)(2,1)S(1)}, u32[]{:S(2)}, u32[]{:S(2)}) collective-permute-start(bf16[576,256]{1,0:T(8,128)(2,1)S(1)} %get-tuple-element.21), channel_id=1, source_target_pairs={{0,64},{16,80},{32,96},{48,112},{64,0},{80,16},{96,32},{112,48},{1... | collective-permute-start | bytes 884744 | tf_op jit(solution)/shard_map/ppermute | solution.py:428
  8.8 1.2 %collective-permute-start.2 = (bf16[576,256]{1,0:T(8,128)(2,1)S(1)}, bf16[576,256]{1,0:T(8,128)(2,1)S(1)}, u32[]{:S(2)}, u32[]{:S(2)}) collective-permute-start(bf16[576,256]{1,0:T(8,128)(2,1)S(1)} %get-tuple-element.22), channel_id=1, source_target_pairs={{0,96},{16,112},{32,0},{48,16},{64,32},{80,48},{96,64},{112,80},{1... | collective-permute-start | bytes 884744 | tf_op jit(solution)/shard_map/ppermute | solution.py:428
  9.9 4.0 %collective-permute-done.refs_1_ = bf16[576,256]{1,0:T(8,128)(2,1)S(1)} collective-permute-done((bf16[576,256]{1,0:T(8,128)(2,1)S(1)}, bf16[576,256]{1,0:T(8,128)(2,1)S(1)}, u32[]{:S(2)}, u32[]{:S(2)}) %collective-permute-start) | collective-permute-done | bytes 294944 | tf_op jit(solution)/shard_map/ppermute | solution.py:428
  13.9 7.6 %collective-permute-done.1.refs_2_ = bf16[576,256]{1,0:T(8,128)(2,1)S(1)} collective-permute-done((bf16[576,256]{1,0:T(8,128)(2,1)S(1)}, bf16[576,256]{1,0:T(8,128)(2,1)S(1)}, u32[]{:S(2)}, u32[]{:S(2)}) %collective-permute-start.1) | collective-permute-done | bytes 294944 | tf_op jit(solution)/shard_map/ppermute | solution.py:428
  21.5 0.0 collective-permute-done.2.refs_3_
  21.5 1.5 %compact_parts.3 = bf16[576,512]{1,0:T(8,128)(2,1)S(1)} custom-call(s32[8,512]{1,0:T(8,128)} %get-tuple-element.23.source_ref, bf16[576,256]{1,0:T(8,128)(2,1)} %get-tuple-element.19.refs_0_, bf16[576,256]{1,0:T(8,128)(2,1)S(1)} %collective-permute-done.refs_1_, bf16[576,256]{1,0:T(8,128)(2,1)S(1)} %collective-permute-done.1.refs_2_, ...), custom_call_target="tpu_custom_call" | custom-call | flops 301989888 | bytes 1769472 | tf_op jit(solution)/shard_map/compact_parts/pallas_call | solution.py:164
  23.0 1.6 %collective-permute-start.3 = (bf16[576,512]{1,0:T(8,128)(2,1)S(1)}, bf16[576,512]{1,0:T(8,128)(2,1)S(1)}, u32[]{:S(2)}, u32[]{:S(2)}) collective-permute-start(bf16[576,512]{1,0:T(8,128)(2,1)S(1)} %compact_parts.3), channel_id=1, source_target_pairs={{0,16},{16,0},{32,48},{48,32},{64,80},{80,64},{96,112},{112,96},{1... | collective-permute-start | bytes 1769480 | tf_op jit(solution)/shard_map/ppermute | solution.py:434
  24.6 0.0 copy-done
  24.6 1.6 %q_by_group.1 = bf16[16,288,128]{2,1,0:T(8,128)(2,1)} custom-call(bf16[8,576,128]{2,1,0:T(8,128)(2,1)S(1)} %bitcast.3), custom_call_target="tpu_custom_call" | custom-call | bytes 2359296 | tf_op jit(solution)/shard_map/q_by_group/pallas_call | solution.py:216
  26.1 7.8 %all-to-all-start = ((bf16[16,288,128]{2,1,0:T(8,128)(2,1)}), bf16[16,288,128]{2,1,0:T(8,128)(2,1)S(1)}, u32[]{:S(2)}, u32[]{:S(2)}) async-start(bf16[16,288,128]{2,1,0:T(8,128)(2,1)} %q_by_group.1), calls=%async_computation | async-start | bytes 2359296 | tf_op jit(solution)/shard_map/all_to_all | solution.py:431
  33.9 0.0 copy-start.1
  33.9 0.0 copy-start.2
  33.9 0.0 copy-start.3
  33.9 1.6 %compact_parts.2.own_ref = bf16[576,512]{1,0:T(8,128)(2,1)S(1)} custom-call(s32[8,512]{1,0:T(8,128)} %get-tuple-element.18.source_ref, bf16[576,256]{1,0:T(8,128)(2,1)} %get-tuple-element.19.refs_0_, bf16[576,256]{1,0:T(8,128)(2,1)S(1)} %collective-permute-done.refs_1_, bf16[576,256]{1,0:T(8,128)(2,1)S(1)} %collective-permute-done.1.refs_2_, ...), custom_call_target="tpu_custom_call" | custom-call | flops 301989888 | bytes 1769472 | tf_op jit(solution)/shard_map/compact_parts/pallas_call | solution.py:164
  35.5 0.0 collective-permute-done.3.other_ref
  35.5 1.1 %spread_parts.1 = (bf16[576,384]{1,0:T(8,128)(2,1)}, bf16[576,384]{1,0:T(8,128)(2,1)}, bf16[576,384]{1,0:T(8,128)(2,1)S(1)}, bf16[576,384]{1,0:T(8,128)(2,1)S(1)}) custom-call(bf16[576,512]{1,0:T(8,128)(2,1)S(1)} %compact_parts.2.own_ref, bf16[576,512]{1,0:T(8,128)(2,1)S(1)} %collective-permute-done.3.other_ref), custom_call_target="tpu_custom_call" | custom-call | flops 294912 | bytes 2949120 | tf_op jit(solution)/shard_map/spread_parts/pallas_call | solution.py:190
  36.6 1.4 %collective-permute-start.4 = (bf16[576,384]{1,0:T(8,128)(2,1)}, bf16[576,384]{1,0:T(8,128)(2,1)S(1)}, u32[]{:S(2)}, u32[]{:S(2)}) collective-permute-start(bf16[576,384]{1,0:T(8,128)(2,1)} %get-tuple-element.24.up_ref), channel_id=1, source_target_pairs={{0,4},{1,5},{2,6},{3,7},{4,8},{5,9},{6,10},{7,11},{8,12},{9,13},{1... | collective-permute-start | bytes 1327112 | tf_op jit(solution)/shard_map/ppermute | solution.py:438
  38.0 1.3 %collective-permute-start.5 = (bf16[576,384]{1,0:T(8,128)(2,1)}, bf16[576,384]{1,0:T(8,128)(2,1)S(1)}, u32[]{:S(2)}, u32[]{:S(2)}) collective-permute-start(bf16[576,384]{1,0:T(8,128)(2,1)} %get-tuple-element.25.down_ref), channel_id=1, source_target_pairs={{0,12},{1,13},{2,14},{3,15},{4,0},{5,1},{6,2},{7,3},{8,4},{9,5},{1... | collective-permute-start | bytes 1327112 | tf_op jit(solution)/shard_map/ppermute | solution.py:438
  39.3 1.4 %collective-permute-start.6 = (bf16[576,384]{1,0:T(8,128)(2,1)S(1)}, bf16[576,384]{1,0:T(8,128)(2,1)S(1)}, u32[]{:S(2)}, u32[]{:S(2)}) collective-permute-start(bf16[576,384]{1,0:T(8,128)(2,1)S(1)} %get-tuple-element.30), channel_id=1, source_target_pairs={{0,1},{1,2},{2,3},{3,0},{4,5},{5,6},{6,7},{7,4},{8,9},{9,10},{10,1... | collective-permute-start | bytes 1327112 | tf_op jit(solution)/shard_map/ppermute | solution.py:438
  40.7 1.3 %collective-permute-start.7 = (bf16[576,384]{1,0:T(8,128)(2,1)S(1)}, bf16[576,384]{1,0:T(8,128)(2,1)}, u32[]{:S(2)}, u32[]{:S(2)}) collective-permute-start(bf16[576,384]{1,0:T(8,128)(2,1)S(1)} %get-tuple-element.31), channel_id=1, source_target_pairs={{0,3},{1,0},{2,1},{3,2},{4,7},{5,4},{6,5},{7,6},{8,11},{9,8},{10,9... | collective-permute-start | bytes 1327112 | tf_op jit(solution)/shard_map/ppermute | solution.py:438
  42.0 0.0 copy-done.1
  42.0 0.0 copy-done.2
  42.0 0.0 copy-done.3
  42.0 6.5 %index_scores.1 = f32[64,2048]{1,0:T(8,128)} custom-call(bf16[64,64,128]{2,1,0:T(8,128)(2,1)S(1)} %copy-done.1, f32[64,64]{1,0:T(8,128)S(1)} %copy-done.3, bf16[2048,128]{1,0:T(8,128)(2,1)S(1)} %copy-done.2), custom_call_target="tpu_custom_call" | custom-call | flops 8589934592 | bytes 1572864 | tf_op jit(solution)/shard_map/index_scores/pallas_call | solution.py:245
  48.5 3.6 %all-to-all-done.packed_ref = bf16[16,288,128]{2,1,0:T(8,128)(2,1)S(1)} async-done(((bf16[16,288,128]{2,1,0:T(8,128)(2,1)}), bf16[16,288,128]{2,1,0:T(8,128)(2,1)S(1)}, u32[]{:S(2)}, u32[]{:S(2)}) %all-to-all-start) | async-done | bytes 1179680 | tf_op jit(solution)/shard_map/all_to_all | solution.py:431
  52.1 2.8 %attend_own.1 = (f32[1024,128]{1,0:T(8,128)S(1)}, f32[1024,128]{1,0:T(8,128)S(1)}, f32[1024,512]{1,0:T(8,128)S(1)}, bf16[1024,576]{1,0:T(8,128)(2,1)S(1)}) custom-call(s32[8,128]{1,0:T(8,128)} %get-tuple-element.17.past_ref, bf16[16,288,128]{2,1,0:T(8,128)(2,1)S(1)} %all-to-all-done.packed_ref, bf16[576,384]{1,0:T(8,128)(2,1)} %get-tuple-element.24.up_ref, ...), custom_call_target="tpu_custom_call" | custom-call | flops 1140850688 | bytes 4456448 | tf_op jit(solution)/shard_map/attend_own/pallas_call | solution.py:315
  54.8 4.5 %collective-permute-done.4.up_ref = bf16[576,384]{1,0:T(8,128)(2,1)S(1)} collective-permute-done((bf16[576,384]{1,0:T(8,128)(2,1)}, bf16[576,384]{1,0:T(8,128)(2,1)S(1)}, u32[]{:S(2)}, u32[]{:S(2)}) %collective-permute-start.4) | collective-permute-done | bytes 442400 | tf_op jit(solution)/shard_map/ppermute | solution.py:438
  59.3 0.0 collective-permute-done.5.down_ref
  59.3 0.9 %collective-permute-done.6.right_ref = bf16[576,384]{1,0:T(8,128)(2,1)S(1)} collective-permute-done((bf16[576,384]{1,0:T(8,128)(2,1)S(1)}, bf16[576,384]{1,0:T(8,128)(2,1)S(1)}, u32[]{:S(2)}, u32[]{:S(2)}) %collective-permute-start.6) | collective-permute-done | bytes 442400 | tf_op jit(solution)/shard_map/ppermute | solution.py:438
  60.2 0.0 collective-permute-done.7.left_ref
  60.2 6.0 %attend_rest.1 = bf16[1024,512]{1,0:T(8,128)(2,1)} custom-call(f32[1024,128]{1,0:T(8,128)S(1)} %get-tuple-element.26.top_ref, f32[1024,128]{1,0:T(8,128)S(1)} %get-tuple-element.27.total_ref, f32[1024,512]{1,0:T(8,128)S(1)} %get-tuple-element.28.mixed_ref, bf16[1024,576]{1,0:T(8,128)(2,1)S(1)} %get-tuple-element.29.q_ref, ...), custom_call_target="tpu_custom_call" | custom-call | flops 3422552064 | bytes 5505024 | tf_op jit(solution)/shard_map/attend_rest/pallas_call | solution.py:398
Async XLA Ops:
  4.2 20.4 %copy-start = (bf16[8,128,576]{1,2,0:T(8,128)(2,1)S(1)}, bf16[8,128,576]{1,2,0:T(8,128)(2,1)}, u32[]{:S(2)}) copy-start(bf16[8,128,576]{1,2,0:T(8,128)(2,1)} %param.7) | copy-start | bytes 3538948
  4.2 9.7 %collective-permute-start = (bf16[576,256]{1,0:T(8,128)(2,1)S(1)}, bf16[576,256]{1,0:T(8,128)(2,1)S(1)}, u32[]{:S(2)}, u32[]{:S(2)}) collective-permute-start(bf16[576,256]{1,0:T(8,128)(2,1)S(1)} %get-tuple-element.20), channel_id=1, source_target_pairs={{0,32},{16,48},{32,64},{48,80},{64,96},{80,112},{96,0},{112,16},{1... | collective-permute-start | bytes 884744 | tf_op jit(solution)/shard_map/ppermute | solution.py:428
  6.3 15.2 %collective-permute-start.1 = (bf16[576,256]{1,0:T(8,128)(2,1)S(1)}, bf16[576,256]{1,0:T(8,128)(2,1)S(1)}, u32[]{:S(2)}, u32[]{:S(2)}) collective-permute-start(bf16[576,256]{1,0:T(8,128)(2,1)S(1)} %get-tuple-element.21), channel_id=1, source_target_pairs={{0,64},{16,80},{32,96},{48,112},{64,0},{80,16},{96,32},{112,48},{1... | collective-permute-start | bytes 884744 | tf_op jit(solution)/shard_map/ppermute | solution.py:428
  8.8 12.7 %collective-permute-start.2 = (bf16[576,256]{1,0:T(8,128)(2,1)S(1)}, bf16[576,256]{1,0:T(8,128)(2,1)S(1)}, u32[]{:S(2)}, u32[]{:S(2)}) collective-permute-start(bf16[576,256]{1,0:T(8,128)(2,1)S(1)} %get-tuple-element.22), channel_id=1, source_target_pairs={{0,96},{16,112},{32,0},{48,16},{64,32},{80,48},{96,64},{112,80},{1... | collective-permute-start | bytes 884744 | tf_op jit(solution)/shard_map/ppermute | solution.py:428
  23.0 12.6 %collective-permute-start.3 = (bf16[576,512]{1,0:T(8,128)(2,1)S(1)}, bf16[576,512]{1,0:T(8,128)(2,1)S(1)}, u32[]{:S(2)}, u32[]{:S(2)}) collective-permute-start(bf16[576,512]{1,0:T(8,128)(2,1)S(1)} %compact_parts.3), channel_id=1, source_target_pairs={{0,16},{16,0},{32,48},{48,32},{64,80},{80,64},{96,112},{112,96},{1... | collective-permute-start | bytes 1769480 | tf_op jit(solution)/shard_map/ppermute | solution.py:434
  26.1 25.9 %all-to-all-start = ((bf16[16,288,128]{2,1,0:T(8,128)(2,1)}), bf16[16,288,128]{2,1,0:T(8,128)(2,1)S(1)}, u32[]{:S(2)}, u32[]{:S(2)}) async-start(bf16[16,288,128]{2,1,0:T(8,128)(2,1)} %q_by_group.1), calls=%async_computation | async-start | bytes 2359296 | tf_op jit(solution)/shard_map/all_to_all | solution.py:431
  33.9 8.1 %copy-start.1 = (bf16[64,64,128]{2,1,0:T(8,128)(2,1)S(1)}, bf16[64,64,128]{2,1,0:T(8,128)(2,1)}, u32[]{:S(2)}) copy-start(bf16[64,64,128]{2,1,0:T(8,128)(2,1)} %query_ref.1) | copy-start | bytes 3145732
  33.9 8.1 %copy-start.2 = (bf16[2048,128]{1,0:T(8,128)(2,1)S(1)}, bf16[2048,128]{1,0:T(8,128)(2,1)}, u32[]{:S(2)}) copy-start(bf16[2048,128]{1,0:T(8,128)(2,1)} %keys_ref.1) | copy-start | bytes 1572868
  33.9 8.0 %copy-start.3 = (f32[64,64]{1,0:T(8,128)S(1)}, f32[64,64]{1,0:T(8,128)}, u32[]{:S(2)}) copy-start(f32[64,64]{1,0:T(8,128)} %weight_ref.1) | copy-start | bytes 49156
  36.6 22.7 %collective-permute-start.4 = (bf16[576,384]{1,0:T(8,128)(2,1)}, bf16[576,384]{1,0:T(8,128)(2,1)S(1)}, u32[]{:S(2)}, u32[]{:S(2)}) collective-permute-start(bf16[576,384]{1,0:T(8,128)(2,1)} %get-tuple-element.24.up_ref), channel_id=1, source_target_pairs={{0,4},{1,5},{2,6},{3,7},{4,8},{5,9},{6,10},{7,11},{8,12},{9,13},{1... | collective-permute-start | bytes 1327112 | tf_op jit(solution)/shard_map/ppermute | solution.py:438
  38.0 21.3 %collective-permute-start.5 = (bf16[576,384]{1,0:T(8,128)(2,1)}, bf16[576,384]{1,0:T(8,128)(2,1)S(1)}, u32[]{:S(2)}, u32[]{:S(2)}) collective-permute-start(bf16[576,384]{1,0:T(8,128)(2,1)} %get-tuple-element.25.down_ref), channel_id=1, source_target_pairs={{0,12},{1,13},{2,14},{3,15},{4,0},{5,1},{6,2},{7,3},{8,4},{9,5},{1... | collective-permute-start | bytes 1327112 | tf_op jit(solution)/shard_map/ppermute | solution.py:438
  39.3 20.9 %collective-permute-start.6 = (bf16[576,384]{1,0:T(8,128)(2,1)S(1)}, bf16[576,384]{1,0:T(8,128)(2,1)S(1)}, u32[]{:S(2)}, u32[]{:S(2)}) collective-permute-start(bf16[576,384]{1,0:T(8,128)(2,1)S(1)} %get-tuple-element.30), channel_id=1, source_target_pairs={{0,1},{1,2},{2,3},{3,0},{4,5},{5,6},{6,7},{7,4},{8,9},{9,10},{10,1... | collective-permute-start | bytes 1327112 | tf_op jit(solution)/shard_map/ppermute | solution.py:438
  40.7 19.6 %collective-permute-start.7 = (bf16[576,384]{1,0:T(8,128)(2,1)S(1)}, bf16[576,384]{1,0:T(8,128)(2,1)}, u32[]{:S(2)}, u32[]{:S(2)}) collective-permute-start(bf16[576,384]{1,0:T(8,128)(2,1)S(1)} %get-tuple-element.31), channel_id=1, source_target_pairs={{0,3},{1,0},{2,1},{3,2},{4,7},{5,4},{6,5},{7,6},{8,11},{9,8},{10,9... | collective-permute-start | bytes 1327112 | tf_op jit(solution)/shard_map/ppermute | solution.py:438
